TPU v7x, 32 devices: a whole 2x2x4 slice. The times are simulated.
32 devices in a mesh: dp: 2 (over x), row: 4 (over z), col: 4 (over y, core).
Axes of the slice: x: 2, y: 2, z: 4, core: 2. Of those that a mesh axis runs over, the one named last changes fastest.
Arguments:
- layer_in: bfloat16 [16384, 1024], P(('dp', 'col'), 'row'), may hold values from -6 to 6
- first_gain: bfloat16 [1024], P('row'), may hold values from 0.099609375 to 1.8984375
- first_shift: bfloat16 [1024], P('row'), may hold values from -4 to 4
- joined_weight: bfloat16 [1024, 3072], P('row', 'col'), may hold values from -0.1875 to 0.1875
- joined_bias: bfloat16 [16, 128], P('col'), may hold values from -6 to 6
- out_weight: bfloat16 [1024, 1024], P('col', 'row'), may hold values from -0.75 to 0.75
- out_bias: bfloat16 [1024], P('row'), may hold values from -4 to 4
- second_gain: bfloat16 [1024], P('row'), may hold values from 0.099609375 to 1.8984375
- second_shift: bfloat16 [1024], P('row'), may hold values from -4 to 4
- up_weight: bfloat16 [1024, 4096], P('row', 'col'), may hold values from -0.1875 to 0.1875
- up_bias: bfloat16 [4096], P('col'), may hold values from -6 to 6
- down_weight: bfloat16 [4096, 1024], P('col', 'row'), may hold values from -0.09375 to 0.09375
- down_bias: bfloat16 [1024], P('row'), may hold values from -4 to 4
- teacher: bfloat16 [16384, 1024], P(('dp', 'col'), 'row'), may hold values from -6 to 6
- valid: int32 [16384], P(('dp', 'col')), may hold values from 0 to 1, as said below
- cotangent: bfloat16 [16384, 1024], P(('dp', 'col'), 'row'), may hold values from -6 to 6
Outputs:
- layer_out: bfloat16 [16384, 1024], P(('dp', 'col'), 'row')
- loss: float32 [], replicated
- input_grad: float32 [16384, 1024], P(('dp', 'col'), 'row')
- first_gain_grad: float32 [1024], P('row')
- first_shift_grad: float32 [1024], P('row')
- joined_weight_grad: float32 [1024, 3072], P('row', 'col')
- joined_bias_grad: float32 [16, 128], P('col')
- out_weight_grad: float32 [1024, 1024], P('col', 'row')
- out_bias_grad: float32 [1024], P('row')
- second_gain_grad: float32 [1024], P('row')
- second_shift_grad: float32 [1024], P('row')
- up_weight_grad: float32 [1024, 4096], P('row', 'col')
- up_bias_grad: float32 [4096], P('col')
- down_weight_grad: float32 [4096, 1024], P('col', 'row')
- down_bias_grad: float32 [1024], P('row')
Inputs may be any that keep to these rules, and one draw needn't show every extreme that they name: The last token is valid.
All inputs are finite; a program needn't handle non-finite values.
Results may differ from a plain program's by a relative error of at most 0.013.
Values may be sent and summed in bfloat16 or wider, within the bound.
A program may use at most 192 MiB of HBM per device.

v0:
```python
import math

import jax
import jax.numpy as jnp
from jax import lax
from jax.sharding import PartitionSpec as P

D = 1024
HEADS = 16
HEAD_DIM = 64
SEQ = 2048
BLOCK = 256
QUERY_ROWS = 512


EPSILON = 1e-05


def spread_col(local_rows):
    return lax.all_gather(local_rows, "col", axis=0, tiled=True)


def spread_row(local_rows):
    return lax.all_gather(local_rows, "row", axis=0, tiled=True)


def feature_totals(first_sum, second):
    return lax.psum((first_sum, second), "row")


def product_term(left_side, right_side, flipped):
    if flipped:
        return lax.dot_general(
            left_side, right_side, (((1,), (1,)), ((), ())), preferred_element_type=jnp.float32
        )
    return jnp.dot(left_side, right_side, preferred_element_type=jnp.float32)


def sum_over_row(left_side, right_side, flipped):
    return lax.psum_scatter(
        product_term(left_side, right_side, flipped), "row", scatter_dimension=0, tiled=True
    )


def sum_over_col(left_side, right_side, flipped):
    return lax.psum_scatter(
        product_term(left_side, right_side, flipped).astype(jnp.bfloat16),
        "col",
        scatter_dimension=0,
        tiled=True,
    ).astype(jnp.float32)


def weight_grad(left_side, right_side):
    return lax.dot_general(
        left_side, right_side, (((0,), (0,)), ((), ())), preferred_element_type=jnp.float32
    )


def norm_forward(inputs, norm_gain, norm_shift):
    first_sum, second = feature_totals(jnp.sum(inputs, 1), jnp.sum(inputs * inputs, 1))
    center = first_sum / D
    spread = second / D - center * center
    inverse = lax.rsqrt(spread + EPSILON)
    standard = (inputs - center[:, None]) * inverse[:, None]
    return (standard, inverse, standard * norm_gain + norm_shift)


def norm_backward(grad_normed, standard, inverse, norm_gain):
    scaled = grad_normed * norm_gain
    first_sum, second = feature_totals(jnp.sum(scaled, 1), jnp.sum(scaled * standard, 1))
    return inverse[:, None] * (scaled - first_sum[:, None] / D - standard * (second[:, None] / D))


def gelu_local(before):
    return jax.nn.gelu(before, approximate=True)


def placed_scores(queries, key_rows, first_place, slopes):
    plain_scores = jnp.einsum(
        "qhd,khd->hqk", queries, key_rows, preferred_element_type=jnp.float32
    ) * (1.0 / math.sqrt(HEAD_DIM))
    query_place = first_place + jnp.arange(queries.shape[0], dtype=jnp.int32)
    key_place = jnp.arange(key_rows.shape[0], dtype=jnp.int32)
    distance = jnp.abs(query_place[:, None] - key_place[None, :]).astype(jnp.float32)
    allowed = key_place[None, :] // BLOCK <= query_place[:, None] // BLOCK
    return jnp.where(
        allowed[None], plain_scores - slopes[:, None, None] * distance[None], -1000000000.0
    )


def masked_scores(queries, key_rows, block_index, slopes):
    return placed_scores(queries, key_rows, block_index * QUERY_ROWS, slopes)


def attention_forward(mixed_low, slopes):
    row_count = mixed_low.shape[0]
    head_count = slopes.shape[0]
    sequences = mixed_low.reshape(row_count // SEQ, SEQ, head_count, 3, HEAD_DIM)

    def one_sequence(sequence):

        def one_block(block_index):
            queries = lax.dynamic_slice_in_dim(
                sequence[:, :, 0], block_index * QUERY_ROWS, QUERY_ROWS, 0
            )
            scores = masked_scores(queries, sequence[:, :, 1], block_index, slopes)
            highest = jnp.max(scores, -1, keepdims=True)
            exponent = jnp.exp(scores - highest)
            totals = jnp.sum(exponent, -1, keepdims=True)
            chances = (exponent / totals).astype(jnp.bfloat16)
            block_out = jnp.einsum(
                "hqk,khd->qhd", chances, sequence[:, :, 2], preferred_element_type=jnp.float32
            )
            return (block_out, (highest + jnp.log(totals))[..., 0])

        return lax.map(one_block, jnp.arange(SEQ // QUERY_ROWS, dtype=jnp.int32))

    attended, log_totals = lax.map(one_sequence, sequences)
    return (attended.reshape(row_count, head_count * HEAD_DIM), log_totals)


def attention_backward(mixed_low, grad_low, log_totals, slopes):
    row_count = mixed_low.shape[0]
    head_count = slopes.shape[0]
    sequences = mixed_low.reshape(row_count // SEQ, SEQ, head_count, 3, HEAD_DIM)
    grad_rows = grad_low.reshape(row_count // SEQ, SEQ, head_count, HEAD_DIM)
    factor = 1.0 / math.sqrt(HEAD_DIM)

    def one_sequence(pieces):
        sequence, grad_sequence, sequence_totals = pieces
        key_rows = sequence[:, :, 1]
        value_rows = sequence[:, :, 2]

        def one_block(running, block_index):
            key_grad, value_grad = running
            queries = lax.dynamic_slice_in_dim(
                sequence[:, :, 0], block_index * QUERY_ROWS, QUERY_ROWS, 0
            )
            grad_block = lax.dynamic_slice_in_dim(
                grad_sequence, block_index * QUERY_ROWS, QUERY_ROWS, 0
            )
            scores = masked_scores(queries, key_rows, block_index, slopes)
            chances = jnp.exp(scores - sequence_totals[block_index][..., None])
            value_grad = value_grad + jnp.einsum(
                "hqk,qhd->khd",
                chances.astype(jnp.bfloat16),
                grad_block,
                preferred_element_type=jnp.float32,
            )
            grad_chances = jnp.einsum(
                "qhd,khd->hqk", grad_block, value_rows, preferred_element_type=jnp.float32
            )
            inner_sum = jnp.sum(chances * grad_chances, -1, keepdims=True)
            score_grad = (chances * (grad_chances - inner_sum)).astype(jnp.bfloat16)
            query_grad = (
                jnp.einsum("hqk,khd->qhd", score_grad, key_rows, preferred_element_type=jnp.float32)
                * factor
            )
            key_grad = (
                key_grad
                + jnp.einsum(
                    "hqk,qhd->khd", score_grad, queries, preferred_element_type=jnp.float32
                )
                * factor
            )
            return ((key_grad, value_grad), query_grad)

        zero_block = jnp.zeros((SEQ, head_count, HEAD_DIM), jnp.float32)
        (key_grad, value_grad), query_grad = lax.scan(
            one_block, (zero_block, zero_block), jnp.arange(SEQ // QUERY_ROWS, dtype=jnp.int32)
        )
        return jnp.stack(
            [query_grad.reshape(SEQ, head_count, HEAD_DIM), key_grad, value_grad], axis=2
        )

    all_grads = lax.map(one_sequence, (sequences, grad_rows, log_totals))
    return all_grads.reshape(row_count, head_count * 3 * HEAD_DIM)


def on_device(
    layer_in,
    first_gain,
    first_shift,
    joined_weight,
    joined_bias,
    out_weight,
    out_bias,
    second_gain,
    second_shift,
    up_weight,
    up_bias,
    down_weight,
    down_bias,
    teacher,
    valid,
    cotangent,
):
    row_size = lax.axis_size("row")
    col_size = lax.axis_size("col")
    token_rows = layer_in.shape[0]
    head_count = joined_bias.shape[0]
    head_index = lax.axis_index("col") * head_count + jnp.arange(head_count, dtype=jnp.int32)
    slopes = jnp.exp2(-8.0 * (head_index.astype(jnp.float32) + 1.0) / HEADS)
    zero_rows = jnp.zeros_like(joined_bias[:, :HEAD_DIM])
    bias_rows = jnp.stack(
        [joined_bias[:, :HEAD_DIM], zero_rows, joined_bias[:, HEAD_DIM:]], axis=1
    ).reshape(-1)
    inputs = layer_in.astype(jnp.float32)
    standard_one, inverse_one, normed = norm_forward(inputs, first_gain, first_shift)
    normed_one = normed.astype(jnp.bfloat16)
    normed_one_all = spread_col(normed_one)
    mixed_rows = sum_over_row(normed_one_all, joined_weight, False) + bias_rows
    mixed_low = mixed_rows.astype(jnp.bfloat16)
    attended, log_totals = attention_forward(mixed_low, slopes)
    attended_low = attended.astype(jnp.bfloat16)
    attended_all = spread_row(attended_low)
    middle = inputs + (sum_over_col(attended_all, out_weight, False) + out_bias)
    standard_two, inverse_two, normed = norm_forward(middle, second_gain, second_shift)
    normed_two = normed.astype(jnp.bfloat16)
    normed_two_all = spread_col(normed_two)
    before = sum_over_row(normed_two_all, up_weight, False) + up_bias
    active, gelu_pull = jax.vjp(gelu_local, before)
    active_low = active.astype(jnp.bfloat16)
    active_all = spread_row(active_low)
    result = middle + (sum_over_col(active_all, down_weight, False) + down_bias)
    error_rows = result - teacher.astype(jnp.float32)
    valid_rows = valid.astype(jnp.float32)[:, None]
    error_sum, valid_count = lax.psum(
        (jnp.sum(valid_rows * error_rows * error_rows), jnp.sum(valid_rows) / row_size),
        ("dp", "row", "col"),
    )
    loss_value = error_sum / (D * valid_count)
    token_total = token_rows * lax.axis_size("dp") * col_size
    grad_result = cotangent.astype(jnp.float32) + valid_rows * error_rows * (
        token_total / valid_count
    )
    grad_low = grad_result.astype(jnp.bfloat16)
    down_bias_grad = jnp.sum(grad_low, 0, dtype=jnp.float32)
    grad_all = spread_col(grad_low)
    down_grad = weight_grad(active_all, grad_all)
    grad_active = sum_over_row(grad_all, down_weight, True)
    grad_before = gelu_pull(grad_active)[0].astype(jnp.bfloat16)
    grad_before_all = spread_row(grad_before)
    up_grad = weight_grad(normed_two_all, grad_before_all)
    up_bias_grad = jnp.sum(grad_before_all, 0, dtype=jnp.float32)
    grad_normed_two = sum_over_col(grad_before_all, up_weight, True)
    grad_middle = grad_result + norm_backward(
        grad_normed_two, standard_two, inverse_two, second_gain
    )
    second_gain_grad = jnp.sum(grad_normed_two * standard_two, 0)
    second_shift_grad = jnp.sum(grad_normed_two, 0)
    branch_grad = grad_middle.astype(jnp.bfloat16)
    out_bias_grad = jnp.sum(branch_grad, 0, dtype=jnp.float32)
    branch_all = spread_col(branch_grad)
    out_grad = weight_grad(attended_all, branch_all)
    attended_grad = sum_over_row(branch_all, out_weight, True).astype(jnp.bfloat16)
    mixed_grad = attention_backward(mixed_low, attended_grad, log_totals, slopes).astype(
        jnp.bfloat16
    )
    mixed_grad_all = spread_row(mixed_grad)
    joined_grad = weight_grad(normed_one_all, mixed_grad_all)
    column_sums = jnp.sum(mixed_grad_all, 0, dtype=jnp.float32).reshape(head_count, 3, HEAD_DIM)
    joined_bias_grad = jnp.concatenate([column_sums[:, 0], column_sums[:, 2]], axis=1)
    grad_normed_one = sum_over_col(mixed_grad_all, joined_weight, True)
    input_grad = grad_middle + norm_backward(grad_normed_one, standard_one, inverse_one, first_gain)
    first_gain_grad = jnp.sum(grad_normed_one * standard_one, 0)
    first_shift_grad = jnp.sum(grad_normed_one, 0)
    joined_grad, joined_bias_grad, out_grad, up_grad, up_bias_grad, down_grad = (
        lax.psum(joined_grad.astype(jnp.bfloat16), "dp").astype(jnp.float32),
        lax.psum(joined_bias_grad.astype(jnp.bfloat16), "dp").astype(jnp.float32),
        lax.psum(out_grad.astype(jnp.bfloat16), "dp").astype(jnp.float32),
        lax.psum(up_grad.astype(jnp.bfloat16), "dp").astype(jnp.float32),
        lax.psum(up_bias_grad.astype(jnp.bfloat16), "dp").astype(jnp.float32),
        lax.psum(down_grad.astype(jnp.bfloat16), "dp").astype(jnp.float32),
    )
    (
        first_gain_grad,
        first_shift_grad,
        out_bias_grad,
        second_gain_grad,
        second_shift_grad,
        down_bias_grad,
    ) = lax.psum(
        (
            first_gain_grad,
            first_shift_grad,
            out_bias_grad,
            second_gain_grad,
            second_shift_grad,
            down_bias_grad,
        ),
        ("dp", "col"),
    )
    return (
        result.astype(jnp.bfloat16),
        loss_value,
        input_grad,
        first_gain_grad,
        first_shift_grad,
        joined_grad,
        joined_bias_grad,
        out_grad,
        out_bias_grad,
        second_gain_grad,
        second_shift_grad,
        up_grad,
        up_bias_grad,
        down_grad,
        down_bias_grad,
    )


def solution(mesh):
    return jax.shard_map(
        on_device,
        mesh=mesh,
        in_specs=(
            P(("dp", "col"), "row"),
            P("row"),
            P("row"),
            P("row", "col"),
            P("col", None),
            P("col", "row"),
            P("row"),
            P("row"),
            P("row"),
            P("row", "col"),
            P("col"),
            P("col", "row"),
            P("row"),
            P(("dp", "col"), "row"),
            P(("dp", "col")),
            P(("dp", "col"), "row"),
        ),
        out_specs=(
            P(("dp", "col"), "row"),
            P(),
            P(("dp", "col"), "row"),
            P("row"),
            P("row"),
            P("row", "col"),
            P("col", None),
            P("col", "row"),
            P("row"),
            P("row"),
            P("row"),
            P("row", "col"),
            P("col"),
            P("col", "row"),
            P("row"),
        ),
        check_vma=False,
    )
```

profile of v0, /device:TPU:13, one launch (start us, length us, event | category | flops | bytes accessed | tf_op | source)
XLA Modules:
  0.0 3505.2 jit_solution(7357203540020591849)
XLA Ops:
  10.5 11.9 all-reduce.4
  25.7 39.3 %all-gather.9.cloned.1.call-done = bf16[8192,256]{1,0:T(8,128)(2,1)} async-done(((bf16[2048,256]{1,0:T(8,128)(2,1)}), bf16[8192,256]{1,0:T(8,128)(2,1)}) %all-gather.9.cloned.1.call-update) | async-done | bytes 4194320 | tf_op jit(solution)/shard_map/all_gather | solution.py:20
  64.9 13.9 fusion.91
  79.8 414.0 %reduce-scatter.9.cloned.1.call-done = f32[2048,768]{1,0:T(8,128)} async-done(((f32[8192,768]{1,0:T(8,128)}), f32[2048,768]{1,0:T(8,128)}) %reduce-scatter.9.cloned.1.call-update) | async-done | bytes 6291472 | tf_op jit(solution)/shard_map/reduce_scatter | solution.py:40
  508.5 103.5 %while.52 = (s32[]{:T(128)}, bf16[4,512,4,64]{1,3,2,0:T(8,128)(2,1)}, f32[4,4,512]{2,1,0:T(4,128)S(1)}, s32[4]{0:T(128)S(1)}, bf16[2048,4,3,64]{0,3,1,2:T(8,128)...) while((s32[]{:T(128)}, bf16[4,512,4,64]{1,3,2,0:T(8,128)(2,1)}, ...), condition=%wide.region_8.9_spmd.clone, body=%wide.region_5.8_spmd.clone.sunk | while | flops 1153456128 | bytes 109929272 | solution.py:117
  524.6 10.1 fusion.144
  550.3 10.1 fusion.144
  576.0 10.1 fusion.144
  601.7 10.1 fusion.144
  615.4 80.5 %all-gather.11.cloned.1.call-done = bf16[8192,256]{0,1:T(8,128)(2,1)} async-done(((bf16[2048,256]{0,1:T(8,128)(2,1)}), bf16[8192,256]{0,1:T(8,128)(2,1)}) %all-gather.11.cloned.1.call-update) | async-done | bytes 4194320 | tf_op jit(solution)/shard_map/all_gather | solution.py:24
  702.0 44.0 %reduce-scatter.11.cloned.1.call-done = bf16[2048,256]{1,0:T(8,128)(2,1)} async-done(((bf16[8192,256]{1,0:T(8,128)(2,1)}), bf16[2048,256]{1,0:T(8,128)(2,1)}) %reduce-scatter.11.cloned.1.call-update) | async-done | bytes 1048592 | tf_op jit(solution)/shard_map/reduce_scatter | solution.py:46
  748.0 11.7 all-reduce.3
  762.3 39.2 %all-gather.13.cloned.1.call-done = bf16[8192,256]{1,0:T(8,128)(2,1)} async-done(((bf16[2048,256]{1,0:T(8,128)(2,1)}), bf16[8192,256]{1,0:T(8,128)(2,1)}) %all-gather.13.cloned.1.call-update) | async-done | bytes 4194320 | tf_op jit(solution)/shard_map/all_gather | solution.py:20
  801.6 15.3 fusion.92
  817.6 549.1 %reduce-scatter.13.cloned.1.call-done = f32[2048,1024]{1,0:T(8,128)} async-done(((f32[8192,1024]{1,0:T(8,128)}), f32[2048,1024]{1,0:T(8,128)}) %reduce-scatter.13.cloned.1.call-update) | async-done | bytes 8388624 | tf_op jit(solution)/shard_map/reduce_scatter | solution.py:40
  1373.4 287.6 %all-gather.15.cloned.1.call-done = bf16[8192,1024]{1,0:T(8,128)(2,1)} async-done(((bf16[2048,1024]{1,0:T(8,128)(2,1)}), bf16[8192,1024]{1,0:T(8,128)(2,1)}) %all-gather.15.cloned.1.call-update) | async-done | bytes 16777232 | tf_op jit(solution)/shard_map/all_gather | solution.py:24
  1661.0 12.2 convolution_convert_fusion.1
  1675.2 41.5 %psum.159 = f32[]{:T(128)} all-reduce(f32[]{:T(128)S(6)} %div.90), channel_id=1, replica_groups=mesh['dp'=2,'row'=4,'col'=4] {'dp','row','col'}, use_global_device_ids=true, to_apply=%region_19.20 | all-reduce | flops 1 | bytes 8 | tf_op jit(solution)/shard_map/psum | solution.py:229
  1722.9 35.2 %all-gather.17.cloned.1.call-done = bf16[8192,256]{1,0:T(8,128)(2,1)} async-done(((bf16[2048,256]{1,0:T(8,128)(2,1)}), bf16[8192,256]{1,0:T(8,128)(2,1)}) %all-gather.17.cloned.1.call-update) | async-done | bytes 4194320 | tf_op jit(solution)/shard_map/all_gather | solution.py:20
  1758.1 15.4 fusion.93
  1774.0 549.3 %reduce-scatter.17.cloned.1.call-done = f32[2048,1024]{1,0:T(8,128)} async-done(((f32[8192,1024]{1,0:T(8,128)}), f32[2048,1024]{1,0:T(8,128)}) %reduce-scatter.17.cloned.1.call-update) | async-done | bytes 8388624 | tf_op jit(solution)/shard_map/reduce_scatter | solution.py:40
  2323.2 10.7 fusion.60
  2334.0 287.9 %all-gather.19.cloned.1.call-done = bf16[8192,1024]{1,0:T(8,128)(2,1)} async-done(((bf16[2048,1024]{1,0:T(8,128)(2,1)}), bf16[8192,1024]{1,0:T(8,128)(2,1)}) %all-gather.19.cloned.1.call-update) | async-done | bytes 16777232 | tf_op jit(solution)/shard_map/all_gather | solution.py:24
  2621.9 12.3 convolution_convert_fusion
  2634.2 44.6 %reduce-scatter.19.cloned.1.call-done = bf16[2048,256]{1,0:T(8,128)(2,1)} async-done(((bf16[8192,256]{1,0:T(8,128)(2,1)}), bf16[2048,256]{1,0:T(8,128)(2,1)}) %reduce-scatter.19.cloned.1.call-update) | async-done | bytes 1048592 | tf_op jit(solution)/shard_map/reduce_scatter | solution.py:46
  2683.1 11.7 all-reduce.2
  2701.1 39.2 %all-gather.21.cloned.1.call-done = bf16[8192,256]{1,0:T(8,128)(2,1)} async-done(((bf16[2048,256]{1,0:T(8,128)(2,1)}), bf16[8192,256]{1,0:T(8,128)(2,1)}) %all-gather.21.cloned.1.call-update) | async-done | bytes 4194320 | tf_op jit(solution)/shard_map/all_gather | solution.py:20
  2749.9 142.0 %reduce-scatter.21.cloned.1.call-done = f32[2048,256]{1,0:T(8,128)} async-done(((f32[8192,256]{1,0:T(8,128)}), f32[2048,256]{1,0:T(8,128)}) %reduce-scatter.21.cloned.1.call-update) | async-done | bytes 2097168 | tf_op jit(solution)/shard_map/reduce_scatter | solution.py:40
  2896.2 230.2 %while.53 = (s32[]{:T(128)}, f32[2048,4,64]{0,2,1:T(8,128)}, f32[2048,4,64]{0,2,1:T(8,128)}, bf16[4,512,4,64]{1,3,2,0:T(8,128)(2,1)}, bf16[2048,4,3,64]{0,3,1,2:...) while((s32[]{:T(128)}, f32[2048,4,64]{0,2,1:T(8,128)}, ...), condition=%wide.region_29.30_spmd.clone, body=%wide.region_27.29_spmd.clone.sunk | while | flops 2737461248 | bytes 231277488 | solution.py:170
  2911.7 14.1 multiply_reduce_fusion.3
  2925.8 11.5 multiply_convert_fusion.3
  2968.1 14.1 multiply_reduce_fusion.3
  2982.2 11.5 multiply_convert_fusion.3
  3025.9 14.1 multiply_reduce_fusion.3
  3040.0 11.5 multiply_convert_fusion.3
  3074.3 9.4 fusion.154
  3083.7 14.1 multiply_reduce_fusion.3
  3097.8 11.5 multiply_convert_fusion.3
  3136.5 12.4 convolution_convert_fusion.4
  3148.9 10.8 convolution_convert_fusion.5
  3161.6 191.4 %all-gather.23.cloned.1.call-done = bf16[8192,768]{0,1:T(8,128)(2,1)} async-done(((bf16[2048,768]{0,1:T(8,128)(2,1)}), bf16[8192,768]{0,1:T(8,128)(2,1)}) %all-gather.23.cloned.1.call-update) | async-done | bytes 12582928 | tf_op jit(solution)/shard_map/all_gather | solution.py:24
  3353.0 10.1 convolution_convert_fusion.6
  3363.2 10.1 convolution_convert_fusion.3
  3373.9 12.2 reduce_sum.207
  3386.1 42.3 %psum.158 = f32[]{:T(128)} all-reduce(f32[]{:T(128)} %get-tuple-element.448), channel_id=1, replica_groups=mesh['dp'=2,'row'=4,'col'=4] {'dp','row','col'}, use_global_device_ids=true, to_apply=%region_17.18 | all-reduce | flops 1 | bytes 8 | tf_op jit(solution)/shard_map/psum | solution.py:229
  3449.4 13.3 reduce-scatter.23.cloned.1.call-done
  3465.1 11.7 all-reduce.1
  3476.9 15.6 all-reduce
  (309 shorter events, 281.4 us)
Async XLA Ops:
  7.2 1653.8 %copy-start = (bf16[1024,256]{1,0:T(8,128)(2,1)S(1)}, bf16[1024,256]{1,0:T(8,128)(2,1)}, u32[]{:S(2)}) copy-start(bf16[1024,256]{1,0:T(8,128)(2,1)} %param.31) | copy-start | bytes 1572868
  7.2 57.7 %copy-start.20 = (bf16[256,768]{1,0:T(8,128)(2,1)S(1)}, bf16[256,768]{1,0:T(8,128)(2,1)}, u32[]{:S(2)}) copy-start(bf16[256,768]{1,0:T(8,128)(2,1)} %param.23) | copy-start | bytes 1179652
  7.2 57.7 %all-gather.9.cloned.1.call-start = ((), (), s32[]{:S(2)}) async-start(), calls=%async_computation.8 | async-start | bytes 5242880 | tf_op jit(solution)/shard_map/all_gather | solution.py:20
  8.0 70.9 %copy-start.27 = (f32[256]{0:T(256)}, f32[256]{0:T(256)S(1)}, u32[]{:S(2)}) copy-start(f32[256]{0:T(256)S(1)} %convert_element_type.195) | copy-start | bytes 3076
  25.6 468.1 %reduce-scatter.9.cloned.1.call-start = ((), (), s32[]{:S(2)}) async-start(), calls=%async_computation.9 | async-start | bytes 31457280 | tf_op jit(solution)/shard_map/reduce_scatter | solution.py:40
  78.9 616.9 %all-gather.11.cloned.1.call-start = ((), (), s32[]{:S(2)}) async-start(), calls=%async_computation.10 | async-start | bytes 5242880 | tf_op jit(solution)/shard_map/all_gather | solution.py:24
  536.6 7.9 copy-start.4
  588.0 7.9 copy-start.4
  612.0 83.9 %copy-start.19 = (bf16[256,256]{1,0:T(8,128)(2,1)S(1)}, bf16[256,256]{1,0:T(8,128)(2,1)}, u32[]{:S(2)}) copy-start(bf16[256,256]{1,0:T(8,128)(2,1)} %param.25) | copy-start | bytes 393220
  615.3 130.7 %reduce-scatter.11.cloned.1.call-start = ((), (), s32[]{:S(2)}) async-start(), calls=%async_computation.11 | async-start | bytes 5242880 | tf_op jit(solution)/shard_map/reduce_scatter | solution.py:46
  701.3 44.7 %copy-start.5 = (bf16[2048,256]{1,0:T(8,128)(2,1)S(1)}, bf16[2048,256]{1,0:T(8,128)(2,1)}, u32[]{:S(2)}) copy-start(bf16[2048,256]{1,0:T(8,128)(2,1)} %param.20) | copy-start | bytes 3145732
  701.3 100.2 %copy-start.18 = (bf16[256,1024]{1,0:T(8,128)(2,1)S(1)}, bf16[256,1024]{1,0:T(8,128)(2,1)}, u32[]{:S(2)}) copy-start(bf16[256,1024]{1,0:T(8,128)(2,1)} %param.29) | copy-start | bytes 1572868
  701.3 100.2 %all-gather.13.cloned.1.call-start = ((), (), s32[]{:S(2)}) async-start(), calls=%async_computation.12 | async-start | bytes 5242880 | tf_op jit(solution)/shard_map/all_gather | solution.py:20
  762.3 604.4 %reduce-scatter.13.cloned.1.call-start = ((), (), s32[]{:S(2)}) async-start(), calls=%async_computation.13 | async-start | bytes 41943040 | tf_op jit(solution)/shard_map/reduce_scatter | solution.py:40
  816.9 844.1 %all-gather.15.cloned.1.call-start = ((), (), s32[]{:S(2)}) async-start(), calls=%async_computation.14 | async-start | bytes 20971520 | tf_op jit(solution)/shard_map/all_gather | solution.py:24
  1373.1 345.4 %reduce-scatter.15.cloned.1.call-start = ((), (), s32[]{:S(2)}) async-start(), calls=%async_computation.15 | async-start | bytes 5242880 | tf_op jit(solution)/shard_map/reduce_scatter | solution.py:46
  1673.2 43.4 %copy-start.38 = (bf16[256]{0:T(256)(128)(2,1)S(1)}, bf16[256]{0:T(256)(128)(2,1)}, u32[]{:S(2)}) copy-start(bf16[256]{0:T(256)(128)(2,1)} %param.32) | copy-start | bytes 1540
  1673.2 45.3 %copy-start.12 = (bf16[2048,256]{1,0:T(8,128)(2,1)S(1)}, bf16[2048,256]{1,0:T(8,128)(2,1)}, u32[]{:S(2)}) copy-start(bf16[2048,256]{1,0:T(8,128)(2,1)} %reduce-scatter.11.cloned.1.call-done) | copy-start | bytes 3145732
  1673.2 84.9 %all-gather.17.cloned.1.call-start = ((), (), s32[]{:S(2)}) async-start(), calls=%async_computation.16 | async-start | bytes 5242880 | tf_op jit(solution)/shard_map/all_gather | solution.py:20
  1722.9 600.3 %reduce-scatter.17.cloned.1.call-start = ((), (), s32[]{:S(2)}) async-start(), calls=%async_computation.17 | async-start | bytes 41943040 | tf_op jit(solution)/shard_map/reduce_scatter | solution.py:40
  1773.5 848.4 %all-gather.19.cloned.1.call-start = ((), (), s32[]{:S(2)}) async-start(), calls=%async_computation.18 | async-start | bytes 20971520 | tf_op jit(solution)/shard_map/all_gather | solution.py:24
  2334.0 344.9 %reduce-scatter.19.cloned.1.call-start = ((), (), s32[]{:S(2)}) async-start(), calls=%async_computation.19 | async-start | bytes 5242880 | tf_op jit(solution)/shard_map/reduce_scatter | solution.py:46
  2634.2 106.2 %all-gather.21.cloned.1.call-start = ((), (), s32[]{:S(2)}) async-start(), calls=%async_computation.20 | async-start | bytes 5242880 | tf_op jit(solution)/shard_map/all_gather | solution.py:20
  2701.1 190.9 %reduce-scatter.21.cloned.1.call-start = ((), (), s32[]{:S(2)}) async-start(), calls=%async_computation.21 | async-start | bytes 10485760 | tf_op jit(solution)/shard_map/reduce_scatter | solution.py:40
  2747.1 605.9 %all-gather.23.cloned.1.call-start = ((), (), s32[]{:S(2)}) async-start(), calls=%async_computation.22 | async-start | bytes 15728640 | tf_op jit(solution)/shard_map/all_gather | solution.py:24
  2901.6 10.2 copy-start.10
  2925.8 15.4 copy-start.2
  2957.9 10.2 copy-start.10
  2982.2 15.4 copy-start.2
  3015.7 10.2 copy-start.10
  3040.0 15.4 copy-start.2
  3073.6 10.2 copy-start.10
  3097.8 15.4 copy-start.2
  3136.4 305.1 %all-reduce.9.cloned.1.call-start = ((), (), s32[]{:S(2)}) async-start(), calls=%async_computation.24 | async-start | bytes 3145728 | tf_op jit(solution)/shard_map/psum | solution.py:270
  3136.5 12.5 copy-start.11
  3148.9 10.8 copy-start.13
  3148.9 10.8 copy-start.14
  3161.6 201.5 %copy-start.21 = (bf16[256,768]{1,0:T(8,128)(2,1)S(1)}, bf16[256,768]{1,0:T(8,128)(2,1)}, u32[]{:S(2)}) copy-start(bf16[256,768]{1,0:T(8,128)(2,1)} %param.23) | copy-start | bytes 1179652
  3363.1 99.5 %reduce-scatter.23.cloned.1.call-start = ((), (), s32[]{:S(2)}) async-start(), calls=%async_computation.23 | async-start | bytes 5242880 | tf_op jit(solution)/shard_map/reduce_scatter | solution.py:46
  3435.8 26.9 copy-start.6
  3435.8 26.9 copy-start.23
  3435.8 26.9 copy-start.25
  3435.8 26.9 copy-start.28
  3435.8 41.1 %copy-start.29 = (f32[256]{0:T(256)S(1)}, f32[256]{0:T(256)}, u32[]{:S(2)}) copy-start(f32[256]{0:T(256)} %get-tuple-element.511) | copy-start | bytes 3076
  3435.8 41.1 %copy-start.30 = (f32[256]{0:T(256)S(1)}, f32[256]{0:T(256)}, u32[]{:S(2)}) copy-start(f32[256]{0:T(256)} %get-tuple-element.513) | copy-start | bytes 3076
  3435.8 41.1 %copy-start.32 = (f32[256]{0:T(256)S(1)}, f32[256]{0:T(256)}, u32[]{:S(2)}) copy-start(f32[256]{0:T(256)} %get-tuple-element.444) | copy-start | bytes 3076
  3435.8 41.1 %copy-start.33 = (f32[256]{0:T(256)S(1)}, f32[256]{0:T(256)}, u32[]{:S(2)}) copy-start(f32[256]{0:T(256)} %get-tuple-element.453) | copy-start | bytes 3076
  3447.2 49.8 %copy-start.1 = (bf16[1024,256]{1,0:T(8,128)(2,1)S(1)}, bf16[1024,256]{1,0:T(8,128)(2,1)}, u32[]{:S(2)}) copy-start(bf16[1024,256]{1,0:T(8,128)(2,1)} %param.31) | copy-start | bytes 1572868
  (29 other events, 86.8 us)
Sparse Core Ops, SparseCore 0:
  25.7 39.1 all-gather.8
  79.0 414.6 reduce-scatter.8
  615.4 80.3 all-gather.10
  701.4 44.5 reduce-scatter.10
  762.4 39.1 all-gather.12
  817.0 549.5 reduce-scatter.12
  1373.2 287.7 all-gather.14
  1673.4 45.0 reduce-scatter.14
  1723.0 35.0 all-gather.16
  1773.6 549.5 reduce-scatter.16
  2334.1 287.7 all-gather.18
  2634.3 44.5 reduce-scatter.18
  2701.2 39.1 all-gather.20
  2747.2 144.7 reduce-scatter.20
  3136.6 216.4 all-gather.22
  3363.2 53.1 all-reduce.8
  3418.9 43.6 reduce-scatter.22
where the time goes:
time: 3520 us; the launch traced here: 3510 us
  waiting for transfers between devices  2760 us (78%)
  matrix products  328 us (9%)
  other arithmetic  165 us (5%)
  blocking collectives  151 us (4%)
  local copies, waits for them, and re-layouts  68.4 us (2%)
    reduce_scatter x4, waiting for transfers between devices, sum_over_row(): lax.psum_scatter(product_term(left_side, right_side, flipped), 'row', sca...  1650 us
    all_gather x4, waiting for transfers between devices, spread_row(): return lax.all_gather(local_rows, 'row', axis=0, tiled=True)  847 us
    all_gather x4, waiting for transfers between devices, spread_col(): return lax.all_gather(local_rows, 'col', axis=0, tiled=True)  153 us
    reduce_scatter x4, waiting for transfers between devices, sum_over_col(): lax.psum_scatter(product_term(left_side, right_side, flipped).astype(jnp....  103 us
    psum x2, blocking collectives, on_device(): lax.psum((jnp.sum(valid_rows * error_rows * error_rows), jnp.sum(valid_ro...  83.8 us
    dot_general x8, matrix products, placed_scores(): jnp.einsum('qhd,khd->hqk', queries, key_rows, preferred_element_type=jnp....  77.2 us
  transfers between devices with their start and end apart: 17, of which 16 were waited for; matrix products, arithmetic and copies ran while one was open for 2% of the time, Pallas kernels for 0%

commit v1 on v0

v1 whole, which is shorter than its diff:
```python
import functools
import math

import jax
import jax.numpy as jnp
from jax import lax
from jax.experimental import pallas as pl
from jax.experimental.pallas import tpu as pltpu
from jax.sharding import PartitionSpec as P

D = 1024
HEADS = 16
SEQ = 2048
EPSILON = 1e-05
LOG2E = 1.4426950408889634
HEAD_DIM=64
BLOCK=256
HALF=64
PAIR=128
SCALE2 = LOG2E/8.0

def nt(a,b):
    return lax.dot_general(a,b,(((1,),(1,)),((),())),preferred_element_type=jnp.float32)
def nn(a,b):
    return jnp.dot(a,b,preferred_element_type=jnp.float32)
def tn(a,b):
    return lax.dot_general(a,b,(((0,),(0,)),((),())),preferred_element_type=jnp.float32)

def low_lanes(rows):
    return lax.broadcasted_iota(jnp.int32,(rows,PAIR),1) < HALF

def swap(a):
    return jnp.concatenate([a[:,HALF:],a[:,:HALF]],axis=1)

def fwd_kernel(heads, slope_ref, mixed_ref, out_ref, lse_ref, qs, ks, vs, bias, sc, mx, ls, acc):
    pairs=heads//2
    blocks=mixed_ref.shape[0]//BLOCK
    lo=low_lanes(BLOCK)
    @pl.loop(0,blocks)
    def _(b):
        rows=pl.ds(pl.multiple_of(b*BLOCK,BLOCK),BLOCK)
        for p in range(pairs):
            t0,t1,t2=(mixed_ref[rows,(3*p+n)*PAIR:(3*p+n+1)*PAIR] for n in range(3))
            zero=jnp.zeros_like(t0)
            qs[2*p,b]=jnp.where(lo,t0,zero)
            qs[2*p+1,b]=jnp.where(lo,zero,t1)
            ks[p,b]=jnp.where(lo,swap(t0),swap(t2))
            vs[p,b,:BLOCK]=jnp.where(lo,t1,zero)
            vs[p,b,BLOCK:]=jnp.where(lo,zero,t2)
    il=lax.broadcasted_iota(jnp.int32,(BLOCK,BLOCK),0)
    jl=lax.broadcasted_iota(jnp.int32,(BLOCK,BLOCK),1)
    tent=jnp.minimum(jl,2*il-jl).astype(jnp.float32)
    for h in range(heads):
        bias[h]=tent*slope_ref[h]
    jrow=lax.broadcasted_iota(jnp.int32,(1,BLOCK),1)
    @pl.loop(0,blocks)
    def _(i):
        for h in range(heads):
            t=nt(qs[h,i],ks[h//2,i])*SCALE2+bias[h]
            sc[h,i]=t
            mx[h]=jnp.maximum(t[:,:PAIR],t[:,PAIR:])
        @pl.loop(0,i)
        def _(j):
            place=(jrow+(j-i)*BLOCK).astype(jnp.float32)
            for h in range(heads):
                t=nt(qs[h,i],ks[h//2,j])*SCALE2+place*slope_ref[h]
                sc[h,j]=t
                mx[h]=jnp.maximum(mx[h],jnp.maximum(t[:,:PAIR],t[:,PAIR:]))
        for h in range(heads):
            mx[h]=jnp.broadcast_to(jnp.max(mx[h],1,keepdims=True),(BLOCK,PAIR))
            ls[h]=jnp.zeros((BLOCK,PAIR),jnp.float32)
        for p in range(pairs):
            acc[p]=jnp.zeros((BLOCK,PAIR),jnp.float32)
        @pl.loop(0,i+1)
        def _(j):
            for p in range(pairs):
                both=[]
                for h in (2*p,2*p+1):
                    m=mx[h]
                    ea=jnp.exp2(sc[h,j,:,:PAIR]-m)
                    eb=jnp.exp2(sc[h,j,:,PAIR:]-m)
                    ls[h]+=ea+eb
                    both+=[ea.astype(jnp.bfloat16),eb.astype(jnp.bfloat16)]
                acc[p]+=nn(jnp.concatenate(both,1),vs[p,j])
        rows=pl.ds(pl.multiple_of(i*BLOCK,BLOCK),BLOCK)
        for p in range(pairs):
            tot=[jnp.broadcast_to(jnp.sum(ls[h],1,keepdims=True),(BLOCK,PAIR)) for h in (2*p,2*p+1)]
            out_ref[rows,p*PAIR:(p+1)*PAIR]=(acc[p]/jnp.where(lo,tot[0],tot[1])).astype(out_ref.dtype)
            for n,h in enumerate((2*p,2*p+1)):
                lse=mx[h]+jnp.log2(tot[n])
                lse_ref[h,pl.ds(i,1),:]=lse.T[:1]

def attention_forward(slopes2, mixed):
    tokens,width=mixed.shape
    heads=width//(3*HEAD_DIM); pairs=heads//2; blocks=tokens//BLOCK
    f32=jnp.float32; bf=jnp.bfloat16
    return pl.pallas_call(
        functools.partial(fwd_kernel,heads),
        out_shape=(jax.ShapeDtypeStruct((tokens,heads*HEAD_DIM),bf),jax.ShapeDtypeStruct((heads,blocks,BLOCK),f32)),
        in_specs=[pl.BlockSpec(memory_space=pltpu.SMEM),pl.BlockSpec(memory_space=pltpu.VMEM)],
        out_specs=(pl.BlockSpec(memory_space=pltpu.VMEM),)*2,
        scratch_shapes=[pltpu.VMEM((heads,blocks,BLOCK,PAIR),bf),pltpu.VMEM((pairs,blocks,BLOCK,PAIR),bf),
            pltpu.VMEM((pairs,blocks,2*BLOCK,PAIR),bf),pltpu.VMEM((heads,BLOCK,BLOCK),f32),
            pltpu.VMEM((heads,blocks,BLOCK,BLOCK),f32),pltpu.VMEM((heads,BLOCK,PAIR),f32),pltpu.VMEM((heads,BLOCK,PAIR),f32),
            pltpu.VMEM((pairs,BLOCK,PAIR),f32)],
        compiler_params=pltpu.CompilerParams(vmem_limit_bytes=40<<20),
        name="attention_forward",
    )(slopes2,mixed)

def bwd_kernel(heads, slope_ref, mixed_ref, dout_ref, out_ref, lse_ref, grad_ref, qs, ks, km, vp, ds_, delta, bias, dq, dk, dv):
    pairs=heads//2
    blocks=mixed_ref.shape[0]//BLOCK
    lo=low_lanes(BLOCK)
    @pl.loop(0,blocks)
    def _(b):
        rows=pl.ds(pl.multiple_of(b*BLOCK,BLOCK),BLOCK)
        for p in range(pairs):
            t0,t1,t2=(mixed_ref[rows,(3*p+n)*PAIR:(3*p+n+1)*PAIR] for n in range(3))
            zero=jnp.zeros_like(t0)
            qs[p,b,:BLOCK]=jnp.where(lo,t0,zero)
            qs[p,b,BLOCK:]=jnp.where(lo,zero,t1)
            k=jnp.where(lo,swap(t0),swap(t2))
            ks[p,b]=k
            km[p,b,:BLOCK]=jnp.where(lo,k,zero)
            km[p,b,BLOCK:]=jnp.where(lo,zero,k)
            vp[p,b]=jnp.where(lo,t1,t2)
            d=dout_ref[rows,p*PAIR:(p+1)*PAIR]
            ds_[p,b,:BLOCK]=jnp.where(lo,d,zero)
            ds_[p,b,BLOCK:]=jnp.where(lo,zero,d)
            prod=(d.astype(jnp.float32)*out_ref[rows,p*PAIR:(p+1)*PAIR].astype(jnp.float32)).T
            delta[2*p,pl.ds(b,1),:]=jnp.sum(prod[:HALF],0,keepdims=True)
            delta[2*p+1,pl.ds(b,1),:]=jnp.sum(prod[HALF:],0,keepdims=True)
    kl=lax.broadcasted_iota(jnp.int32,(BLOCK,BLOCK),0)
    ql=lax.broadcasted_iota(jnp.int32,(BLOCK,BLOCK),1)
    tent=jnp.minimum(kl,2*ql-kl).astype(jnp.float32)
    ramp=kl.astype(jnp.float32)
    for h in range(heads):
        bias[0,h]=tent*slope_ref[h]
        bias[1,h]=ramp*slope_ref[h]
    def block(i,j,first):
        for p in range(pairs):
            ps=[];gs=[]
            for n,h in enumerate((2*p,2*p+1)):
                q=qs[p,i,n*BLOCK:(n+1)*BLOCK]
                d=ds_[p,i,n*BLOCK:(n+1)*BLOCK]
                row=slope_ref[h]*((j-i)*BLOCK).astype(jnp.float32)-lse_ref[h,pl.ds(i,1),:]
                t=nt(ks[p,j],q)*SCALE2+row+bias[0 if first else 1,h]
                e=jnp.exp2(t)
                g=e*(nt(vp[p,j],d)-delta[h,pl.ds(i,1),:])
                ps.append(e.astype(jnp.bfloat16)); gs.append(g.astype(jnp.bfloat16))
            gv=nn(jnp.concatenate(ps,1),ds_[p,i])
            gk=nn(jnp.concatenate(gs,1),qs[p,i])
            gq=tn(jnp.concatenate(gs,0),km[p,j])
            if first:
                dv[p,j]=gv; dk[p,j]=gk; dq[p,i]=gq
            else:
                dv[p,j]+=gv; dk[p,j]+=gk; dq[p,i]+=gq
    @pl.loop(0,blocks)
    def _(i):
        block(i,i,True)
        @pl.loop(0,i)
        def _(j):
            block(i,j,False)
    @pl.loop(0,blocks)
    def _(b):
        rows=pl.ds(pl.multiple_of(b*BLOCK,BLOCK),BLOCK)
        for p in range(pairs):
            a=dq[p,b]*0.125; k=swap(dk[p,b]*0.125); v=dv[p,b]
            for n,t in enumerate((jnp.where(lo,a,k),jnp.where(lo,v,a),jnp.where(lo,k,v))):
                grad_ref[rows,(3*p+n)*PAIR:(3*p+n+1)*PAIR]=t.astype(grad_ref.dtype)

def attention_backward(slopes2, mixed, dout, out, lse):
    tokens,width=mixed.shape
    heads=width//(3*HEAD_DIM); pairs=heads//2; blocks=tokens//BLOCK
    f32=jnp.float32; bf=jnp.bfloat16
    V=pl.BlockSpec(memory_space=pltpu.VMEM)
    return pl.pallas_call(
        functools.partial(bwd_kernel,heads),
        out_shape=jax.ShapeDtypeStruct((tokens,width),bf),
        in_specs=[pl.BlockSpec(memory_space=pltpu.SMEM),V,V,V,V],
        out_specs=V,
        scratch_shapes=[pltpu.VMEM((pairs,blocks,2*BLOCK,PAIR),bf),pltpu.VMEM((pairs,blocks,BLOCK,PAIR),bf),
            pltpu.VMEM((pairs,blocks,2*BLOCK,PAIR),bf),pltpu.VMEM((pairs,blocks,BLOCK,PAIR),bf),
            pltpu.VMEM((pairs,blocks,2*BLOCK,PAIR),bf),pltpu.VMEM((heads,blocks,BLOCK),f32),
            pltpu.VMEM((2,heads,BLOCK,BLOCK),f32)]+[pltpu.VMEM((pairs,blocks,BLOCK,PAIR),f32)]*3,
        compiler_params=pltpu.CompilerParams(vmem_limit_bytes=40<<20),
        name="attention_backward",
    )(slopes2,mixed,dout,out,lse)


PLANE = (0, 3, 1, 2)


def plane_of(col_size):
    return PLANE if col_size == len(PLANE) else tuple(range(col_size))


def pick(stacked, index):
    return lax.dynamic_index_in_dim(stacked, index, 0, keepdims=False)


def to_tokens(local_rows):
    row_size, col_size = lax.axis_size("row"), lax.axis_size("col")
    row, col = lax.axis_index("row"), lax.axis_index("col")
    plane = plane_of(col_size)
    blocks = local_rows.reshape(col_size, local_rows.shape[0] // col_size, -1)
    came = []
    for step in range(row_size):
        moves = [
            (r * col_size + c, plane[c] * col_size + (r + step) % col_size)
            for r in range(row_size)
            for c in range(col_size)
        ]
        came.append(lax.ppermute(pick(blocks, (row + step) % col_size), ("row", "col"), moves))
    came = jnp.stack(came)
    return jnp.concatenate([pick(came, (col - f) % row_size) for f in range(row_size)], axis=1)


def to_features(local_tokens):
    row_size, col_size = lax.axis_size("row"), lax.axis_size("col")
    row, col = lax.axis_index("row"), lax.axis_index("col")
    plane = plane_of(col_size)
    width = local_tokens.shape[1] // row_size
    blocks = jnp.stack([local_tokens[:, f * width : (f + 1) * width] for f in range(row_size)])
    came = []
    for step in range(row_size):
        moves = [
            (plane[c] * col_size + (r + step) % col_size, r * col_size + c)
            for r in range(row_size)
            for c in range(col_size)
        ]
        came.append(lax.ppermute(pick(blocks, (col - step) % row_size), ("row", "col"), moves))
    came = jnp.stack(came)
    return jnp.concatenate([pick(came, (q - row) % row_size) for q in range(col_size)], axis=0)


def swap_with(value, axis, bit):
    size = lax.axis_size(axis)
    return lax.ppermute(value, axis, [(i, i ^ bit) for i in range(size)])


def small_sum(value, axes):
    for axis in axes:
        bit = 1
        while bit < lax.axis_size(axis):
            value = value + swap_with(value, axis, bit)
            bit *= 2
    return value


def gather_row(value):
    size, row = lax.axis_size("row"), lax.axis_index("row")
    came = [value]
    for step in range(1, size):
        came.append(lax.ppermute(value, "row", [(i, (i + step) % size) for i in range(size)]))
    came = jnp.stack(came)
    return jnp.stack([pick(came, (row - r) % size) for r in range(size)])


def exchange_col(value):
    size, col = lax.axis_size("col"), lax.axis_index("col")
    came = [pick(value, col)]
    for bit in range(1, size):
        came.append(swap_with(pick(value, col ^ bit), "col", bit))
    came = jnp.stack(came)
    return jnp.stack([pick(came, col ^ q) for q in range(size)])


def gather_col(value):
    size, col = lax.axis_size("col"), lax.axis_index("col")
    far = swap_with(value, "col", 2)
    near = swap_with(value, "col", 1)
    far_near = swap_with(far, "col", 1)
    came = jnp.stack([value, near, far, far_near])
    return jnp.stack([pick(came, col ^ q) for q in range(size)])


def scatter_col(value):
    col = lax.axis_index("col")
    core, chip = col % 2, col // 2
    pairs = value.reshape((2, 2) + value.shape[1:])
    mine = lax.dynamic_index_in_dim(pairs, core, 1, keepdims=False)
    other = lax.dynamic_index_in_dim(pairs, 1 - core, 1, keepdims=False)
    near = mine.astype(jnp.float32) + swap_with(other, "col", 1).astype(jnp.float32)
    keep = pick(near, chip)
    send = pick(near, 1 - chip).astype(jnp.bfloat16)
    return keep + swap_with(send, "col", 2).astype(jnp.float32)


def scatter_row(value):
    return lax.psum_scatter(value, "row", scatter_dimension=0, tiled=True)


def sum_dp(value):
    return small_sum(value, ("dp",))


def standardize(inputs):
    center = jnp.mean(inputs, 1, keepdims=True)
    spread = jnp.mean(inputs * inputs, 1, keepdims=True) - center * center
    inverse = lax.rsqrt(spread + EPSILON)
    return (inputs - center) * inverse, inverse


def norm_backward(grad_normed, standard, inverse, norm_gain):
    scaled = grad_normed * norm_gain
    first = jnp.mean(scaled, 1, keepdims=True)
    second = jnp.mean(scaled * standard, 1, keepdims=True)
    return inverse * (scaled - first - standard * second)


def gelu_local(before):
    return jax.nn.gelu(before, approximate=True)


def low(value):
    return value.astype(jnp.bfloat16)


def on_device(
    layer_in,
    first_gain,
    first_shift,
    joined_weight,
    joined_bias,
    out_weight,
    out_bias,
    second_gain,
    second_shift,
    up_weight,
    up_bias,
    down_weight,
    down_bias,
    teacher,
    valid,
    cotangent,
):
    row_size, col_size = lax.axis_size("row"), lax.axis_size("col")
    row, col = lax.axis_index("row"), lax.axis_index("col")
    f32 = jnp.float32
    head_count = joined_bias.shape[0]
    quarter = layer_in.shape[0] // col_size
    head_index = col * head_count + jnp.arange(head_count, dtype=jnp.int32)
    slopes = jnp.exp2(-8.0 * (head_index.astype(f32) + 1.0) / HEADS) * LOG2E

    tokens = to_tokens(layer_in)
    vectors = jnp.stack([first_gain, first_shift, out_bias, second_gain, second_shift, down_bias])
    vectors = gather_row(vectors).transpose(1, 0, 2).reshape(6, D).astype(f32)
    gain_one, shift_one, bias_out, gain_two, shift_two, bias_down = (vectors[i] for i in range(6))
    joined_all = gather_row(joined_weight).reshape(D, -1)
    zero_rows = jnp.zeros_like(joined_bias[:, :HEAD_DIM])
    bias_rows = jnp.stack(
        [joined_bias[:, :HEAD_DIM], zero_rows, joined_bias[:, HEAD_DIM:]], axis=1
    ).reshape(-1)

    inputs = tokens.astype(f32)
    standard_one, inverse_one = standardize(inputs)
    normed_one = low(standard_one * gain_one + shift_one)
    normed_one_all = gather_col(normed_one).reshape(-1, D)
    mixed = low(nn(normed_one_all, joined_all) + bias_rows)
    attended, log_totals = attention_forward(slopes, mixed)

    out_all = gather_row(out_weight)
    out_all = jnp.concatenate([out_all[r] for r in range(row_size)], axis=1)
    out_all = gather_col(out_all).reshape(D, D)
    up_own = gather_row(up_weight).reshape(D, -1)
    up_far = gather_row(swap_with(up_weight, "col", 2)).reshape(D, -1)
    down_own = gather_row(down_weight)
    down_far = swap_with(down_own, "col", 2)
    down_own = jnp.concatenate([down_own[r] for r in range(row_size)], axis=1)
    down_far = jnp.concatenate([down_far[r] for r in range(row_size)], axis=1)
    bias_far = swap_with(up_bias, "col", 2)

    target = to_tokens(teacher)
    cotangent_tokens = to_tokens(cotangent)
    plane = plane_of(col_size)
    valid_tokens = lax.ppermute(
        pick(valid.reshape(col_size, quarter), row),
        ("row", "col"),
        [(r * col_size + c, plane[c] * col_size + r) for r in range(row_size) for c in range(col_size)],
    ).astype(f32)[:, None]
    valid_count = small_sum(jnp.sum(valid.astype(f32)).reshape(1, 1), ("dp", "col"))[0, 0]

    attended_tokens = exchange_col(attended.reshape(col_size, quarter, -1))
    attended_tokens = jnp.concatenate([attended_tokens[q] for q in range(col_size)], axis=1)
    middle = inputs + (nn(attended_tokens, out_all) + bias_out)
    standard_two, inverse_two = standardize(middle)
    normed_two = low(standard_two * gain_two + shift_two)
    normed_chip = jnp.concatenate([normed_two, swap_with(normed_two, "col", 1)], axis=0)
    before_own = nn(normed_chip, up_own) + up_bias.astype(f32)
    before_far = nn(normed_chip, up_far) + bias_far.astype(f32)
    active_own, pull_own = jax.vjp(gelu_local, before_own)
    active_far, pull_far = jax.vjp(gelu_local, before_far)
    active_own, active_far = low(active_own), low(active_far)
    branch = nn(active_own, down_own) + nn(active_far, down_far)
    result = middle + (
        branch[:quarter] + swap_with(low(branch[quarter:]), "col", 1).astype(f32) + bias_down
    )
    layer_out = to_features(low(result))

    error_rows = result - target.astype(f32)
    error_sum = jnp.sum(valid_tokens * error_rows * error_rows)
    token_total = layer_in.shape[0] * lax.axis_size("dp") * col_size
    grad_result = cotangent_tokens.astype(f32) + valid_tokens * error_rows * (
        token_total / valid_count
    )
    grad_low = low(grad_result)
    grad_chip = jnp.concatenate([grad_low, swap_with(grad_low, "col", 1)], axis=0)
    grad_before_own = low(pull_own(nt(grad_chip, down_own))[0])
    grad_before_far = low(pull_far(nt(grad_chip, down_far))[0])
    back = nt(grad_before_own, up_own) + nt(grad_before_far, up_far)
    grad_normed_two = back[:quarter] + swap_with(low(back[quarter:]), "col", 1).astype(f32)
    grad_middle = grad_result + norm_backward(grad_normed_two, standard_two, inverse_two, gain_two)
    branch_grad = low(grad_middle)
    attended_grad = low(nt(branch_grad, out_all))
    width = attended_grad.shape[1] // col_size
    attended_grad = exchange_col(
        jnp.stack([attended_grad[:, q * width : (q + 1) * width] for q in range(col_size)])
    ).reshape(-1, width)

    down_grad_own = low(tn(grad_chip, active_own))
    down_grad_far = low(tn(grad_chip, active_far))
    up_grad_own = low(tn(normed_chip, grad_before_own))
    up_grad_far = low(tn(normed_chip, grad_before_far))
    down_grad = low(down_grad_own.astype(f32) + swap_with(down_grad_far, "col", 2).astype(f32))
    up_grad = low(up_grad_own.astype(f32) + swap_with(up_grad_far, "col", 2).astype(f32))
    down_grad = sum_dp(scatter_row(down_grad)).astype(f32).T
    up_grad = sum_dp(scatter_row(up_grad)).astype(f32)
    out_grad = low(tn(branch_grad, attended_tokens))
    out_grad = jnp.stack([out_grad[:, q * width : (q + 1) * width] for q in range(col_size)])
    out_grad = low(scatter_col(out_grad))
    out_grad = sum_dp(scatter_row(out_grad)).astype(f32).T

    mixed_grad = attention_backward(slopes, mixed, attended_grad, attended, log_totals)
    grad_normed_one = low(nt(mixed_grad, joined_all)).reshape(col_size, quarter, D)
    grad_normed_one = scatter_col(grad_normed_one)
    input_grad = grad_middle + norm_backward(grad_normed_one, standard_one, inverse_one, gain_one)
    input_grad = to_features(low(input_grad)).astype(f32)
    joined_grad = sum_dp(scatter_row(low(tn(normed_one_all, mixed_grad)))).astype(f32)

    early = jnp.stack(
        [
            jnp.sum(branch_grad, 0, dtype=f32),
            jnp.sum(grad_normed_two * standard_two, 0),
            jnp.sum(grad_normed_two, 0),
            jnp.sum(grad_low, 0, dtype=f32),
            jnp.full((D,), error_sum),
        ]
    )
    early = small_sum(early, ("dp", "row", "col"))
    loss = early[4, 0] / (D * valid_count)
    early = lax.dynamic_slice_in_dim(early, row * (D // row_size), D // row_size, 1)
    up_sums = jnp.sum(grad_before_own, 0, dtype=f32) + swap_with(
        jnp.sum(grad_before_far, 0, dtype=f32), "col", 2
    )
    up_bias_grad = small_sum(up_sums, ("dp", "row"))
    column_sums = small_sum(jnp.sum(mixed_grad, 0, dtype=f32), ("dp", "row"))
    column_sums = column_sums.reshape(head_count, 3, HEAD_DIM)
    joined_bias_grad = jnp.concatenate([column_sums[:, 0], column_sums[:, 2]], axis=1)
    late = jnp.stack([jnp.sum(grad_normed_one * standard_one, 0), jnp.sum(grad_normed_one, 0)])
    late = small_sum(late, ("dp", "row", "col"))
    late = lax.dynamic_slice_in_dim(late, row * (D // row_size), D // row_size, 1)
    return (
        layer_out,
        loss,
        input_grad,
        late[0],
        late[1],
        joined_grad,
        joined_bias_grad,
        out_grad,
        early[0],
        early[1],
        early[2],
        up_grad,
        up_bias_grad,
        down_grad,
        early[3],
    )


def solution(mesh):
    return jax.shard_map(
        on_device,
        mesh=mesh,
        in_specs=(
            P(("dp", "col"), "row"),
            P("row"),
            P("row"),
            P("row", "col"),
            P("col", None),
            P("col", "row"),
            P("row"),
            P("row"),
            P("row"),
            P("row", "col"),
            P("col"),
            P("col", "row"),
            P("row"),
            P(("dp", "col"), "row"),
            P(("dp", "col")),
            P(("dp", "col"), "row"),
        ),
        out_specs=(
            P(("dp", "col"), "row"),
            P(),
            P(("dp", "col"), "row"),
            P("row"),
            P("row"),
            P("row", "col"),
            P("col", None),
            P("col", "row"),
            P("row"),
            P("row"),
            P("row"),
            P("row", "col"),
            P("col"),
            P("col", "row"),
            P("row"),
        ),
        check_vma=False,
    )
```

time: 3520 us -> 787 us (0.22)
  waiting for transfers between devices: 2760 us -> 322 us
  matrix products: 328 us -> 66.5 us
  starting transfers between devices: 1.32 us -> 201 us
  blocking collectives: 151 us -> 0 us
  other arithmetic: 165 us -> 64.2 us
  Pallas kernels: 0 us -> 66.6 us
    reduce_scatter x8 -> x4, waiting for transfers between devices: 1760 us -> 0.05 us  [scatter_row(): return lax.psum_scatter(value, 'row', scatter_dimension=0, tiled=True)]
    all_gather x8 -> x0, waiting for transfers between devices: 1000 us -> none  [the longest x4 847 us: spread_row(): return lax.all_gather(local_rows, 'row', axis=0, tiled=True)]
    ppermute x0 -> x88, waiting for transfers between devices: none -> 322 us  [the longest x18 126 us: gather_row(): lax.ppermute(value, 'row', [(i, (i + step) % size) for i in range(size)])]
    dot_general x40 -> x18, matrix products: 328 us -> 66.5 us  [the longest x6 23.7 us: tn(): lax.dot_general(a, b, (((0,), (0,)), ((), ())), preferred_element_type=jn...]
    ppermute x0 -> x88, starting transfers between devices: none -> 200 us  [the longest x49 61.1 us: swap_with(): return lax.ppermute(value, axis, [(i, i ^ bit) for i in range(size)])]
    psum x8 -> x0, blocking collectives: 151 us -> none  [the longest x2 83.8 us: on_device(): lax.psum((jnp.sum(valid_rows * error_rows * error_rows), jnp.sum(valid_ro...]
    convert_element_type x33 -> x15, other arithmetic: 91.2 us -> 15.1 us  [the longest x7 11.5 us: low(): return value.astype(jnp.bfloat16)]
    pallas_call x0 -> x2, Pallas kernels: none -> 66.6 us  [the longest x1 38 us: attention_backward(): pl.pallas_call(functools.partial(bwd_kernel, heads), out_shape=jax.ShapeD...]
  transfers between devices with their start and end apart: 17 -> 92, of which waited for: 16 -> 36; matrix products, arithmetic and copies ran while one was open for 2% -> 14% of each run, Pallas kernels for 0% -> 9%
where the time goes in v1:
time: 787 us; the launch traced here: 779 us
  waiting for transfers between devices  322 us (41%)
  starting transfers between devices  201 us (26%)
  Pallas kernels  66.6 us (8%)
  matrix products  66.5 us (8%)
  other arithmetic  64.2 us (8%)
  local copies, waits for them, and re-layouts  39.3 us (5%)
  between operations  20.5 us (3%)
    ppermute x18, waiting for transfers between devices, gather_row(): lax.ppermute(value, 'row', [(i, (i + step) % size) for i in range(size)])  126 us
    ppermute x49, waiting for transfers between devices, swap_with(): return lax.ppermute(value, axis, [(i, i ^ bit) for i in range(size)])  122 us
    ppermute x49, starting transfers between devices, swap_with(): return lax.ppermute(value, axis, [(i, i ^ bit) for i in range(size)])  61.1 us
    ppermute x12, starting transfers between devices, to_tokens(): lax.ppermute(pick(blocks, (row + step) % col_size), ('row', 'col'), moves)  59.2 us
    ppermute x8, waiting for transfers between devices, to_features(): lax.ppermute(pick(blocks, (col - step) % row_size), ('row', 'col'), moves)  53.7 us
    ppermute x18, starting transfers between devices, gather_row(): lax.ppermute(value, 'row', [(i, (i + step) % size) for i in range(size)])  42.9 us
    pallas_call x1, Pallas kernels, attention_backward(): pl.pallas_call(functools.partial(bwd_kernel, heads), out_shape=jax.ShapeD...  38 us
    ppermute x8, starting transfers between devices, to_features(): lax.ppermute(pick(blocks, (col - step) % row_size), ('row', 'col'), moves)  34.1 us
  transfers between devices with their start and end apart: 92, of which 36 were waited for; matrix products, arithmetic and copies ran while one was open for 14% of the time, Pallas kernels for 9%

profile of v1, /device:TPU:13, one launch (start us, length us, event | category | flops | bytes accessed | tf_op | source)
XLA Modules:
  0.0 779.5 jit_solution(13964994678411494841)
XLA Ops:
  21.3 4.4 collective-permute-start.3
  37.4 17.7 %collective-permute-start.33 = (bf16[1024]{0:T(1024)(128)(2,1)S(1)}, bf16[1024]{0:T(1024)(128)(2,1)S(1)}, u32[]{:S(2)}, u32[]{:S(2)}) collective-permute-start(bf16[1024]{0:T(1024)(128)(2,1)S(1)} %copy-done.65), channel_id=1, source_target_pairs={{0,2},{1,3},{2,0},{3,1},{4,6},{5,7},{6,4},{7,5},{8,10},{9,11},{10,... | collective-permute-start | bytes 6152 | tf_op jit(solution)/shard_map/ppermute | solution.py:239
  61.5 5.7 collective-permute-start.11
  69.0 4.3 collective-permute-start.28
  74.5 25.7 %collective-permute-done.12 = bf16[256,768]{1,0:T(8,128)(2,1)S(1)} collective-permute-done((bf16[256,768]{1,0:T(8,128)(2,1)S(1)}, bf16[256,768]{1,0:T(8,128)(2,1)S(1)}, u32[]{:S(2)}, u32[]{:S(2)}) %collective-permute-start.12) | collective-permute-done | bytes 393248 | tf_op jit(solution)/shard_map/ppermute | solution.py:255
  103.2 33.9 %collective-permute-done.26 = bf16[1024,256]{1,0:T(8,128)(2,1)S(1)} collective-permute-done((bf16[1024,256]{1,0:T(8,128)(2,1)}, bf16[1024,256]{1,0:T(8,128)(2,1)S(1)}, u32[]{:S(2)}, u32[]{:S(2)}) %collective-permute-start.26) | collective-permute-done | bytes 524320 | tf_op jit(solution)/shard_map/ppermute | solution.py:255
  139.3 15.6 %collective-permute-done.28 = bf16[1024,256]{1,0:T(8,128)(2,1)S(1)} collective-permute-done((bf16[1024,256]{1,0:T(8,128)(2,1)}, bf16[1024,256]{1,0:T(8,128)(2,1)S(1)}, u32[]{:S(2)}, u32[]{:S(2)}) %collective-permute-start.28) | collective-permute-done | bytes 524320 | tf_op jit(solution)/shard_map/ppermute | solution.py:255
  156.1 11.2 %collective-permute-start.25 = (bf16[256,1024]{1,0:T(8,128)(2,1)}, bf16[256,1024]{1,0:T(8,128)(2,1)S(1)}, u32[]{:S(2)}, u32[]{:S(2)}) collective-permute-start(bf16[256,1024]{1,0:T(8,128)(2,1)} %param.25), channel_id=1, source_target_pairs={{0,12},{4,0},{8,4},{12,8},{1,13},{5,1},{9,5},{13,9},{2,14},{6,2},{... | collective-permute-start | bytes 1572872 | tf_op jit(solution)/shard_map/ppermute | solution.py:255
  169.9 12.2 %collective-permute-done.23 = bf16[256,1024]{1,0:T(8,128)(2,1)S(1)} collective-permute-done((bf16[256,1024]{1,0:T(8,128)(2,1)}, bf16[256,1024]{1,0:T(8,128)(2,1)S(1)}, u32[]{:S(2)}, u32[]{:S(2)}) %collective-permute-start.23) | collective-permute-done | bytes 524320 | tf_op jit(solution)/shard_map/ppermute | solution.py:255
  182.8 3.6 collective-permute-done.25
  194.3 3.6 add_convert_fusion.mixed_ref
  197.9 28.6 %attention_forward.1 = (bf16[2048,256]{1,0:T(8,128)(2,1)S(1)}, f32[4,8,256]{2,1,0:T(8,128)S(1)}) custom-call(f32[4]{0:T(128)S(1)} %exponential_multiply_fusion.slope_ref, bf16[2048,768]{1,0:T(8,128)(2,1)S(1)} %add_convert_fusion.mixed_ref), custom_call_target="tpu_custom_call" | custom-call | tf_op jit(solution)/shard_map/attention_forward/pallas_call | solution.py:97
  230.8 4.4 collective-permute-done.15
  250.2 21.3 %collective-permute-done.31 = bf16[256,1024]{1,0:T(8,128)(2,1)S(1)} collective-permute-done((bf16[256,1024]{1,0:T(8,128)(2,1)S(1)}, bf16[256,1024]{1,0:T(8,128)(2,1)S(1)}, u32[]{:S(2)}, u32[]{:S(2)}) %collective-permute-start.31) | collective-permute-done | bytes 524320 | tf_op jit(solution)/shard_map/ppermute | solution.py:255
  271.5 11.2 %collective-permute-done.30 = bf16[256,1024]{1,0:T(8,128)(2,1)S(1)} collective-permute-done((bf16[256,1024]{1,0:T(8,128)(2,1)S(1)}, bf16[256,1024]{1,0:T(8,128)(2,1)S(1)}, u32[]{:S(2)}, u32[]{:S(2)}) %collective-permute-start.30) | collective-permute-done | bytes 524320 | tf_op jit(solution)/shard_map/ppermute | solution.py:255
  287.5 4.7 fusion.37
  294.6 6.5 convolution_add_fusion.1
  305.3 3.8 collective-permute-start.45
  317.6 6.3 collective-permute-start.47
  327.0 24.7 %collective-permute-start.40 = (bf16[512,256]{1,0:T(8,128)(2,1)S(1)}, bf16[512,256]{1,0:T(8,128)(2,1)S(1)}, u32[]{:S(2)}, u32[]{:S(2)}) collective-permute-start(bf16[512,256]{1,0:T(8,128)(2,1)S(1)} %get-tuple-element.132), channel_id=1, source_target_pairs={{0,0},{1,12},{2,4},{3,8},{4,1},{5,13},{6,5},{7,9},{8,2},{9,14},{10... | collective-permute-start | bytes 786440 | tf_op jit(solution)/shard_map/ppermute | solution.py:214
  351.8 5.5 collective-permute-start.42
  363.6 11.2 %collective-permute-done.41 = bf16[512,256]{1,0:T(8,128)(2,1)S(1)} collective-permute-done((bf16[512,256]{1,0:T(8,128)(2,1)S(1)}, bf16[512,256]{1,0:T(8,128)(2,1)S(1)}, u32[]{:S(2)}, u32[]{:S(2)}) %collective-permute-start.41) | collective-permute-done | bytes 262176 | tf_op jit(solution)/shard_map/ppermute | solution.py:214
  376.8 10.5 %convert_reduce_fusion.4 = (f32[1024]{0:T(1024)S(1)}, bf16[512,1024]{1,0:T(8,128)(2,1)S(1)}, f32[512,1024]{1,0:T(8,128)}, bf16[512,1024]{1,0:T(8,128)(2,1)}) fusion(f32[]{:T(128)} %bitcast.125, f32[512,1024]{1,0:T(8,128)S(1)} %get-tuple-element.63, bf16[512,256]{1,0:T(8,128)(2,1)S(1)} %get-tuple-element.165, bf16[512,256]{1,0:T(8,128)(2,1)S(1)} %get-tuple-element.166, ...), kind=kLoop, calls=%fused_computation.75 | loop fusion | flops 12581888 | bytes 8394756 | tf_op jit(solution)/shard_map/reduce_sum | solution.py:446
  390.0 4.8 convert_reduce_fusion.2
  397.3 4.8 convert_reduce_fusion.1
  410.8 3.5 multiply_reduce_fusion
  439.1 15.2 %collective-permute-done.61 = bf16[512,256]{1,0:T(8,128)(2,1)} collective-permute-done((bf16[512,256]{1,0:T(8,128)(2,1)}, bf16[512,256]{1,0:T(8,128)(2,1)}, u32[]{:S(2)}, u32[]{:S(2)}) %collective-permute-start.61) | collective-permute-done | bytes 262176 | tf_op jit(solution)/shard_map/ppermute | solution.py:239
  454.3 5.3 collective-permute-done.60
  465.4 38.0 %attention_backward.1 = bf16[2048,768]{1,0:T(8,128)(2,1)S(1)} custom-call(f32[4]{0:T(128)S(1)} %exponential_multiply_fusion.slope_ref, bf16[2048,768]{1,0:T(8,128)(2,1)S(1)} %add_convert_fusion.mixed_ref, bf16[2048,256]{1,0:T(8,128)(2,1)S(1)} %bitcast.294, bf16[2048,256]{1,0:T(8,128)(2,1)S(1)} %copy-done.3, f32[4,8,256]{2,1,0:T(8,128)S(1)} %get-tuple-element.18.lse_ref), custom_call_target="tpu_custom_call" | custom-call | tf_op jit(solution)/shard_map/attention_backward/pallas_call | solution.py:177
  505.1 4.7 convolution_convert_fusion.4
  510.4 4.9 convolution_convert_fusion.1
  519.2 42.6 %collective-permute-done.86 = bf16[1024,1024]{1,0:T(8,128)(2,1)S(1)} collective-permute-done((bf16[1024,1024]{1,0:T(8,128)(2,1)S(1)}, bf16[1024,1024]{1,0:T(8,128)(2,1)S(1)}, u32[]{:S(2)}, u32[]{:S(2)}) %collective-permute-start.86) | collective-permute-done | bytes 2097184 | tf_op jit(solution)/shard_map/ppermute | solution.py:239
  565.5 6.2 convolution_convert_fusion.2
  572.6 3.7 convolution_convert_fusion
  587.6 28.4 %collective-permute-done.36 = bf16[512,256]{1,0:T(8,128)(2,1)} collective-permute-done((bf16[512,256]{1,0:T(8,128)(2,1)}, bf16[512,256]{1,0:T(8,128)(2,1)}, u32[]{:S(2)}, u32[]{:S(2)}) %collective-permute-start.36) | collective-permute-done | bytes 262176 | tf_op jit(solution)/shard_map/ppermute | solution.py:232
  615.9 15.1 %collective-permute-start.38 = (bf16[512,256]{1,0:T(8,128)(2,1)}, bf16[512,256]{1,0:T(8,128)(2,1)}, u32[]{:S(2)}, u32[]{:S(2)}) collective-permute-start(bf16[512,256]{1,0:T(8,128)(2,1)} %get-tuple-element.142), channel_id=1, source_target_pairs={{2,0},{14,1},{6,2},{10,3},{3,4},{15,5},{7,6},{11,7},{0,8},{12,9},{... | collective-permute-start | bytes 786440 | tf_op jit(solution)/shard_map/ppermute | solution.py:232
  633.4 8.2 %collective-permute-done.37 = bf16[512,256]{1,0:T(8,128)(2,1)} collective-permute-done((bf16[512,256]{1,0:T(8,128)(2,1)}, bf16[512,256]{1,0:T(8,128)(2,1)}, u32[]{:S(2)}, u32[]{:S(2)}) %collective-permute-start.37) | collective-permute-done | bytes 262176 | tf_op jit(solution)/shard_map/ppermute | solution.py:232
  646.2 4.0 fusion.49
  653.0 4.0 add_convert_fusion.2
  667.3 19.5 %collective-permute-done.58 = f32[5,1024]{1,0:T(8,128)S(1)} collective-permute-done((f32[5,1024]{1,0:T(8,128)S(1)}, f32[5,1024]{1,0:T(8,128)S(1)}, u32[]{:S(2)}, u32[]{:S(2)}) %collective-permute-start.58) | collective-permute-done | bytes 20512 | tf_op jit(solution)/shard_map/ppermute | solution.py:239
  692.4 3.5 collective-permute-done.79
  709.5 5.9 collective-permute-start.71
  716.4 5.1 collective-permute-start.64
  724.5 4.6 collective-permute-start.65
  730.6 5.9 collective-permute-done.64
  736.4 7.6 collective-permute-done.67
  753.6 10.3 %collective-permute-done.87 = bf16[256,1024]{1,0:T(8,128)(2,1)} collective-permute-done((bf16[256,1024]{1,0:T(8,128)(2,1)}, bf16[256,1024]{1,0:T(8,128)(2,1)}, u32[]{:S(2)}, u32[]{:S(2)}) %collective-permute-start.87) | collective-permute-done | bytes 524320 | tf_op jit(solution)/shard_map/ppermute | solution.py:239
  766.3 4.3 collective-permute-done.81
  (448 shorter events, 222.3 us)
Async XLA Ops:
  7.2 684.2 %reduce-scatter.7.cloned.1.call-start = ((), (), s32[]{:S(2)}) async-start(), calls=%async_computation.5 | async-start | bytes 655360 | tf_op jit(solution)/shard_map/reduce_scatter | solution.py:291
  16.1 45.4 %collective-permute-start.16 = (bf16[256,256]{1,0:T(8,128)(2,1)}, bf16[256,256]{1,0:T(8,128)(2,1)}, u32[]{:S(2)}, u32[]{:S(2)}) collective-permute-start(bf16[256,256]{1,0:T(8,128)(2,1)} %param.21), channel_id=1, source_target_pairs={{0,4},{4,8},{8,12},{12,0},{1,5},{5,9},{9,13},{13,1},{2,6},{6,10},{... | collective-permute-start | bytes 393224 | tf_op jit(solution)/shard_map/ppermute | solution.py:255
  27.7 27.3 %collective-permute-start.1 = (bf16[512,256]{1,0:T(8,128)(2,1)S(1)}, bf16[512,256]{1,0:T(8,128)(2,1)S(1)}, u32[]{:S(2)}, u32[]{:S(2)}) collective-permute-start(bf16[512,256]{1,0:T(8,128)(2,1)S(1)} %get-tuple-element.163), channel_id=1, source_target_pairs={{0,1},{1,13},{2,5},{3,9},{4,2},{5,14},{6,6},{7,10},{8,3},{9,15},{1... | collective-permute-start | bytes 786440 | tf_op jit(solution)/shard_map/ppermute | solution.py:214
  29.7 37.5 %collective-permute-start.18 = (bf16[256,256]{1,0:T(8,128)(2,1)S(1)}, bf16[256,256]{1,0:T(8,128)(2,1)S(1)}, u32[]{:S(2)}, u32[]{:S(2)}) collective-permute-start(bf16[256,256]{1,0:T(8,128)(2,1)S(1)} %copy-done.55), channel_id=1, source_target_pairs={{0,12},{4,0},{8,4},{12,8},{1,13},{5,1},{9,5},{13,9},{2,14},{6,2},{... | collective-permute-start | bytes 393224 | tf_op jit(solution)/shard_map/ppermute | solution.py:255
  34.9 33.1 %collective-permute-start.17 = (bf16[256,256]{1,0:T(8,128)(2,1)S(1)}, bf16[256,256]{1,0:T(8,128)(2,1)}, u32[]{:S(2)}, u32[]{:S(2)}) collective-permute-start(bf16[256,256]{1,0:T(8,128)(2,1)S(1)} %copy-done.55), channel_id=1, source_target_pairs={{0,8},{4,12},{8,0},{12,4},{1,9},{5,13},{9,1},{13,5},{2,10},{6,14},... | collective-permute-start | bytes 393224 | tf_op jit(solution)/shard_map/ppermute | solution.py:255
  58.4 41.7 %collective-permute-start.12 = (bf16[256,768]{1,0:T(8,128)(2,1)S(1)}, bf16[256,768]{1,0:T(8,128)(2,1)S(1)}, u32[]{:S(2)}, u32[]{:S(2)}) collective-permute-start(bf16[256,768]{1,0:T(8,128)(2,1)S(1)} %copy-done.39), channel_id=1, source_target_pairs={{0,12},{4,0},{8,4},{12,8},{1,13},{5,1},{9,5},{13,9},{2,14},{6,2},{... | collective-permute-start | bytes 1179656 | tf_op jit(solution)/shard_map/ppermute | solution.py:255
  61.5 38.8 %collective-permute-start.11 = (bf16[256,768]{1,0:T(8,128)(2,1)S(1)}, bf16[256,768]{1,0:T(8,128)(2,1)}, u32[]{:S(2)}, u32[]{:S(2)}) collective-permute-start(bf16[256,768]{1,0:T(8,128)(2,1)S(1)} %copy-done.39), channel_id=1, source_target_pairs={{0,8},{4,12},{8,0},{12,4},{1,9},{5,13},{9,1},{13,5},{2,10},{6,14},... | collective-permute-start | bytes 1179656 | tf_op jit(solution)/shard_map/ppermute | solution.py:255
  67.9 99.6 %collective-permute-start.8 = (bf16[512,1024]{1,0:T(8,128)(2,1)}, bf16[512,1024]{1,0:T(8,128)(2,1)}, u32[]{:S(2)}, u32[]{:S(2)}) collective-permute-start(bf16[512,1024]{1,0:T(8,128)(2,1)} %fusion.23), channel_id=1, source_target_pairs={{0,2},{1,3},{2,0},{3,1},{4,6},{5,7},{6,4},{7,5},{8,10},{9,11},{10,... | collective-permute-start | bytes 3145736 | tf_op jit(solution)/shard_map/ppermute | solution.py:239
  68.0 69.1 %collective-permute-start.26 = (bf16[1024,256]{1,0:T(8,128)(2,1)}, bf16[1024,256]{1,0:T(8,128)(2,1)S(1)}, u32[]{:S(2)}, u32[]{:S(2)}) collective-permute-start(bf16[1024,256]{1,0:T(8,128)(2,1)} %param.27), channel_id=1, source_target_pairs={{0,4},{4,8},{8,12},{12,0},{1,5},{5,9},{9,13},{13,1},{2,6},{6,10},{... | collective-permute-start | bytes 1572872 | tf_op jit(solution)/shard_map/ppermute | solution.py:255
  69.0 85.9 %collective-permute-start.28 = (bf16[1024,256]{1,0:T(8,128)(2,1)}, bf16[1024,256]{1,0:T(8,128)(2,1)S(1)}, u32[]{:S(2)}, u32[]{:S(2)}) collective-permute-start(bf16[1024,256]{1,0:T(8,128)(2,1)} %param.27), channel_id=1, source_target_pairs={{0,12},{4,0},{8,4},{12,8},{1,13},{5,1},{9,5},{13,9},{2,14},{6,2},{... | collective-permute-start | bytes 1572872 | tf_op jit(solution)/shard_map/ppermute | solution.py:255
  100.1 56.0 %collective-permute-start.27 = (bf16[1024,256]{1,0:T(8,128)(2,1)}, bf16[1024,256]{1,0:T(8,128)(2,1)S(1)}, u32[]{:S(2)}, u32[]{:S(2)}) collective-permute-start(bf16[1024,256]{1,0:T(8,128)(2,1)} %param.27), channel_id=1, source_target_pairs={{0,8},{4,12},{8,0},{12,4},{1,9},{5,13},{9,1},{13,5},{2,10},{6,14},... | collective-permute-start | bytes 1572872 | tf_op jit(solution)/shard_map/ppermute | solution.py:255
  100.9 66.6 %collective-permute-start.24 = (bf16[256,1024]{1,0:T(8,128)(2,1)}, bf16[256,1024]{1,0:T(8,128)(2,1)S(1)}, u32[]{:S(2)}, u32[]{:S(2)}) collective-permute-start(bf16[256,1024]{1,0:T(8,128)(2,1)} %param.25), channel_id=1, source_target_pairs={{0,8},{4,12},{8,0},{12,4},{1,9},{5,13},{9,1},{13,5},{2,10},{6,14},... | collective-permute-start | bytes 1572872 | tf_op jit(solution)/shard_map/ppermute | solution.py:255
  137.2 45.0 %collective-permute-start.23 = (bf16[256,1024]{1,0:T(8,128)(2,1)}, bf16[256,1024]{1,0:T(8,128)(2,1)S(1)}, u32[]{:S(2)}, u32[]{:S(2)}) collective-permute-start(bf16[256,1024]{1,0:T(8,128)(2,1)} %param.25), channel_id=1, source_target_pairs={{0,4},{4,8},{8,12},{12,0},{1,5},{5,9},{9,13},{13,1},{2,6},{6,10},{... | collective-permute-start | bytes 1572872 | tf_op jit(solution)/shard_map/ppermute | solution.py:255
  154.9 27.7 %collective-permute-start.20 = (bf16[256,1024]{1,0:T(8,128)(2,1)S(1)}, bf16[256,1024]{1,0:T(8,128)(2,1)S(1)}, u32[]{:S(2)}, u32[]{:S(2)}) collective-permute-start(bf16[256,1024]{1,0:T(8,128)(2,1)S(1)} %get-tuple-element.173), channel_id=1, source_target_pairs={{0,2},{1,3},{2,0},{3,1},{4,6},{5,7},{6,4},{7,5},{8,10},{9,11},{10,... | collective-permute-start | bytes 1572872 | tf_op jit(solution)/shard_map/ppermute | solution.py:239
  156.1 30.3 %collective-permute-start.25 = (bf16[256,1024]{1,0:T(8,128)(2,1)}, bf16[256,1024]{1,0:T(8,128)(2,1)S(1)}, u32[]{:S(2)}, u32[]{:S(2)}) collective-permute-start(bf16[256,1024]{1,0:T(8,128)(2,1)} %param.25), channel_id=1, source_target_pairs={{0,12},{4,0},{8,4},{12,8},{1,13},{5,1},{9,5},{13,9},{2,14},{6,2},{... | collective-permute-start | bytes 1572872 | tf_op jit(solution)/shard_map/ppermute | solution.py:255
  167.5 22.2 %collective-permute-start.7 = (bf16[512,1024]{1,0:T(8,128)(2,1)}, bf16[512,1024]{1,0:T(8,128)(2,1)S(1)}, u32[]{:S(2)}, u32[]{:S(2)}) collective-permute-start(bf16[512,1024]{1,0:T(8,128)(2,1)} %fusion.23), channel_id=1, source_target_pairs={{0,1},{1,0},{2,3},{3,2},{4,5},{5,4},{6,7},{7,6},{8,9},{9,8},{10,11... | collective-permute-start | bytes 3145736 | tf_op jit(solution)/shard_map/ppermute | solution.py:239
  167.5 22.1 %collective-permute-start.9 = (bf16[512,1024]{1,0:T(8,128)(2,1)}, bf16[512,1024]{1,0:T(8,128)(2,1)S(1)}, u32[]{:S(2)}, u32[]{:S(2)}) collective-permute-start(bf16[512,1024]{1,0:T(8,128)(2,1)} %collective-permute-done.8), channel_id=1, source_target_pairs={{0,1},{1,0},{2,3},{3,2},{4,5},{5,4},{6,7},{7,6},{8,9},{9,8},{10,11... | collective-permute-start | bytes 3145736 | tf_op jit(solution)/shard_map/ppermute | solution.py:239
  186.4 42.8 %collective-permute-start.29 = (bf16[256,1024]{1,0:T(8,128)(2,1)}, bf16[256,1024]{1,0:T(8,128)(2,1)S(1)}, u32[]{:S(2)}, u32[]{:S(2)}) collective-permute-start(bf16[256,1024]{1,0:T(8,128)(2,1)} %param.25), channel_id=1, source_target_pairs={{0,2},{1,3},{2,0},{3,1},{4,6},{5,7},{6,4},{7,5},{8,10},{9,11},{10,... | collective-permute-start | bytes 1572872 | tf_op jit(solution)/shard_map/ppermute | solution.py:239
  188.1 123.6 %collective-permute-start.49 = (f32[1,1]{1,0:T(1,128)}, f32[1,1]{1,0:T(1,128)}, u32[]{:S(2)}, u32[]{:S(2)}) collective-permute-start(f32[1,1]{1,0:T(1,128)} %bitcast.124), channel_id=1, source_target_pairs={{0,16},{16,0},{1,17},{17,1},{2,18},{18,2},{3,19},{19,3},{4,20},{20... | collective-permute-start | bytes 20 | tf_op jit(solution)/shard_map/ppermute | solution.py:239
  229.3 55.8 %collective-permute-start.34 = (bf16[4,1024,256]{2,1,0:T(8,128)(2,1)S(1)}, bf16[4,1024,256]{2,1,0:T(8,128)(2,1)S(1)}, u32[]{:S(2)}, u32[]{:S(2)}) collective-permute-start(bf16[4,1024,256]{2,1,0:T(8,128)(2,1)S(1)} %pad_maximum_fusion.11), channel_id=1, source_target_pairs={{0,2},{1,3},{2,0},{3,1},{4,6},{5,7},{6,4},{7,5},{8,10},{9,11},{10,... | collective-permute-start | bytes 6291464 | tf_op jit(solution)/shard_map/ppermute | solution.py:239
  240.1 31.4 %collective-permute-start.31 = (bf16[256,1024]{1,0:T(8,128)(2,1)S(1)}, bf16[256,1024]{1,0:T(8,128)(2,1)S(1)}, u32[]{:S(2)}, u32[]{:S(2)}) collective-permute-start(bf16[256,1024]{1,0:T(8,128)(2,1)S(1)} %collective-permute-done.29), channel_id=1, source_target_pairs={{0,8},{4,12},{8,0},{12,4},{1,9},{5,13},{9,1},{13,5},{2,10},{6,14},... | collective-permute-start | bytes 1572872 | tf_op jit(solution)/shard_map/ppermute | solution.py:255
  242.1 40.7 %collective-permute-start.30 = (bf16[256,1024]{1,0:T(8,128)(2,1)S(1)}, bf16[256,1024]{1,0:T(8,128)(2,1)S(1)}, u32[]{:S(2)}, u32[]{:S(2)}) collective-permute-start(bf16[256,1024]{1,0:T(8,128)(2,1)S(1)} %collective-permute-done.29), channel_id=1, source_target_pairs={{0,4},{4,8},{8,12},{12,0},{1,5},{5,9},{9,13},{13,1},{2,6},{6,10},{... | collective-permute-start | bytes 1572872 | tf_op jit(solution)/shard_map/ppermute | solution.py:255
  248.8 36.4 %collective-permute-start.22 = (bf16[512,1024]{1,0:T(8,128)(2,1)S(1)}, bf16[512,1024]{1,0:T(8,128)(2,1)S(1)}, u32[]{:S(2)}, u32[]{:S(2)}) collective-permute-start(bf16[512,1024]{1,0:T(8,128)(2,1)S(1)} %add_convert_fusion.3), channel_id=1, source_target_pairs={{0,1},{1,0},{2,3},{3,2},{4,5},{5,4},{6,7},{7,6},{8,9},{9,8},{10,11... | collective-permute-start | bytes 3145736 | tf_op jit(solution)/shard_map/ppermute | solution.py:239
  301.3 73.8 %collective-permute-start.35 = (bf16[512,1024]{1,0:T(8,128)(2,1)S(1)}, bf16[512,1024]{1,0:T(8,128)(2,1)S(1)}, u32[]{:S(2)}, u32[]{:S(2)}) collective-permute-start(bf16[512,1024]{1,0:T(8,128)(2,1)S(1)} %slice.248), channel_id=1, source_target_pairs={{0,1},{1,0},{2,3},{3,2},{4,5},{5,4},{6,7},{7,6},{8,9},{9,8},{10,11... | collective-permute-start | bytes 3145736 | tf_op jit(solution)/shard_map/ppermute | solution.py:239
  302.3 21.6 %collective-permute-start.44 = (s32[512]{0:T(512)S(1)}, s32[512]{0:T(512)S(1)}, u32[]{:S(2)}, u32[]{:S(2)}) collective-permute-start(s32[512]{0:T(512)S(1)} %bitcast.407), channel_id=1, source_target_pairs={{0,0},{1,12},{2,4},{3,8},{4,1},{5,13},{6,5},{7,9},{8,2},{9,14},{10... | collective-permute-start | bytes 6152 | tf_op jit(solution)/shard_map/ppermute | solution.py:377
  305.3 21.7 %collective-permute-start.45 = (bf16[512,256]{1,0:T(8,128)(2,1)S(1)}, bf16[512,256]{1,0:T(8,128)(2,1)S(1)}, u32[]{:S(2)}, u32[]{:S(2)}) collective-permute-start(bf16[512,256]{1,0:T(8,128)(2,1)S(1)} %get-tuple-element.168), channel_id=1, source_target_pairs={{0,0},{1,12},{2,4},{3,8},{4,1},{5,13},{6,5},{7,9},{8,2},{9,14},{10... | collective-permute-start | bytes 786440 | tf_op jit(solution)/shard_map/ppermute | solution.py:214
  309.1 42.7 %collective-permute-start.48 = (bf16[512,256]{1,0:T(8,128)(2,1)S(1)}, bf16[512,256]{1,0:T(8,128)(2,1)S(1)}, u32[]{:S(2)}, u32[]{:S(2)}) collective-permute-start(bf16[512,256]{1,0:T(8,128)(2,1)S(1)} %get-tuple-element.169), channel_id=1, source_target_pairs={{0,3},{1,15},{2,7},{3,11},{4,0},{5,12},{6,4},{7,8},{8,1},{9,13},{1... | collective-permute-start | bytes 786440 | tf_op jit(solution)/shard_map/ppermute | solution.py:214
  317.6 34.2 %collective-permute-start.47 = (bf16[512,256]{1,0:T(8,128)(2,1)S(1)}, bf16[512,256]{1,0:T(8,128)(2,1)S(1)}, u32[]{:S(2)}, u32[]{:S(2)}) collective-permute-start(bf16[512,256]{1,0:T(8,128)(2,1)S(1)} %get-tuple-element.170), channel_id=1, source_target_pairs={{0,2},{1,14},{2,6},{3,10},{4,3},{5,15},{6,7},{7,11},{8,0},{9,12},{... | collective-permute-start | bytes 786440 | tf_op jit(solution)/shard_map/ppermute | solution.py:214
  323.9 33.5 %collective-permute-start.46 = (bf16[512,256]{1,0:T(8,128)(2,1)S(1)}, bf16[512,256]{1,0:T(8,128)(2,1)S(1)}, u32[]{:S(2)}, u32[]{:S(2)}) collective-permute-start(bf16[512,256]{1,0:T(8,128)(2,1)S(1)} %get-tuple-element.171), channel_id=1, source_target_pairs={{0,1},{1,13},{2,5},{3,9},{4,2},{5,14},{6,6},{7,10},{8,3},{9,15},{1... | collective-permute-start | bytes 786440 | tf_op jit(solution)/shard_map/ppermute | solution.py:214
  327.0 33.2 %collective-permute-start.40 = (bf16[512,256]{1,0:T(8,128)(2,1)S(1)}, bf16[512,256]{1,0:T(8,128)(2,1)S(1)}, u32[]{:S(2)}, u32[]{:S(2)}) collective-permute-start(bf16[512,256]{1,0:T(8,128)(2,1)S(1)} %get-tuple-element.132), channel_id=1, source_target_pairs={{0,0},{1,12},{2,4},{3,8},{4,1},{5,13},{6,5},{7,9},{8,2},{9,14},{10... | collective-permute-start | bytes 786440 | tf_op jit(solution)/shard_map/ppermute | solution.py:214
  432.5 29.3 %collective-permute-start.78 = (bf16[1024,256]{0,1:T(8,128)(2,1)}, bf16[1024,256]{0,1:T(8,128)(2,1)}, u32[]{:S(2)}, u32[]{:S(2)}) collective-permute-start(bf16[1024,256]{0,1:T(8,128)(2,1)} %fusion.34), channel_id=1, source_target_pairs={{0,2},{1,3},{2,0},{3,1},{4,6},{5,7},{6,4},{7,5},{8,10},{9,11},{10,... | collective-permute-start | bytes 1572872 | tf_op jit(solution)/shard_map/ppermute | solution.py:239
  437.0 22.5 %collective-permute-start.60 = (bf16[512,256]{1,0:T(8,128)(2,1)}, bf16[512,256]{1,0:T(8,128)(2,1)}, u32[]{:S(2)}, u32[]{:S(2)}) collective-permute-start(bf16[512,256]{1,0:T(8,128)(2,1)} %get-tuple-element.122), channel_id=1, source_target_pairs={{0,2},{1,3},{2,0},{3,1},{4,6},{5,7},{6,4},{7,5},{8,10},{9,11},{10,... | collective-permute-start | bytes 786440 | tf_op jit(solution)/shard_map/ppermute | solution.py:239
  463.9 265.2 %reduce-scatter.5.cloned.1.call-start = ((), (), s32[]{:S(2)}) async-start(), calls=%async_computation.4 | async-start | bytes 1966080 | tf_op jit(solution)/shard_map/reduce_scatter | solution.py:291
  509.9 239.8 %reduce-scatter.11.cloned.1.call-start = ((), (), s32[]{:S(2)}) async-start(), calls=%async_computation.7 | async-start | bytes 2621440 | tf_op jit(solution)/shard_map/reduce_scatter | solution.py:291
  515.3 46.5 %collective-permute-start.86 = (bf16[1024,1024]{1,0:T(8,128)(2,1)S(1)}, bf16[1024,1024]{1,0:T(8,128)(2,1)S(1)}, u32[]{:S(2)}, u32[]{:S(2)}) collective-permute-start(bf16[1024,1024]{1,0:T(8,128)(2,1)S(1)} %convolution_convert_fusion.1), channel_id=1, source_target_pairs={{0,2},{1,3},{2,0},{3,1},{4,6},{5,7},{6,4},{7,5},{8,10},{9,11},{10,... | collective-permute-start | bytes 6291464 | tf_op jit(solution)/shard_map/ppermute | solution.py:239
  564.2 187.8 %reduce-scatter.9.cloned.1.call-start = ((), (), s32[]{:S(2)}) async-start(), calls=%async_computation.6 | async-start | bytes 2621440 | tf_op jit(solution)/shard_map/reduce_scatter | solution.py:291
  571.6 81.4 %collective-permute-start.80 = (bf16[1024,1024]{1,0:T(8,128)(2,1)}, bf16[1024,1024]{1,0:T(8,128)(2,1)}, u32[]{:S(2)}, u32[]{:S(2)}) collective-permute-start(bf16[1024,1024]{1,0:T(8,128)(2,1)} %convolution_convert_fusion.2), channel_id=1, source_target_pairs={{0,2},{1,3},{2,0},{3,1},{4,6},{5,7},{6,4},{7,5},{8,10},{9,11},{10,... | collective-permute-start | bytes 6291464 | tf_op jit(solution)/shard_map/ppermute | solution.py:239
  579.0 78.0 %collective-permute-start.62 = (bf16[2,512,1024]{2,1,0:T(8,128)(2,1)}, bf16[2,512,1024]{2,1,0:T(8,128)(2,1)}, u32[]{:S(2)}, u32[]{:S(2)}) collective-permute-start(bf16[2,512,1024]{2,1,0:T(8,128)(2,1)} %dynamic-slice_bitcast_fusion), channel_id=1, source_target_pairs={{0,1},{1,0},{2,3},{3,2},{4,5},{5,4},{6,7},{7,6},{8,9},{9,8},{10,11... | collective-permute-start | bytes 6291464 | tf_op jit(solution)/shard_map/ppermute | solution.py:239
  582.3 33.7 %collective-permute-start.36 = (bf16[512,256]{1,0:T(8,128)(2,1)}, bf16[512,256]{1,0:T(8,128)(2,1)}, u32[]{:S(2)}, u32[]{:S(2)}) collective-permute-start(bf16[512,256]{1,0:T(8,128)(2,1)} %get-tuple-element.140), channel_id=1, source_target_pairs={{0,0},{12,1},{4,2},{8,3},{1,4},{13,5},{5,6},{9,7},{2,8},{14,9},{6,... | collective-permute-start | bytes 786440 | tf_op jit(solution)/shard_map/ppermute | solution.py:232
  586.3 44.7 %collective-permute-start.54 = (f32[5,1024]{1,0:T(8,128)S(1)}, f32[5,1024]{1,0:T(8,128)S(1)}, u32[]{:S(2)}, u32[]{:S(2)}) collective-permute-start(f32[5,1024]{1,0:T(8,128)S(1)} %stack.478), channel_id=1, source_target_pairs={{0,16},{16,0},{1,17},{17,1},{2,18},{18,2},{3,19},{19,3},{4,20},{20... | collective-permute-start | bytes 61448 | tf_op jit(solution)/shard_map/ppermute | solution.py:239
  586.6 46.6 %collective-permute-start.39 = (bf16[512,256]{1,0:T(8,128)(2,1)}, bf16[512,256]{1,0:T(8,128)(2,1)}, u32[]{:S(2)}, u32[]{:S(2)}) collective-permute-start(bf16[512,256]{1,0:T(8,128)(2,1)} %get-tuple-element.141), channel_id=1, source_target_pairs={{3,0},{15,1},{7,2},{11,3},{0,4},{12,5},{4,6},{8,7},{1,8},{13,9},{5... | collective-permute-start | bytes 786440 | tf_op jit(solution)/shard_map/ppermute | solution.py:232
  661.3 36.3 %collective-permute-start.63 = (bf16[512,1024]{1,0:T(8,128)(2,1)}, bf16[512,1024]{1,0:T(8,128)(2,1)}, u32[]{:S(2)}, u32[]{:S(2)}) collective-permute-start(bf16[512,1024]{1,0:T(8,128)(2,1)} %fusion.32), channel_id=1, source_target_pairs={{0,2},{1,3},{2,0},{3,1},{4,6},{5,7},{6,4},{7,5},{8,10},{9,11},{10,... | collective-permute-start | bytes 3145736 | tf_op jit(solution)/shard_map/ppermute | solution.py:239
  665.2 21.7 %collective-permute-start.58 = (f32[5,1024]{1,0:T(8,128)S(1)}, f32[5,1024]{1,0:T(8,128)S(1)}, u32[]{:S(2)}, u32[]{:S(2)}) collective-permute-start(f32[5,1024]{1,0:T(8,128)S(1)} %add.604), channel_id=1, source_target_pairs={{0,2},{1,3},{2,0},{3,1},{4,6},{5,7},{6,4},{7,5},{8,10},{9,11},{10,... | collective-permute-start | bytes 61448 | tf_op jit(solution)/shard_map/ppermute | solution.py:239
  665.7 21.1 %collective-permute-start.75 = (f32[768]{0:T(1024)S(1)}, f32[768]{0:T(1024)S(1)}, u32[]{:S(2)}, u32[]{:S(2)}) collective-permute-start(f32[768]{0:T(1024)S(1)} %add.621), channel_id=1, source_target_pairs={{0,4},{4,0},{8,12},{12,8},{1,5},{5,1},{9,13},{13,9},{2,6},{6,2},{1... | collective-permute-start | bytes 9224 | tf_op jit(solution)/shard_map/ppermute | solution.py:239
  721.4 22.6 %collective-permute-start.67 = (bf16[512,256]{1,0:T(8,128)(2,1)S(1)}, bf16[512,256]{1,0:T(8,128)(2,1)S(1)}, u32[]{:S(2)}, u32[]{:S(2)}) collective-permute-start(bf16[512,256]{1,0:T(8,128)(2,1)S(1)} %get-tuple-element.109), channel_id=1, source_target_pairs={{3,0},{15,1},{7,2},{11,3},{0,4},{12,5},{4,6},{8,7},{1,8},{13,9},{5... | collective-permute-start | bytes 786440 | tf_op jit(solution)/shard_map/ppermute | solution.py:232
  722.6 24.2 %collective-permute-start.66 = (bf16[512,256]{1,0:T(8,128)(2,1)S(1)}, bf16[512,256]{1,0:T(8,128)(2,1)S(1)}, u32[]{:S(2)}, u32[]{:S(2)}) collective-permute-start(bf16[512,256]{1,0:T(8,128)(2,1)S(1)} %get-tuple-element.110), channel_id=1, source_target_pairs={{2,0},{14,1},{6,2},{10,3},{3,4},{15,5},{7,6},{11,7},{0,8},{12,9},{... | collective-permute-start | bytes 786440 | tf_op jit(solution)/shard_map/ppermute | solution.py:232
  724.5 23.2 %collective-permute-start.65 = (bf16[512,256]{1,0:T(8,128)(2,1)S(1)}, bf16[512,256]{1,0:T(8,128)(2,1)S(1)}, u32[]{:S(2)}, u32[]{:S(2)}) collective-permute-start(bf16[512,256]{1,0:T(8,128)(2,1)S(1)} %get-tuple-element.111), channel_id=1, source_target_pairs={{1,0},{13,1},{5,2},{9,3},{2,4},{14,5},{6,6},{10,7},{3,8},{15,9},{7... | collective-permute-start | bytes 786440 | tf_op jit(solution)/shard_map/ppermute | solution.py:232
  729.1 23.5 %collective-permute-start.73 = (bf16[256,768]{1,0:T(8,128)(2,1)}, bf16[256,768]{1,0:T(8,128)(2,1)S(1)}, u32[]{:S(2)}, u32[]{:S(2)}) collective-permute-start(bf16[256,768]{1,0:T(8,128)(2,1)} %reduce-scatter.5.cloned.1.call-done), channel_id=1, source_target_pairs={{0,16},{16,0},{1,17},{17,1},{2,18},{18,2},{3,19},{19,3},{4,20},{20... | collective-permute-start | bytes 1179656 | tf_op jit(solution)/shard_map/ppermute | solution.py:239
  (120 other events, 2026.0 us)
Sparse Core Ops, SparseCore 0:
  464.0 18.5 reduce-scatter.6
  510.0 34.2 reduce-scatter.4
  564.3 58.0 reduce-scatter.10
  657.1 41.9 reduce-scatter.8

commit v2 on v1

--- a/solution.py
+++ b/solution.py
@@ -32,7 +32,7 @@
 def swap(a):
     return jnp.concatenate([a[:,HALF:],a[:,:HALF]],axis=1)
 
-def fwd_kernel(heads, slope_ref, mixed_ref, out_ref, lse_ref, qs, ks, vs, bias, sc, mx, ls, acc):
+def attention_rows(heads, order, after, slope_ref, mixed_ref, out_ref, lse_ref, qs, ks, vs, bias, sc, mx, ls, acc):
     pairs=heads//2
     blocks=mixed_ref.shape[0]//BLOCK
     lo=low_lanes(BLOCK)
@@ -54,7 +54,8 @@
         bias[h]=tent*slope_ref[h]
     jrow=lax.broadcasted_iota(jnp.int32,(1,BLOCK),1)
     @pl.loop(0,blocks)
-    def _(i):
+    def _(it):
+        i=order(it)
         for h in range(heads):
             t=nt(qs[h,i],ks[h//2,i])*SCALE2+bias[h]
             sc[h,i]=t
@@ -89,23 +90,7 @@
             for n,h in enumerate((2*p,2*p+1)):
                 lse=mx[h]+jnp.log2(tot[n])
                 lse_ref[h,pl.ds(i,1),:]=lse.T[:1]
-
-def attention_forward(slopes2, mixed):
-    tokens,width=mixed.shape
-    heads=width//(3*HEAD_DIM); pairs=heads//2; blocks=tokens//BLOCK
-    f32=jnp.float32; bf=jnp.bfloat16
-    return pl.pallas_call(
-        functools.partial(fwd_kernel,heads),
-        out_shape=(jax.ShapeDtypeStruct((tokens,heads*HEAD_DIM),bf),jax.ShapeDtypeStruct((heads,blocks,BLOCK),f32)),
-        in_specs=[pl.BlockSpec(memory_space=pltpu.SMEM),pl.BlockSpec(memory_space=pltpu.VMEM)],
-        out_specs=(pl.BlockSpec(memory_space=pltpu.VMEM),)*2,
-        scratch_shapes=[pltpu.VMEM((heads,blocks,BLOCK,PAIR),bf),pltpu.VMEM((pairs,blocks,BLOCK,PAIR),bf),
-            pltpu.VMEM((pairs,blocks,2*BLOCK,PAIR),bf),pltpu.VMEM((heads,BLOCK,BLOCK),f32),
-            pltpu.VMEM((heads,blocks,BLOCK,BLOCK),f32),pltpu.VMEM((heads,BLOCK,PAIR),f32),pltpu.VMEM((heads,BLOCK,PAIR),f32),
-            pltpu.VMEM((pairs,BLOCK,PAIR),f32)],
-        compiler_params=pltpu.CompilerParams(vmem_limit_bytes=40<<20),
-        name="attention_forward",
-    )(slopes2,mixed)
+        after(it,i)
 
 def bwd_kernel(heads, slope_ref, mixed_ref, dout_ref, out_ref, lse_ref, grad_ref, qs, ks, km, vp, ds_, delta, bias, dq, dk, dv):
     pairs=heads//2
@@ -188,6 +173,461 @@
     )(slopes2,mixed,dout,out,lse)
 
 
+MESH = pl.DeviceIdType.MESH
+
+
+def hint(index, size):
+    return pl.ds(pl.multiple_of(index * size, size), size)
+
+
+def remote(src, dst, sems, number, target):
+    send, recv = sems
+    return pltpu.make_async_remote_copy(
+        src_ref=src, dst_ref=dst, send_sem=send.at[number], recv_sem=recv.at[number],
+        device_id=target, device_id_type=MESH,
+    )
+
+
+def partner(index, bit):
+    return index + bit - 2 * bit * ((index // bit) % 2)
+
+
+class Place:
+    def __init__(self):
+        self.dp, self.row, self.col = (lax.axis_index(a) for a in ("dp", "row", "col"))
+        self.dps = lax.axis_size("dp")
+        self.core, self.chip = self.col % 2, self.col // 2
+        self.near, self.far = partner(self.col, 1), partner(self.col, 2)
+        self.twin = partner(self.dp, 1)
+        self.half = self.dp % 2
+        self.plane = 3 * self.core + self.chip - 2 * self.core * self.chip
+        self.source = 2 * (((self.row + 1) // 2) % 2) + self.row // 2
+        self.stays = self.plane == self.row
+
+
+def greet(place, transpose, counts):
+    barrier = pltpu.get_barrier_semaphore()
+
+    def signal(target):
+        pl.semaphore_signal(barrier, inc=1, device_id=target, device_id_type=MESH)
+
+    for step in (1, 2, 3):
+        signal({"row": (place.row + step) % 4})
+    signal({"col": place.near})
+    signal({"col": place.far})
+    signal({"dp": place.twin})
+    amount = 6
+    if counts:
+        bit = 2
+        while bit < place.dps:
+            signal({"dp": partner(place.dp, bit)})
+            amount += 1
+            bit *= 2
+    if transpose:
+        for other in range(4):
+            @pl.when(jnp.logical_not(jnp.logical_and(place.stays, place.col == other)))
+            def _():
+                signal({"row": place.plane, "col": other})
+
+            @pl.when(jnp.logical_not(jnp.logical_and(place.stays, place.row == other)))
+            def _():
+                signal({"row": other, "col": place.source})
+        amount = amount + 8 - 2 * place.stays.astype(jnp.int32)
+    pl.semaphore_wait(barrier, amount)
+
+
+class Transpose:
+    def __init__(self, place, src, dst, sems, first):
+        self.place, self.src, self.dst, self.sems, self.first = place, src, dst, sems, first
+        self.rows, self.width = src.shape[0] // 4, src.shape[1]
+
+    def out(self, other):
+        p = self.place
+        send, recv = self.sems
+        return pltpu.make_async_remote_copy(
+            src_ref=self.src.at[pl.ds(other * self.rows, self.rows)],
+            dst_ref=self.dst.at[:, hint(p.row, self.width)],
+            send_sem=send.at[self.first + other], recv_sem=recv.at[self.first + p.row],
+            device_id={"row": p.plane, "col": other}, device_id_type=MESH,
+        )
+
+    def kept(self):
+        p = self.place
+        return pltpu.make_async_copy(
+            self.src.at[hint(p.col, self.rows)],
+            self.dst.at[:, hint(p.row, self.width)],
+            self.sems[1].at[self.first + p.row],
+        )
+
+    def start(self):
+        p = self.place
+        for other in range(4):
+            @pl.when(jnp.logical_not(jnp.logical_and(p.stays, p.col == other)))
+            def _():
+                self.out(other).start()
+
+        @pl.when(p.stays)
+        def _():
+            self.kept().start()
+
+    def wait_recv(self):
+        p = self.place
+        for other in range(4):
+            mine = jnp.logical_and(p.stays, p.row == other)
+            part = self.dst.at[:, pl.ds(other * self.width, self.width)]
+
+            @pl.when(jnp.logical_not(mine))
+            def _():
+                pltpu.make_async_remote_copy(
+                    src_ref=part, dst_ref=part, send_sem=self.sems[0].at[self.first + other],
+                    recv_sem=self.sems[1].at[self.first + other],
+                    device_id={"row": other, "col": p.source}, device_id_type=MESH,
+                ).wait_recv()
+
+            @pl.when(mine)
+            def _():
+                self.kept().wait()
+
+    def wait_send(self):
+        p = self.place
+        for other in range(4):
+            @pl.when(jnp.logical_not(jnp.logical_and(p.stays, p.col == other)))
+            def _():
+                self.out(other).wait_send()
+
+
+class Weight:
+    def __init__(self, place, src, dst, offset, by_rows, sems, first):
+        self.place, self.src, self.dst, self.offset, self.by_rows = place, src, dst, offset, by_rows
+        self.sems, self.first = sems, first
+        self.rows, self.width = src.shape
+        self.part = self.rows // 2
+
+    def whole(self, side, row):
+        if self.by_rows:
+            return self.dst.at[side, hint(row, self.rows)]
+        return self.dst.at[side, pl.ds(self.offset, self.rows), hint(row, self.width)]
+
+    def piece(self, side, row, half):
+        if self.by_rows:
+            return self.dst.at[side, hint(row * 2 + half, self.part)]
+        start = pl.multiple_of(self.offset + half * self.part, self.part)
+        return self.dst.at[side, pl.ds(start, self.part), hint(row, self.width)]
+
+    def own(self):
+        return pltpu.make_async_copy(self.src, self.whole(0, self.place.row), self.sems[1].at[self.first])
+
+    def across(self):
+        return remote(
+            self.src, self.whole(1, self.place.row), self.sems, self.first + 1, {"col": self.place.far}
+        )
+
+    def along(self, side, step):
+        p = self.place
+        src = self.src.at[hint(p.half, self.part)] if side == 0 else self.piece(1, p.row, p.half)
+        return remote(
+            src, self.piece(side, p.row, p.half), self.sems, self.first + 2 + 3 * side + step - 1,
+            {"row": (p.row + step) % 4},
+        )
+
+    def came(self, side, step):
+        p = self.place
+        part = self.piece(side, (p.row + 4 - step) % 4, p.half)
+        return remote(
+            part, part, self.sems, self.first + 2 + 3 * side + step - 1, {"row": (p.row + step) % 4}
+        )
+
+    def twin(self, side, step):
+        p = self.place
+        part = self.piece(side, (p.row + 4 - step) % 4, p.half)
+        return remote(part, part, self.sems, self.first + 8 + 3 * side + step - 1, {"dp": p.twin})
+
+    def from_twin(self, side, step):
+        p = self.place
+        part = self.piece(side, (p.row + 4 - step) % 4, 1 - p.half)
+        return remote(part, part, self.sems, self.first + 8 + 3 * side + step - 1, {"dp": p.twin})
+
+
+WEIGHT_SEMS = 14
+
+
+def first_kernel(
+    heads, token_total,
+    slope_ref, bias_ref, vector_ref, joined_ref, layer_ref, up_ref, down_ref, out_ref, up_bias_ref,
+    teacher_ref, cot_ref, valid_ref,
+    xt_ref, nall_ref, mixed_ref, att_ref, lse_ref, chip_ref, jall_ref, vall_ref, gt_ref, vt_ref, scale_ref,
+    up2_ref, dn2_ref, ub2_ref,
+    qs, ks, vs, bias, sc, mx, ls, acc, grad, count, sends, recvs,
+):
+    sems = (sends, recvs)
+    p = Place()
+    quarter = xt_ref.shape[0]
+    greet(p, True, True)
+    moved = Transpose(p, layer_ref, xt_ref, sems, 0)
+    target = Transpose(p, grad, gt_ref, sems, 4)
+    base = 8
+    weights = []
+    for n, (src, dst, offset, by_rows) in enumerate(
+        ((out_ref, dn2_ref, down_ref.shape[0], False), (up_ref, up2_ref, 0, True), (down_ref, dn2_ref, 0, False))
+    ):
+        weights.append(Weight(p, src, dst, offset, by_rows, sems, base + n * WEIGHT_SEMS))
+    base += 3 * WEIGHT_SEMS
+    moved.start()
+    small_base, joined_base, bias_base = base, base + 4, base + 8
+    base += 10
+
+    def small(step):
+        return remote(
+            vector_ref, vall_ref.at[:, hint(p.row, 256)], sems, small_base + step, {"row": (p.row + step) % 4}
+        )
+
+    def small_came(step):
+        part = vall_ref.at[:, hint((p.row + 4 - step) % 4, 256)]
+        return remote(part, part, sems, small_base + step, {"row": (p.row + step) % 4})
+
+    def joined(step):
+        return remote(
+            joined_ref, jall_ref.at[hint(p.row, 256)], sems, joined_base + step, {"row": (p.row + step) % 4}
+        )
+
+    def joined_came(step):
+        part = jall_ref.at[hint((p.row + 4 - step) % 4, 256)]
+        return remote(part, part, sems, joined_base + step, {"row": (p.row + step) % 4})
+
+    small_own = pltpu.make_async_copy(vector_ref, vall_ref.at[:, hint(p.row, 256)], recvs.at[small_base])
+    joined_own = pltpu.make_async_copy(joined_ref, jall_ref.at[hint(p.row, 256)], recvs.at[joined_base])
+    bias_own = pltpu.make_async_copy(up_bias_ref, ub2_ref.at[0], recvs.at[bias_base])
+    bias_far = remote(up_bias_ref, ub2_ref.at[1], sems, bias_base + 1, {"col": p.far})
+    small_own.start()
+    joined_own.start()
+    for step in (1, 2, 3):
+        small(step).start()
+    bias_own.start()
+    bias_far.start()
+    for w in weights:
+        w.own().start()
+        w.across().start()
+
+    total = jnp.sum(jnp.sum(valid_ref[...], axis=0, keepdims=True), axis=1, keepdims=True) * (1.0 / 128.0)
+    count[0] = jnp.broadcast_to(total, (8, 128))
+    steps = [("col", 1), ("col", 2)]
+    bit = 1
+    while bit < p.dps:
+        steps.append(("dp", bit))
+        bit *= 2
+    for n, (axis, bit) in enumerate(steps):
+        other = partner(p.col if axis == "col" else p.dp, bit)
+        tally = remote(count.at[2 * n], count.at[2 * n + 1], sems, base + n, {axis: other})
+        tally.start()
+        tally.wait()
+        count[2 * n + 2] = count[2 * n] + count[2 * n + 1]
+    base += len(steps)
+    scale_ref[...] = token_total / count[2 * len(steps)]
+    scale = scale_ref[:1, :1]
+
+    @pl.loop(0, 16)
+    def _(n):
+        rows = hint(n, grad.shape[0] // 16)
+        factor = valid_ref[rows, :] * scale
+        for f in range(grad.shape[1] // 128):
+            cols = slice(f * 128, (f + 1) * 128)
+            grad[rows, cols] = (
+                cot_ref[rows, cols].astype(jnp.float32) - factor * teacher_ref[rows, cols].astype(jnp.float32)
+            ).astype(grad.dtype)
+
+    valid_base = base
+    base += 1
+
+    def valid_out():
+        return pltpu.make_async_remote_copy(
+            src_ref=valid_ref.at[hint(p.row, quarter)], dst_ref=vt_ref,
+            send_sem=sends.at[valid_base], recv_sem=recvs.at[valid_base],
+            device_id={"row": p.plane, "col": p.row}, device_id_type=MESH,
+        )
+
+    same = jnp.logical_and(p.stays, p.col == p.row)
+    valid_kept = pltpu.make_async_copy(valid_ref.at[hint(p.row, quarter)], vt_ref, recvs.at[valid_base])
+
+    @pl.when(jnp.logical_not(same))
+    def _():
+        valid_out().start()
+
+    @pl.when(same)
+    def _():
+        valid_kept.start()
+
+    for step in (1, 2, 3):
+        small_came(step).wait_recv()
+        small(step).wait_send()
+    small_own.wait()
+    moved.wait_recv()
+    joined_own.wait()
+    for step in (1, 2, 3):
+        joined(step).start()
+
+    first = p.col * quarter
+    @pl.loop(0, quarter // 128)
+    def _(n):
+        rows = hint(n, 128)
+        x = xt_ref[rows, :].astype(jnp.float32)
+        center = jnp.mean(x, 1, keepdims=True)
+        spread = jnp.mean(x * x, 1, keepdims=True) - center * center
+        standard = (x - center) * lax.rsqrt(spread + EPSILON)
+        place = pl.ds(pl.multiple_of(first + n * 128, 128), 128)
+        nall_ref[place, :] = (standard * vall_ref[0:1, :] + vall_ref[1:2, :]).astype(nall_ref.dtype)
+
+    mine = nall_ref.at[hint(p.col, quarter)]
+    to_far = remote(mine, mine, sems, base, {"col": p.far})
+    to_near = remote(mine, mine, sems, base + 1, {"col": p.near})
+    theirs = nall_ref.at[hint(p.far, quarter)]
+    far_came = remote(theirs, theirs, sems, base, {"col": p.far})
+    pass_on = remote(theirs, theirs, sems, base + 2, {"col": p.near})
+    beside = nall_ref.at[hint(p.near, quarter)]
+    near_came = remote(beside, beside, sems, base + 1, {"col": p.near})
+    corner = partner(p.far, 1)
+    across = nall_ref.at[hint(corner, quarter)]
+    corner_came = remote(across, across, sems, base + 2, {"col": p.near})
+    base += 3
+    to_far.start()
+    to_near.start()
+    for w in weights:
+        for step in (1, 2, 3):
+            w.along(0, step).start()
+        w.across().wait()
+        for step in (1, 2, 3):
+            w.along(1, step).start()
+    target.start()
+
+    def project(index):
+        @pl.loop(0, quarter // 256)
+        def _(n):
+            rows = pl.ds(pl.multiple_of(index * quarter + n * 256, 256), 256)
+            mixed_ref[rows, :] = (nn(nall_ref[rows, :], jall_ref[...]) + bias_ref[...]).astype(mixed_ref.dtype)
+
+    for step in (1, 2, 3):
+        joined_came(step).wait_recv()
+        joined(step).wait_send()
+    project(p.col)
+    near_came.wait_recv()
+    project(p.near)
+    far_came.wait_recv()
+    pass_on.start()
+    project(p.far)
+    corner_came.wait_recv()
+    project(corner)
+
+    own_heads = att_ref.shape[1]
+    blocks = mixed_ref.shape[0] // BLOCK
+    per_chip = blocks // 2
+
+    share_base = base
+
+    def share(n, i):
+        return pltpu.make_async_remote_copy(
+            src_ref=att_ref.at[hint(i, BLOCK)], dst_ref=chip_ref.at[hint(chip_place(n), BLOCK), pl.ds(own_heads, own_heads)],
+            send_sem=sends.at[share_base + n], recv_sem=recvs.at[share_base + n],
+            device_id={"col": p.far}, device_id_type=MESH,
+        )
+
+    def chip_place(n):
+        half = per_chip // 2
+        return ((n // half + p.core) % 2) * half + n % half
+
+    def after(it, i):
+        @pl.when(it < per_chip)
+        def _():
+            share(it, i).start()
+
+        @pl.when(it >= per_chip)
+        def _():
+            chip_ref[hint(chip_place(it - per_chip), BLOCK), :own_heads] = att_ref[hint(i, BLOCK), :]
+
+        for at, n, side in ((4, 0, 0), (4, 0, 1), (5, 1, 0), (6, 1, 1), (7, 2, 0), (7, 2, 1)):
+            @pl.when(it == at)
+            def _():
+                for step in (1, 2, 3):
+                    weights[n].came(side, step).wait_recv()
+                    weights[n].twin(side, step).start()
+
+    attention_rows(
+        heads, lambda it: (it + per_chip * (1 - p.chip)) % blocks, after,
+        slope_ref, mixed_ref, att_ref, lse_ref, qs, ks, vs, bias, sc, mx, ls, acc,
+    )
+    @pl.loop(0, per_chip)
+    def _(n):
+        share(n, n + per_chip * (1 - p.chip)).wait()
+
+    moved.wait_send()
+    to_far.wait_send()
+    to_near.wait_send()
+    pass_on.wait_send()
+    bias_own.wait()
+    bias_far.wait()
+
+    @pl.when(jnp.logical_not(same))
+    def _():
+        valid_out().wait_send()
+
+    kept_in = jnp.logical_and(p.stays, p.col == p.row)
+
+    @pl.when(jnp.logical_not(kept_in))
+    def _():
+        valid_out().wait_recv()
+
+    @pl.when(kept_in)
+    def _():
+        valid_kept.wait()
+
+    for w in weights:
+        w.own().wait()
+        for side in (0, 1):
+            for step in (1, 2, 3):
+                w.along(side, step).wait_send()
+                w.twin(side, step).wait_send()
+                w.from_twin(side, step).wait_recv()
+    target.wait_recv()
+    target.wait_send()
+
+
+def first_stage(slopes, bias_rows, vectors, joined, layer_in, up, down, out, up_bias, teacher, cot, valid, token_total):
+    tokens, width = layer_in.shape
+    quarter = tokens // 4
+    row_size = lax.axis_size("row")
+    features = width * row_size
+    joined_width = joined.shape[1]
+    heads = joined_width // (3 * HEAD_DIM)
+    pairs, blocks = heads // 2, tokens // BLOCK
+    f32, bf = jnp.float32, jnp.bfloat16
+    hidden, head_rows = down.shape[0], out.shape[0]
+    vmem, anyspace = pl.BlockSpec(memory_space=pltpu.VMEM), pl.BlockSpec(memory_space=pl.ANY)
+    shape = jax.ShapeDtypeStruct
+    bits = 2
+    while (1 << (bits - 2)) < lax.axis_size("dp"):
+        bits += 1
+    count = 8 + 3 * WEIGHT_SEMS + 8 + 2 + bits + 1 + 3 + blocks
+    return pl.pallas_call(
+        functools.partial(first_kernel, heads, token_total),
+        out_shape=(
+            shape((quarter, features), bf), shape((tokens, features), bf), shape((tokens, joined_width), bf),
+            shape((tokens, heads * HEAD_DIM), bf), shape((heads, blocks, BLOCK), f32),
+            shape((tokens // 2, 2 * heads * HEAD_DIM), bf), shape((features, joined_width), bf),
+            shape((8, features), f32), shape((quarter, features), bf), shape((quarter, 128), f32), shape((8, 128), f32),
+            shape((2, features, up.shape[1]), bf), shape((2, hidden + head_rows, features), bf), shape((2, 8, hidden), f32),
+        ),
+        in_specs=[pl.BlockSpec(memory_space=pltpu.SMEM), vmem, vmem, anyspace, anyspace, anyspace, anyspace, anyspace,
+                  anyspace, vmem, vmem, vmem],
+        out_specs=(vmem,) * 8 + (anyspace, anyspace, vmem, anyspace, anyspace, anyspace),
+        scratch_shapes=[pltpu.VMEM((heads,blocks,BLOCK,PAIR),bf),pltpu.VMEM((pairs,blocks,BLOCK,PAIR),bf),
+            pltpu.VMEM((pairs,blocks,2*BLOCK,PAIR),bf),pltpu.VMEM((heads,BLOCK,BLOCK),f32),
+            pltpu.VMEM((heads,blocks,BLOCK,BLOCK),f32),pltpu.VMEM((heads,BLOCK,PAIR),f32),pltpu.VMEM((heads,BLOCK,PAIR),f32),
+            pltpu.VMEM((pairs,BLOCK,PAIR),f32),
+            pltpu.VMEM((tokens, width), bf), pltpu.VMEM((2 * bits + 1, 8, 128), f32),
+            pltpu.SemaphoreType.DMA((count,)), pltpu.SemaphoreType.DMA((count,))],
+        compiler_params=pltpu.CompilerParams(vmem_limit_bytes=48 << 20, collective_id=1, has_side_effects=True),
+        name="first_stage",
+    )(slopes, bias_rows, vectors, joined, layer_in, up, down, out, up_bias, teacher, cot, valid)
+
+
 PLANE = (0, 3, 1, 2)
 
 
@@ -315,6 +755,12 @@
 
 def low(value):
     return value.astype(jnp.bfloat16)
+
+
+def partner_index(col, other):
+    core = (col + other) % 2
+    chip = (col // 2 + other // 2) % 2
+    return 2 * chip + core
 
 
 def on_device(
@@ -343,52 +789,42 @@
     head_index = col * head_count + jnp.arange(head_count, dtype=jnp.int32)
     slopes = jnp.exp2(-8.0 * (head_index.astype(f32) + 1.0) / HEADS) * LOG2E
 
-    tokens = to_tokens(layer_in)
-    vectors = jnp.stack([first_gain, first_shift, out_bias, second_gain, second_shift, down_bias])
-    vectors = gather_row(vectors).transpose(1, 0, 2).reshape(6, D).astype(f32)
-    gain_one, shift_one, bias_out, gain_two, shift_two, bias_down = (vectors[i] for i in range(6))
-    joined_all = gather_row(joined_weight).reshape(D, -1)
     zero_rows = jnp.zeros_like(joined_bias[:, :HEAD_DIM])
     bias_rows = jnp.stack(
         [joined_bias[:, :HEAD_DIM], zero_rows, joined_bias[:, HEAD_DIM:]], axis=1
-    ).reshape(-1)
+    ).reshape(1, -1).astype(f32)
+    nothing = jnp.zeros_like(first_gain)
+    vectors = jnp.stack(
+        [first_gain, first_shift, out_bias, second_gain, second_shift, down_bias, nothing, nothing]
+    ).astype(f32)
+    token_total = layer_in.shape[0] * lax.axis_size("dp") * col_size
+    (
+        tokens, normed_one_all, mixed, attended, log_totals, attended_chip, joined_all,
+        vectors, target, valid_tokens, scale, up_all, down_all, bias_all,
+    ) = first_stage(
+        slopes, bias_rows, vectors, joined_weight, layer_in, up_weight, down_weight, out_weight,
+        jnp.broadcast_to(up_bias.astype(f32), (8, up_bias.shape[0])), teacher, cotangent,
+        jnp.broadcast_to(valid.astype(f32)[:, None], (valid.shape[0], 128)), token_total,
+    )
+    gain_one, shift_one, bias_out, gain_two, shift_two, bias_down = (vectors[i] for i in range(6))
+    valid_tokens, scale = valid_tokens[:, :1], scale[0, 0]
+    hidden = down_weight.shape[0]
+    up_own, up_far = up_all[0], up_all[1]
+    down_own, down_far = down_all[0, :hidden], down_all[1, :hidden]
+    out_own, out_far = down_all[0, hidden:], down_all[1, hidden:]
+    head_width = attended.shape[1]
 
     inputs = tokens.astype(f32)
     standard_one, inverse_one = standardize(inputs)
-    normed_one = low(standard_one * gain_one + shift_one)
-    normed_one_all = gather_col(normed_one).reshape(-1, D)
-    mixed = low(nn(normed_one_all, joined_all) + bias_rows)
-    attended, log_totals = attention_forward(slopes, mixed)
-
-    out_all = gather_row(out_weight)
-    out_all = jnp.concatenate([out_all[r] for r in range(row_size)], axis=1)
-    out_all = gather_col(out_all).reshape(D, D)
-    up_own = gather_row(up_weight).reshape(D, -1)
-    up_far = gather_row(swap_with(up_weight, "col", 2)).reshape(D, -1)
-    down_own = gather_row(down_weight)
-    down_far = swap_with(down_own, "col", 2)
-    down_own = jnp.concatenate([down_own[r] for r in range(row_size)], axis=1)
-    down_far = jnp.concatenate([down_far[r] for r in range(row_size)], axis=1)
-    bias_far = swap_with(up_bias, "col", 2)
-
-    target = to_tokens(teacher)
-    cotangent_tokens = to_tokens(cotangent)
-    plane = plane_of(col_size)
-    valid_tokens = lax.ppermute(
-        pick(valid.reshape(col_size, quarter), row),
-        ("row", "col"),
-        [(r * col_size + c, plane[c] * col_size + r) for r in range(row_size) for c in range(col_size)],
-    ).astype(f32)[:, None]
-    valid_count = small_sum(jnp.sum(valid.astype(f32)).reshape(1, 1), ("dp", "col"))[0, 0]
-
-    attended_tokens = exchange_col(attended.reshape(col_size, quarter, -1))
-    attended_tokens = jnp.concatenate([attended_tokens[q] for q in range(col_size)], axis=1)
-    middle = inputs + (nn(attended_tokens, out_all) + bias_out)
+    branch = nn(attended_chip[:, :head_width], out_own) + nn(attended_chip[:, head_width:], out_far)
+    middle = inputs + (
+        branch[:quarter] + swap_with(low(branch[quarter:]), "col", 1).astype(f32) + bias_out
+    )
     standard_two, inverse_two = standardize(middle)
     normed_two = low(standard_two * gain_two + shift_two)
     normed_chip = jnp.concatenate([normed_two, swap_with(normed_two, "col", 1)], axis=0)
-    before_own = nn(normed_chip, up_own) + up_bias.astype(f32)
-    before_far = nn(normed_chip, up_far) + bias_far.astype(f32)
+    before_own = nn(normed_chip, up_own) + bias_all[0, 0]
+    before_far = nn(normed_chip, up_far) + bias_all[1, 0]
     active_own, pull_own = jax.vjp(gelu_local, before_own)
     active_far, pull_far = jax.vjp(gelu_local, before_far)
     active_own, active_far = low(active_own), low(active_far)
@@ -397,13 +833,9 @@
         branch[:quarter] + swap_with(low(branch[quarter:]), "col", 1).astype(f32) + bias_down
     )
     layer_out = to_features(low(result))
-
-    error_rows = result - target.astype(f32)
-    error_sum = jnp.sum(valid_tokens * error_rows * error_rows)
-    token_total = layer_in.shape[0] * lax.axis_size("dp") * col_size
-    grad_result = cotangent_tokens.astype(f32) + valid_tokens * error_rows * (
-        token_total / valid_count
-    )
+    layer_error = layer_out.astype(f32) - teacher.astype(f32)
+    error_sum = jnp.sum(valid.astype(f32)[:, None] * layer_error * layer_error)
+    grad_result = target.astype(f32) + valid_tokens * scale * result
     grad_low = low(grad_result)
     grad_chip = jnp.concatenate([grad_low, swap_with(grad_low, "col", 1)], axis=0)
     grad_before_own = low(pull_own(nt(grad_chip, down_own))[0])
@@ -412,11 +844,11 @@
     grad_normed_two = back[:quarter] + swap_with(low(back[quarter:]), "col", 1).astype(f32)
     grad_middle = grad_result + norm_backward(grad_normed_two, standard_two, inverse_two, gain_two)
     branch_grad = low(grad_middle)
-    attended_grad = low(nt(branch_grad, out_all))
-    width = attended_grad.shape[1] // col_size
-    attended_grad = exchange_col(
-        jnp.stack([attended_grad[:, q * width : (q + 1) * width] for q in range(col_size)])
-    ).reshape(-1, width)
+    branch_chip = jnp.concatenate([branch_grad, swap_with(branch_grad, "col", 1)], axis=0)
+    grad_own = low(nt(branch_chip, out_own))
+    grad_far = swap_with(low(nt(branch_chip, out_far)), "col", 2)
+    pieces = jnp.stack([grad_own[:quarter], grad_own[quarter:], grad_far[:quarter], grad_far[quarter:]])
+    attended_grad = jnp.concatenate([pick(pieces, partner_index(col, q)) for q in range(col_size)])
 
     down_grad_own = low(tn(grad_chip, active_own))
     down_grad_far = low(tn(grad_chip, active_far))
@@ -426,9 +858,9 @@
     up_grad = low(up_grad_own.astype(f32) + swap_with(up_grad_far, "col", 2).astype(f32))
     down_grad = sum_dp(scatter_row(down_grad)).astype(f32).T
     up_grad = sum_dp(scatter_row(up_grad)).astype(f32)
-    out_grad = low(tn(branch_grad, attended_tokens))
-    out_grad = jnp.stack([out_grad[:, q * width : (q + 1) * width] for q in range(col_size)])
-    out_grad = low(scatter_col(out_grad))
+    out_grad_own = low(tn(branch_chip, attended_chip[:, :head_width]))
+    out_grad_far = low(tn(branch_chip, attended_chip[:, head_width:]))
+    out_grad = low(out_grad_own.astype(f32) + swap_with(out_grad_far, "col", 2).astype(f32))
     out_grad = sum_dp(scatter_row(out_grad)).astype(f32).T
 
     mixed_grad = attention_backward(slopes, mixed, attended_grad, attended, log_totals)
@@ -448,7 +880,7 @@
         ]
     )
     early = small_sum(early, ("dp", "row", "col"))
-    loss = early[4, 0] / (D * valid_count)
+    loss = early[4, 0] * scale / (D * token_total)
     early = lax.dynamic_slice_in_dim(early, row * (D // row_size), D // row_size, 1)
     up_sums = jnp.sum(grad_before_own, 0, dtype=f32) + swap_with(
         jnp.sum(grad_before_far, 0, dtype=f32), "col", 2

time: 787 us -> 671 us (0.85)
  Pallas kernels: 66.6 us -> 267 us
  waiting for transfers between devices: 322 us -> 180 us
  starting transfers between devices: 201 us -> 63.3 us
  other arithmetic: 64.2 us -> 35.6 us
  local copies, waits for them, and re-layouts: 39.3 us -> 25.6 us
    pallas_call x1, Pallas kernels: 28.6 us -> 230 us  [first_stage(): pl.pallas_call(functools.partial(first_kernel, heads, token_total), out_s...]
    ppermute x31 -> x0, waiting for transfers between devices: 146 us -> none  [the longest x18 126 us: gather_row(): lax.ppermute(value, 'row', [(i, (i + step) % size) for i in range(size)])]
    ppermute x31 -> x0, starting transfers between devices: 105 us -> none  [the longest x12 59.2 us: to_tokens(): lax.ppermute(pick(blocks, (row + step) % col_size), ('row', 'col'), moves)]
    ppermute x49 -> x33, starting transfers between devices: 61.1 us -> 38.3 us  [swap_with(): return lax.ppermute(value, axis, [(i, i ^ bit) for i in range(size)])]
    another operation x23 -> x1, other arithmetic: 12.8 us -> 0.13 us  [on_device(): jnp.stack([grad_own[:quarter], grad_own[quarter:], grad_far[:quarter], gr...]
    reduce_sum x1, other arithmetic: 10.5 us -> 1.04 us  [on_device(): jnp.sum(grad_low, 0, dtype=f32)]
    ppermute x8, starting transfers between devices: 34.1 us -> 24.6 us  [to_features(): lax.ppermute(pick(blocks, (col - step) % row_size), ('row', 'col'), moves)]
    unnamed x154 -> x72, local copies, waits for them, and re-layouts: 16.4 us -> 10.7 us
  transfers between devices with their start and end apart: 92 -> 45, of which waited for: 36 -> 29; matrix products, arithmetic and copies ran while one was open for 14% -> 11% of each run, Pallas kernels for 9% -> 6%
where the time goes in v2:
time: 671 us; the launch traced here: 663 us
  Pallas kernels  267 us (40%)
  waiting for transfers between devices  180 us (27%)
  matrix products  73.1 us (11%)
  starting transfers between devices  63.3 us (9%)
  other arithmetic  35.6 us (5%)
  local copies, waits for them, and re-layouts  25.6 us (4%)
  between operations  17.6 us (3%)
    pallas_call x1, Pallas kernels, first_stage(): pl.pallas_call(functools.partial(first_kernel, heads, token_total), out_s...  230 us
    ppermute x33, waiting for transfers between devices, swap_with(): return lax.ppermute(value, axis, [(i, i ^ bit) for i in range(size)])  125 us
    ppermute x8, waiting for transfers between devices, to_features(): lax.ppermute(pick(blocks, (col - step) % row_size), ('row', 'col'), moves)  55 us
    ppermute x33, starting transfers between devices, swap_with(): return lax.ppermute(value, axis, [(i, i ^ bit) for i in range(size)])  38.3 us
    pallas_call x1, Pallas kernels, attention_backward(): pl.pallas_call(functools.partial(bwd_kernel, heads), out_shape=jax.ShapeD...  37.8 us
    dot_general x7, matrix products, tn(): lax.dot_general(a, b, (((0,), (0,)), ((), ())), preferred_element_type=jn...  28.6 us
    dot_general x7, matrix products, nt(): lax.dot_general(a, b, (((1,), (1,)), ((), ())), preferred_element_type=jn...  25.4 us
    ppermute x8, starting transfers between devices, to_features(): lax.ppermute(pick(blocks, (col - step) % row_size), ('row', 'col'), moves)  24.6 us
  transfers between devices with their start and end apart: 45, of which 29 were waited for; matrix products, arithmetic and copies ran while one was open for 11% of the time, Pallas kernels for 6%

profile of v2, /device:TPU:13, one launch (start us, length us, event | category | flops | bytes accessed | tf_op | source)
XLA Modules:
  0.0 662.8 jit_solution(6006604552806173296)
XLA Ops:
  19.0 229.6 %first_stage.1 = (bf16[512,1024]{1,0:T(8,128)(2,1)S(1)}, bf16[2048,1024]{1,0:T(8,128)(2,1)}, bf16[2048,768]{1,0:T(8,128)(2,1)}, bf16[2048,256]{1,0:T(8,128)(2,1)...) custom-call(f32[4]{0:T(128)S(1)} %exponential_multiply_fusion.slope_, ...), custom_call_target="tpu_custom_call" | custom-call | tf_op jit(solution)/shard_map/first_stage/pallas_call | solution.py:608
  253.0 2.6 collective-permute-done
  257.4 2.5 collective-permute-done.1
  260.0 2.3 fusion.37
  262.3 4.8 fusion.31
  267.1 2.3 fusion.47
  269.5 6.6 fusion.52
  280.2 2.5 collective-permute-done.7
  282.8 6.2 convert_reduce_fusion.1
  288.9 2.4 fusion.35
  291.4 6.2 convert_reduce_fusion.2
  297.6 2.4 fusion.49
  300.4 2.5 collective-permute-done.8
  304.0 2.9 convert_reduce_fusion.5
  307.0 2.7 collective-permute-done.14
  309.7 2.4 convolution_convert_fusion.4
  312.1 6.6 collective-permute-start.31
  320.9 2.5 convolution_convert_fusion.7
  323.4 7.2 %collective-permute-done.31 = bf16[1024,256]{1,0:T(8,128)(2,1)S(1)} collective-permute-done((bf16[1024,256]{1,0:T(8,128)(2,1)S(1)}, bf16[1024,256]{1,0:T(8,128)(2,1)S(1)}, u32[]{:S(2)}, u32[]{:S(2)}) %collective-permute-start.31) | collective-permute-done | bytes 524320 | tf_op jit(solution)/shard_map/ppermute | solution.py:679
  330.7 2.8 fusion.66
  333.5 8.4 %collective-permute-done.15 = bf16[1024,256]{1,0:T(8,128)(2,1)S(1)} collective-permute-done((bf16[1024,256]{1,0:T(8,128)(2,1)S(1)}, bf16[1024,256]{1,0:T(8,128)(2,1)S(1)}, u32[]{:S(2)}, u32[]{:S(2)}) %collective-permute-start.15) | collective-permute-done | bytes 524320 | tf_op jit(solution)/shard_map/ppermute | solution.py:679
  344.1 37.8 %attention_backward.1 = bf16[2048,768]{1,0:T(8,128)(2,1)S(1)} custom-call(f32[4]{0:T(128)S(1)} %exponential_multiply_fusion.slope_ref, bf16[2048,768]{1,0:T(8,128)(2,1)S(1)} %copy-done.2, bf16[2048,256]{1,0:T(8,128)(2,1)S(1)} %pad_maximum_fusion.7.dout_ref, bf16[2048,256]{1,0:T(8,128)(2,1)S(1)} %copy-done.4, f32[4,8,256]{2,1,0:T(8,128)S(1)} %get-tuple-element.40.lse_ref), custom_call_target="tpu_custom_call" | custom-call | tf_op jit(solution)/shard_map/attention_backward/pallas_call | solution.py:162
  381.9 4.7 convolution_convert_fusion.3
  386.8 5.6 convolution_convert_fusion.1
  393.6 2.6 fusion.83
  396.2 42.5 %collective-permute-done.39 = bf16[1024,1024]{1,0:T(8,128)(2,1)S(1)} collective-permute-done((bf16[1024,1024]{1,0:T(8,128)(2,1)S(1)}, bf16[1024,1024]{1,0:T(8,128)(2,1)S(1)}, u32[]{:S(2)}, u32[]{:S(2)}) %collective-permute-start.39) | collective-permute-done | bytes 2097184 | tf_op jit(solution)/shard_map/ppermute | solution.py:679
  441.2 6.0 convolution_convert_fusion.2
  448.7 3.7 convolution_convert_fusion
  457.0 8.8 %collective-permute-start.3 = (bf16[512,256]{1,0:T(8,128)(2,1)S(1)}, bf16[512,256]{1,0:T(8,128)(2,1)S(1)}, u32[]{:S(2)}, u32[]{:S(2)}) collective-permute-start(bf16[512,256]{1,0:T(8,128)(2,1)S(1)} %get-tuple-element.119), channel_id=1, source_target_pairs={{0,0},{12,1},{4,2},{8,3},{1,4},{13,5},{5,6},{9,7},{2,8},{14,9},{6,... | collective-permute-start | bytes 786440 | tf_op jit(solution)/shard_map/ppermute | solution.py:672
  469.6 20.2 %collective-permute-done.3 = bf16[512,256]{1,0:T(8,128)(2,1)S(1)} collective-permute-done((bf16[512,256]{1,0:T(8,128)(2,1)S(1)}, bf16[512,256]{1,0:T(8,128)(2,1)S(1)}, u32[]{:S(2)}, u32[]{:S(2)}) %collective-permute-start.3) | collective-permute-done | bytes 262176 | tf_op jit(solution)/shard_map/ppermute | solution.py:672
  490.9 16.6 %collective-permute-done.4 = bf16[512,256]{1,0:T(8,128)(2,1)} collective-permute-done((bf16[512,256]{1,0:T(8,128)(2,1)}, bf16[512,256]{1,0:T(8,128)(2,1)}, u32[]{:S(2)}, u32[]{:S(2)}) %collective-permute-start.4) | collective-permute-done | bytes 262176 | tf_op jit(solution)/shard_map/ppermute | solution.py:672
  507.4 3.8 collective-permute-done.6
  512.6 4.5 fusion.14
  521.2 4.5 collective-permute-start.35
  529.6 4.6 fusion.84
  536.0 3.0 collective-permute-start.12
  539.0 3.9 add_convert_fusion.1
  543.0 3.1 convert_add_fusion
  552.8 20.4 %collective-permute-done.13 = f32[5,1024]{1,0:T(8,128)S(1)} collective-permute-done((f32[5,1024]{1,0:T(8,128)S(1)}, f32[5,1024]{1,0:T(8,128)S(1)}, u32[]{:S(2)}, u32[]{:S(2)}) %collective-permute-start.13) | collective-permute-done | bytes 20512 | tf_op jit(solution)/shard_map/ppermute | solution.py:679
  578.1 3.3 collective-permute-done.32
  583.2 3.5 fusion.25
  595.4 6.0 collective-permute-start.25
  602.3 3.4 collective-permute-start.18
  609.6 4.5 collective-permute-start.21
  615.7 6.6 %collective-permute-done.18 = bf16[512,256]{1,0:T(8,128)(2,1)S(1)} collective-permute-done((bf16[512,256]{1,0:T(8,128)(2,1)S(1)}, bf16[512,256]{1,0:T(8,128)(2,1)S(1)}, u32[]{:S(2)}, u32[]{:S(2)}) %collective-permute-start.18) | collective-permute-done | bytes 262176 | tf_op jit(solution)/shard_map/ppermute | solution.py:672
  622.3 5.7 collective-permute-done.19
  635.3 9.3 %collective-permute-done.40 = bf16[256,1024]{1,0:T(8,128)(2,1)S(1)} collective-permute-done((bf16[256,1024]{1,0:T(8,128)(2,1)}, bf16[256,1024]{1,0:T(8,128)(2,1)S(1)}, u32[]{:S(2)}, u32[]{:S(2)}) %collective-permute-start.40) | collective-permute-done | bytes 524320 | tf_op jit(solution)/shard_map/ppermute | solution.py:679
  646.0 7.6 %collective-permute-done.34 = bf16[256,1024]{1,0:T(8,128)(2,1)S(1)} collective-permute-done((bf16[256,1024]{1,0:T(8,128)(2,1)}, bf16[256,1024]{1,0:T(8,128)(2,1)S(1)}, u32[]{:S(2)}, u32[]{:S(2)}) %collective-permute-start.34) | collective-permute-done | bytes 524320 | tf_op jit(solution)/shard_map/ppermute | solution.py:679
  (230 shorter events, 90.5 us)
Async XLA Ops:
  7.2 569.8 %reduce-scatter.7.cloned.1.call-start = ((), (), s32[]{:S(2)}) async-start(), calls=%async_computation.5 | async-start | bytes 655360 | tf_op jit(solution)/shard_map/reduce_scatter | solution.py:731
  252.9 2.7 collective-permute-start
  257.2 2.7 collective-permute-start.1
  269.5 21.9 %copy-start.30 = (f32[1024,1024]{1,0:T(8,128)}, f32[1024,1024]{1,0:T(8,128)S(1)}, u32[]{:S(2)}) copy-start(f32[1024,1024]{1,0:T(8,128)S(1)} %fusion.47) | copy-start | bytes 12582916
  276.2 2.7 collective-permute-start.2
  280.0 2.7 collective-permute-start.7
  300.2 2.7 collective-permute-start.8
  306.8 2.9 collective-permute-start.14
  312.1 18.6 %collective-permute-start.31 = (bf16[1024,256]{1,0:T(8,128)(2,1)S(1)}, bf16[1024,256]{1,0:T(8,128)(2,1)S(1)}, u32[]{:S(2)}, u32[]{:S(2)}) collective-permute-start(bf16[1024,256]{1,0:T(8,128)(2,1)S(1)} %convolution_convert_fusion.4), channel_id=1, source_target_pairs={{0,2},{1,3},{2,0},{3,1},{4,6},{5,7},{6,4},{7,5},{8,10},{9,11},{10,... | collective-permute-start | bytes 1572872 | tf_op jit(solution)/shard_map/ppermute | solution.py:679
  320.8 21.1 %collective-permute-start.15 = (bf16[1024,256]{1,0:T(8,128)(2,1)S(1)}, bf16[1024,256]{1,0:T(8,128)(2,1)S(1)}, u32[]{:S(2)}, u32[]{:S(2)}) collective-permute-start(bf16[1024,256]{1,0:T(8,128)(2,1)S(1)} %convolution_convert_fusion.6), channel_id=1, source_target_pairs={{0,2},{1,3},{2,0},{3,1},{4,6},{5,7},{6,4},{7,5},{8,10},{9,11},{10,... | collective-permute-start | bytes 1572872 | tf_op jit(solution)/shard_map/ppermute | solution.py:679
  333.5 280.7 %reduce-scatter.5.cloned.1.call-start = ((), (), s32[]{:S(2)}) async-start(), calls=%async_computation.4 | async-start | bytes 1966080 | tf_op jit(solution)/shard_map/reduce_scatter | solution.py:731
  344.1 37.8 %copy-start.22 = (bf16[2048,1024]{1,0:T(8,128)(2,1)S(1)}, bf16[2048,1024]{1,0:T(8,128)(2,1)}, u32[]{:S(2)}) copy-start(bf16[2048,1024]{1,0:T(8,128)(2,1)} %get-tuple-element.42) | copy-start | bytes 12582916
  386.6 243.8 %reduce-scatter.11.cloned.1.call-start = ((), (), s32[]{:S(2)}) async-start(), calls=%async_computation.7 | async-start | bytes 2621440 | tf_op jit(solution)/shard_map/reduce_scatter | solution.py:731
  392.4 46.3 %collective-permute-start.39 = (bf16[1024,1024]{1,0:T(8,128)(2,1)S(1)}, bf16[1024,1024]{1,0:T(8,128)(2,1)S(1)}, u32[]{:S(2)}, u32[]{:S(2)}) collective-permute-start(bf16[1024,1024]{1,0:T(8,128)(2,1)S(1)} %convolution_convert_fusion.1), channel_id=1, source_target_pairs={{0,2},{1,3},{2,0},{3,1},{4,6},{5,7},{6,4},{7,5},{8,10},{9,11},{10,... | collective-permute-start | bytes 6291464 | tf_op jit(solution)/shard_map/ppermute | solution.py:679
  441.1 191.2 %reduce-scatter.9.cloned.1.call-start = ((), (), s32[]{:S(2)}) async-start(), calls=%async_computation.6 | async-start | bytes 2621440 | tf_op jit(solution)/shard_map/reduce_scatter | solution.py:731
  447.2 91.8 %collective-permute-start.33 = (bf16[1024,1024]{1,0:T(8,128)(2,1)}, bf16[1024,1024]{1,0:T(8,128)(2,1)}, u32[]{:S(2)}, u32[]{:S(2)}) collective-permute-start(bf16[1024,1024]{1,0:T(8,128)(2,1)} %convolution_convert_fusion.2), channel_id=1, source_target_pairs={{0,2},{1,3},{2,0},{3,1},{4,6},{5,7},{6,4},{7,5},{8,10},{9,11},{10,... | collective-permute-start | bytes 6291464 | tf_op jit(solution)/shard_map/ppermute | solution.py:679
  454.0 88.9 %collective-permute-start.16 = (bf16[2,512,1024]{2,1,0:T(8,128)(2,1)}, bf16[2,512,1024]{2,1,0:T(8,128)(2,1)}, u32[]{:S(2)}, u32[]{:S(2)}) collective-permute-start(bf16[2,512,1024]{2,1,0:T(8,128)(2,1)} %dynamic-slice_bitcast_fusion), channel_id=1, source_target_pairs={{0,1},{1,0},{2,3},{3,2},{4,5},{5,4},{6,7},{7,6},{8,9},{9,8},{10,11... | collective-permute-start | bytes 6291464 | tf_op jit(solution)/shard_map/ppermute | solution.py:679
  457.0 32.9 %collective-permute-start.3 = (bf16[512,256]{1,0:T(8,128)(2,1)S(1)}, bf16[512,256]{1,0:T(8,128)(2,1)S(1)}, u32[]{:S(2)}, u32[]{:S(2)}) collective-permute-start(bf16[512,256]{1,0:T(8,128)(2,1)S(1)} %get-tuple-element.119), channel_id=1, source_target_pairs={{0,0},{12,1},{4,2},{8,3},{1,4},{13,5},{5,6},{9,7},{2,8},{14,9},{6,... | collective-permute-start | bytes 786440 | tf_op jit(solution)/shard_map/ppermute | solution.py:672
  465.7 41.7 %collective-permute-start.4 = (bf16[512,256]{1,0:T(8,128)(2,1)}, bf16[512,256]{1,0:T(8,128)(2,1)}, u32[]{:S(2)}, u32[]{:S(2)}) collective-permute-start(bf16[512,256]{1,0:T(8,128)(2,1)} %get-tuple-element.122), channel_id=1, source_target_pairs={{1,0},{13,1},{5,2},{9,3},{2,4},{14,5},{6,6},{10,7},{3,8},{15,9},{7... | collective-permute-start | bytes 786440 | tf_op jit(solution)/shard_map/ppermute | solution.py:672
  467.7 39.8 %collective-permute-start.5 = (bf16[512,256]{1,0:T(8,128)(2,1)}, bf16[512,256]{1,0:T(8,128)(2,1)}, u32[]{:S(2)}, u32[]{:S(2)}) collective-permute-start(bf16[512,256]{1,0:T(8,128)(2,1)} %get-tuple-element.121), channel_id=1, source_target_pairs={{2,0},{14,1},{6,2},{10,3},{3,4},{15,5},{7,6},{11,7},{0,8},{12,9},{... | collective-permute-start | bytes 786440 | tf_op jit(solution)/shard_map/ppermute | solution.py:672
  490.5 20.7 %collective-permute-start.6 = (bf16[512,256]{1,0:T(8,128)(2,1)S(1)}, bf16[512,256]{1,0:T(8,128)(2,1)}, u32[]{:S(2)}, u32[]{:S(2)}) collective-permute-start(bf16[512,256]{1,0:T(8,128)(2,1)S(1)} %get-tuple-element.120), channel_id=1, source_target_pairs={{3,0},{15,1},{7,2},{11,3},{0,4},{12,5},{4,6},{8,7},{1,8},{13,9},{5... | collective-permute-start | bytes 786440 | tf_op jit(solution)/shard_map/ppermute | solution.py:672
  490.9 21.8 %copy-start.12 = (bf16[2048,256]{1,0:T(8,128)(2,1)S(1)}, bf16[2048,256]{1,0:T(8,128)(2,1)}, u32[]{:S(2)}) copy-start(bf16[2048,256]{1,0:T(8,128)(2,1)} %teacher_ref.1) | copy-start | bytes 3145732
  517.9 3.3 collective-permute-start.9
  521.2 6.5 collective-permute-start.10
  521.2 5.5 collective-permute-start.35
  526.6 7.6 %collective-permute-start.36 = (f32[1024]{0:T(1024)S(1)}, f32[1024]{0:T(1024)S(1)}, u32[]{:S(2)}, u32[]{:S(2)}) collective-permute-start(f32[1024]{0:T(1024)S(1)} %add.450), channel_id=1, source_target_pairs={{0,16},{16,0},{1,17},{17,1},{2,18},{18,2},{3,19},{19,3},{4,20},{20... | collective-permute-start | bytes 12296 | tf_op jit(solution)/shard_map/ppermute | solution.py:679
  527.7 8.3 %collective-permute-start.11 = (f32[5,1024]{1,0:T(8,128)S(1)}, f32[5,1024]{1,0:T(8,128)S(1)}, u32[]{:S(2)}, u32[]{:S(2)}) collective-permute-start(f32[5,1024]{1,0:T(8,128)S(1)} %add.406), channel_id=1, source_target_pairs={{0,8},{4,12},{8,0},{12,4},{1,9},{5,13},{9,1},{13,5},{2,10},{6,14},... | collective-permute-start | bytes 61448 | tf_op jit(solution)/shard_map/ppermute | solution.py:679
  534.2 14.5 %collective-permute-start.37 = (f32[1024]{0:T(1024)S(1)}, f32[1024]{0:T(1024)S(1)}, u32[]{:S(2)}, u32[]{:S(2)}) collective-permute-start(f32[1024]{0:T(1024)S(1)} %add.451), channel_id=1, source_target_pairs={{0,4},{4,0},{8,12},{12,8},{1,5},{5,1},{9,13},{13,9},{2,6},{6,2},{1... | collective-permute-start | bytes 12296 | tf_op jit(solution)/shard_map/ppermute | solution.py:679
  536.0 12.8 %collective-permute-start.12 = (f32[5,1024]{1,0:T(8,128)S(1)}, f32[5,1024]{1,0:T(8,128)S(1)}, u32[]{:S(2)}, u32[]{:S(2)}) collective-permute-start(f32[5,1024]{1,0:T(8,128)S(1)} %add.407), channel_id=1, source_target_pairs={{0,1},{1,0},{2,3},{3,2},{4,5},{5,4},{6,7},{7,6},{8,9},{9,8},{10,11... | collective-permute-start | bytes 61448 | tf_op jit(solution)/shard_map/ppermute | solution.py:679
  547.4 35.8 %collective-permute-start.17 = (bf16[512,1024]{1,0:T(8,128)(2,1)}, bf16[512,1024]{1,0:T(8,128)(2,1)}, u32[]{:S(2)}, u32[]{:S(2)}) collective-permute-start(bf16[512,1024]{1,0:T(8,128)(2,1)} %fusion.67), channel_id=1, source_target_pairs={{0,2},{1,3},{2,0},{3,1},{4,6},{5,7},{6,4},{7,5},{8,10},{9,11},{10,... | collective-permute-start | bytes 3145736 | tf_op jit(solution)/shard_map/ppermute | solution.py:679
  548.4 2.9 collective-permute-start.28
  548.7 3.5 collective-permute-start.38
  548.8 24.4 %collective-permute-start.13 = (f32[5,1024]{1,0:T(8,128)S(1)}, f32[5,1024]{1,0:T(8,128)S(1)}, u32[]{:S(2)}, u32[]{:S(2)}) collective-permute-start(f32[5,1024]{1,0:T(8,128)S(1)} %add.408), channel_id=1, source_target_pairs={{0,2},{1,3},{2,0},{3,1},{4,6},{5,7},{6,4},{7,5},{8,10},{9,11},{10,... | collective-permute-start | bytes 61448 | tf_op jit(solution)/shard_map/ppermute | solution.py:679
  551.2 21.9 %collective-permute-start.29 = (f32[768]{0:T(1024)S(1)}, f32[768]{0:T(1024)S(1)}, u32[]{:S(2)}, u32[]{:S(2)}) collective-permute-start(f32[768]{0:T(1024)S(1)} %add.443), channel_id=1, source_target_pairs={{0,4},{4,0},{8,12},{12,8},{1,5},{5,1},{9,13},{13,9},{2,6},{6,2},{1... | collective-permute-start | bytes 9224 | tf_op jit(solution)/shard_map/ppermute | solution.py:679
  573.2 3.7 collective-permute-start.30
  577.0 4.5 collective-permute-start.32
  586.7 2.6 collective-permute-start.22
  589.3 2.6 collective-permute-start.23
  591.9 3.5 collective-permute-start.24
  595.4 6.8 %collective-permute-start.25 = (f32[2,1024]{1,0:T(2,128)S(1)}, f32[2,1024]{1,0:T(2,128)S(1)}, u32[]{:S(2)}, u32[]{:S(2)}) collective-permute-start(f32[2,1024]{1,0:T(2,128)S(1)} %add.438), channel_id=1, source_target_pairs={{0,1},{1,0},{2,3},{3,2},{4,5},{5,4},{6,7},{7,6},{8,9},{9,8},{10,11... | collective-permute-start | bytes 24584 | tf_op jit(solution)/shard_map/ppermute | solution.py:679
  602.2 11.9 %collective-permute-start.26 = (f32[2,1024]{1,0:T(2,128)S(1)}, f32[2,1024]{1,0:T(2,128)S(1)}, u32[]{:S(2)}, u32[]{:S(2)}) collective-permute-start(f32[2,1024]{1,0:T(2,128)S(1)} %add.439), channel_id=1, source_target_pairs={{0,2},{1,3},{2,0},{3,1},{4,6},{5,7},{6,4},{7,5},{8,10},{9,11},{10,... | collective-permute-start | bytes 24584 | tf_op jit(solution)/shard_map/ppermute | solution.py:679
  602.3 20.0 %collective-permute-start.18 = (bf16[512,256]{1,0:T(8,128)(2,1)S(1)}, bf16[512,256]{1,0:T(8,128)(2,1)S(1)}, u32[]{:S(2)}, u32[]{:S(2)}) collective-permute-start(bf16[512,256]{1,0:T(8,128)(2,1)S(1)} %get-tuple-element.100), channel_id=1, source_target_pairs={{0,0},{12,1},{4,2},{8,3},{1,4},{13,5},{5,6},{9,7},{2,8},{14,9},{6,... | collective-permute-start | bytes 786440 | tf_op jit(solution)/shard_map/ppermute | solution.py:672
  605.8 22.2 %collective-permute-start.19 = (bf16[512,256]{1,0:T(8,128)(2,1)S(1)}, bf16[512,256]{1,0:T(8,128)(2,1)S(1)}, u32[]{:S(2)}, u32[]{:S(2)}) collective-permute-start(bf16[512,256]{1,0:T(8,128)(2,1)S(1)} %get-tuple-element.103), channel_id=1, source_target_pairs={{1,0},{13,1},{5,2},{9,3},{2,4},{14,5},{6,6},{10,7},{3,8},{15,9},{7... | collective-permute-start | bytes 786440 | tf_op jit(solution)/shard_map/ppermute | solution.py:672
  607.7 21.1 %collective-permute-start.20 = (bf16[512,256]{1,0:T(8,128)(2,1)S(1)}, bf16[512,256]{1,0:T(8,128)(2,1)S(1)}, u32[]{:S(2)}, u32[]{:S(2)}) collective-permute-start(bf16[512,256]{1,0:T(8,128)(2,1)S(1)} %get-tuple-element.102), channel_id=1, source_target_pairs={{2,0},{14,1},{6,2},{10,3},{3,4},{15,5},{7,6},{11,7},{0,8},{12,9},{... | collective-permute-start | bytes 786440 | tf_op jit(solution)/shard_map/ppermute | solution.py:672
  609.6 20.4 %collective-permute-start.21 = (bf16[512,256]{1,0:T(8,128)(2,1)S(1)}, bf16[512,256]{1,0:T(8,128)(2,1)S(1)}, u32[]{:S(2)}, u32[]{:S(2)}) collective-permute-start(bf16[512,256]{1,0:T(8,128)(2,1)S(1)} %get-tuple-element.101), channel_id=1, source_target_pairs={{3,0},{15,1},{7,2},{11,3},{0,4},{12,5},{4,6},{8,7},{1,8},{13,9},{5... | collective-permute-start | bytes 786440 | tf_op jit(solution)/shard_map/ppermute | solution.py:672
  614.2 19.2 %collective-permute-start.27 = (bf16[256,768]{1,0:T(8,128)(2,1)}, bf16[256,768]{1,0:T(8,128)(2,1)}, u32[]{:S(2)}, u32[]{:S(2)}) collective-permute-start(bf16[256,768]{1,0:T(8,128)(2,1)} %reduce-scatter.5.cloned.1.call-done), channel_id=1, source_target_pairs={{0,16},{16,0},{1,17},{17,1},{2,18},{18,2},{3,19},{19,3},{4,20},{20... | collective-permute-start | bytes 1179656 | tf_op jit(solution)/shard_map/ppermute | solution.py:679
  630.3 14.3 %collective-permute-start.40 = (bf16[256,1024]{1,0:T(8,128)(2,1)}, bf16[256,1024]{1,0:T(8,128)(2,1)S(1)}, u32[]{:S(2)}, u32[]{:S(2)}) collective-permute-start(bf16[256,1024]{1,0:T(8,128)(2,1)} %reduce-scatter.11.cloned.1.call-done), channel_id=1, source_target_pairs={{0,16},{16,0},{1,17},{17,1},{2,18},{18,2},{3,19},{19,3},{4,20},{20... | collective-permute-start | bytes 1572872 | tf_op jit(solution)/shard_map/ppermute | solution.py:679
  632.3 21.4 %collective-permute-start.34 = (bf16[256,1024]{1,0:T(8,128)(2,1)}, bf16[256,1024]{1,0:T(8,128)(2,1)S(1)}, u32[]{:S(2)}, u32[]{:S(2)}) collective-permute-start(bf16[256,1024]{1,0:T(8,128)(2,1)} %reduce-scatter.9.cloned.1.call-done), channel_id=1, source_target_pairs={{0,16},{16,0},{1,17},{17,1},{2,18},{18,2},{3,19},{19,3},{4,20},{20... | collective-permute-start | bytes 1572872 | tf_op jit(solution)/shard_map/ppermute | solution.py:679
  (32 other events, 194.5 us)
Sparse Core Ops, SparseCore 0:
  333.6 24.4 reduce-scatter.6
  386.7 39.3 reduce-scatter.4
  441.2 68.0 reduce-scatter.10
  543.1 39.6 reduce-scatter.8

commit v3 on v2

--- a/solution.py
+++ b/solution.py
@@ -92,7 +92,7 @@
                 lse_ref[h,pl.ds(i,1),:]=lse.T[:1]
         after(it,i)
 
-def bwd_kernel(heads, slope_ref, mixed_ref, dout_ref, out_ref, lse_ref, grad_ref, qs, ks, km, vp, ds_, delta, bias, dq, dk, dv):
+def attention_rows_backward(heads, slope_ref, mixed_ref, dout_ref, out_ref, lse_ref, grad_ref, qs, ks, km, vp, ds_, delta, bias, steep, dq, dk, dv):
     pairs=heads//2
     blocks=mixed_ref.shape[0]//BLOCK
     lo=low_lanes(BLOCK)
@@ -120,8 +120,8 @@
     tent=jnp.minimum(kl,2*ql-kl).astype(jnp.float32)
     ramp=kl.astype(jnp.float32)
     for h in range(heads):
-        bias[0,h]=tent*slope_ref[h]
-        bias[1,h]=ramp*slope_ref[h]
+        bias[h]=tent*slope_ref[h]
+        steep[h]=ramp[:,:PAIR]*slope_ref[h]
     def block(i,j,first):
         for p in range(pairs):
             ps=[];gs=[]
@@ -129,7 +129,7 @@
                 q=qs[p,i,n*BLOCK:(n+1)*BLOCK]
                 d=ds_[p,i,n*BLOCK:(n+1)*BLOCK]
                 row=slope_ref[h]*((j-i)*BLOCK).astype(jnp.float32)-lse_ref[h,pl.ds(i,1),:]
-                t=nt(ks[p,j],q)*SCALE2+row+bias[0 if first else 1,h]
+                t=nt(ks[p,j],q)*SCALE2+row+(bias[h] if first else jnp.concatenate([steep[h],steep[h]],1))
                 e=jnp.exp2(t)
                 g=e*(nt(vp[p,j],d)-delta[h,pl.ds(i,1),:])
                 ps.append(e.astype(jnp.bfloat16)); gs.append(g.astype(jnp.bfloat16))
@@ -153,24 +153,6 @@
             a=dq[p,b]*0.125; k=swap(dk[p,b]*0.125); v=dv[p,b]
             for n,t in enumerate((jnp.where(lo,a,k),jnp.where(lo,v,a),jnp.where(lo,k,v))):
                 grad_ref[rows,(3*p+n)*PAIR:(3*p+n+1)*PAIR]=t.astype(grad_ref.dtype)
-
-def attention_backward(slopes2, mixed, dout, out, lse):
-    tokens,width=mixed.shape
-    heads=width//(3*HEAD_DIM); pairs=heads//2; blocks=tokens//BLOCK
-    f32=jnp.float32; bf=jnp.bfloat16
-    V=pl.BlockSpec(memory_space=pltpu.VMEM)
-    return pl.pallas_call(
-        functools.partial(bwd_kernel,heads),
-        out_shape=jax.ShapeDtypeStruct((tokens,width),bf),
-        in_specs=[pl.BlockSpec(memory_space=pltpu.SMEM),V,V,V,V],
-        out_specs=V,
-        scratch_shapes=[pltpu.VMEM((pairs,blocks,2*BLOCK,PAIR),bf),pltpu.VMEM((pairs,blocks,BLOCK,PAIR),bf),
-            pltpu.VMEM((pairs,blocks,2*BLOCK,PAIR),bf),pltpu.VMEM((pairs,blocks,BLOCK,PAIR),bf),
-            pltpu.VMEM((pairs,blocks,2*BLOCK,PAIR),bf),pltpu.VMEM((heads,blocks,BLOCK),f32),
-            pltpu.VMEM((2,heads,BLOCK,BLOCK),f32)]+[pltpu.VMEM((pairs,blocks,BLOCK,PAIR),f32)]*3,
-        compiler_params=pltpu.CompilerParams(vmem_limit_bytes=40<<20),
-        name="attention_backward",
-    )(slopes2,mixed,dout,out,lse)
 
 
 MESH = pl.DeviceIdType.MESH
@@ -628,50 +610,425 @@
     )(slopes, bias_rows, vectors, joined, layer_in, up, down, out, up_bias, teacher, cot, valid)
 
 
-PLANE = (0, 3, 1, 2)
-
-
-def plane_of(col_size):
-    return PLANE if col_size == len(PLANE) else tuple(range(col_size))
-
-
-def pick(stacked, index):
-    return lax.dynamic_index_in_dim(stacked, index, 0, keepdims=False)
-
-
-def to_tokens(local_rows):
-    row_size, col_size = lax.axis_size("row"), lax.axis_size("col")
-    row, col = lax.axis_index("row"), lax.axis_index("col")
-    plane = plane_of(col_size)
-    blocks = local_rows.reshape(col_size, local_rows.shape[0] // col_size, -1)
-    came = []
-    for step in range(row_size):
-        moves = [
-            (r * col_size + c, plane[c] * col_size + (r + step) % col_size)
-            for r in range(row_size)
-            for c in range(col_size)
+class Untranspose:
+    def __init__(self, place, src, dst, sems, first):
+        self.place, self.src, self.dst, self.sems, self.first = place, src, dst, sems, first
+        self.rows, self.width = src.shape[0], src.shape[1] // 4
+
+    def out(self, other):
+        p = self.place
+        return pltpu.make_async_remote_copy(
+            src_ref=self.src.at[:, pl.ds(other * self.width, self.width)],
+            dst_ref=self.dst.at[hint(p.col, self.rows)],
+            send_sem=self.sems[0].at[self.first + other], recv_sem=self.sems[1].at[self.first + p.col],
+            device_id={"row": other, "col": p.source}, device_id_type=MESH,
+        )
+
+    def kept(self):
+        p = self.place
+        return pltpu.make_async_copy(
+            self.src.at[:, hint(p.row, self.width)],
+            self.dst.at[hint(p.col, self.rows)],
+            self.sems[1].at[self.first + p.col],
+        )
+
+    def start(self):
+        p = self.place
+        for other in range(4):
+            @pl.when(jnp.logical_not(jnp.logical_and(p.stays, p.row == other)))
+            def _():
+                self.out(other).start()
+
+        @pl.when(p.stays)
+        def _():
+            self.kept().start()
+
+    def wait_recv(self):
+        p = self.place
+        for other in range(4):
+            mine = jnp.logical_and(p.stays, p.col == other)
+            part = self.dst.at[pl.ds(other * self.rows, self.rows)]
+
+            @pl.when(jnp.logical_not(mine))
+            def _():
+                pltpu.make_async_remote_copy(
+                    src_ref=part, dst_ref=part, send_sem=self.sems[0].at[self.first + other],
+                    recv_sem=self.sems[1].at[self.first + other],
+                    device_id={"row": p.plane, "col": other}, device_id_type=MESH,
+                ).wait_recv()
+
+            @pl.when(mine)
+            def _():
+                self.kept().wait()
+
+    def wait_send(self):
+        p = self.place
+        for other in range(4):
+            @pl.when(jnp.logical_not(jnp.logical_and(p.stays, p.row == other)))
+            def _():
+                self.out(other).wait_send()
+
+
+def add_into(total, pieces, rows=128):
+    @pl.loop(0, total.shape[0] // rows)
+    def _(n):
+        part = hint(n, rows)
+        value = total[part, :].astype(jnp.float32)
+        for piece in pieces:
+            value = value + piece[part, :].astype(jnp.float32)
+        total[part, :] = value.astype(total.dtype)
+
+
+class Share:
+    def __init__(self, place, kind, own, far, result, buffers, sems, first):
+        self.p, self.kind, self.own, self.far, self.result, self.sems, self.first = (
+            place, kind, own, far, result, sems, first
+        )
+        self.width = own.shape[1]
+        self.part = self.width // 2
+        self.block = own.shape[0] // 4
+        self.mine, self.theirs = hint(place.half, self.part), hint(1 - place.half, self.part)
+        self.buffers = buffers
+
+    def first_copies(self):
+        p, b = self.p, self.buffers
+        if self.kind == "xy":
+            return [
+                remote(src.at[:, self.theirs], b["came"].at[n], self.sems, self.first + n, {"dp": p.twin})
+                for n, src in enumerate((self.own, self.far))
+            ]
+        if self.kind == "yx":
+            return [remote(self.far, b["came"], self.sems, self.first, {"col": p.far})]
+        return [remote(self.own.at[:, self.theirs], b["half"], self.sems, self.first, {"dp": p.twin})]
+
+    def start(self):
+        for copy in self.first_copies():
+            copy.start()
+
+    def add_own(self, totals, sources):
+        load = self.buffers["load"]
+        parts = [
+            (total.at[pl.ds(n * self.block, self.block)], source.at[pl.ds(n * self.block, self.block)])
+            for total, source in zip(totals, sources)
+            for n in range(4)
         ]
-        came.append(lax.ppermute(pick(blocks, (row + step) % col_size), ("row", "col"), moves))
-    came = jnp.stack(came)
-    return jnp.concatenate([pick(came, (col - f) % row_size) for f in range(row_size)], axis=1)
-
-
-def to_features(local_tokens):
-    row_size, col_size = lax.axis_size("row"), lax.axis_size("col")
-    row, col = lax.axis_index("row"), lax.axis_index("col")
-    plane = plane_of(col_size)
-    width = local_tokens.shape[1] // row_size
-    blocks = jnp.stack([local_tokens[:, f * width : (f + 1) * width] for f in range(row_size)])
-    came = []
-    for step in range(row_size):
-        moves = [
-            (plane[c] * col_size + (r + step) % col_size, r * col_size + c)
-            for r in range(row_size)
-            for c in range(col_size)
+        copies = [
+            pltpu.make_async_copy(source, load.at[n % 2], self.sems[1].at[self.first + 8 + n % 2])
+            for n, (_, source) in enumerate(parts)
         ]
-        came.append(lax.ppermute(pick(blocks, (col - step) % row_size), ("row", "col"), moves))
-    came = jnp.stack(came)
-    return jnp.concatenate([pick(came, (q - row) % row_size) for q in range(col_size)], axis=0)
+        copies[0].start()
+        for n, (total, _) in enumerate(parts):
+            if n + 1 < len(parts):
+                copies[n + 1].start()
+            copies[n].wait()
+            add_into(total, [load.at[n % 2]])
+
+    def second_copy(self):
+        p, b = self.p, self.buffers
+        if self.kind == "xy":
+            return remote(b["came"].at[1], b["other"], self.sems, self.first + 2, {"col": p.far})
+        return remote(b["came"].at[:, self.theirs], b["half"], self.sems, self.first + 2, {"dp": p.twin})
+
+    def first_sum(self):
+        b = self.buffers
+        for copy in self.first_copies():
+            copy.wait()
+        if self.kind == "xy":
+            self.add_own(
+                [b["came"].at[n] for n in (0, 1)], [src.at[:, self.mine] for src in (self.own, self.far)]
+            )
+        elif self.kind == "yx":
+            self.add_own([b["came"]], [self.own])
+        else:
+            add_into(b["half"], [self.own.at[:, self.mine]])
+
+    def total(self):
+        return self.buffers["came"].at[0] if self.kind == "xy" else self.buffers["half"]
+
+    def second_sum(self):
+        b = self.buffers
+        self.second_copy().wait()
+        if self.kind == "xy":
+            add_into(b["came"].at[0], [b["other"]])
+        else:
+            add_into(b["half"], [b["came"].at[:, self.mine]])
+
+    def row_copy(self, step):
+        p = self.p
+        target = (p.row + step) % 4
+        return remote(
+            self.total().at[hint(target, self.block)], self.buffers["rows"].at[step - 1], self.sems,
+            self.first + 2 + step, {"row": target},
+        )
+
+    def start_rows(self):
+        for step in (1, 2, 3):
+            self.row_copy(step).start()
+
+    def last_copy(self):
+        part = self.buffers["last"]
+        return remote(part.at[self.p.half], part.at[self.p.half], self.sems, self.first + 6, {"dp": self.p.twin})
+
+    def last_came(self):
+        part = self.buffers["last"]
+        return remote(part.at[1 - self.p.half], part.at[1 - self.p.half], self.sems, self.first + 6, {"dp": self.p.twin})
+
+    def row_sum(self):
+        for step in (1, 2, 3):
+            self.row_copy(step).wait()
+        b = self.buffers
+        total, last = self.total(), b["last"]
+
+        @pl.loop(0, self.block // 64)
+        def _(n):
+            part = hint(n, 64)
+            rows = pl.ds(pl.multiple_of(self.p.row * self.block + n * 64, 64), 64)
+            value = total[rows, :].astype(jnp.float32)
+            for step in range(3):
+                value = value + b["rows"][step, part, :].astype(jnp.float32)
+            last[self.p.half, part, :] = value.astype(last.dtype)
+
+        self.last_copy().start()
+
+    def finish(self):
+        self.last_copy().wait_send()
+        self.last_came().wait_recv()
+        for half in (0, 1):
+            self.result[:, half * self.part : (half + 1) * self.part] = self.buffers["last"][half].astype(
+                self.result.dtype
+            )
+
+
+SHARE_SEMS = 10
+
+
+def share_scratch(kind, features, width):
+    bf, part = jnp.bfloat16, width // 2
+    if kind == "xy":
+        own = dict(load=(2, features // 4, part), came=(2, features, part), other=(features, part))
+    elif kind == "yx":
+        own = dict(load=(2, features // 4, width), came=(features, width), half=(features, part))
+    else:
+        own = dict(half=(features, part))
+    own["rows"] = (3, features // 4, part)
+    own["last"] = (2, features // 4, part)
+    return {name: pltpu.VMEM(shape, bf) for name, shape in own.items()}
+
+
+def last_kernel(
+    heads, kinds,
+    slope_ref, mixed_ref, att_ref, lse_ref, nall_ref, jall_ref, xt_ref, middle_ref, gain_ref, early_ref,
+    up_sums_ref, teacher_ref, valid_ref, grads_own_ref, grads_far_ref, result_ref,
+    up_own, up_far, down_own, down_far, out_own, out_far,
+    layer_out_ref, input_grad_ref, up_ref, down_ref, out_ref, joined_ref, vector_ref,
+    dout, grad_mixed, qs, ks, km, vp, ds_, delta, bias, steep, dq, dk, dv,
+    gn, near_in, far_in, jgrad, vectors, scratch, sends, recvs,
+):
+    sems = (sends, recvs)
+    p = Place()
+    f32, bf = jnp.float32, jnp.bfloat16
+    quarter, features = xt_ref.shape
+    tokens = mixed_ref.shape[0]
+    greet(p, True, True)
+    base = 0
+    back = Untranspose(p, result_ref, layer_out_ref, sems, base)
+    ingrad = gn.at[0]
+    grad_back = Untranspose(p, ingrad, input_grad_ref, sems, base + 4)
+    base += 8
+
+    def natural(chip, n):
+        return 2 * chip + (p.core + n) % 2
+
+    share_att = [
+        remote(
+            grads_far_ref.at[pl.ds(n * quarter, quarter)], dout.at[hint(natural(p.chip, n), quarter)], sems,
+            base + n, {"col": p.far},
+        )
+        for n in (0, 1)
+    ]
+    for copy in share_att:
+        copy.start()
+    came_att = [
+        remote(
+            dout.at[hint(natural(1 - p.chip, n), quarter)], dout.at[hint(natural(1 - p.chip, n), quarter)], sems,
+            base + n, {"col": p.far},
+        )
+        for n in (0, 1)
+    ]
+    base += 2
+    up = Share(p, kinds[0], up_own, up_far, up_ref, scratch["up"], sems, base)
+    down = Share(p, kinds[1], down_own, down_far, down_ref, scratch["down"], sems, base + SHARE_SEMS)
+    out = Share(p, kinds[2], out_own, out_far, out_ref, scratch["out"], sems, base + 2 * SHARE_SEMS)
+    joined = Share(p, "x", jgrad, None, joined_ref, scratch["joined"], sems, base + 3 * SHARE_SEMS)
+    base += 4 * SHARE_SEMS
+    up.start()
+    out.start()
+    down.start()
+    back.start()
+    for n in (0, 1):
+        dout[hint(natural(p.chip, n), quarter), :] = grads_own_ref[n * quarter : (n + 1) * quarter, :]
+    for copy in came_att:
+        copy.wait_recv()
+    for copy in share_att:
+        copy.wait_send()
+
+    attention_rows_backward(
+        heads, slope_ref, mixed_ref, dout, att_ref, lse_ref, grad_mixed, qs, ks, km, vp, ds_, delta, bias, steep, dq, dk, dv
+    )
+
+    def product(index, slot):
+        @pl.loop(0, quarter // 256)
+        def _(n):
+            rows = pl.ds(pl.multiple_of(index * quarter + n * 256, 256), 256)
+            gn[slot, hint(n, 256), :] = nt(grad_mixed[rows, :], jall_ref[...]).astype(bf)
+
+    corner = partner(p.far, 1)
+    to_near = [
+        remote(gn.at[n], near_in.at[n], sems, base + n, {"col": p.near}) for n in (0, 1)
+    ]
+    to_far = remote(gn.at[2], far_in, sems, base + 2, {"col": p.far})
+    base += 3
+    product(corner, 0)
+    to_near[0].start()
+    product(p.near, 1)
+    to_near[1].start()
+    product(p.far, 2)
+    to_near[0].wait()
+    add_into(gn.at[2], [near_in.at[0]])
+    to_far.start()
+    product(p.col, 3)
+    up.first_sum()
+
+    @pl.loop(0, features // 128)
+    def _(f):
+        cols = hint(f, 128)
+        value = tn(nall_ref[:, cols], grad_mixed[...])
+        jgrad[cols, :] = value.astype(bf)
+
+    joined.start()
+    sums = jnp.zeros((1, mixed_ref.shape[1]), f32)
+    for n in range(tokens // 256):
+        sums = sums + jnp.sum(grad_mixed[n * 256 : (n + 1) * 256, :].astype(f32), axis=0, keepdims=True)
+    vectors[0, 0:2, :] = jnp.zeros((2, features), f32)
+    vectors[0, 2:8, :] = early_ref[2:8, :]
+    vectors[0, 8:16, :] = jnp.zeros((8, features), f32)
+    vectors[0, pl.ds(8 + p.col, 1), :] = up_sums_ref[0:1, :]
+    vectors[0, pl.ds(8 + p.far, 1), :] = up_sums_ref[1:2, :]
+    vectors[0, pl.ds(12 + p.col, 1), 0 : sums.shape[1]] = sums
+
+    to_near[1].wait()
+    to_far.wait()
+
+    @pl.loop(0, quarter // 64)
+    def _(n):
+        rows = hint(n, 64)
+        grad = gn[3, rows, :].astype(f32) + near_in[1, rows, :].astype(f32) + far_in[rows, :].astype(f32)
+        x = xt_ref[rows, :].astype(f32)
+        center = jnp.mean(x, 1, keepdims=True)
+        spread = jnp.mean(x * x, 1, keepdims=True) - center * center
+        inverse = lax.rsqrt(spread + EPSILON)
+        standard = (x - center) * inverse
+        vectors[0, 0:1, :] += jnp.sum(grad * standard, axis=0, keepdims=True)
+        vectors[0, 1:2, :] += jnp.sum(grad, axis=0, keepdims=True)
+        scaled = grad * gain_ref[0:1, :]
+        first = jnp.mean(scaled, 1, keepdims=True)
+        second = jnp.mean(scaled * standard, 1, keepdims=True)
+        ingrad[rows, :] = (middle_ref[rows, :] + inverse * (scaled - first - standard * second)).astype(bf)
+
+    grad_back.start()
+    up.second_copy().start()
+    out.first_sum()
+    out.second_copy().start()
+    down.first_sum()
+    down.second_copy().start()
+    joined.first_sum()
+    joined.start_rows()
+
+    back.wait_recv()
+    width = layer_out_ref.shape[1]
+    error = jnp.zeros((1, 128), f32)
+    for n in range(tokens // 128):
+        rows = slice(n * 128, (n + 1) * 128)
+        for f in range(width // 128):
+            cols = slice(f * 128, (f + 1) * 128)
+            off = layer_out_ref[rows, cols].astype(f32) - teacher_ref[rows, cols].astype(f32)
+            error = error + jnp.sum(off * off * valid_ref[rows, :].astype(f32), axis=0, keepdims=True)
+    vectors[0, 6:7, 0:128] = error
+
+    steps = [("row", 1), ("row", 2), ("col", 1), ("col", 2)]
+    bit = 1
+    while bit < p.dps:
+        steps.append(("dp", bit))
+        bit *= 2
+    up.second_sum()
+    up.start_rows()
+    for n, (axis, bit) in enumerate(steps):
+        other = partner({"row": p.row, "col": p.col, "dp": p.dp}[axis], bit)
+        tally = remote(vectors.at[2 * n], vectors.at[2 * n + 1], sems, base + n, {axis: other})
+        tally.start()
+        tally.wait()
+        vectors[2 * n + 2] = vectors[2 * n] + vectors[2 * n + 1]
+    vector_ref[...] = vectors[2 * len(steps)]
+    out.second_sum()
+    out.start_rows()
+    down.second_sum()
+    down.start_rows()
+    joined.row_sum()
+    up.row_sum()
+    out.row_sum()
+    down.row_sum()
+    for share in (joined, up, out, down):
+        share.finish()
+    back.wait_send()
+    grad_back.wait_recv()
+    grad_back.wait_send()
+
+
+def last_stage(slopes, mixed, att, lse, nall, jall, xt, middle, gain, early, up_sums, teacher, valid, grads, result,
+               up_pair, down_pair, out_pair):
+    tokens, joined_width = mixed.shape
+    quarter, features = xt.shape
+    heads = joined_width // (3 * HEAD_DIM)
+    pairs, blocks = heads // 2, tokens // BLOCK
+    f32, bf = jnp.float32, jnp.bfloat16
+    block = features // 4
+    kinds = ("xy", "yx", "yx")
+    vmem, anyspace = pl.BlockSpec(memory_space=pltpu.VMEM), pl.BlockSpec(memory_space=pl.ANY)
+    shape = jax.ShapeDtypeStruct
+    bits = 4
+    while (1 << (bits - 4)) < lax.axis_size("dp"):
+        bits += 1
+    count = 8 + 2 + 4 * SHARE_SEMS + 3 + bits
+    widths = (up_pair[0].shape[1], down_pair[0].shape[1], out_pair[0].shape[1])
+    scratch = {
+        name: share_scratch(kind, features, width)
+        for name, kind, width in zip(("up", "down", "out", "joined"), kinds + ("x",), widths + (joined_width,))
+    }
+    return pl.pallas_call(
+        functools.partial(last_kernel, heads, kinds),
+        out_shape=(
+            shape((tokens, block), bf), shape((tokens, block), bf), shape((block, widths[0]), bf),
+            shape((block, widths[1]), bf), shape((block, widths[2]), bf), shape((block, joined_width), bf),
+            shape((16, features), f32),
+        ),
+        in_specs=[pl.BlockSpec(memory_space=pltpu.SMEM)] + [vmem] * 13 + [anyspace] + [anyspace] + [anyspace] * 6,
+        out_specs=(vmem, anyspace) + (vmem,) * 5,
+        scratch_shapes=[
+            pltpu.VMEM((tokens, heads * HEAD_DIM), bf), pltpu.VMEM((tokens, joined_width), bf),
+            pltpu.VMEM((pairs,blocks,2*BLOCK,PAIR),bf),pltpu.VMEM((pairs,blocks,BLOCK,PAIR),bf),
+            pltpu.VMEM((pairs,blocks,2*BLOCK,PAIR),bf),pltpu.VMEM((pairs,blocks,BLOCK,PAIR),bf),
+            pltpu.VMEM((pairs,blocks,2*BLOCK,PAIR),bf),pltpu.VMEM((heads,blocks,BLOCK),f32),
+            pltpu.VMEM((heads,BLOCK,BLOCK),f32), pltpu.VMEM((heads,BLOCK,PAIR),f32),
+            pltpu.VMEM((pairs,blocks,BLOCK,PAIR),f32), pltpu.VMEM((pairs,blocks,BLOCK,PAIR),f32), pltpu.VMEM((pairs,blocks,BLOCK,PAIR),f32),
+            pltpu.VMEM((4, quarter, features), bf), pltpu.VMEM((2, quarter, features), bf), pltpu.VMEM((quarter, features), bf),
+            pltpu.VMEM((features, joined_width), bf),
+            pltpu.VMEM((2 * bits + 1, 16, features), f32), scratch,
+            pltpu.SemaphoreType.DMA((count,)), pltpu.SemaphoreType.DMA((count,)),
+        ],
+        compiler_params=pltpu.CompilerParams(vmem_limit_bytes=62 << 20, collective_id=2, has_side_effects=True),
+        name="last_stage",
+    )(slopes, mixed, att, lse, nall, jall, xt, middle, gain, early, up_sums, teacher, valid, grads[0], grads[1], result,
+      *up_pair, *down_pair, *out_pair)
 
 
 def swap_with(value, axis, bit):
@@ -688,53 +1045,6 @@
     return value
 
 
-def gather_row(value):
-    size, row = lax.axis_size("row"), lax.axis_index("row")
-    came = [value]
-    for step in range(1, size):
-        came.append(lax.ppermute(value, "row", [(i, (i + step) % size) for i in range(size)]))
-    came = jnp.stack(came)
-    return jnp.stack([pick(came, (row - r) % size) for r in range(size)])
-
-
-def exchange_col(value):
-    size, col = lax.axis_size("col"), lax.axis_index("col")
-    came = [pick(value, col)]
-    for bit in range(1, size):
-        came.append(swap_with(pick(value, col ^ bit), "col", bit))
-    came = jnp.stack(came)
-    return jnp.stack([pick(came, col ^ q) for q in range(size)])
-
-
-def gather_col(value):
-    size, col = lax.axis_size("col"), lax.axis_index("col")
-    far = swap_with(value, "col", 2)
-    near = swap_with(value, "col", 1)
-    far_near = swap_with(far, "col", 1)
-    came = jnp.stack([value, near, far, far_near])
-    return jnp.stack([pick(came, col ^ q) for q in range(size)])
-
-
-def scatter_col(value):
-    col = lax.axis_index("col")
-    core, chip = col % 2, col // 2
-    pairs = value.reshape((2, 2) + value.shape[1:])
-    mine = lax.dynamic_index_in_dim(pairs, core, 1, keepdims=False)
-    other = lax.dynamic_index_in_dim(pairs, 1 - core, 1, keepdims=False)
-    near = mine.astype(jnp.float32) + swap_with(other, "col", 1).astype(jnp.float32)
-    keep = pick(near, chip)
-    send = pick(near, 1 - chip).astype(jnp.bfloat16)
-    return keep + swap_with(send, "col", 2).astype(jnp.float32)
-
-
-def scatter_row(value):
-    return lax.psum_scatter(value, "row", scatter_dimension=0, tiled=True)
-
-
-def sum_dp(value):
-    return small_sum(value, ("dp",))
-
-
 def standardize(inputs):
     center = jnp.mean(inputs, 1, keepdims=True)
     spread = jnp.mean(inputs * inputs, 1, keepdims=True) - center * center
@@ -757,10 +1067,16 @@
     return value.astype(jnp.bfloat16)
 
 
-def partner_index(col, other):
-    core = (col + other) % 2
-    chip = (col // 2 + other // 2) % 2
-    return 2 * chip + core
+def pick(stacked, index):
+    return lax.dynamic_index_in_dim(stacked, index, 0, keepdims=False)
+
+
+def sum_other_pairs(value):
+    bit = 2
+    while bit < lax.axis_size("dp"):
+        value = value + swap_with(low(value), "dp", bit).astype(jnp.float32)
+        bit *= 2
+    return value
 
 
 def on_device(
@@ -832,9 +1148,6 @@
     result = middle + (
         branch[:quarter] + swap_with(low(branch[quarter:]), "col", 1).astype(f32) + bias_down
     )
-    layer_out = to_features(low(result))
-    layer_error = layer_out.astype(f32) - teacher.astype(f32)
-    error_sum = jnp.sum(valid.astype(f32)[:, None] * layer_error * layer_error)
     grad_result = target.astype(f32) + valid_tokens * scale * result
     grad_low = low(grad_result)
     grad_chip = jnp.concatenate([grad_low, swap_with(grad_low, "col", 1)], axis=0)
@@ -845,69 +1158,58 @@
     grad_middle = grad_result + norm_backward(grad_normed_two, standard_two, inverse_two, gain_two)
     branch_grad = low(grad_middle)
     branch_chip = jnp.concatenate([branch_grad, swap_with(branch_grad, "col", 1)], axis=0)
-    grad_own = low(nt(branch_chip, out_own))
-    grad_far = swap_with(low(nt(branch_chip, out_far)), "col", 2)
-    pieces = jnp.stack([grad_own[:quarter], grad_own[quarter:], grad_far[:quarter], grad_far[quarter:]])
-    attended_grad = jnp.concatenate([pick(pieces, partner_index(col, q)) for q in range(col_size)])
-
-    down_grad_own = low(tn(grad_chip, active_own))
-    down_grad_far = low(tn(grad_chip, active_far))
-    up_grad_own = low(tn(normed_chip, grad_before_own))
-    up_grad_far = low(tn(normed_chip, grad_before_far))
-    down_grad = low(down_grad_own.astype(f32) + swap_with(down_grad_far, "col", 2).astype(f32))
-    up_grad = low(up_grad_own.astype(f32) + swap_with(up_grad_far, "col", 2).astype(f32))
-    down_grad = sum_dp(scatter_row(down_grad)).astype(f32).T
-    up_grad = sum_dp(scatter_row(up_grad)).astype(f32)
-    out_grad_own = low(tn(branch_chip, attended_chip[:, :head_width]))
-    out_grad_far = low(tn(branch_chip, attended_chip[:, head_width:]))
-    out_grad = low(out_grad_own.astype(f32) + swap_with(out_grad_far, "col", 2).astype(f32))
-    out_grad = sum_dp(scatter_row(out_grad)).astype(f32).T
-
-    mixed_grad = attention_backward(slopes, mixed, attended_grad, attended, log_totals)
-    grad_normed_one = low(nt(mixed_grad, joined_all)).reshape(col_size, quarter, D)
-    grad_normed_one = scatter_col(grad_normed_one)
-    input_grad = grad_middle + norm_backward(grad_normed_one, standard_one, inverse_one, gain_one)
-    input_grad = to_features(low(input_grad)).astype(f32)
-    joined_grad = sum_dp(scatter_row(low(tn(normed_one_all, mixed_grad)))).astype(f32)
-
+    grads = (low(nt(branch_chip, out_own)), low(nt(branch_chip, out_far)))
+    down_pair = (low(tn(grad_chip, active_own)), low(tn(grad_chip, active_far)))
+    up_pair = (low(tn(normed_chip, grad_before_own)), low(tn(normed_chip, grad_before_far)))
+    out_pair = (
+        low(tn(branch_chip, attended_chip[:, :head_width])),
+        low(tn(branch_chip, attended_chip[:, head_width:])),
+    )
+    nothing = jnp.zeros((D,), f32)
     early = jnp.stack(
         [
+            nothing,
+            nothing,
             jnp.sum(branch_grad, 0, dtype=f32),
             jnp.sum(grad_normed_two * standard_two, 0),
             jnp.sum(grad_normed_two, 0),
             jnp.sum(grad_low, 0, dtype=f32),
-            jnp.full((D,), error_sum),
+            nothing,
+            nothing,
         ]
     )
-    early = small_sum(early, ("dp", "row", "col"))
-    loss = early[4, 0] * scale / (D * token_total)
-    early = lax.dynamic_slice_in_dim(early, row * (D // row_size), D // row_size, 1)
-    up_sums = jnp.sum(grad_before_own, 0, dtype=f32) + swap_with(
-        jnp.sum(grad_before_far, 0, dtype=f32), "col", 2
+    up_sums = jnp.stack(
+        [jnp.sum(grad_before_own, 0, dtype=f32), jnp.sum(grad_before_far, 0, dtype=f32)]
     )
-    up_bias_grad = small_sum(up_sums, ("dp", "row"))
-    column_sums = small_sum(jnp.sum(mixed_grad, 0, dtype=f32), ("dp", "row"))
-    column_sums = column_sums.reshape(head_count, 3, HEAD_DIM)
+    layer_out, input_grad, up_grad, down_grad, out_grad, joined_grad, sums = last_stage(
+        slopes, mixed, attended, log_totals, normed_one_all, joined_all, tokens, grad_middle, vectors, early,
+        up_sums, teacher, jnp.broadcast_to(low(valid)[:, None], (valid.shape[0], 128)), grads, low(result),
+        up_pair, down_pair, out_pair,
+    )
+    up_grad, down_grad, out_grad, joined_grad = (
+        sum_other_pairs(g.astype(f32)) for g in (up_grad, down_grad, out_grad, joined_grad)
+    )
+    mine = lax.dynamic_slice_in_dim(sums, row * (D // row_size), D // row_size, 1)
+    loss = jnp.sum(sums[6, :128]) * scale / (D * token_total)
+    up_bias_grad = pick(sums[8:12], col)
+    column_sums = pick(sums[12:16], col)[: mixed.shape[1]].reshape(head_count, 3, HEAD_DIM)
     joined_bias_grad = jnp.concatenate([column_sums[:, 0], column_sums[:, 2]], axis=1)
-    late = jnp.stack([jnp.sum(grad_normed_one * standard_one, 0), jnp.sum(grad_normed_one, 0)])
-    late = small_sum(late, ("dp", "row", "col"))
-    late = lax.dynamic_slice_in_dim(late, row * (D // row_size), D // row_size, 1)
     return (
         layer_out,
         loss,
-        input_grad,
-        late[0],
-        late[1],
+        input_grad.astype(f32),
+        mine[0],
+        mine[1],
         joined_grad,
         joined_bias_grad,
-        out_grad,
-        early[0],
-        early[1],
-        early[2],
+        out_grad.T,
+        mine[2],
+        mine[3],
+        mine[4],
         up_grad,
         up_bias_grad,
-        down_grad,
-        early[3],
+        down_grad.T,
+        mine[5],
     )
 
 

time: 671 us -> 588 us (0.88)
  Pallas kernels: 267 us -> 459 us
  waiting for transfers between devices: 180 us -> 9.22 us
  starting transfers between devices: 63.3 us -> 1.26 us
  other arithmetic: 35.6 us -> 20.1 us
  between operations: 17.6 us -> 3.68 us
  matrix products: 73.1 us -> 64.1 us
    pallas_call x1, Pallas kernels: 37.8 us -> 229 us  [last_stage(): pl.pallas_call(functools.partial(last_kernel, heads, kinds), out_shape=(s...]
    ppermute x33 -> x6, waiting for transfers between devices: 125 us -> 9.22 us  [swap_with(): return lax.ppermute(value, axis, [(i, i ^ bit) for i in range(size)])]
    ppermute x8 -> x0, waiting for transfers between devices: 55 us -> none  [to_features(): lax.ppermute(pick(blocks, (col - step) % row_size), ('row', 'col'), moves)]
    ppermute x33 -> x6, starting transfers between devices: 38.3 us -> 1.26 us  [swap_with(): return lax.ppermute(value, axis, [(i, i ^ bit) for i in range(size)])]
    ppermute x8 -> x0, starting transfers between devices: 24.6 us -> none  [to_features(): lax.ppermute(pick(blocks, (col - step) % row_size), ('row', 'col'), moves)]
    reduce_sum x4 -> x2, other arithmetic: 9.74 us -> 1.99 us  [the longest x1 1.37 us: on_device(): loss = jnp.sum(sums[6, :128]) * scale / (D * token_total)]
    dot_general x7 -> x6, matrix products: 28.6 us -> 24.5 us  [tn(): lax.dot_general(a, b, (((0,), (0,)), ((), ())), preferred_element_type=jn...]
    dot_general x7 -> x6, matrix products: 25.4 us -> 26.2 us  [nt(): lax.dot_general(a, b, (((1,), (1,)), ((), ())), preferred_element_type=jn...]
  transfers between devices with their start and end apart: 45 -> 6, of which waited for: 29 -> 4; matrix products, arithmetic and copies ran while one was open for 11% -> 4% of each run, Pallas kernels for 6% -> 0%
where the time goes in v3:
time: 588 us; the launch traced here: 579 us
  Pallas kernels  459 us (78%)
  matrix products  64.1 us (11%)
  local copies, waits for them, and re-layouts  21.5 us (4%)
  other arithmetic  20.1 us (3%)
  waiting for transfers between devices  9.22 us (2%)
    pallas_call x1, Pallas kernels, first_stage(): pl.pallas_call(functools.partial(first_kernel, heads, token_total), out_s...  230 us
    pallas_call x1, Pallas kernels, last_stage(): pl.pallas_call(functools.partial(last_kernel, heads, kinds), out_shape=(s...  229 us
    dot_general x6, matrix products, nt(): lax.dot_general(a, b, (((1,), (1,)), ((), ())), preferred_element_type=jn...  26.2 us
    dot_general x6, matrix products, tn(): lax.dot_general(a, b, (((0,), (0,)), ((), ())), preferred_element_type=jn...  24.5 us
    dot_general x6, matrix products, nn(): return jnp.dot(a, b, preferred_element_type=jnp.float32)  13.4 us
  transfers between devices with their start and end apart: 6, of which 4 were waited for; matrix products, arithmetic and copies ran while one was open for 4% of the time, Pallas kernels for 0%

profile of v3, /device:TPU:13, one launch (start us, length us, event | category | flops | bytes accessed | tf_op | source)
XLA Modules:
  0.0 578.9 jit_solution(17214894885338187712)
XLA Ops:
  4.6 0.8 slice_bitcast_fusion.1
  7.2 1.3 broadcast_in_dim.7.valid_ref
  8.5 1.0 copy-done.4
  9.6 1.0 copy-done.5
  10.6 1.0 copy-done.6
  11.6 0.9 copy-done.7
  12.5 229.6 %first_stage.1 = (bf16[512,1024]{1,0:T(8,128)(2,1)S(1)}, bf16[2048,1024]{1,0:T(8,128)(2,1)}, bf16[2048,768]{1,0:T(8,128)(2,1)}, bf16[2048,256]{1,0:T(8,128)(2,1)...) custom-call(f32[4]{0:T(128)S(1)} %exponential_multiply_fusion.slope_, ...), custom_call_target="tpu_custom_call" | custom-call | tf_op jit(solution)/shard_map/first_stage/pallas_call | solution.py:590
  242.2 2.3 fusion.56
  244.5 1.4 copy-done.17
  245.9 0.8 convolution_add_fusion
  247.0 2.6 collective-permute-done
  250.9 2.5 collective-permute-done.1
  253.4 2.3 fusion.26
  255.8 2.8 fusion.20
  258.6 2.3 fusion.36
  260.9 2.9 fusion.41
  264.7 0.8 multiply_reduce_fusion.4
  265.5 1.2 collective-permute-done.2
  266.7 1.7 fusion.68
  268.5 1.4 convert_reduce_fusion.2
  270.0 2.9 collective-permute-done.3
  272.9 8.2 %convert_reduce_fusion = (f32[1024]{0:T(1024)S(1)}, bf16[1024,1024]{1,0:T(8,128)(2,1)S(1)}) fusion(f32[1024,1024]{1,0:T(8,128)} %copy-done.22, f32[1024]{0:T(1024)S(1)} %bitcast.93, bf16[2,1280,1024]{2,1,0:T(8,128)(2,1)} %get-tuple-element.46, bf16[512,1024]{1,0:T(8,128)(2,1)} %collective-permute-done.3, bf16[512,1024]{1,0:T(8,128)(2,1)} %get-tuple-element.96), kind=kOutput, calls=%fused_computation.18 | convolution fusion | flops 2175794176 | bytes 10493952 | tf_op jit(solution)/shard_map/dot_general | solution.py:23
  281.1 2.4 fusion.24
  283.5 7.0 %convert_reduce_fusion.1 = (f32[1024]{0:T(1024)S(1)}, bf16[1024,1024]{1,0:T(8,128)(2,1)S(1)}) fusion(f32[1024,1024]{1,0:T(8,128)S(1)} %copy-done.25, f32[1024]{0:T(1024)S(1)} %bitcast.96, bf16[2,1280,1024]{2,1,0:T(8,128)(2,1)} %get-tuple-element.46, bf16[512,1024]{1,0:T(8,128)(2,1)} %collective-permute-done.3, bf16[512,1024]{1,0:T(8,128)(2,1)} %get-tuple-element.96), kind=kOutput, calls=%fused_computation.19 | convolution fusion | flops 2175794176 | bytes 10493952 | tf_op jit(solution)/shard_map/dot_general | solution.py:23
  290.5 2.6 fusion.38
  293.6 3.7 convolution_convert_fusion.3.up_own
  297.3 5.7 convolution_convert_fusion.1.down_own
  303.1 1.1 multiply_reduce_fusion
  304.1 2.9 convert_reduce_fusion.3
  307.5 3.7 convolution_convert_fusion.2.up_far
  311.9 5.5 convolution_convert_fusion.down_far
  318.0 2.9 convolution_convert_fusion.6.grads_far_ref
  320.9 3.0 convolution_convert_fusion.7.grads_own_ref
  324.0 2.9 convolution_convert_fusion.5.out_own
  326.8 2.9 convolution_convert_fusion.4.out_far
  329.7 1.1 broadcast_in_dim.8.valid_ref
  330.8 229.4 %last_stage.1 = (bf16[2048,256]{1,0:T(8,128)(2,1)}, bf16[2048,256]{1,0:T(8,128)(2,1)}, bf16[256,1024]{1,0:T(8,128)(2,1)}, bf16[256,1024]{1,0:T(8,128)(2,1)}, bf1...) custom-call(f32[4]{0:T(128)} %copy-done.10, bf16[2048,768]{1,0:T(8,128)(2,1)} %get-tuple-element.36.mixed_ref, ...), custom_call_target="tpu_custom_call" | custom-call | tf_op jit(solution)/shard_map/last_stage/pallas_call | solution.py:1007
  560.3 1.4 slice_reduce_fusion
  561.7 0.8 fusion.73
  564.5 0.9 convert_bitcast_fusion.1
  565.4 0.8 copy.38
  566.3 1.9 convert_element_type.142
  568.2 2.2 convert_element_type.143
  570.4 1.1 convert_bitcast_fusion
  571.6 1.3 copy.39
  572.9 1.5 convert_element_type.141
  575.0 1.6 fusion.72
  576.6 1.0 copy.42
  (89 shorter events, 11.7 us)
Async XLA Ops:
  0.7 243.8 %copy-start.10 = (f32[4]{0:T(128)}, f32[4]{0:T(128)S(1)}, u32[]{:S(2)}) copy-start(f32[4]{0:T(128)S(1)} %exponential_multiply_fusion.slope_ref) | copy-start | bytes 52
  8.5 1.0 copy-start.4
  9.6 1.0 copy-start.5
  10.6 1.0 copy-start.6
  11.6 0.9 copy-start.7
  242.1 2.4 copy-start.1
  242.1 2.4 copy-start.3
  242.1 2.4 copy-start.9
  242.1 4.8 copy-start.8
  242.1 7.5 %copy-start = (bf16[512,1024]{1,0:T(8,128)(2,1)}, bf16[512,1024]{1,0:T(8,128)(2,1)S(1)}, u32[]{:S(2)}) copy-start(bf16[512,1024]{1,0:T(8,128)(2,1)S(1)} %get-tuple-element.41.xt_ref) | copy-start | bytes 3145732
  242.2 3.8 copy-start.17
  246.9 2.7 collective-permute-start
  249.6 3.8 copy-start.18
  250.2 16.5 %copy-start.11 = (f32[512,1024]{1,0:T(8,128)}, f32[512,1024]{1,0:T(8,128)S(1)}, u32[]{:S(2)}) copy-start(f32[512,1024]{1,0:T(8,128)S(1)} %get-tuple-element.100) | copy-start | bytes 6291460
  250.7 7.9 %copy-start.14 = (bf16[512,1024]{1,0:T(8,128)(2,1)}, bf16[512,1024]{1,0:T(8,128)(2,1)S(1)}, u32[]{:S(2)}) copy-start(bf16[512,1024]{1,0:T(8,128)(2,1)S(1)} %add_convert_fusion) | copy-start | bytes 3145732
  250.7 2.7 collective-permute-start.1
  253.4 5.2 copy-start.20
  255.8 2.8 copy-start.22
  260.9 2.9 copy-start.24
  264.0 2.7 collective-permute-start.2
  269.9 3.0 collective-permute-start.3
  270.0 11.1 %copy-start.19 = (bf16[2,1024,1024]{2,1,0:T(8,128)(2,1)S(1)}, bf16[2,1024,1024]{2,1,0:T(8,128)(2,1)}, u32[]{:S(2)}) copy-start(bf16[2,1024,1024]{2,1,0:T(8,128)(2,1)} %get-tuple-element.48) | copy-start | bytes 12582916
  281.1 2.4 copy-start.25
  290.5 3.0 copy-start.15
  290.5 3.0 copy-start.21
  293.3 9.7 %collective-permute-start.4 = (bf16[512,1024]{1,0:T(8,128)(2,1)S(1)}, bf16[512,1024]{1,0:T(8,128)(2,1)S(1)}, u32[]{:S(2)}, u32[]{:S(2)}) collective-permute-start(bf16[512,1024]{1,0:T(8,128)(2,1)S(1)} %slice.242), channel_id=1, source_target_pairs={{0,1},{1,0},{2,3},{3,2},{4,5},{5,4},{6,7},{7,6},{8,9},{9,8},{10,11... | collective-permute-start | bytes 3145736 | tf_op jit(solution)/shard_map/ppermute | solution.py:1036
  297.3 5.7 copy-start.12
  307.1 4.8 copy-start.23
  307.1 10.9 %collective-permute-start.5 = (bf16[512,1024]{1,0:T(8,128)(2,1)}, bf16[512,1024]{1,0:T(8,128)(2,1)S(1)}, u32[]{:S(2)}, u32[]{:S(2)}) collective-permute-start(bf16[512,1024]{1,0:T(8,128)(2,1)} %get-tuple-element.98), channel_id=1, source_target_pairs={{0,1},{1,0},{2,3},{3,2},{4,5},{5,4},{6,7},{7,6},{8,9},{9,8},{10,11... | collective-permute-start | bytes 3145736 | tf_op jit(solution)/shard_map/ppermute | solution.py:1036
  320.9 3.0 copy-start.2
  560.3 12.6 %copy-start.13 = (bf16[2048,256]{1,0:T(8,128)(2,1)S(1)}, bf16[2048,256]{1,0:T(8,128)(2,1)}, u32[]{:S(2)}) copy-start(bf16[2048,256]{1,0:T(8,128)(2,1)} %get-tuple-element.52) | copy-start | bytes 3145732
  568.2 8.4 %copy-start.16 = (bf16[2048,256]{1,0:T(8,128)(2,1)S(1)}, bf16[2048,256]{1,0:T(8,128)(2,1)}, u32[]{:S(2)}) copy-start(bf16[2048,256]{1,0:T(8,128)(2,1)} %get-tuple-element.144) | copy-start | bytes 3145732

commit v4 on v3

--- a/solution.py
+++ b/solution.py
@@ -279,8 +279,8 @@
 
 
 class Weight:
-    def __init__(self, place, src, dst, offset, by_rows, sems, first):
-        self.place, self.src, self.dst, self.offset, self.by_rows = place, src, dst, offset, by_rows
+    def __init__(self, place, src, dst, offset, by_rows, last, sems, first):
+        self.p, self.src, self.dst, self.offset, self.by_rows, self.last = place, src, dst, offset, by_rows, last
         self.sems, self.first = sems, first
         self.rows, self.width = src.shape
         self.part = self.rows // 2
@@ -296,67 +296,198 @@
         start = pl.multiple_of(self.offset + half * self.part, self.part)
         return self.dst.at[side, pl.ds(start, self.part), hint(row, self.width)]
 
+    def other(self, step):
+        return (self.p.row + 4 - step) % 4
+
+    def move(self, src, dst, number, target):
+        return remote(src, dst, self.sems, self.first + number, target)
+
+    def pass_on(self, side, step, half, number, target):
+        src = self.piece(side, self.other(step), half)
+        dst = self.piece(1 if "col" in target else side, self.other(step), half)
+        return self.move(src, dst, number + step - 1, target)
+
     def own(self):
-        return pltpu.make_async_copy(self.src, self.whole(0, self.place.row), self.sems[1].at[self.first])
+        return pltpu.make_async_copy(self.src, self.whole(0, self.p.row), self.sems[1].at[self.first])
 
     def across(self):
+        return self.move(self.src, self.whole(1, self.p.row), 1, {"col": self.p.far})
+
+    def along(self, step):
+        p = self.p
+        return self.move(
+            self.src.at[hint(p.half, self.part)], self.piece(0, p.row, p.half), 1 + step, {"row": (p.row + step) % 4}
+        )
+
+    def to_twin(self, step):
+        return self.pass_on(0, step, self.p.half, 5, {"dp": self.p.twin})
+
+    def to_far(self, step):
+        return self.pass_on(0, step, self.p.half, 8, {"col": self.p.far})
+
+    def onward(self, step):
+        if self.last == "y":
+            return self.pass_on(0, step, 1 - self.p.half, 11, {"col": self.p.far})
+        return self.pass_on(1, step, self.p.half, 11, {"dp": self.p.twin})
+
+    def arrival(self, side, step, half, number):
+        part = self.piece(side, self.other(step), half)
+        return self.move(part, part, number + step - 1, {"dp": self.p.twin})
+
+    def start(self):
+        self.own().start()
+        self.across().start()
+
+    def start_along(self):
+        for step in (1, 2, 3):
+            self.along(step).start()
+
+    def spread(self):
+        for step in (1, 2, 3):
+            self.arrival(0, step, self.p.half, 2).wait_recv()
+            self.to_twin(step).start()
+            self.to_far(step).start()
+
+    def spread_last(self):
+        p = self.p
+        for step in (1, 2, 3):
+            if self.last == "y":
+                self.arrival(0, step, 1 - p.half, 5).wait_recv()
+            else:
+                self.arrival(1, step, p.half, 8).wait_recv()
+            self.onward(step).start()
+
+    def ready(self):
+        p = self.p
+        self.own().wait()
+        self.across().wait_recv()
+        for step in (1, 2, 3):
+            if self.last == "y":
+                self.arrival(1, step, p.half, 8).wait_recv()
+            else:
+                self.arrival(0, step, 1 - p.half, 5).wait_recv()
+            self.arrival(1, step, 1 - p.half, 11).wait_recv()
+
+    def sent(self):
+        self.across().wait_send()
+        for step in (1, 2, 3):
+            for copy in (self.along(step), self.to_twin(step), self.to_far(step), self.onward(step)):
+                copy.wait_send()
+
+
+WEIGHT_SEMS = 14
+
+
+class Halves:
+    def __init__(self, place, src, dst, sems, first):
+        self.p, self.src, self.dst, self.sems, self.first = place, src, dst, sems, first
+        self.rows = src.shape[0]
+        self.part = self.rows // 2
+
+    def own(self):
+        return pltpu.make_async_copy(self.src, self.dst.at[hint(self.p.row, self.rows)], self.sems[1].at[self.first])
+
+    def along(self, step):
+        p = self.p
         return remote(
-            self.src, self.whole(1, self.place.row), self.sems, self.first + 1, {"col": self.place.far}
-        )
-
-    def along(self, side, step):
-        p = self.place
-        src = self.src.at[hint(p.half, self.part)] if side == 0 else self.piece(1, p.row, p.half)
-        return remote(
-            src, self.piece(side, p.row, p.half), self.sems, self.first + 2 + 3 * side + step - 1,
-            {"row": (p.row + step) % 4},
-        )
-
-    def came(self, side, step):
-        p = self.place
-        part = self.piece(side, (p.row + 4 - step) % 4, p.half)
-        return remote(
-            part, part, self.sems, self.first + 2 + 3 * side + step - 1, {"row": (p.row + step) % 4}
-        )
-
-    def twin(self, side, step):
-        p = self.place
-        part = self.piece(side, (p.row + 4 - step) % 4, p.half)
-        return remote(part, part, self.sems, self.first + 8 + 3 * side + step - 1, {"dp": p.twin})
-
-    def from_twin(self, side, step):
-        p = self.place
-        part = self.piece(side, (p.row + 4 - step) % 4, 1 - p.half)
-        return remote(part, part, self.sems, self.first + 8 + 3 * side + step - 1, {"dp": p.twin})
-
-
-WEIGHT_SEMS = 14
+            self.src.at[hint(p.half, self.part)], self.dst.at[hint(2 * p.row + p.half, self.part)], self.sems,
+            self.first + step, {"row": (p.row + step) % 4},
+        )
+
+    def part_of(self, step, half):
+        return self.dst.at[hint(2 * ((self.p.row + 4 - step) % 4) + half, self.part)]
+
+    def to_twin(self, step, half):
+        part = self.part_of(step, half)
+        return remote(part, part, self.sems, self.first + 3 + step, {"dp": self.p.twin})
+
+    def start(self):
+        self.own().start()
+        for step in (1, 2, 3):
+            self.along(step).start()
+
+    def ready(self):
+        p = self.p
+        for step in (1, 2, 3):
+            part = self.part_of(step, p.half)
+            remote(part, part, self.sems, self.first + step, {"dp": p.twin}).wait_recv()
+            self.to_twin(step, p.half).start()
+        for step in (1, 2, 3):
+            self.to_twin(step, 1 - p.half).wait_recv()
+        self.own().wait()
+
+    def sent(self):
+        for step in (1, 2, 3):
+            self.along(step).wait_send()
+            self.to_twin(step, self.p.half).wait_send()
+
+
+HALVES_SEMS = 7
+
+
+GELU_ROOT = math.sqrt(2.0 / math.pi)
+GELU_CUBE = 0.044715
+
+
+def gelu_pair(x):
+    square = x * x
+    t = jnp.tanh(GELU_ROOT * x * (1.0 + GELU_CUBE * square))
+    half = 0.5 * (1.0 + t)
+    slope = half + 0.5 * x * (1.0 - t * t) * (GELU_ROOT * (1.0 + 3.0 * GELU_CUBE * square))
+    return x * half, slope
+
+
+def moments(x):
+    center = jnp.mean(x, 1, keepdims=True)
+    spread = jnp.mean(x * x, 1, keepdims=True) - center * center
+    inverse = lax.rsqrt(spread + EPSILON)
+    return (x - center) * inverse, inverse
+
+
+class Chip:
+    def __init__(self, place, sems, first):
+        self.p, self.sems, self.first = place, sems, first
+
+    def copy(self, number, src, dst):
+        return remote(src, dst, self.sems, self.first + number, {"col": self.p.near})
 
 
 def first_kernel(
     heads, token_total,
     slope_ref, bias_ref, vector_ref, joined_ref, layer_ref, up_ref, down_ref, out_ref, up_bias_ref,
     teacher_ref, cot_ref, valid_ref,
-    xt_ref, nall_ref, mixed_ref, att_ref, lse_ref, chip_ref, jall_ref, vall_ref, gt_ref, vt_ref, scale_ref,
-    up2_ref, dn2_ref, ub2_ref,
-    qs, ks, vs, bias, sc, mx, ls, acc, grad, count, sends, recvs,
+    xt_ref, nall_ref, mixed_ref, att_ref, lse_ref, jall_ref, vall_ref, scale_ref,
+    layer_out_ref, gmid_ref, gown_ref, gfar_ref, early_ref, up_sums_ref,
+    upg_own, upg_far, dng_own, dng_far, outg_own, outg_far,
+    chip_ref, gt_ref, vt_ref, up2_ref, dn2_ref, ub2_ref, normed, gchip, bchip, give, take, middle, gres, low_ref, stage,
+    grad, count, sends, recvs,
 ):
     sems = (sends, recvs)
+    f32, bf = jnp.float32, jnp.bfloat16
     p = Place()
-    quarter = xt_ref.shape[0]
+    quarter, features = xt_ref.shape
+    hidden = down_ref.shape[0]
     greet(p, True, True)
     moved = Transpose(p, layer_ref, xt_ref, sems, 0)
     target = Transpose(p, grad, gt_ref, sems, 4)
-    base = 8
-    weights = []
-    for n, (src, dst, offset, by_rows) in enumerate(
-        ((out_ref, dn2_ref, down_ref.shape[0], False), (up_ref, up2_ref, 0, True), (down_ref, dn2_ref, 0, False))
-    ):
-        weights.append(Weight(p, src, dst, offset, by_rows, sems, base + n * WEIGHT_SEMS))
-    base += 3 * WEIGHT_SEMS
+    back = Untranspose(p, low_ref, layer_out_ref, sems, 8)
+    base = 12
+    w_out = Weight(p, out_ref, dn2_ref, hidden, False, "y", sems, base)
+    w_up = Weight(p, up_ref, up2_ref, 0, True, "y", sems, base + WEIGHT_SEMS)
+    w_downs = [
+        Weight(
+            p, down_ref.at[pl.ds(n * (hidden // 2), hidden // 2)], dn2_ref, n * (hidden // 2), False, "x", sems,
+            base + (2 + n) * WEIGHT_SEMS,
+        )
+        for n in (0, 1)
+    ]
+    weights = [w_out, w_up] + w_downs
+    base += 4 * WEIGHT_SEMS
+    w_joined = Halves(p, joined_ref, jall_ref, sems, base)
+    base += HALVES_SEMS
     moved.start()
-    small_base, joined_base, bias_base = base, base + 4, base + 8
-    base += 10
+    small_base, bias_base = base, base + 4
+    base += 6
 
     def small(step):
         return remote(
@@ -367,31 +498,24 @@
         part = vall_ref.at[:, hint((p.row + 4 - step) % 4, 256)]
         return remote(part, part, sems, small_base + step, {"row": (p.row + step) % 4})
 
-    def joined(step):
-        return remote(
-            joined_ref, jall_ref.at[hint(p.row, 256)], sems, joined_base + step, {"row": (p.row + step) % 4}
-        )
-
-    def joined_came(step):
-        part = jall_ref.at[hint((p.row + 4 - step) % 4, 256)]
-        return remote(part, part, sems, joined_base + step, {"row": (p.row + step) % 4})
-
     small_own = pltpu.make_async_copy(vector_ref, vall_ref.at[:, hint(p.row, 256)], recvs.at[small_base])
-    joined_own = pltpu.make_async_copy(joined_ref, jall_ref.at[hint(p.row, 256)], recvs.at[joined_base])
     bias_own = pltpu.make_async_copy(up_bias_ref, ub2_ref.at[0], recvs.at[bias_base])
     bias_far = remote(up_bias_ref, ub2_ref.at[1], sems, bias_base + 1, {"col": p.far})
     small_own.start()
-    joined_own.start()
     for step in (1, 2, 3):
         small(step).start()
     bias_own.start()
     bias_far.start()
     for w in weights:
-        w.own().start()
-        w.across().start()
-
-    total = jnp.sum(jnp.sum(valid_ref[...], axis=0, keepdims=True), axis=1, keepdims=True) * (1.0 / 128.0)
-    count[0] = jnp.broadcast_to(total, (8, 128))
+        w.start()
+
+    tokens = valid_ref.shape[0]
+    counted = jnp.zeros((8, 128), f32)
+    for n in range(tokens // 256):
+        counted = counted + jnp.sum(
+            valid_ref[n * 256 : (n + 1) * 256, :].astype(f32), axis=0, keepdims=True
+        )
+    count[0] = counted
     steps = [("col", 1), ("col", 2)]
     bit = 1
     while bit < p.dps:
@@ -407,15 +531,15 @@
     scale_ref[...] = token_total / count[2 * len(steps)]
     scale = scale_ref[:1, :1]
 
-    @pl.loop(0, 16)
+    @pl.loop(0, 32)
     def _(n):
-        rows = hint(n, grad.shape[0] // 16)
-        factor = valid_ref[rows, :] * scale
+        rows = hint(n, grad.shape[0] // 32)
+        factor = valid_ref[rows, :].astype(f32) * scale
         for f in range(grad.shape[1] // 128):
             cols = slice(f * 128, (f + 1) * 128)
             grad[rows, cols] = (
-                cot_ref[rows, cols].astype(jnp.float32) - factor * teacher_ref[rows, cols].astype(jnp.float32)
-            ).astype(grad.dtype)
+                cot_ref[rows, cols].astype(f32) - factor * teacher_ref[rows, cols].astype(f32)
+            ).astype(bf)
 
     valid_base = base
     base += 1
@@ -430,34 +554,22 @@
     same = jnp.logical_and(p.stays, p.col == p.row)
     valid_kept = pltpu.make_async_copy(valid_ref.at[hint(p.row, quarter)], vt_ref, recvs.at[valid_base])
 
-    @pl.when(jnp.logical_not(same))
-    def _():
-        valid_out().start()
-
-    @pl.when(same)
-    def _():
-        valid_kept.start()
-
     for step in (1, 2, 3):
         small_came(step).wait_recv()
         small(step).wait_send()
     small_own.wait()
     moved.wait_recv()
-    joined_own.wait()
-    for step in (1, 2, 3):
-        joined(step).start()
+    w_joined.start()
 
     first = p.col * quarter
-    @pl.loop(0, quarter // 128)
-    def _(n):
+
+    def norm_one(n):
         rows = hint(n, 128)
-        x = xt_ref[rows, :].astype(jnp.float32)
-        center = jnp.mean(x, 1, keepdims=True)
-        spread = jnp.mean(x * x, 1, keepdims=True) - center * center
-        standard = (x - center) * lax.rsqrt(spread + EPSILON)
+        standard, _ = moments(xt_ref[rows, :].astype(f32))
         place = pl.ds(pl.multiple_of(first + n * 128, 128), 128)
-        nall_ref[place, :] = (standard * vall_ref[0:1, :] + vall_ref[1:2, :]).astype(nall_ref.dtype)
-
+        nall_ref[place, :] = (standard * vall_ref[0:1, :] + vall_ref[1:2, :]).astype(bf)
+
+    pl.loop(0, quarter // 128)(norm_one)
     mine = nall_ref.at[hint(p.col, quarter)]
     to_far = remote(mine, mine, sems, base, {"col": p.far})
     to_near = remote(mine, mine, sems, base + 1, {"col": p.near})
@@ -472,23 +584,24 @@
     base += 3
     to_far.start()
     to_near.start()
-    for w in weights:
-        for step in (1, 2, 3):
-            w.along(0, step).start()
-        w.across().wait()
-        for step in (1, 2, 3):
-            w.along(1, step).start()
-    target.start()
+
+    @pl.when(jnp.logical_not(same))
+    def _():
+        valid_out().start()
+
+    @pl.when(same)
+    def _():
+        valid_kept.start()
 
     def project(index):
         @pl.loop(0, quarter // 256)
         def _(n):
             rows = pl.ds(pl.multiple_of(index * quarter + n * 256, 256), 256)
-            mixed_ref[rows, :] = (nn(nall_ref[rows, :], jall_ref[...]) + bias_ref[...]).astype(mixed_ref.dtype)
-
-    for step in (1, 2, 3):
-        joined_came(step).wait_recv()
-        joined(step).wait_send()
+            mixed_ref[rows, :] = (nn(nall_ref[rows, :], jall_ref[...]) + bias_ref[...]).astype(bf)
+
+    w_joined.ready()
+    w_out.start_along()
+    w_up.start_along()
     project(p.col)
     near_came.wait_recv()
     project(p.near)
@@ -497,12 +610,17 @@
     project(p.far)
     corner_came.wait_recv()
     project(corner)
+    w_out.spread()
 
     own_heads = att_ref.shape[1]
-    blocks = mixed_ref.shape[0] // BLOCK
+    blocks = tokens // BLOCK
     per_chip = blocks // 2
-
     share_base = base
+    base += per_chip
+
+    def chip_place(n):
+        half = per_chip // 2
+        return ((n // half + p.core) % 2) * half + n % half
 
     def share(n, i):
         return pltpu.make_async_remote_copy(
@@ -511,10 +629,6 @@
             device_id={"col": p.far}, device_id_type=MESH,
         )
 
-    def chip_place(n):
-        half = per_chip // 2
-        return ((n // half + p.core) % 2) * half + n % half
-
     def after(it, i):
         @pl.when(it < per_chip)
         def _():
@@ -524,61 +638,267 @@
         def _():
             chip_ref[hint(chip_place(it - per_chip), BLOCK), :own_heads] = att_ref[hint(i, BLOCK), :]
 
-        for at, n, side in ((4, 0, 0), (4, 0, 1), (5, 1, 0), (6, 1, 1), (7, 2, 0), (7, 2, 1)):
-            @pl.when(it == at)
-            def _():
-                for step in (1, 2, 3):
-                    weights[n].came(side, step).wait_recv()
-                    weights[n].twin(side, step).start()
-
-    attention_rows(
-        heads, lambda it: (it + per_chip * (1 - p.chip)) % blocks, after,
-        slope_ref, mixed_ref, att_ref, lse_ref, qs, ks, vs, bias, sc, mx, ls, acc,
+        @pl.when(it == p.chip)
+        def _():
+            w_out.spread_last()
+
+        @pl.when(it == 2 + 3 * p.chip)
+        def _():
+            w_up.spread()
+            w_downs[0].start_along()
+            w_downs[1].start_along()
+
+    def attend(*scratch):
+        attention_rows(
+            heads, lambda it: (it + per_chip * (1 - p.chip)) % blocks, after,
+            slope_ref, mixed_ref, att_ref, lse_ref, *scratch,
+        )
+
+    pairs = heads // 2
+    pl.run_scoped(
+        attend,
+        pltpu.VMEM((heads, blocks, BLOCK, PAIR), bf), pltpu.VMEM((pairs, blocks, BLOCK, PAIR), bf),
+        pltpu.VMEM((pairs, blocks, 2 * BLOCK, PAIR), bf), pltpu.VMEM((heads, BLOCK, BLOCK), f32),
+        pltpu.VMEM((heads, blocks, BLOCK, BLOCK), f32), pltpu.VMEM((heads, BLOCK, PAIR), f32),
+        pltpu.VMEM((heads, BLOCK, PAIR), f32), pltpu.VMEM((pairs, BLOCK, PAIR), f32),
     )
+
     @pl.loop(0, per_chip)
     def _(n):
         share(n, n + per_chip * (1 - p.chip)).wait()
+
+    w_out.ready()
+    w_up.spread_last()
+    target.start()
+    core = Chip(p, sems, base)
+    base += 12
+    ROWS = 256
+    halves = quarter // ROWS
+
+    def swap_rows(number, buffer, n):
+        return core.copy(
+            number + n, buffer.at[pl.ds(n * ROWS, ROWS)], buffer.at[pl.ds(quarter + n * ROWS, ROWS)]
+        )
+
+    def swap_came(number, buffer, n):
+        part = buffer.at[pl.ds(quarter + n * ROWS, ROWS)]
+        return core.copy(number + n, part, part)
+
+    def give_rows(number, n):
+        return core.copy(number + n, give.at[pl.ds(n * ROWS, ROWS)], take.at[pl.ds(n * ROWS, ROWS)])
+
+    def take_rows(number, n):
+        part = take.at[pl.ds(n * ROWS, ROWS)]
+        return core.copy(number + n, part, part)
+
+    def partial(number, keep, product, again):
+        if again:
+            for n in range(halves):
+                give_rows(number - 4, n).wait_send()
+        for n in range(halves):
+            give[n * ROWS : (n + 1) * ROWS, :] = product(pl.ds(quarter + n * ROWS, ROWS)).astype(bf)
+            give_rows(number, n).start()
+        for n in range(halves):
+            keep[n * ROWS : (n + 1) * ROWS, :] = product(pl.ds(n * ROWS, ROWS))
+
+    partial(
+        0, middle,
+        lambda rows: nn(chip_ref[rows, :own_heads], dn2_ref[0, hidden:, :])
+        + nn(chip_ref[rows, own_heads:], dn2_ref[1, hidden:, :]),
+        False,
+    )
+    for n in range(halves):
+        take_rows(0, n).wait_recv()
+
+        @pl.loop(0, ROWS // 64)
+        def _(m):
+            rows = pl.ds(pl.multiple_of(n * ROWS + m * 64, 64), 64)
+            value = xt_ref[rows, :].astype(f32) + (
+                middle[rows, :] + take[rows, :].astype(f32) + vall_ref[2:3, :]
+            )
+            middle[rows, :] = value
+            standard, _ = moments(value)
+            normed[rows, :] = (standard * vall_ref[3:4, :] + vall_ref[4:5, :]).astype(bf)
+
+        swap_rows(2, normed, n).start()
+    for w in w_downs:
+        w.spread()
+    w_up.ready()
+    bias_own.wait()
+    bias_far.wait()
+
+    def middle_part(act, der, keep):
+        wide = 256
+
+        def up_rows(n):
+            rows = pl.ds(pl.multiple_of(n * ROWS, ROWS), ROWS)
+
+            @pl.loop(0, 2 * hidden // wide, unroll=2)
+            def _(m):
+                side, cols = m // (hidden // wide), hint(m % (hidden // wide), wide)
+                before = nn(normed[rows, :], up2_ref[side, :, cols]) + ub2_ref[side, 0:1, cols]
+                value, slope = gelu_pair(before)
+                act[side, rows, cols] = value.astype(bf)
+                der[side, rows, cols] = slope.astype(bf)
+
+        pl.loop(0, halves)(up_rows)
+        for n in range(halves):
+            swap_came(2, normed, n).wait_recv()
+        for w in w_downs:
+            w.spread_last()
+        pl.loop(halves, 2 * halves)(up_rows)
+        for w in w_downs:
+            w.ready()
+        partial(
+            4, gres,
+            lambda rows: nn(act[0, rows, :], dn2_ref[0, :hidden, :]) + nn(act[1, rows, :], dn2_ref[1, :hidden, :]),
+            True,
+        )
+        target.wait_recv()
+
+        @pl.when(jnp.logical_not(same))
+        def _():
+            valid_out().wait_send()
+            valid_out().wait_recv()
+
+        @pl.when(same)
+        def _():
+            valid_kept.wait()
+
+        early_ref[...] = jnp.zeros_like(early_ref)
+        for n in range(halves):
+            take_rows(4, n).wait_recv()
+
+            @pl.loop(0, ROWS // 64)
+            def _(m):
+                rows = pl.ds(pl.multiple_of(n * ROWS + m * 64, 64), 64)
+                result = middle[rows, :] + (gres[rows, :] + take[rows, :].astype(f32) + vall_ref[5:6, :])
+                low_ref[rows, :] = result.astype(bf)
+                factor = vt_ref[rows, :].astype(f32)[:, :1] * scale
+                value = gt_ref[rows, :].astype(f32) + factor * result
+                gres[rows, :] = value
+                rounded = value.astype(bf)
+                gchip[rows, :] = rounded
+                early_ref[5:6, :] += jnp.sum(rounded.astype(f32), axis=0, keepdims=True)
+
+            swap_rows(6, gchip, n).start()
+        back.start()
+        up_sums_ref[...] = jnp.zeros_like(up_sums_ref)
+
+        def before_rows(n):
+            rows = pl.ds(pl.multiple_of(n * ROWS, ROWS), ROWS)
+
+            @pl.loop(0, 2 * hidden // wide, unroll=2)
+            def _(m):
+                side, cols = m // (hidden // wide), hint(m % (hidden // wide), wide)
+                value = nt(gchip[rows, :], dn2_ref[side, cols, :]) * der[side, rows, cols].astype(f32)
+                rounded = value.astype(bf)
+                der[side, rows, cols] = rounded
+                up_sums_ref[side, 0:1, cols] += jnp.sum(rounded.astype(f32), axis=0, keepdims=True)
+
+        pl.loop(0, halves)(before_rows)
+        for n in range(halves):
+            swap_came(6, gchip, n).wait_recv()
+        pl.loop(halves, 2 * halves)(before_rows)
+        partial(
+            8, keep, lambda rows: nt(der[0, rows, :], up2_ref[0]) + nt(der[1, rows, :], up2_ref[1]), True
+        )
+
+        outs = [(dng_own, gchip, act, 0), (dng_far, gchip, act, 1), (upg_own, normed, der, 0), (upg_far, normed, der, 1)]
+
+        def weight_grad(slot, source, values, sinks):
+            @pl.loop(0, features // 256)
+            def _(f):
+                cols = hint(f, 256)
+                turned = source[:, cols].T
+                for side, sink in enumerate(sinks):
+                    copy = pltpu.make_async_copy(stage.at[side], sink.at[cols], recvs.at[slot + side])
+
+                    @pl.when(f > 0)
+                    def _():
+                        copy.wait()
+
+                    stage[side] = nn(turned, values[side]).astype(bf)
+                    copy.start()
+
+            for side, sink in enumerate(sinks):
+                pltpu.make_async_copy(stage.at[side], sink.at[pl.ds(0, 256)], recvs.at[slot + side]).wait()
+
+        weight_grad(stage_base, gchip, act, (dng_own, dng_far))
+        for n in range(halves):
+            take_rows(8, n).wait_recv()
+
+            @pl.loop(0, ROWS // 64)
+            def _(m):
+                rows = pl.ds(pl.multiple_of(n * ROWS + m * 64, 64), 64)
+                value = keep[rows, :] + take[rows, :].astype(f32)
+                standard, inverse = moments(middle[rows, :])
+                early_ref[3:4, :] += jnp.sum(value * standard, axis=0, keepdims=True)
+                early_ref[4:5, :] += jnp.sum(value, axis=0, keepdims=True)
+                scaled = value * vall_ref[3:4, :]
+                one = jnp.mean(scaled, 1, keepdims=True)
+                two = jnp.mean(scaled * standard, 1, keepdims=True)
+                value = gres[rows, :] + inverse * (scaled - one - standard * two)
+                gmid_ref[rows, :] = value
+                rounded = value.astype(bf)
+                bchip[rows, :] = rounded
+                early_ref[2:3, :] += jnp.sum(rounded.astype(f32), axis=0, keepdims=True)
+
+            swap_rows(10, bchip, n).start()
+        weight_grad(stage_base, normed, der, (upg_own, upg_far))
+
+    stage_base = base
+    base += 2
+    pl.run_scoped(
+        middle_part,
+        pltpu.VMEM((2, 2 * quarter, hidden), bf), pltpu.VMEM((2, 2 * quarter, hidden), bf), pltpu.VMEM((quarter, features), f32),
+    )
+    for n in range(halves):
+        swap_came(10, bchip, n).wait_recv()
+    for n in range(2 * halves):
+        rows = pl.ds(n * ROWS, ROWS)
+        gown_ref[rows, :] = nt(bchip[rows, :], dn2_ref[0, hidden:, :]).astype(bf)
+        gfar_ref[rows, :] = nt(bchip[rows, :], dn2_ref[1, hidden:, :]).astype(bf)
+
+    @pl.loop(0, features // 256)
+    def _(f):
+        cols = hint(f, 256)
+        turned = bchip[:, cols].T
+        outg_own[cols, :] = nn(turned, chip_ref[:, :own_heads]).astype(bf)
+        outg_far[cols, :] = nn(turned, chip_ref[:, own_heads:]).astype(bf)
+
+    back.wait_recv()
+    error = jnp.zeros((1, 128), f32)
+    for n in range(tokens // 128):
+        rows = slice(n * 128, (n + 1) * 128)
+        for f in range(layer_out_ref.shape[1] // 128):
+            cols = slice(f * 128, (f + 1) * 128)
+            off = layer_out_ref[rows, cols].astype(f32) - teacher_ref[rows, cols].astype(f32)
+            error = error + jnp.sum(off * off * valid_ref[rows, :].astype(f32), axis=0, keepdims=True)
+    early_ref[6:7, 0:128] = error
 
     moved.wait_send()
     to_far.wait_send()
     to_near.wait_send()
     pass_on.wait_send()
-    bias_own.wait()
-    bias_far.wait()
-
-    @pl.when(jnp.logical_not(same))
-    def _():
-        valid_out().wait_send()
-
-    kept_in = jnp.logical_and(p.stays, p.col == p.row)
-
-    @pl.when(jnp.logical_not(kept_in))
-    def _():
-        valid_out().wait_recv()
-
-    @pl.when(kept_in)
-    def _():
-        valid_kept.wait()
-
+    w_joined.sent()
     for w in weights:
-        w.own().wait()
-        for side in (0, 1):
-            for step in (1, 2, 3):
-                w.along(side, step).wait_send()
-                w.twin(side, step).wait_send()
-                w.from_twin(side, step).wait_recv()
-    target.wait_recv()
+        w.sent()
     target.wait_send()
+    back.wait_send()
+    for n in range(halves):
+        for number, buffer in ((2, normed), (6, gchip), (10, bchip)):
+            swap_rows(number, buffer, n).wait_send()
+        give_rows(8, n).wait_send()
 
 
 def first_stage(slopes, bias_rows, vectors, joined, layer_in, up, down, out, up_bias, teacher, cot, valid, token_total):
     tokens, width = layer_in.shape
     quarter = tokens // 4
-    row_size = lax.axis_size("row")
-    features = width * row_size
+    features = width * lax.axis_size("row")
     joined_width = joined.shape[1]
     heads = joined_width // (3 * HEAD_DIM)
-    pairs, blocks = heads // 2, tokens // BLOCK
+    blocks = tokens // BLOCK
     f32, bf = jnp.float32, jnp.bfloat16
     hidden, head_rows = down.shape[0], out.shape[0]
     vmem, anyspace = pl.BlockSpec(memory_space=pltpu.VMEM), pl.BlockSpec(memory_space=pl.ANY)
@@ -586,26 +906,28 @@
     bits = 2
     while (1 << (bits - 2)) < lax.axis_size("dp"):
         bits += 1
-    count = 8 + 3 * WEIGHT_SEMS + 8 + 2 + bits + 1 + 3 + blocks
+    count = 12 + 4 * WEIGHT_SEMS + HALVES_SEMS + 6 + bits + 1 + 3 + blocks // 2 + 12 + 2
     return pl.pallas_call(
         functools.partial(first_kernel, heads, token_total),
         out_shape=(
             shape((quarter, features), bf), shape((tokens, features), bf), shape((tokens, joined_width), bf),
             shape((tokens, heads * HEAD_DIM), bf), shape((heads, blocks, BLOCK), f32),
-            shape((tokens // 2, 2 * heads * HEAD_DIM), bf), shape((features, joined_width), bf),
-            shape((8, features), f32), shape((quarter, features), bf), shape((quarter, 128), f32), shape((8, 128), f32),
-            shape((2, features, up.shape[1]), bf), shape((2, hidden + head_rows, features), bf), shape((2, 8, hidden), f32),
-        ),
-        in_specs=[pl.BlockSpec(memory_space=pltpu.SMEM), vmem, vmem, anyspace, anyspace, anyspace, anyspace, anyspace,
-                  anyspace, vmem, vmem, vmem],
-        out_specs=(vmem,) * 8 + (anyspace, anyspace, vmem, anyspace, anyspace, anyspace),
-        scratch_shapes=[pltpu.VMEM((heads,blocks,BLOCK,PAIR),bf),pltpu.VMEM((pairs,blocks,BLOCK,PAIR),bf),
-            pltpu.VMEM((pairs,blocks,2*BLOCK,PAIR),bf),pltpu.VMEM((heads,BLOCK,BLOCK),f32),
-            pltpu.VMEM((heads,blocks,BLOCK,BLOCK),f32),pltpu.VMEM((heads,BLOCK,PAIR),f32),pltpu.VMEM((heads,BLOCK,PAIR),f32),
-            pltpu.VMEM((pairs,BLOCK,PAIR),f32),
-            pltpu.VMEM((tokens, width), bf), pltpu.VMEM((2 * bits + 1, 8, 128), f32),
-            pltpu.SemaphoreType.DMA((count,)), pltpu.SemaphoreType.DMA((count,))],
-        compiler_params=pltpu.CompilerParams(vmem_limit_bytes=48 << 20, collective_id=1, has_side_effects=True),
+            shape((features, joined_width), bf), shape((8, features), f32), shape((8, 128), f32),
+            shape((tokens, width), bf), shape((quarter, features), f32), shape((2 * quarter, head_rows), bf),
+            shape((2 * quarter, head_rows), bf), shape((8, features), f32), shape((2, 1, hidden), f32),
+        ) + (shape((features, hidden), bf),) * 4 + (shape((features, head_rows), bf),) * 2,
+        in_specs=[pl.BlockSpec(memory_space=pltpu.SMEM), vmem, vmem] + [anyspace] * 6 + [vmem] * 3,
+        out_specs=(vmem,) * 14 + (anyspace,) * 4 + (vmem,) * 2,
+        scratch_shapes=[
+            pltpu.VMEM((2 * quarter, 2 * head_rows), bf), pltpu.VMEM((quarter, features), bf), pltpu.VMEM((quarter, 128), bf),
+            pltpu.VMEM((2, features, hidden), bf), pltpu.VMEM((2, hidden + head_rows, features), bf),
+            pltpu.VMEM((2, 8, hidden), f32), pltpu.VMEM((2 * quarter, features), bf), pltpu.VMEM((2 * quarter, features), bf),
+            pltpu.VMEM((2 * quarter, features), bf), pltpu.VMEM((quarter, features), bf), pltpu.VMEM((quarter, features), bf),
+            pltpu.VMEM((quarter, features), f32), pltpu.VMEM((quarter, features), f32), pltpu.VMEM((quarter, features), bf),
+            pltpu.VMEM((2, 256, hidden), bf), pltpu.VMEM((tokens, width), bf), pltpu.VMEM((2 * bits + 1, 8, 128), f32),
+            pltpu.SemaphoreType.DMA((count,)), pltpu.SemaphoreType.DMA((count,)),
+        ],
+        compiler_params=pltpu.CompilerParams(vmem_limit_bytes=62 << 20, collective_id=1, has_side_effects=True),
         name="first_stage",
     )(slopes, bias_rows, vectors, joined, layer_in, up, down, out, up_bias, teacher, cot, valid)
 
@@ -818,9 +1140,9 @@
 def last_kernel(
     heads, kinds,
     slope_ref, mixed_ref, att_ref, lse_ref, nall_ref, jall_ref, xt_ref, middle_ref, gain_ref, early_ref,
-    up_sums_ref, teacher_ref, valid_ref, grads_own_ref, grads_far_ref, result_ref,
+    up_sums_ref, grads_own_ref, grads_far_ref,
     up_own, up_far, down_own, down_far, out_own, out_far,
-    layer_out_ref, input_grad_ref, up_ref, down_ref, out_ref, joined_ref, vector_ref,
+    input_grad_ref, up_ref, down_ref, out_ref, joined_ref, vector_ref,
     dout, grad_mixed, qs, ks, km, vp, ds_, delta, bias, steep, dq, dk, dv,
     gn, near_in, far_in, jgrad, vectors, scratch, sends, recvs,
 ):
@@ -831,10 +1153,9 @@
     tokens = mixed_ref.shape[0]
     greet(p, True, True)
     base = 0
-    back = Untranspose(p, result_ref, layer_out_ref, sems, base)
     ingrad = gn.at[0]
-    grad_back = Untranspose(p, ingrad, input_grad_ref, sems, base + 4)
-    base += 8
+    grad_back = Untranspose(p, ingrad, input_grad_ref, sems, base)
+    base += 4
 
     def natural(chip, n):
         return 2 * chip + (p.core + n) % 2
@@ -864,7 +1185,6 @@
     up.start()
     out.start()
     down.start()
-    back.start()
     for n in (0, 1):
         dout[hint(natural(p.chip, n), quarter), :] = grads_own_ref[n * quarter : (n + 1) * quarter, :]
     for copy in came_att:
@@ -912,8 +1232,8 @@
     vectors[0, 0:2, :] = jnp.zeros((2, features), f32)
     vectors[0, 2:8, :] = early_ref[2:8, :]
     vectors[0, 8:16, :] = jnp.zeros((8, features), f32)
-    vectors[0, pl.ds(8 + p.col, 1), :] = up_sums_ref[0:1, :]
-    vectors[0, pl.ds(8 + p.far, 1), :] = up_sums_ref[1:2, :]
+    vectors[0, pl.ds(8 + p.col, 1), :] = up_sums_ref[0]
+    vectors[0, pl.ds(8 + p.far, 1), :] = up_sums_ref[1]
     vectors[0, pl.ds(12 + p.col, 1), 0 : sums.shape[1]] = sums
 
     to_near[1].wait()
@@ -943,17 +1263,6 @@
     down.second_copy().start()
     joined.first_sum()
     joined.start_rows()
-
-    back.wait_recv()
-    width = layer_out_ref.shape[1]
-    error = jnp.zeros((1, 128), f32)
-    for n in range(tokens // 128):
-        rows = slice(n * 128, (n + 1) * 128)
-        for f in range(width // 128):
-            cols = slice(f * 128, (f + 1) * 128)
-            off = layer_out_ref[rows, cols].astype(f32) - teacher_ref[rows, cols].astype(f32)
-            error = error + jnp.sum(off * off * valid_ref[rows, :].astype(f32), axis=0, keepdims=True)
-    vectors[0, 6:7, 0:128] = error
 
     steps = [("row", 1), ("row", 2), ("col", 1), ("col", 2)]
     bit = 1
@@ -979,12 +1288,11 @@
     down.row_sum()
     for share in (joined, up, out, down):
         share.finish()
-    back.wait_send()
     grad_back.wait_recv()
     grad_back.wait_send()
 
 
-def last_stage(slopes, mixed, att, lse, nall, jall, xt, middle, gain, early, up_sums, teacher, valid, grads, result,
+def last_stage(slopes, mixed, att, lse, nall, jall, xt, middle, gain, early, up_sums, grads,
                up_pair, down_pair, out_pair):
     tokens, joined_width = mixed.shape
     quarter, features = xt.shape
@@ -998,7 +1306,7 @@
     bits = 4
     while (1 << (bits - 4)) < lax.axis_size("dp"):
         bits += 1
-    count = 8 + 2 + 4 * SHARE_SEMS + 3 + bits
+    count = 4 + 2 + 4 * SHARE_SEMS + 3 + bits
     widths = (up_pair[0].shape[1], down_pair[0].shape[1], out_pair[0].shape[1])
     scratch = {
         name: share_scratch(kind, features, width)
@@ -1007,12 +1315,12 @@
     return pl.pallas_call(
         functools.partial(last_kernel, heads, kinds),
         out_shape=(
-            shape((tokens, block), bf), shape((tokens, block), bf), shape((block, widths[0]), bf),
+            shape((tokens, block), bf), shape((block, widths[0]), bf),
             shape((block, widths[1]), bf), shape((block, widths[2]), bf), shape((block, joined_width), bf),
             shape((16, features), f32),
         ),
-        in_specs=[pl.BlockSpec(memory_space=pltpu.SMEM)] + [vmem] * 13 + [anyspace] + [anyspace] + [anyspace] * 6,
-        out_specs=(vmem, anyspace) + (vmem,) * 5,
+        in_specs=[pl.BlockSpec(memory_space=pltpu.SMEM)] + [vmem] * 11 + [anyspace] * 7,
+        out_specs=(anyspace,) + (vmem,) * 5,
         scratch_shapes=[
             pltpu.VMEM((tokens, heads * HEAD_DIM), bf), pltpu.VMEM((tokens, joined_width), bf),
             pltpu.VMEM((pairs,blocks,2*BLOCK,PAIR),bf),pltpu.VMEM((pairs,blocks,BLOCK,PAIR),bf),
@@ -1027,40 +1335,13 @@
         ],
         compiler_params=pltpu.CompilerParams(vmem_limit_bytes=62 << 20, collective_id=2, has_side_effects=True),
         name="last_stage",
-    )(slopes, mixed, att, lse, nall, jall, xt, middle, gain, early, up_sums, teacher, valid, grads[0], grads[1], result,
+    )(slopes, mixed, att, lse, nall, jall, xt, middle, gain, early, up_sums, grads[0], grads[1],
       *up_pair, *down_pair, *out_pair)
 
 
 def swap_with(value, axis, bit):
     size = lax.axis_size(axis)
     return lax.ppermute(value, axis, [(i, i ^ bit) for i in range(size)])
-
-
-def small_sum(value, axes):
-    for axis in axes:
-        bit = 1
-        while bit < lax.axis_size(axis):
-            value = value + swap_with(value, axis, bit)
-            bit *= 2
-    return value
-
-
-def standardize(inputs):
-    center = jnp.mean(inputs, 1, keepdims=True)
-    spread = jnp.mean(inputs * inputs, 1, keepdims=True) - center * center
-    inverse = lax.rsqrt(spread + EPSILON)
-    return (inputs - center) * inverse, inverse
-
-
-def norm_backward(grad_normed, standard, inverse, norm_gain):
-    scaled = grad_normed * norm_gain
-    first = jnp.mean(scaled, 1, keepdims=True)
-    second = jnp.mean(scaled * standard, 1, keepdims=True)
-    return inverse * (scaled - first - standard * second)
-
-
-def gelu_local(before):
-    return jax.nn.gelu(before, approximate=True)
 
 
 def low(value):
@@ -1115,82 +1396,22 @@
     ).astype(f32)
     token_total = layer_in.shape[0] * lax.axis_size("dp") * col_size
     (
-        tokens, normed_one_all, mixed, attended, log_totals, attended_chip, joined_all,
-        vectors, target, valid_tokens, scale, up_all, down_all, bias_all,
+        tokens, normed_one_all, mixed, attended, log_totals, joined_all, vectors, scale, layer_out, grad_middle,
+        grads_own, grads_far, early, up_sums, up_own, up_far, down_own, down_far, out_own, out_far,
     ) = first_stage(
         slopes, bias_rows, vectors, joined_weight, layer_in, up_weight, down_weight, out_weight,
         jnp.broadcast_to(up_bias.astype(f32), (8, up_bias.shape[0])), teacher, cotangent,
-        jnp.broadcast_to(valid.astype(f32)[:, None], (valid.shape[0], 128)), token_total,
+        jnp.broadcast_to(low(valid)[:, None], (valid.shape[0], 128)), token_total,
     )
-    gain_one, shift_one, bias_out, gain_two, shift_two, bias_down = (vectors[i] for i in range(6))
-    valid_tokens, scale = valid_tokens[:, :1], scale[0, 0]
-    hidden = down_weight.shape[0]
-    up_own, up_far = up_all[0], up_all[1]
-    down_own, down_far = down_all[0, :hidden], down_all[1, :hidden]
-    out_own, out_far = down_all[0, hidden:], down_all[1, hidden:]
-    head_width = attended.shape[1]
-
-    inputs = tokens.astype(f32)
-    standard_one, inverse_one = standardize(inputs)
-    branch = nn(attended_chip[:, :head_width], out_own) + nn(attended_chip[:, head_width:], out_far)
-    middle = inputs + (
-        branch[:quarter] + swap_with(low(branch[quarter:]), "col", 1).astype(f32) + bias_out
-    )
-    standard_two, inverse_two = standardize(middle)
-    normed_two = low(standard_two * gain_two + shift_two)
-    normed_chip = jnp.concatenate([normed_two, swap_with(normed_two, "col", 1)], axis=0)
-    before_own = nn(normed_chip, up_own) + bias_all[0, 0]
-    before_far = nn(normed_chip, up_far) + bias_all[1, 0]
-    active_own, pull_own = jax.vjp(gelu_local, before_own)
-    active_far, pull_far = jax.vjp(gelu_local, before_far)
-    active_own, active_far = low(active_own), low(active_far)
-    branch = nn(active_own, down_own) + nn(active_far, down_far)
-    result = middle + (
-        branch[:quarter] + swap_with(low(branch[quarter:]), "col", 1).astype(f32) + bias_down
-    )
-    grad_result = target.astype(f32) + valid_tokens * scale * result
-    grad_low = low(grad_result)
-    grad_chip = jnp.concatenate([grad_low, swap_with(grad_low, "col", 1)], axis=0)
-    grad_before_own = low(pull_own(nt(grad_chip, down_own))[0])
-    grad_before_far = low(pull_far(nt(grad_chip, down_far))[0])
-    back = nt(grad_before_own, up_own) + nt(grad_before_far, up_far)
-    grad_normed_two = back[:quarter] + swap_with(low(back[quarter:]), "col", 1).astype(f32)
-    grad_middle = grad_result + norm_backward(grad_normed_two, standard_two, inverse_two, gain_two)
-    branch_grad = low(grad_middle)
-    branch_chip = jnp.concatenate([branch_grad, swap_with(branch_grad, "col", 1)], axis=0)
-    grads = (low(nt(branch_chip, out_own)), low(nt(branch_chip, out_far)))
-    down_pair = (low(tn(grad_chip, active_own)), low(tn(grad_chip, active_far)))
-    up_pair = (low(tn(normed_chip, grad_before_own)), low(tn(normed_chip, grad_before_far)))
-    out_pair = (
-        low(tn(branch_chip, attended_chip[:, :head_width])),
-        low(tn(branch_chip, attended_chip[:, head_width:])),
-    )
-    nothing = jnp.zeros((D,), f32)
-    early = jnp.stack(
-        [
-            nothing,
-            nothing,
-            jnp.sum(branch_grad, 0, dtype=f32),
-            jnp.sum(grad_normed_two * standard_two, 0),
-            jnp.sum(grad_normed_two, 0),
-            jnp.sum(grad_low, 0, dtype=f32),
-            nothing,
-            nothing,
-        ]
-    )
-    up_sums = jnp.stack(
-        [jnp.sum(grad_before_own, 0, dtype=f32), jnp.sum(grad_before_far, 0, dtype=f32)]
-    )
-    layer_out, input_grad, up_grad, down_grad, out_grad, joined_grad, sums = last_stage(
+    input_grad, up_grad, down_grad, out_grad, joined_grad, sums = last_stage(
         slopes, mixed, attended, log_totals, normed_one_all, joined_all, tokens, grad_middle, vectors, early,
-        up_sums, teacher, jnp.broadcast_to(low(valid)[:, None], (valid.shape[0], 128)), grads, low(result),
-        up_pair, down_pair, out_pair,
+        up_sums, (grads_own, grads_far), (up_own, up_far), (down_own, down_far), (out_own, out_far),
     )
     up_grad, down_grad, out_grad, joined_grad = (
         sum_other_pairs(g.astype(f32)) for g in (up_grad, down_grad, out_grad, joined_grad)
     )
     mine = lax.dynamic_slice_in_dim(sums, row * (D // row_size), D // row_size, 1)
-    loss = jnp.sum(sums[6, :128]) * scale / (D * token_total)
+    loss = jnp.sum(sums[6, :128]) * scale[0, 0] / (D * token_total)
     up_bias_grad = pick(sums[8:12], col)
     column_sums = pick(sums[12:16], col)[: mixed.shape[1]].reshape(head_count, 3, HEAD_DIM)
     joined_bias_grad = jnp.concatenate([column_sums[:, 0], column_sums[:, 2]], axis=1)

time: 588 us -> 485 us (0.82)
  matrix products: 64.1 us -> 0 us
  other arithmetic: 20.1 us -> 9.5 us
  waiting for transfers between devices: 9.22 us -> 0 us
  local copies, waits for them, and re-layouts: 21.5 us -> 15.4 us
  Pallas kernels: 459 us -> 453 us
    dot_general x18 -> x0, matrix products: 64.1 us -> none  [the longest x6 26.2 us: nt(): lax.dot_general(a, b, (((1,), (1,)), ((), ())), preferred_element_type=jn...]
    ppermute x6 -> x0, waiting for transfers between devices: 9.22 us -> none  [swap_with(): return lax.ppermute(value, axis, [(i, i ^ bit) for i in range(size)])]
    pallas_call x1, Pallas kernels: 230 us -> 221 us  [first_stage(): pl.pallas_call(functools.partial(first_kernel, heads, token_total), out_s...]
    reduce_sum x5 -> x1, other arithmetic: 7.39 us -> 1.37 us  [on_device(): loss = jnp.sum(sums[6, :128]) * scale[0, 0] / (D * token_total)]
  transfers between devices with their start and end apart: 6 -> 0, of which waited for: 4 -> 0; matrix products, arithmetic and copies ran while one was open for 4% -> 0% of each run, Pallas kernels for 0% -> 0%
where the time goes in v4:
time: 485 us; the launch traced here: 481 us
  Pallas kernels  453 us (93%)
  local copies, waits for them, and re-layouts  15.4 us (3%)
  other arithmetic  9.5 us (2%)
    pallas_call x1, Pallas kernels, last_stage(): pl.pallas_call(functools.partial(last_kernel, heads, kinds), out_shape=(s...  232 us
    pallas_call x1, Pallas kernels, first_stage(): pl.pallas_call(functools.partial(first_kernel, heads, token_total), out_s...  221 us

profile of v4, /device:TPU:13, one launch (start us, length us, event | category | flops | bytes accessed | tf_op | source)
XLA Modules:
  0.0 480.6 jit_solution(12323680091466755866)
XLA Ops:
  0.7 0.5 exponential_multiply_fusion.slope_ref
  1.2 0.1 pad.3.clone
  1.3 0.7 stack.36
  1.9 0.7 stack.37
  2.6 0.7 stack.38
  3.2 0.7 stack.39
  3.9 0.7 stack.40
  4.5 0.7 stack.41
  5.2 0.8 slice_bitcast_fusion.1
  6.1 0.1 maximum_convert_fusion
  6.1 0.7 reshape.52.bias_ref
  6.8 0.6 convert_element_type.31.vector_ref
  7.4 0.7 convert_element_type.33
  8.1 1.3 broadcast_in_dim.4.up_bias_ref
  9.4 1.1 broadcast_in_dim.10.valid_ref
  10.5 220.6 %first_stage.1 = (bf16[512,1024]{1,0:T(8,128)(2,1)}, bf16[2048,1024]{1,0:T(8,128)(2,1)}, bf16[2048,768]{1,0:T(8,128)(2,1)}, bf16[2048,256]{1,0:T(8,128)(2,1)}, f...) custom-call(f32[4]{0:T(128)} %exponential_multiply_fusion.slope_ref,, ...), custom_call_target="tpu_custom_call" | custom-call | tf_op jit(solution)/shard_map/first_stage/pallas_call | solution.py:910
  231.1 1.2 slice.49
  232.3 231.9 %last_stage.1 = (bf16[2048,256]{1,0:T(8,128)(2,1)}, bf16[256,1024]{1,0:T(8,128)(2,1)}, bf16[256,1024]{1,0:T(8,128)(2,1)}, bf16[256,256]{1,0:T(8,128)(2,1)}, bf16...) custom-call(f32[4]{0:T(128)} %exponential_multiply_fusion.slope_ref, bf16[2048,768]{1,0:T(8,128)(2,1)} %get-tuple-element.42.mixed_ref, ...), custom_call_target="tpu_custom_call" | custom-call | tf_op jit(solution)/shard_map/last_stage/pallas_call | solution.py:1315
  464.3 0.0 copy-start
  464.3 1.4 slice_reduce_fusion
  466.9 1.6 fusion
  468.5 0.8 fusion.1
  469.4 0.6 constant_dynamic-slice_fusion.1
  470.0 0.1 reshape.51
  470.1 0.7 pad_maximum_fusion
  470.7 0.9 convert_bitcast_fusion.1
  471.6 0.8 copy.38
  472.5 0.0 copy-start.3
  472.5 2.0 convert_element_type.35
  474.5 0.0 copy-done
  474.5 0.0 copy-start.2
  474.5 1.5 convert_element_type.34
  476.0 0.0 copy-done.3
  476.0 1.1 convert_element_type.36
  477.0 0.0 copy-done.2
  477.0 0.0 copy-start.1
  477.0 0.1 convert_bitcast_fusion
  477.2 1.3 copy.39
  478.5 0.0 copy-done.1
  478.5 1.0 copy.42
  (5 shorter events, 0.1 us)
Async XLA Ops:
  464.3 10.2 %copy-start = (bf16[2048,256]{1,0:T(8,128)(2,1)S(1)}, bf16[2048,256]{1,0:T(8,128)(2,1)}, u32[]{:S(2)}) copy-start(bf16[2048,256]{1,0:T(8,128)(2,1)} %get-tuple-element.62) | copy-start | bytes 3145732
  472.5 3.5 copy-start.3
  474.5 2.6 copy-start.2
  477.0 1.4 copy-start.1

commit v5 on v1

v5 whole, which is shorter than its diff:
```python
import functools
import math

import jax
import jax.numpy as jnp
from jax import lax
from jax.experimental import pallas as pl
from jax.experimental.pallas import tpu as pltpu
from jax.sharding import PartitionSpec as P

D = 1024
HEADS = 16
SEQ = 2048
EPSILON = 1e-05
LOG2E = 1.4426950408889634
HEAD_DIM=64
BLOCK=256
HALF=64
PAIR=128
SCALE2 = LOG2E/8.0

def nt(a,b):
    return lax.dot_general(a,b,(((1,),(1,)),((),())),preferred_element_type=jnp.float32)
def nn(a,b):
    return jnp.dot(a,b,preferred_element_type=jnp.float32)
def tn(a,b):
    return lax.dot_general(a,b,(((0,),(0,)),((),())),preferred_element_type=jnp.float32)

def low_lanes(rows):
    return lax.broadcasted_iota(jnp.int32,(rows,PAIR),1) < HALF

def swap(a):
    return jnp.concatenate([a[:,HALF:],a[:,:HALF]],axis=1)

def attention_rows(heads, order, after, slope_ref, mixed_ref, out_ref, lse_ref, qs, ks, vs, bias, sc, mx, ls, acc):
    pairs=heads//2
    blocks=mixed_ref.shape[0]//BLOCK
    lo=low_lanes(BLOCK)
    @pl.loop(0,blocks)
    def _(b):
        rows=pl.ds(pl.multiple_of(b*BLOCK,BLOCK),BLOCK)
        for p in range(pairs):
            t0,t1,t2=(mixed_ref[rows,(3*p+n)*PAIR:(3*p+n+1)*PAIR] for n in range(3))
            zero=jnp.zeros_like(t0)
            qs[2*p,b]=jnp.where(lo,t0,zero)
            qs[2*p+1,b]=jnp.where(lo,zero,t1)
            ks[p,b]=jnp.where(lo,swap(t0),swap(t2))
            vs[p,b,:BLOCK]=jnp.where(lo,t1,zero)
            vs[p,b,BLOCK:]=jnp.where(lo,zero,t2)
    il=lax.broadcasted_iota(jnp.int32,(BLOCK,BLOCK),0)
    jl=lax.broadcasted_iota(jnp.int32,(BLOCK,BLOCK),1)
    tent=jnp.minimum(jl,2*il-jl).astype(jnp.float32)
    for h in range(heads):
        bias[h]=tent*slope_ref[h]
    jrow=lax.broadcasted_iota(jnp.int32,(1,BLOCK),1)
    @pl.loop(0,blocks)
    def _(it):
        i=order(it)
        for h in range(heads):
            t=nt(qs[h,i],ks[h//2,i])*SCALE2+bias[h]
            sc[h,i]=t
            mx[h]=jnp.maximum(t[:,:PAIR],t[:,PAIR:])
        @pl.loop(0,i)
        def _(j):
            place=(jrow+(j-i)*BLOCK).astype(jnp.float32)
            for h in range(heads):
                t=nt(qs[h,i],ks[h//2,j])*SCALE2+place*slope_ref[h]
                sc[h,j]=t
                mx[h]=jnp.maximum(mx[h],jnp.maximum(t[:,:PAIR],t[:,PAIR:]))
        for h in range(heads):
            mx[h]=jnp.broadcast_to(jnp.max(mx[h],1,keepdims=True),(BLOCK,PAIR))
            ls[h]=jnp.zeros((BLOCK,PAIR),jnp.float32)
        for p in range(pairs):
            acc[p]=jnp.zeros((BLOCK,PAIR),jnp.float32)
        @pl.loop(0,i+1)
        def _(j):
            for p in range(pairs):
                both=[]
                for h in (2*p,2*p+1):
                    m=mx[h]
                    ea=jnp.exp2(sc[h,j,:,:PAIR]-m)
                    eb=jnp.exp2(sc[h,j,:,PAIR:]-m)
                    ls[h]+=ea+eb
                    both+=[ea.astype(jnp.bfloat16),eb.astype(jnp.bfloat16)]
                acc[p]+=nn(jnp.concatenate(both,1),vs[p,j])
        rows=pl.ds(pl.multiple_of(i*BLOCK,BLOCK),BLOCK)
        for p in range(pairs):
            tot=[jnp.broadcast_to(jnp.sum(ls[h],1,keepdims=True),(BLOCK,PAIR)) for h in (2*p,2*p+1)]
            out_ref[rows,p*PAIR:(p+1)*PAIR]=(acc[p]/jnp.where(lo,tot[0],tot[1])).astype(out_ref.dtype)
            for n,h in enumerate((2*p,2*p+1)):
                lse=mx[h]+jnp.log2(tot[n])
                lse_ref[h,pl.ds(i,1),:]=lse.T[:1]
        after(it,i)

def attention_rows_backward(heads, after, slope_ref, mixed_ref, dout_ref, out_ref, lse_ref, grad_ref, qs, ks, km, vp, ds_, delta, bias, steep, dq, dk, dv):
    pairs=heads//2
    blocks=mixed_ref.shape[0]//BLOCK
    lo=low_lanes(BLOCK)
    @pl.loop(0,blocks)
    def _(b):
        rows=pl.ds(pl.multiple_of(b*BLOCK,BLOCK),BLOCK)
        for p in range(pairs):
            t0,t1,t2=(mixed_ref[rows,(3*p+n)*PAIR:(3*p+n+1)*PAIR] for n in range(3))
            zero=jnp.zeros_like(t0)
            qs[p,b,:BLOCK]=jnp.where(lo,t0,zero)
            qs[p,b,BLOCK:]=jnp.where(lo,zero,t1)
            k=jnp.where(lo,swap(t0),swap(t2))
            ks[p,b]=k
            km[p,b,:BLOCK]=jnp.where(lo,k,zero)
            km[p,b,BLOCK:]=jnp.where(lo,zero,k)
            vp[p,b]=jnp.where(lo,t1,t2)
            d=dout_ref[rows,p*PAIR:(p+1)*PAIR]
            ds_[p,b,:BLOCK]=jnp.where(lo,d,zero)
            ds_[p,b,BLOCK:]=jnp.where(lo,zero,d)
            prod=(d.astype(jnp.float32)*out_ref[rows,p*PAIR:(p+1)*PAIR].astype(jnp.float32)).T
            delta[2*p,pl.ds(b,1),:]=jnp.sum(prod[:HALF],0,keepdims=True)
            delta[2*p+1,pl.ds(b,1),:]=jnp.sum(prod[HALF:],0,keepdims=True)
    kl=lax.broadcasted_iota(jnp.int32,(BLOCK,BLOCK),0)
    ql=lax.broadcasted_iota(jnp.int32,(BLOCK,BLOCK),1)
    tent=jnp.minimum(kl,2*ql-kl).astype(jnp.float32)
    ramp=kl.astype(jnp.float32)
    for h in range(heads):
        bias[h]=tent*slope_ref[h]
        steep[h]=ramp[:,:PAIR]*slope_ref[h]
    def block(i,j,first):
        for p in range(pairs):
            ps=[];gs=[]
            for n,h in enumerate((2*p,2*p+1)):
                q=qs[p,i,n*BLOCK:(n+1)*BLOCK]
                d=ds_[p,i,n*BLOCK:(n+1)*BLOCK]
                row=slope_ref[h]*((j-i)*BLOCK).astype(jnp.float32)-lse_ref[h,pl.ds(i,1),:]
                t=nt(ks[p,j],q)*SCALE2+row+(bias[h] if first else jnp.concatenate([steep[h],steep[h]],1))
                e=jnp.exp2(t)
                g=e*(nt(vp[p,j],d)-delta[h,pl.ds(i,1),:])
                ps.append(e.astype(jnp.bfloat16)); gs.append(g.astype(jnp.bfloat16))
            gv=nn(jnp.concatenate(ps,1),ds_[p,i])
            gk=nn(jnp.concatenate(gs,1),qs[p,i])
            gq=tn(jnp.concatenate(gs,0),km[p,j])
            if first:
                dv[p,j]=gv; dk[p,j]=gk; dq[p,i]=gq
            else:
                dv[p,j]+=gv; dk[p,j]+=gk; dq[p,i]+=gq
    @pl.loop(0,blocks)
    def _(i):
        block(i,i,True)
        @pl.loop(0,i)
        def _(j):
            block(i,j,False)
        after(i)
    @pl.loop(0,blocks)
    def _(b):
        rows=pl.ds(pl.multiple_of(b*BLOCK,BLOCK),BLOCK)
        for p in range(pairs):
            a=dq[p,b]*0.125; k=swap(dk[p,b]*0.125); v=dv[p,b]
            for n,t in enumerate((jnp.where(lo,a,k),jnp.where(lo,v,a),jnp.where(lo,k,v))):
                grad_ref[rows,(3*p+n)*PAIR:(3*p+n+1)*PAIR]=t.astype(grad_ref.dtype)


MESH = pl.DeviceIdType.MESH


def hint(index, size):
    return pl.ds(pl.multiple_of(index * size, size), size)


def remote(src, dst, sems, number, target):
    send, recv = sems
    return pltpu.make_async_remote_copy(
        src_ref=src, dst_ref=dst, send_sem=send.at[number], recv_sem=recv.at[number],
        device_id=target, device_id_type=MESH,
    )


def partner(index, bit):
    return index + bit - 2 * bit * ((index // bit) % 2)


class Place:
    def __init__(self):
        self.dp, self.row, self.col = (lax.axis_index(a) for a in ("dp", "row", "col"))
        self.dps = lax.axis_size("dp")
        self.core, self.chip = self.col % 2, self.col // 2
        self.near, self.far = partner(self.col, 1), partner(self.col, 2)
        self.twin = partner(self.dp, 1)
        self.half = self.dp % 2
        self.plane = 3 * self.core + self.chip - 2 * self.core * self.chip
        self.source = 2 * (((self.row + 1) // 2) % 2) + self.row // 2
        self.corner = partner(self.far, 1)
        self.stays = self.plane == self.row
        self.far_plane = 3 * self.core + (1 - self.chip) - 2 * self.core * (1 - self.chip)
        self.sender = 2 * self.chip + self.source % 2
        self.home = jnp.logical_or(self.stays, self.far_plane == self.row)


def greet(place):
    barrier = pltpu.get_barrier_semaphore()

    def signal(target):
        pl.semaphore_signal(barrier, inc=1, device_id=target, device_id_type=MESH)

    for step in (1, 2, 3):
        signal({"row": (place.row + step) % 4})
    for col in (place.near, place.far, place.corner):
        signal({"col": col})
    amount = 6
    bit = 1
    while bit < place.dps:
        signal({"dp": partner(place.dp, bit)})
        amount += 1
        bit *= 2

    for plane, stays in ((place.plane, place.stays), (place.far_plane, place.far_plane == place.row)):
        signal({"row": plane, "col": place.near})

        @pl.when(jnp.logical_not(stays))
        def _():
            signal({"row": plane, "col": place.col})

    for other in range(4):
        @pl.when(jnp.logical_not(jnp.logical_and(place.home, place.row == other)))
        def _():
            signal({"row": other, "col": place.sender})

        @pl.when(jnp.logical_not(jnp.logical_and(place.stays, place.col == other)))
        def _():
            signal({"row": place.plane, "col": other})

        @pl.when(jnp.logical_not(jnp.logical_and(place.stays, place.row == other)))
        def _():
            signal({"row": other, "col": place.source})

    amount = amount + 16 - 2 * place.home.astype(jnp.int32) - 2 * place.stays.astype(jnp.int32)
    pl.semaphore_wait(barrier, amount)


class Transpose:
    def __init__(self, place, src, dst, relay, sems, first):
        self.p, self.src, self.dst, self.relay, self.sems, self.first = place, src, dst, relay, sems, first
        self.rows, self.width = src.shape[0] // 4, src.shape[1]

    def part(self):
        return self.dst.at[:, hint(self.p.row, self.width)]

    def cross(self, n):
        src = self.src.at[hint(2 * (1 - self.p.chip) + n, self.rows)]
        return remote(src, self.relay.at[n], self.sems, self.first + 4 + n, {"col": self.p.far})

    def out(self, relayed, n):
        p = self.p
        col = p.col if n == 0 else p.near
        src = self.relay.at[col % 2] if relayed else self.src.at[hint(col, self.rows)]
        return pltpu.make_async_remote_copy(
            src_ref=src, dst_ref=self.part(),
            send_sem=self.sems[0].at[self.first + 2 * relayed + n], recv_sem=self.sems[1].at[self.first + p.row],
            device_id={"row": p.far_plane if relayed else p.plane, "col": col}, device_id_type=MESH,
        )

    def kept(self, relayed):
        p = self.p
        src = self.relay.at[p.core] if relayed else self.src.at[hint(p.col, self.rows)]
        return pltpu.make_async_copy(src, self.part(), self.sems[1].at[self.first + p.row])

    def leaves(self, relayed):
        return (self.p.far_plane if relayed else self.p.plane) != self.p.row

    def send(self, relayed):
        self.out(relayed, 1).start()

        @pl.when(self.leaves(relayed))
        def _():
            self.out(relayed, 0).start()

        @pl.when(jnp.logical_not(self.leaves(relayed)))
        def _():
            self.kept(relayed).start()

    def start_cross(self):
        for n in (0, 1):
            self.cross(n).start()

    def forward(self):
        for n in (0, 1):
            self.cross(n).wait_recv()
        self.send(1)

    def wait_recv(self):
        p = self.p
        for other in range(4):
            mine = jnp.logical_and(p.home, p.row == other)
            part = self.dst.at[:, pl.ds(other * self.width, self.width)]

            @pl.when(jnp.logical_not(mine))
            def _():
                pltpu.make_async_remote_copy(
                    src_ref=part, dst_ref=part, send_sem=self.sems[0].at[self.first + other],
                    recv_sem=self.sems[1].at[self.first + other],
                    device_id={"row": other, "col": p.sender}, device_id_type=MESH,
                ).wait_recv()

            @pl.when(mine)
            def _():
                self.kept(0).wait()

    def wait_send(self):
        for n in (0, 1):
            self.cross(n).wait_send()
        for relayed in (0, 1):
            self.out(relayed, 1).wait_send()

            @pl.when(self.leaves(relayed))
            def _():
                self.out(relayed, 0).wait_send()


TRANSPOSE_SEMS = 6


class Weight:
    def __init__(self, place, src, dst, offset, by_rows, last, sems, first):
        self.p, self.src, self.dst, self.offset, self.by_rows, self.last = place, src, dst, offset, by_rows, last
        self.sems, self.first = sems, first
        self.rows, self.width = src.shape
        self.part = self.rows // 2

    def whole(self, side, row):
        if self.by_rows:
            return self.dst.at[side, hint(row, self.rows)]
        return self.dst.at[side, pl.ds(self.offset, self.rows), hint(row, self.width)]

    def piece(self, side, row, half):
        if self.by_rows:
            return self.dst.at[side, hint(row * 2 + half, self.part)]
        start = pl.multiple_of(self.offset + half * self.part, self.part)
        return self.dst.at[side, pl.ds(start, self.part), hint(row, self.width)]

    def other(self, step):
        return (self.p.row + 4 - step) % 4

    def move(self, src, dst, number, target):
        return remote(src, dst, self.sems, self.first + number, target)

    def pass_on(self, side, step, half, number, target):
        src = self.piece(side, self.other(step), half)
        dst = self.piece(1 if "col" in target else side, self.other(step), half)
        return self.move(src, dst, number + step - 1, target)

    def own(self):
        return pltpu.make_async_copy(self.src, self.whole(0, self.p.row), self.sems[1].at[self.first])

    def across(self):
        return self.move(self.src, self.whole(1, self.p.row), 1, {"col": self.p.far})

    def along(self, step):
        p = self.p
        return self.move(
            self.src.at[hint(p.half, self.part)], self.piece(0, p.row, p.half), 1 + step, {"row": (p.row + step) % 4}
        )

    def to_twin(self, step):
        return self.pass_on(0, step, self.p.half, 5, {"dp": self.p.twin})

    def to_far(self, step):
        return self.pass_on(0, step, self.p.half, 8, {"col": self.p.far})

    def onward(self, step):
        if self.last == "y":
            return self.pass_on(0, step, 1 - self.p.half, 11, {"col": self.p.far})
        return self.pass_on(1, step, self.p.half, 11, {"dp": self.p.twin})

    def arrival(self, side, step, half, number):
        part = self.piece(side, self.other(step), half)
        return self.move(part, part, number + step - 1, {"dp": self.p.twin})

    def start_along(self):
        for step in (1, 2, 3):
            self.along(step).start()

    def spread(self, steps=(1, 2, 3)):
        for step in steps:
            self.arrival(0, step, self.p.half, 2).wait_recv()
            self.to_twin(step).start()
            self.to_far(step).start()

    def spread_last(self, steps=(1, 2, 3)):
        p = self.p
        for step in steps:
            if self.last == "y":
                self.arrival(0, step, 1 - p.half, 5).wait_recv()
            else:
                self.arrival(1, step, p.half, 8).wait_recv()
            self.onward(step).start()

    def ready(self, side):
        p = self.p
        if side == 0:
            self.own().wait()
        else:
            self.across().wait_recv()
        for step in (1, 2, 3):
            if side == 0 and self.last == "x":
                self.arrival(0, step, 1 - p.half, 5).wait_recv()
            if side == 1 and self.last == "y":
                self.arrival(1, step, p.half, 8).wait_recv()
            if side == 1:
                self.arrival(1, step, 1 - p.half, 11).wait_recv()

    def sent(self):
        self.across().wait_send()
        for step in (1, 2, 3):
            for copy in (self.along(step), self.to_twin(step), self.to_far(step), self.onward(step)):
                copy.wait_send()


WEIGHT_SEMS = 14


class Halves:
    def __init__(self, place, src, dst, sems, first):
        self.p, self.src, self.dst, self.sems, self.first = place, src, dst, sems, first
        self.rows = src.shape[0]
        self.part = self.rows // 2

    def own(self):
        return pltpu.make_async_copy(self.src, self.dst.at[hint(self.p.row, self.rows)], self.sems[1].at[self.first])

    def along(self, step):
        p = self.p
        return remote(
            self.src.at[hint(p.half, self.part)], self.dst.at[hint(2 * p.row + p.half, self.part)], self.sems,
            self.first + step, {"row": (p.row + step) % 4},
        )

    def part_of(self, step, half):
        return self.dst.at[hint(2 * ((self.p.row + 4 - step) % 4) + half, self.part)]

    def to_twin(self, step, half):
        part = self.part_of(step, half)
        return remote(part, part, self.sems, self.first + 3 + step, {"dp": self.p.twin})

    def start(self):
        self.own().start()
        for step in (1, 2, 3):
            self.along(step).start()

    def spread(self):
        p = self.p
        for step in (1, 2, 3):
            part = self.part_of(step, p.half)
            remote(part, part, self.sems, self.first + step, {"dp": p.twin}).wait_recv()
            self.to_twin(step, p.half).start()

    def ready(self):
        p = self.p
        for step in (1, 2, 3):
            self.to_twin(step, 1 - p.half).wait_recv()
        self.own().wait()

    def sent(self):
        for step in (1, 2, 3):
            self.along(step).wait_send()
            self.to_twin(step, self.p.half).wait_send()


HALVES_SEMS = 7


GELU_ROOT = math.sqrt(2.0 / math.pi)
GELU_CUBE = 0.044715


def gelu_pair(x):
    square = x * x
    t = jnp.tanh(GELU_ROOT * x * (1.0 + GELU_CUBE * square))
    half = 0.5 * (1.0 + t)
    slope = half + 0.5 * x * (1.0 - t * t) * (GELU_ROOT * (1.0 + 3.0 * GELU_CUBE * square))
    return x * half, slope


def moments(x):
    center = jnp.mean(x, 1, keepdims=True)
    spread = jnp.mean(x * x, 1, keepdims=True) - center * center
    inverse = lax.rsqrt(spread + EPSILON)
    return (x - center) * inverse, inverse


class Chip:
    def __init__(self, place, sems, first):
        self.p, self.sems, self.first = place, sems, first

    def copy(self, number, src, dst):
        return remote(src, dst, self.sems, self.first + number, {"col": self.p.near})


class Untranspose:
    def __init__(self, place, src, dst, sems, first):
        self.place, self.src, self.dst, self.sems, self.first = place, src, dst, sems, first
        self.rows, self.width = src.shape[0], src.shape[1] // 4

    def out(self, other):
        p = self.place
        return pltpu.make_async_remote_copy(
            src_ref=self.src.at[:, pl.ds(other * self.width, self.width)],
            dst_ref=self.dst.at[hint(p.col, self.rows)],
            send_sem=self.sems[0].at[self.first + other], recv_sem=self.sems[1].at[self.first + p.col],
            device_id={"row": other, "col": p.source}, device_id_type=MESH,
        )

    def kept(self):
        p = self.place
        return pltpu.make_async_copy(
            self.src.at[:, hint(p.row, self.width)],
            self.dst.at[hint(p.col, self.rows)],
            self.sems[1].at[self.first + p.col],
        )

    def start(self):
        p = self.place
        for other in range(4):
            @pl.when(jnp.logical_not(jnp.logical_and(p.stays, p.row == other)))
            def _():
                self.out(other).start()

        @pl.when(p.stays)
        def _():
            self.kept().start()

    def wait_recv(self):
        p = self.place
        for other in range(4):
            mine = jnp.logical_and(p.stays, p.col == other)
            part = self.dst.at[pl.ds(other * self.rows, self.rows)]

            @pl.when(jnp.logical_not(mine))
            def _():
                pltpu.make_async_remote_copy(
                    src_ref=part, dst_ref=part, send_sem=self.sems[0].at[self.first + other],
                    recv_sem=self.sems[1].at[self.first + other],
                    device_id={"row": p.plane, "col": other}, device_id_type=MESH,
                ).wait_recv()

            @pl.when(mine)
            def _():
                self.kept().wait()

    def wait_send(self):
        p = self.place
        for other in range(4):
            @pl.when(jnp.logical_not(jnp.logical_and(p.stays, p.row == other)))
            def _():
                self.out(other).wait_send()


def add_rows(total, pieces, rows=64):
    @pl.loop(0, total.shape[0] // rows)
    def _(n):
        part = hint(n, rows)
        value = pieces[0][part, :].astype(jnp.float32)
        for piece in pieces[1:]:
            value = value + piece[part, :].astype(jnp.float32)
        total[part, :] = value.astype(total.dtype)


class Share:
    def __init__(self, place, kind, own, far, result, came, other, rows, totals, slots, sems, first):
        self.p, self.kind, self.own, self.far, self.result = place, kind, own, far, result
        self.came, self.other_ref, self.rows, self.totals, self.slots = came, other, rows, totals, slots
        self.sems, self.first = sems, first
        self.width = own.shape[1]
        self.part = self.width // 2
        self.block = own.shape[0] // 4
        self.mine, self.theirs = hint(place.half, self.part), hint(1 - place.half, self.part)

    def first_copies(self):
        p = self.p
        if self.kind == "xy":
            return [
                remote(src.at[:, self.theirs], self.came.at[n], self.sems, self.first + n, {"dp": p.twin})
                for n, src in enumerate((self.own, self.far))
            ]
        if self.kind == "yx":
            return [remote(self.far, self.came, self.sems, self.first, {"col": p.far})]
        return [remote(self.own.at[:, self.theirs], self.came, self.sems, self.first, {"dp": p.twin})]

    def start(self):
        for copy in self.first_copies():
            copy.start()

    def gather_sum(self, jobs):
        blocks = []
        for total, sources in jobs:
            for n in range(4):
                part = pl.ds(n * self.block, self.block)
                blocks.append((total.at[part], [src.at[part] for src in sources]))
        copies = []
        for n, (_, sources) in enumerate(blocks):
            copies.append([
                pltpu.make_async_copy(
                    src, self.slots[2 * (n % 2) + m].at[:, : src.shape[1]],
                    self.sems[1].at[self.first + 8 + 2 * (n % 2) + m],
                )
                for m, src in enumerate(sources)
            ])
        for copy in copies[0]:
            copy.start()
        for n, (total, sources) in enumerate(blocks):
            if n + 1 < len(blocks):
                for copy in copies[n + 1]:
                    copy.start()
            for copy in copies[n]:
                copy.wait()
            add_rows(total, [self.slots[2 * (n % 2) + m].at[:, : total.shape[1]] for m in range(len(sources))])

    def second_copy(self):
        p = self.p
        if self.kind == "xy":
            return remote(self.totals[1], self.other_ref, self.sems, self.first + 2, {"col": p.far})
        return remote(self.totals[0].at[:, self.theirs], self.other_ref, self.sems, self.first + 2, {"dp": p.twin})

    def first_sum(self):
        for copy in self.first_copies():
            copy.wait()
        if self.kind == "xy":
            self.gather_sum([
                (self.totals[1], [self.came.at[1], self.far.at[:, self.mine]]),
                (self.totals[0], [self.came.at[0], self.own.at[:, self.mine]]),
            ])
        elif self.kind == "yx":
            self.gather_sum([(self.totals[0], [self.came, self.own])])
        else:
            self.gather_sum([(self.totals[0], [self.came, self.own.at[:, self.mine]])])

    def total(self):
        return self.totals[1] if self.kind == "yx" else self.totals[0]

    def second_sum(self):
        self.second_copy().wait()
        if self.kind == "xy":
            self.gather_sum([(self.totals[0], [self.other_ref, self.totals[0]])])
        else:
            self.gather_sum([(self.totals[1], [self.other_ref, self.totals[0].at[:, self.mine]])])

    def row_copy(self, step):
        row = self.p.row
        target = partner(row, 1) if step < 2 else partner(row, 2)
        block = partner(target, 2) if step == 1 else target
        return remote(
            self.total().at[hint(block, self.block)], self.rows.at[step], self.sems, self.first + 3 + step, {"row": target}
        )

    def start_rows(self):
        for step in (1, 0):
            self.row_copy(step).start()

    def row_add(self, block, step, target):
        load = pltpu.make_async_copy(
            self.rows.at[step], self.slots[step].at[:, : self.part], self.sems[1].at[self.first + 8 + step]
        )
        load.start()
        load.wait()
        add_rows(target, [self.total().at[hint(block, self.block)], self.slots[step].at[:, : self.part]])

    def row_half(self):
        other = partner(self.p.row, 2)
        self.row_copy(1).wait()
        self.row_add(other, 1, self.total().at[hint(other, self.block)])
        self.row_copy(2).start()
        self.row_copy(0).wait()
        self.row_add(self.p.row, 0, self.total().at[hint(self.p.row, self.block)])

    def last_copy(self, half):
        part = self.result.at[:, hint(half, self.part)]
        return remote(part, part, self.sems, self.first + 6, {"dp": self.p.twin})

    def row_sum(self):
        self.row_copy(2).wait()
        self.row_add(self.p.row, 2, self.result.at[:, self.mine])
        self.last_copy(self.p.half).start()

    def finish(self):
        self.last_copy(self.p.half).wait_send()
        self.last_copy(1 - self.p.half).wait_recv()


SHARE_SEMS = 12


class Tally:
    def __init__(self, place, slots, axes, sems, first):
        self.slots = slots
        p = place
        peers = dict(
            row=[{"row": (p.row + step) % 4} for step in (1, 2, 3)],
            col=[{"col": p.near}, {"col": p.far}, {"col": p.corner}],
        )
        bit = 1
        while bit < p.dps:
            peers["dp%d" % bit] = [{"dp": partner(p.dp, bit)}]
            bit *= 2
        names = []
        for axis in axes:
            names += [name for name in peers if name.startswith(axis)]
        self.stages, at = [], 0
        for name in names:
            copies = [
                remote(slots.at[at], slots.at[at + 1 + n], sems, first + n, target)
                for n, target in enumerate(peers[name])
            ]
            self.stages.append((at, copies))
            at += len(copies) + 1
            first += len(copies)
        self.names, self.last, self.next_sem = names, at, first

    def send(self, n):
        for copy in self.stages[n][1]:
            copy.start()

    def add(self, n):
        at, copies = self.stages[n]
        value = self.slots[at]
        for m, copy in enumerate(copies):
            copy.wait()
            value = value + self.slots[at + 1 + m]
        self.slots[at + len(copies) + 1] = value

    def after(self, n):
        at, copies = self.stages[n]
        return at + len(copies) + 1


def tally_slots(bits, axes):
    return sum({"row": 4, "col": 4, "dp": 2 * bits}[axis] for axis in axes) + 1


def layer_kernel(
    heads, token_total,
    slope_ref, bias_ref, vector_ref, joined_ref, layer_ref, up_ref, down_ref, out_ref, up_bias_ref,
    teacher_ref, cot_ref, valid_ref,
    layer_out_ref, input_grad_ref, upg_ref, dng_ref, outg_ref, joinedg_ref, vector_sum_ref, scale_ref,
    upg_own, upg_far, dng_own, dng_far, came_up, came_down, came_out, came_joined, other_up, other_down, other_out,
    rows_up, rows_down, rows_out, rows_joined,
    xt_ref, nall_ref, mixed_ref, att_ref, lse_ref, jall_ref, vall_ref, early_ref, up_sums_ref,
    chip_ref, gt_ref, vt_ref, up2_ref, dn2_ref, ub2_ref, normed, gchip, bchip, give, take, middle, gres, low_ref, stage,
    grad, gfar, dout, relay, vectors, late, count, sends, recvs,
):
    sems = (sends, recvs)
    f32, bf = jnp.float32, jnp.bfloat16
    p = Place()
    quarter, features = xt_ref.shape
    hidden = down_ref.shape[0]
    moved = Transpose(p, layer_ref, xt_ref, relay.at[0], sems, 0)
    target = Transpose(p, grad, gt_ref, relay.at[1], sems, TRANSPOSE_SEMS)
    base = 2 * TRANSPOSE_SEMS
    back = Untranspose(p, low_ref, layer_out_ref, sems, base)
    base += 4
    w_out = Weight(p, out_ref, dn2_ref, hidden, False, "y", sems, base)
    w_up = Weight(p, up_ref, up2_ref, 0, True, "y", sems, base + WEIGHT_SEMS)
    w_downs = [
        Weight(
            p, down_ref.at[pl.ds(n * (hidden // 2), hidden // 2)], dn2_ref, n * (hidden // 2), False, "x", sems,
            base + (2 + n) * WEIGHT_SEMS,
        )
        for n in (0, 1)
    ]
    weights = [w_out, w_up] + w_downs
    base += 4 * WEIGHT_SEMS
    w_joined = Halves(p, joined_ref, jall_ref, sems, base)
    base += HALVES_SEMS
    small_base, bias_base = base, base + 4
    base += 6

    def small(step):
        return remote(
            vector_ref, vall_ref.at[:, hint(p.row, 256)], sems, small_base + step, {"row": (p.row + step) % 4}
        )

    def small_came(step):
        part = vall_ref.at[:, hint((p.row + 4 - step) % 4, 256)]
        return remote(part, part, sems, small_base + step, {"row": (p.row + step) % 4})

    small_own = pltpu.make_async_copy(vector_ref, vall_ref.at[:, hint(p.row, 256)], recvs.at[small_base])
    bias_own = pltpu.make_async_copy(up_bias_ref, ub2_ref.at[0], recvs.at[bias_base])
    bias_far = remote(up_bias_ref, ub2_ref.at[1], sems, bias_base + 1, {"col": p.far})
    counted = Tally(p, count, ("col", "dp"), sems, base)
    base = counted.next_sem
    tokens = valid_ref.shape[0]
    number = jnp.zeros((8, 128), f32)
    for n in range(tokens // 256):
        number = number + jnp.sum(valid_ref[n * 256 : (n + 1) * 256, :].astype(f32), axis=0, keepdims=True)
    count[0] = number
    greet(p)
    counted.send(0)
    for step in (1, 2, 3):
        small(step).start()
    moved.start_cross()
    moved.send(0)
    bias_far.start()
    w_out.across().start()
    w_up.across().start()
    small_own.start()
    bias_own.start()
    for w in weights:
        w.own().start()
    for n in range(len(counted.stages)):
        counted.add(n)
        if n + 1 < len(counted.stages):
            counted.send(n + 1)
    moved.forward()

    scale_ref[...] = token_total / count[counted.last]
    scale = scale_ref[:1, :1]

    @pl.loop(0, 32)
    def _(n):
        rows = hint(n, grad.shape[0] // 32)
        factor = valid_ref[rows, :].astype(f32) * scale
        for f in range(grad.shape[1] // 128):
            cols = slice(f * 128, (f + 1) * 128)
            grad[rows, cols] = (
                cot_ref[rows, cols].astype(f32) - factor * teacher_ref[rows, cols].astype(f32)
            ).astype(bf)

    valid_base = base
    base += 1

    def valid_out():
        return pltpu.make_async_remote_copy(
            src_ref=valid_ref.at[hint(p.row, quarter)], dst_ref=vt_ref,
            send_sem=sends.at[valid_base], recv_sem=recvs.at[valid_base],
            device_id={"row": p.plane, "col": p.row}, device_id_type=MESH,
        )

    same = jnp.logical_and(p.stays, p.col == p.row)
    valid_kept = pltpu.make_async_copy(valid_ref.at[hint(p.row, quarter)], vt_ref, recvs.at[valid_base])

    for step in (1, 2, 3):
        small_came(step).wait_recv()
        small(step).wait_send()
    small_own.wait()
    moved.wait_recv()
    w_joined.start()

    first = p.col * quarter

    def norm_one(n):
        rows = hint(n, 128)
        standard, _ = moments(xt_ref[rows, :].astype(f32))
        place = pl.ds(pl.multiple_of(first + n * 128, 128), 128)
        nall_ref[place, :] = (standard * vall_ref[0:1, :] + vall_ref[1:2, :]).astype(bf)

    pl.loop(0, quarter // 128)(norm_one)
    mine = nall_ref.at[hint(p.col, quarter)]
    to_far = remote(mine, mine, sems, base, {"col": p.far})
    to_near = remote(mine, mine, sems, base + 1, {"col": p.near})
    theirs = nall_ref.at[hint(p.far, quarter)]
    far_came = remote(theirs, theirs, sems, base, {"col": p.far})
    pass_on = remote(theirs, theirs, sems, base + 2, {"col": p.near})
    beside = nall_ref.at[hint(p.near, quarter)]
    near_came = remote(beside, beside, sems, base + 1, {"col": p.near})
    across = nall_ref.at[hint(p.corner, quarter)]
    corner_came = remote(across, across, sems, base + 2, {"col": p.near})
    base += 3
    to_far.start()
    to_near.start()
    for w in w_downs:
        w.across().start()

    @pl.when(jnp.logical_not(same))
    def _():
        valid_out().start()

    @pl.when(same)
    def _():
        valid_kept.start()

    def project(index):
        @pl.loop(0, quarter // 256)
        def _(n):
            rows = pl.ds(pl.multiple_of(index * quarter + n * 256, 256), 256)
            mixed_ref[rows, :] = (nn(nall_ref[rows, :], jall_ref[...]) + bias_ref[...]).astype(bf)

    w_joined.spread()
    for w in weights:
        w.start_along()
    w_joined.ready()
    project(p.col)
    near_came.wait_recv()
    project(p.near)
    far_came.wait_recv()
    pass_on.start()
    project(p.far)
    corner_came.wait_recv()
    project(p.corner)
    w_out.spread()

    own_heads = att_ref.shape[1]
    blocks = tokens // BLOCK
    per_chip = blocks // 2
    share_base = base
    base += per_chip

    def chip_place(n):
        half = per_chip // 2
        return ((n // half + p.core) % 2) * half + n % half

    def share(n, i):
        return pltpu.make_async_remote_copy(
            src_ref=att_ref.at[hint(i, BLOCK)], dst_ref=chip_ref.at[hint(chip_place(n), BLOCK), pl.ds(own_heads, own_heads)],
            send_sem=sends.at[share_base + n], recv_sem=recvs.at[share_base + n],
            device_id={"col": p.far}, device_id_type=MESH,
        )

    def after(it, i):
        @pl.when(it < per_chip)
        def _():
            share(it, i).start()

        @pl.when(it >= per_chip)
        def _():
            chip_ref[hint(chip_place(it - per_chip), BLOCK), :own_heads] = att_ref[hint(i, BLOCK), :]

        for units, action in plan:
            @pl.when(it == at_units(units))
            def _():
                action()

    order = (
        [per_chip + n + 1 for n in range(per_chip)] + [n + 1 for n in range(per_chip)],
        [n + 1 for n in range(blocks)],
    )

    def at_units(units):
        found = []
        for counts in order:
            total, it = 0, 0
            for it, n in enumerate(counts):
                total += n
                if total >= units:
                    break
            found.append(it)
        return found[0] * (1 - p.chip) + found[1] * p.chip

    plan = [
        (3, lambda: w_out.spread_last()),
        (6, lambda: w_up.spread((1,))),
        (11, lambda: w_up.spread((2,))),
        (18, lambda: w_up.spread((3,))),
        (27, lambda: w_up.spread_last((1, 2))),
        (32, lambda: w_downs[0].spread((1, 2))),
    ]

    def attend(*scratch):
        attention_rows(
            heads, lambda it: (it + per_chip * (1 - p.chip)) % blocks, after,
            slope_ref, mixed_ref, att_ref, lse_ref, *scratch,
        )

    pairs = heads // 2
    pl.run_scoped(
        attend,
        pltpu.VMEM((heads, blocks, BLOCK, PAIR), bf), pltpu.VMEM((pairs, blocks, BLOCK, PAIR), bf),
        pltpu.VMEM((pairs, blocks, 2 * BLOCK, PAIR), bf), pltpu.VMEM((heads, BLOCK, BLOCK), f32),
        pltpu.VMEM((heads, blocks, BLOCK, BLOCK), f32), pltpu.VMEM((heads, BLOCK, PAIR), f32),
        pltpu.VMEM((heads, BLOCK, PAIR), f32), pltpu.VMEM((pairs, BLOCK, PAIR), f32),
    )

    @pl.loop(0, per_chip)
    def _(n):
        share(n, n + per_chip * (1 - p.chip)).wait()

    w_up.spread_last((3,))
    w_downs[0].spread((3,))
    target.start_cross()
    w_out.ready(0)
    w_out.ready(1)
    core = Chip(p, sems, base)
    base += 12
    ROWS = 256
    halves = quarter // ROWS

    def swap_rows(number, buffer, n):
        return core.copy(
            number + n, buffer.at[pl.ds(n * ROWS, ROWS)], buffer.at[pl.ds(quarter + n * ROWS, ROWS)]
        )

    def swap_came(number, buffer, n):
        part = buffer.at[pl.ds(quarter + n * ROWS, ROWS)]
        return core.copy(number + n, part, part)

    def give_rows(number, n):
        return core.copy(number + n, give.at[pl.ds(n * ROWS, ROWS)], take.at[pl.ds(n * ROWS, ROWS)])

    def take_rows(number, n):
        part = take.at[pl.ds(n * ROWS, ROWS)]
        return core.copy(number + n, part, part)

    def partial(number, keep, product, again):
        if again:
            for n in range(halves):
                give_rows(number - 4, n).wait_send()
        for n in range(halves):
            give[n * ROWS : (n + 1) * ROWS, :] = product(pl.ds(quarter + n * ROWS, ROWS)).astype(bf)
            give_rows(number, n).start()
        for n in range(halves):
            keep[n * ROWS : (n + 1) * ROWS, :] = product(pl.ds(n * ROWS, ROWS))

    partial(
        0, middle,
        lambda rows: nn(chip_ref[rows, :own_heads], dn2_ref[0, hidden:, :])
        + nn(chip_ref[rows, own_heads:], dn2_ref[1, hidden:, :]),
        False,
    )
    w_downs[1].spread()
    target.send(0)
    for n in range(halves):
        take_rows(0, n).wait_recv()

        @pl.loop(0, ROWS // 64)
        def _(m):
            rows = pl.ds(pl.multiple_of(n * ROWS + m * 64, 64), 64)
            value = xt_ref[rows, :].astype(f32) + (
                middle[rows, :] + take[rows, :].astype(f32) + vall_ref[2:3, :]
            )
            middle[rows, :] = value
            standard, _ = moments(value)
            normed[rows, :] = (standard * vall_ref[3:4, :] + vall_ref[4:5, :]).astype(bf)

        swap_rows(2, normed, n).start()
    w_up.ready(0)
    bias_own.wait()
    bias_far.wait()

    slots = [give.at[pl.ds(256 * (n // 2), 256), pl.ds(hidden // 2 * (n % 2), hidden // 2)] for n in range(4)]
    outg_own, outg_far = (dn2_ref.at[0, :features, pl.ds(own_heads * n, own_heads)] for n in (0, 1))
    jgrad = dn2_ref.at[1, :features, : mixed_ref.shape[1]]
    s_down = Share(
        p, "xy", dng_own, dng_far, dng_ref, came_down, other_down, rows_down,
        [up2_ref.at[1, :, pl.ds(hidden // 2 * n, hidden // 2)] for n in (0, 1)], slots, sems, base,
    )
    s_up = Share(
        p, "xy", upg_own, upg_far, upg_ref, came_up, other_up, rows_up,
        [up2_ref.at[0, :, pl.ds(hidden // 2 * n, hidden // 2)] for n in (0, 1)], slots, sems, base + SHARE_SEMS,
    )
    s_out = Share(
        p, "yx", outg_own, outg_far, outg_ref, came_out, other_out, rows_out,
        [dn2_ref.at[1, :features, pl.ds(768, 256)], dn2_ref.at[0, :features, pl.ds(896, 128)]], slots, sems,
        base + 2 * SHARE_SEMS,
    )
    s_joined = Share(
        p, "x", jgrad, None, joinedg_ref, came_joined, None, rows_joined,
        [dn2_ref.at[0, :features, pl.ds(512, 384)]], slots, sems, base + 3 * SHARE_SEMS,
    )
    base += 4 * SHARE_SEMS

    def natural(chip, n):
        return hint(2 * chip + (p.core + n) % 2, quarter)

    att_base = base
    base += 2

    def share_grad(n):
        return remote(
            gfar.at[pl.ds(n * quarter, quarter)], dout.at[natural(p.chip, n)], sems, att_base + n, {"col": p.far}
        )

    def share_grad_came(n):
        part = dout.at[natural(1 - p.chip, n)]
        return remote(part, part, sems, att_base + n, {"col": p.far})

    stage_base = base
    base += 2

    def middle_part(act, der, keep):
        wide = 256

        def up_rows(side):
            def body(n):
                rows = pl.ds(pl.multiple_of(n * ROWS, ROWS), ROWS)

                @pl.loop(0, hidden // wide, unroll=2)
                def _(m):
                    cols = hint(m, wide)
                    before = nn(normed[rows, :], up2_ref[side, :, cols]) + ub2_ref[side, 0:1, cols]
                    value, slope = gelu_pair(before)
                    act[side, rows, cols] = value.astype(bf)
                    der[side, rows, cols] = slope.astype(bf)

            return body

        pl.loop(0, halves)(up_rows(0))
        for n in range(halves):
            swap_came(2, normed, n).wait_recv()
        w_downs[0].spread_last()
        target.forward()
        pl.loop(halves, 2 * halves)(up_rows(0))
        w_up.ready(1)
        pl.loop(0, 2 * halves)(up_rows(1))
        w_downs[1].spread_last()
        for w in w_downs:
            w.ready(0)
            w.ready(1)
        partial(
            4, gres,
            lambda rows: nn(act[0, rows, :], dn2_ref[0, :hidden, :]) + nn(act[1, rows, :], dn2_ref[1, :hidden, :]),
            True,
        )
        target.wait_recv()

        @pl.when(jnp.logical_not(same))
        def _():
            valid_out().wait_send()
            valid_out().wait_recv()

        @pl.when(same)
        def _():
            valid_kept.wait()

        early_ref[...] = jnp.zeros_like(early_ref)
        for n in range(halves):
            take_rows(4, n).wait_recv()

            @pl.loop(0, ROWS // 64)
            def _(m):
                rows = pl.ds(pl.multiple_of(n * ROWS + m * 64, 64), 64)
                result = middle[rows, :] + (gres[rows, :] + take[rows, :].astype(f32) + vall_ref[5:6, :])
                low_ref[rows, :] = result.astype(bf)
                factor = vt_ref[rows, :].astype(f32)[:, :1] * scale
                value = gt_ref[rows, :].astype(f32) + factor * result
                gres[rows, :] = value
                rounded = value.astype(bf)
                gchip[rows, :] = rounded
                early_ref[5:6, :] += jnp.sum(rounded.astype(f32), axis=0, keepdims=True)

            swap_rows(6, gchip, n).start()
        back.start()
        up_sums_ref[...] = jnp.zeros_like(up_sums_ref)

        def before_rows(n):
            rows = pl.ds(pl.multiple_of(n * ROWS, ROWS), ROWS)

            @pl.loop(0, 2 * hidden // wide, unroll=2)
            def _(m):
                side, cols = m // (hidden // wide), hint(m % (hidden // wide), wide)
                value = nt(gchip[rows, :], dn2_ref[side, cols, :]) * der[side, rows, cols].astype(f32)
                rounded = value.astype(bf)
                der[side, rows, cols] = rounded
                up_sums_ref[side, 0:1, cols] += jnp.sum(rounded.astype(f32), axis=0, keepdims=True)

        def weight_grad(slot, source, values, sinks):
            @pl.loop(0, features // 256)
            def _(f):
                cols = hint(f, 256)
                turned = source[:, cols].T
                for side, sink in enumerate(sinks):
                    copy = pltpu.make_async_copy(stage.at[side], sink.at[cols], recvs.at[slot + side])

                    @pl.when(f > 0)
                    def _():
                        copy.wait()

                    stage[side] = nn(turned, values[side]).astype(bf)
                    copy.start()

            for side, sink in enumerate(sinks):
                pltpu.make_async_copy(stage.at[side], sink.at[pl.ds(0, 256)], recvs.at[slot + side]).wait()

        pl.loop(0, halves)(before_rows)
        for n in range(halves):
            swap_came(6, gchip, n).wait_recv()
        weight_grad(stage_base, gchip, act, (dng_own, dng_far))
        s_down.start()
        pl.loop(halves, 2 * halves)(before_rows)
        partial(
            8, keep, lambda rows: nt(der[0, rows, :], up2_ref[0]) + nt(der[1, rows, :], up2_ref[1]), True
        )

        for n in range(halves):
            for number, buffer in ((2, normed), (6, gchip)):
                swap_rows(number, buffer, n).wait_send()
        for n in range(halves):
            take_rows(8, n).wait_recv()

            @pl.loop(0, ROWS // 64)
            def _(m):
                rows = pl.ds(pl.multiple_of(n * ROWS + m * 64, 64), 64)
                value = keep[rows, :] + take[rows, :].astype(f32)
                standard, inverse = moments(middle[rows, :])
                early_ref[3:4, :] += jnp.sum(value * standard, axis=0, keepdims=True)
                early_ref[4:5, :] += jnp.sum(value, axis=0, keepdims=True)
                scaled = value * vall_ref[3:4, :]
                one = jnp.mean(scaled, 1, keepdims=True)
                two = jnp.mean(scaled * standard, 1, keepdims=True)
                value = gres[rows, :] + inverse * (scaled - one - standard * two)
                gres[rows, :] = value
                rounded = value.astype(bf)
                bchip[rows, :] = rounded
                early_ref[2:3, :] += jnp.sum(rounded.astype(f32), axis=0, keepdims=True)

            swap_rows(10, bchip, n).start()
        for n in range(2 * halves):
            if n >= halves:
                swap_came(10, bchip, n - halves).wait_recv()
            rows = pl.ds(n * ROWS, ROWS)
            place = pl.ds(
                pl.multiple_of((2 * p.chip + (p.core + n // halves) % 2) * quarter + n % halves * ROWS, ROWS), ROWS
            )
            dout[place, :] = nt(bchip[rows, :], dn2_ref[0, hidden:, :]).astype(bf)
            gfar[rows, :] = nt(bchip[rows, :], dn2_ref[1, hidden:, :]).astype(bf)
            if n % halves == halves - 1:
                share_grad(n // halves).start()
        weight_grad(stage_base, normed, der, (upg_own, upg_far))
        s_up.start()

    pl.run_scoped(
        middle_part,
        pltpu.VMEM((2, 2 * quarter, hidden), bf), pltpu.VMEM((2, 2 * quarter, hidden), bf), pltpu.VMEM((quarter, features), f32),
    )

    for w in weights:
        w.sent()

    @pl.loop(0, features // 256)
    def _(f):
        cols = hint(f, 256)
        turned = bchip[:, cols].T
        outg_own[cols, :] = nn(turned, chip_ref[:, :own_heads]).astype(bf)
        outg_far[cols, :] = nn(turned, chip_ref[:, own_heads:]).astype(bf)

    for n in range(halves):
        give_rows(8, n).wait_send()
        swap_rows(10, bchip, n).wait_send()
    back.wait_recv()
    target.wait_send()
    fetch = pltpu.make_async_copy(layer_out_ref, grad, recvs.at[stage_base])
    fetch.start()
    fetch.wait()
    error = jnp.zeros((1, 128), f32)
    for n in range(tokens // 128):
        rows = slice(n * 128, (n + 1) * 128)
        for f in range(grad.shape[1] // 128):
            cols = slice(f * 128, (f + 1) * 128)
            off = grad[rows, cols].astype(f32) - teacher_ref[rows, cols].astype(f32)
            error = error + jnp.sum(off * off * valid_ref[rows, :].astype(f32), axis=0, keepdims=True)
    early_ref[6:7, 0:128] = error
    vectors[0, 0:8, :] = early_ref[...]
    vectors[0, 8:16, :] = jnp.zeros((8, features), f32)
    vectors[0, pl.ds(8 + p.col, 1), :] = up_sums_ref[0]
    vectors[0, pl.ds(8 + p.far, 1), :] = up_sums_ref[1]
    summed = Tally(p, vectors, ("row", "col", "dp"), sems, base)
    base = summed.next_sem
    lately = Tally(p, late, ("row", "dp", "col"), sems, base)
    base = lately.next_sem
    for n in (0, 1):
        share_grad_came(n).wait_recv()
        share_grad(n).wait_send()
    s_out.start()


    def turn(i):
        for at, stage_number in ((0, 0), (2, 1), (3, 2)):
            @pl.when(i == at)
            def _():
                if stage_number > 0:
                    summed.add(stage_number - 1)
                summed.send(stage_number)

        @pl.when(i == 4)
        def _():
            s_down.first_sum()
            s_down.second_copy().start()

    def attend_back(*scratch):
        attention_rows_backward(heads, turn, slope_ref, mixed_ref, dout, att_ref, lse_ref, mixed_ref, *scratch)

    pl.run_scoped(
        attend_back,
        pltpu.VMEM((pairs, blocks, 2 * BLOCK, PAIR), bf), pltpu.VMEM((pairs, blocks, BLOCK, PAIR), bf),
        pltpu.VMEM((pairs, blocks, 2 * BLOCK, PAIR), bf), pltpu.VMEM((pairs, blocks, BLOCK, PAIR), bf),
        pltpu.VMEM((pairs, blocks, 2 * BLOCK, PAIR), bf), pltpu.VMEM((heads, blocks, BLOCK), f32),
        pltpu.VMEM((heads, BLOCK, BLOCK), f32), pltpu.VMEM((heads, BLOCK, PAIR), f32),
        pltpu.VMEM((pairs, blocks, BLOCK, PAIR), f32), pltpu.VMEM((pairs, blocks, BLOCK, PAIR), f32),
        pltpu.VMEM((pairs, blocks, BLOCK, PAIR), f32),
    )

    sums_at = [bchip.at[pl.ds(0, quarter)], bchip.at[pl.ds(quarter, quarter)],
               normed.at[pl.ds(0, quarter)], normed.at[pl.ds(quarter, quarter)]]
    near_in = [gchip.at[pl.ds(0, quarter)], gchip.at[pl.ds(quarter, quarter)]]

    def product(index, slot):
        @pl.loop(0, quarter // 256)
        def _(n):
            rows = pl.ds(pl.multiple_of(index * quarter + n * 256, 256), 256)
            sums_at[slot][hint(n, 256), :] = nt(mixed_ref[rows, :], jall_ref[...]).astype(bf)

    grad_near = [remote(sums_at[n], near_in[n], sems, base + n, {"col": p.near}) for n in (0, 1)]
    grad_far = remote(sums_at[2], take, sems, base + 2, {"col": p.far})
    base += 3
    product(p.corner, 0)
    grad_near[0].start()
    product(p.near, 1)
    grad_near[1].start()
    product(p.far, 2)
    grad_near[0].wait()
    add_rows(sums_at[2], [sums_at[2], near_in[0]])
    grad_far.start()
    product(p.col, 3)
    s_down.second_sum()
    s_down.start_rows()

    @pl.loop(0, features // 128)
    def _(f):
        cols = hint(f, 128)
        jgrad[cols, :] = tn(nall_ref[:, cols], mixed_ref[...]).astype(bf)

    s_joined.start()
    s_out.first_sum()
    s_out.second_copy().start()
    sums = jnp.zeros((1, mixed_ref.shape[1]), f32)
    for n in range(tokens // 256):
        sums = sums + jnp.sum(mixed_ref[n * 256 : (n + 1) * 256, :].astype(f32), axis=0, keepdims=True)
    late[0] = jnp.zeros((8, features), f32)
    late[0, 2:3, 0 : sums.shape[1]] = sums
    s_down.row_half()
    s_up.first_sum()
    s_up.second_copy().start()
    grad_near[1].wait()
    grad_far.wait()
    gin = bchip.at[pl.ds(0, quarter)]
    grad_back = Untranspose(p, gin, input_grad_ref, sems, base)
    base += 4

    @pl.loop(0, quarter // 64)
    def _(n):
        rows = hint(n, 64)
        value = sums_at[3][rows, :].astype(f32) + near_in[1][rows, :].astype(f32) + take[rows, :].astype(f32)
        standard, inverse = moments(xt_ref[rows, :].astype(f32))
        late[0, 0:1, :] += jnp.sum(value * standard, axis=0, keepdims=True)
        late[0, 1:2, :] += jnp.sum(value, axis=0, keepdims=True)
        scaled = value * vall_ref[0:1, :]
        one = jnp.mean(scaled, 1, keepdims=True)
        two = jnp.mean(scaled * standard, 1, keepdims=True)
        gin[rows, :] = (gres[rows, :] + inverse * (scaled - one - standard * two)).astype(bf)

    lately.send(0)
    grad_back.start()
    s_joined.first_sum()
    s_joined.start_rows()
    s_out.second_sum()
    s_out.start_rows()
    s_down.row_sum()
    for n in range(2, len(summed.stages)):
        summed.add(n)
        if n + 1 < len(summed.stages):
            summed.send(n + 1)
    lately.add(0)
    lately.send(1)
    s_up.second_sum()
    s_up.start_rows()
    s_joined.row_half()
    s_out.row_half()
    for n in range(1, len(lately.stages)):
        lately.add(n)
        if n + 1 < len(lately.stages):
            lately.send(n + 1)
    s_up.row_half()
    vector_sum_ref[...] = vectors[summed.last]
    vector_sum_ref[0:2, :] = late[lately.last, 0:2, :]
    joined_at = lately.after(len(lately.stages) - 2)
    vector_sum_ref[7:8, :] = late[joined_at, 2:3, :]
    for share in (s_joined, s_out, s_up):
        share.row_sum()
    for share in (s_down, s_joined, s_out, s_up):
        share.finish()
    grad_back.wait_recv()
    grad_back.wait_send()
    moved.wait_send()
    to_far.wait_send()
    to_near.wait_send()
    pass_on.wait_send()
    w_joined.sent()
    back.wait_send()


def layer_stage(slopes, bias_rows, vectors, joined, layer_in, up, down, out, up_bias, teacher, cot, valid, token_total):
    tokens, width = layer_in.shape
    quarter = tokens // 4
    features = width * lax.axis_size("row")
    joined_width = joined.shape[1]
    heads = joined_width // (3 * HEAD_DIM)
    blocks = tokens // BLOCK
    f32, bf = jnp.float32, jnp.bfloat16
    hidden, head_rows = down.shape[0], out.shape[0]
    vmem, anyspace = pl.BlockSpec(memory_space=pltpu.VMEM), pl.BlockSpec(memory_space=pl.ANY)
    shape = jax.ShapeDtypeStruct
    bits = 0
    while (1 << bits) < lax.axis_size("dp"):
        bits += 1
    count = (
        2 * TRANSPOSE_SEMS + 4 + 4 * WEIGHT_SEMS + HALVES_SEMS + 6 + (3 + bits) + 1 + 3 + blocks // 2 + 12
        + 4 * SHARE_SEMS + 2 + 2 + 2 * (6 + bits) + 3 + 4
    )
    outs = pl.pallas_call(
        functools.partial(layer_kernel, heads, token_total),
        out_shape=(
            shape((tokens, width), bf), shape((tokens, width), bf), shape((width, hidden), bf), shape((width, hidden), bf),
            shape((width, head_rows), bf), shape((width, joined_width), bf), shape((16, features), f32), shape((8, 128), f32),
        ) + (shape((features, hidden), bf),) * 4 + (
            shape((2, features, hidden // 2), bf), shape((2, features, hidden // 2), bf), shape((features, head_rows), bf),
            shape((features, joined_width // 2), bf), shape((features, hidden // 2), bf), shape((features, hidden // 2), bf),
            shape((features, head_rows // 2), bf), shape((3, width, hidden // 2), bf), shape((3, width, hidden // 2), bf),
            shape((3, width, head_rows // 2), bf), shape((3, width, joined_width // 2), bf),
        ),
        in_specs=[pl.BlockSpec(memory_space=pltpu.SMEM), vmem, vmem] + [anyspace] * 6 + [vmem] * 3,
        out_specs=(anyspace,) * 2 + (vmem,) * 6 + (anyspace,) * 15,
        scratch_shapes=[
            pltpu.VMEM((quarter, features), bf), pltpu.VMEM((tokens, features), bf), pltpu.VMEM((tokens, joined_width), bf),
            pltpu.VMEM((tokens, heads * HEAD_DIM), bf), pltpu.VMEM((heads, blocks, BLOCK), f32),
            pltpu.VMEM((features, joined_width), bf), pltpu.VMEM((8, features), f32), pltpu.VMEM((8, features), f32),
            pltpu.VMEM((2, 1, hidden), f32),
            pltpu.VMEM((2 * quarter, 2 * head_rows), bf), pltpu.VMEM((quarter, features), bf), pltpu.VMEM((quarter, 128), bf),
            pltpu.VMEM((2, features, hidden), bf), pltpu.VMEM((2, hidden + head_rows, features), bf),
            pltpu.VMEM((2, 8, hidden), f32), pltpu.VMEM((2 * quarter, features), bf), pltpu.VMEM((2 * quarter, features), bf),
            pltpu.VMEM((2 * quarter, features), bf), pltpu.VMEM((quarter, features), bf), pltpu.VMEM((quarter, features), bf),
            pltpu.VMEM((quarter, features), f32), pltpu.VMEM((quarter, features), f32), pltpu.VMEM((quarter, features), bf),
            pltpu.VMEM((2, 256, hidden), bf), pltpu.VMEM((tokens, width), bf), pltpu.VMEM((2 * quarter, head_rows), bf),
            pltpu.VMEM((tokens, head_rows), bf), pltpu.VMEM((2, 2, quarter, width), bf),
            pltpu.VMEM((tally_slots(bits, ("row", "col", "dp")), 16, features), f32),
            pltpu.VMEM((tally_slots(bits, ("row", "col", "dp")), 8, features), f32),
            pltpu.VMEM((tally_slots(bits, ("col", "dp")), 8, 128), f32),
            pltpu.SemaphoreType.DMA((count,)), pltpu.SemaphoreType.DMA((count,)),
        ],
        compiler_params=pltpu.CompilerParams(vmem_limit_bytes=63 << 20, collective_id=1, has_side_effects=True),
        name="layer_stage",
    )(slopes, bias_rows, vectors, joined, layer_in, up, down, out, up_bias, teacher, cot, valid)
    return outs[:8]


def swap_with(value, axis, bit):
    size = lax.axis_size(axis)
    return lax.ppermute(value, axis, [(i, i ^ bit) for i in range(size)])


def low(value):
    return value.astype(jnp.bfloat16)


def pick(stacked, index):
    return lax.dynamic_index_in_dim(stacked, index, 0, keepdims=False)


def sum_other_pairs(value):
    bit = 2
    while bit < lax.axis_size("dp"):
        value = value + swap_with(low(value), "dp", bit).astype(jnp.float32)
        bit *= 2
    return value


def on_device(
    layer_in,
    first_gain,
    first_shift,
    joined_weight,
    joined_bias,
    out_weight,
    out_bias,
    second_gain,
    second_shift,
    up_weight,
    up_bias,
    down_weight,
    down_bias,
    teacher,
    valid,
    cotangent,
):
    row_size, col_size = lax.axis_size("row"), lax.axis_size("col")
    row, col = lax.axis_index("row"), lax.axis_index("col")
    f32 = jnp.float32
    head_count = joined_bias.shape[0]
    quarter = layer_in.shape[0] // col_size
    head_index = col * head_count + jnp.arange(head_count, dtype=jnp.int32)
    slopes = jnp.exp2(-8.0 * (head_index.astype(f32) + 1.0) / HEADS) * LOG2E

    zero_rows = jnp.zeros_like(joined_bias[:, :HEAD_DIM])
    bias_rows = jnp.stack(
        [joined_bias[:, :HEAD_DIM], zero_rows, joined_bias[:, HEAD_DIM:]], axis=1
    ).reshape(1, -1).astype(f32)
    nothing = jnp.zeros_like(first_gain)
    vectors = jnp.stack(
        [first_gain, first_shift, out_bias, second_gain, second_shift, down_bias, nothing, nothing]
    ).astype(f32)
    token_total = layer_in.shape[0] * lax.axis_size("dp") * col_size
    layer_out, input_grad, up_grad, down_grad, out_grad, joined_grad, sums, scale = layer_stage(
        slopes, bias_rows, vectors, joined_weight, layer_in, up_weight, down_weight, out_weight,
        jnp.broadcast_to(up_bias.astype(f32), (8, up_bias.shape[0])), teacher, cotangent,
        jnp.broadcast_to(low(valid)[:, None], (valid.shape[0], 128)), token_total,
    )
    up_grad, down_grad, out_grad, joined_grad = (
        sum_other_pairs(g.astype(f32)) for g in (up_grad, down_grad, out_grad, joined_grad)
    )
    mine = lax.dynamic_slice_in_dim(sums, row * (D // row_size), D // row_size, 1)
    loss = jnp.sum(sums[6, :128]) * scale[0, 0] / (D * token_total)
    up_bias_grad = pick(sums[8:12], col)
    column_sums = sums[7, : joined_weight.shape[1]].reshape(head_count, 3, HEAD_DIM)
    joined_bias_grad = jnp.concatenate([column_sums[:, 0], column_sums[:, 2]], axis=1)
    return (
        layer_out,
        loss,
        input_grad.astype(f32),
        mine[0],
        mine[1],
        joined_grad,
        joined_bias_grad,
        out_grad.T,
        mine[2],
        mine[3],
        mine[4],
        up_grad,
        up_bias_grad,
        down_grad.T,
        mine[5],
    )


def solution(mesh):
    return jax.shard_map(
        on_device,
        mesh=mesh,
        in_specs=(
            P(("dp", "col"), "row"),
            P("row"),
            P("row"),
            P("row", "col"),
            P("col", None),
            P("col", "row"),
            P("row"),
            P("row"),
            P("row"),
            P("row", "col"),
            P("col"),
            P("col", "row"),
            P("row"),
            P(("dp", "col"), "row"),
            P(("dp", "col")),
            P(("dp", "col"), "row"),
        ),
        out_specs=(
            P(("dp", "col"), "row"),
            P(),
            P(("dp", "col"), "row"),
            P("row"),
            P("row"),
            P("row", "col"),
            P("col", None),
            P("col", "row"),
            P("row"),
            P("row"),
            P("row"),
            P("row", "col"),
            P("col"),
            P("col", "row"),
            P("row"),
        ),
        check_vma=False,
    )
```

time: 787 us -> 398 us (0.51)
  waiting for transfers between devices: 322 us -> 0 us
  Pallas kernels: 66.6 us -> 363 us
  starting transfers between devices: 201 us -> 0 us
  matrix products: 66.5 us -> 0 us
  other arithmetic: 64.2 us -> 8.69 us
  local copies, waits for them, and re-layouts: 39.3 us -> 16.1 us
  between operations: 20.5 us -> 3.15 us
    ppermute x88 -> x0, waiting for transfers between devices: 322 us -> none  [the longest x18 126 us: gather_row(): lax.ppermute(value, 'row', [(i, (i + step) % size) for i in range(size)])]
    pallas_call x2 -> x1, Pallas kernels: 66.6 us -> 363 us  [layer_stage(): pl.pallas_call(functools.partial(layer_kernel, heads, token_total), out_s...]
    ppermute x88 -> x0, starting transfers between devices: 200 us -> none  [the longest x49 61.1 us: swap_with(): return lax.ppermute(value, axis, [(i, i ^ bit) for i in range(size)])]
    dot_general x18 -> x0, matrix products: 66.5 us -> none  [the longest x6 23.7 us: tn(): lax.dot_general(a, b, (((0,), (0,)), ((), ())), preferred_element_type=jn...]
    reduce_sum x8 -> x1, other arithmetic: 22.9 us -> 1.29 us  [on_device(): loss = jnp.sum(sums[6, :128]) * scale[0, 0] / (D * token_total)]
    another operation x28 -> x0, other arithmetic: 16.4 us -> none  [the longest x6 5.58 us: gather_row(): came = jnp.stack(came)]
    unnamed x154 -> x13, local copies, waits for them, and re-layouts: 16.4 us -> 3.13 us
    convert_element_type x7 -> x1, other arithmetic: 11.5 us -> 0.7 us  [low(): return value.astype(jnp.bfloat16)]
  transfers between devices with their start and end apart: 92 -> 0, of which waited for: 36 -> 0; matrix products, arithmetic and copies ran while one was open for 14% -> 0% of each run, Pallas kernels for 9% -> 0%
where the time goes in v5:
time: 398 us; the launch traced here: 391 us
  Pallas kernels  363 us (91%)
  local copies, waits for them, and re-layouts  16.1 us (4%)
  other arithmetic  8.69 us (2%)
    pallas_call x1, Pallas kernels, layer_stage(): pl.pallas_call(functools.partial(layer_kernel, heads, token_total), out_s...  363 us

profile of v5, /device:TPU:13, one launch (start us, length us, event | category | flops | bytes accessed | tf_op | source)
XLA Modules:
  0.0 391.4 jit_solution(10373722784906116020)
XLA Ops:
  0.6 0.5 exponential_multiply_fusion.slope_ref
  1.2 0.8 slice_bitcast_fusion.1
  2.0 0.1 pad.3.clone
  2.1 0.1 maximum_convert_fusion
  2.2 0.7 reshape.46.bias_ref
  2.8 0.7 convert_element_type.33
  3.5 1.1 broadcast_in_dim.10.valid_ref
  4.7 1.3 broadcast_in_dim.4.up_bias_ref
  6.0 0.7 stack.36
  6.6 0.7 stack.37
  7.3 0.7 stack.38
  7.9 0.7 stack.39
  8.6 0.7 stack.40
  9.2 0.7 stack.41
  9.9 0.6 convert_element_type.31.vector_ref
  10.5 363.4 %layer_stage.1 = (bf16[2048,256]{1,0:T(8,128)(2,1)}, bf16[2048,256]{1,0:T(8,128)(2,1)}, bf16[256,1024]{1,0:T(8,128)(2,1)}, bf16[256,1024]{1,0:T(8,128)(2,1)}, bf...) custom-call(f32[4]{0:T(128)} %exponential_multiply_fusion.slope_ref,, ...), custom_call_target="tpu_custom_call" | custom-call | tf_op jit(solution)/shard_map/layer_stage/pallas_call | solution.py:1401
  374.0 0.0 copy-start.2
  374.0 0.8 slice_reduce_fusion
  374.8 0.1 reshape_squeeze.3
  374.9 0.7 pad_maximum_fusion
  375.5 1.6 fusion
  377.1 1.3 slice_reduce_fusion.1
  378.4 1.2 slice.45
  380.9 0.8 slice.54
  381.6 0.6 constant_dynamic-slice_fusion.1
  382.2 2.7 convert_element_type.34
  384.9 0.0 copy-start.1
  384.9 0.0 copy-done.2
  384.9 0.1 convert_bitcast_fusion
  385.1 0.0 copy-start.3
  385.1 0.0 copy-start.4
  385.1 1.3 copy.39
  386.4 0.0 copy-start
  386.4 0.0 copy-done.1
  386.4 1.1 convert_element_type.36
  387.5 0.0 copy-done.3
  387.5 0.9 convert_element_type.35
  388.4 0.0 copy-done.4
  388.4 0.8 copy.38
  389.3 0.0 copy-done
  389.3 1.0 copy.42
  (5 shorter events, 0.1 us)
Async XLA Ops:
  374.0 11.0 %copy-start.2 = (bf16[256,1024]{1,0:T(8,128)(2,1)S(1)}, bf16[256,1024]{1,0:T(8,128)(2,1)}, u32[]{:S(2)}) copy-start(bf16[256,1024]{1,0:T(8,128)(2,1)} %get-tuple-element.30) | copy-start | bytes 1572868
  384.9 1.4 copy-start.1
  385.1 2.4 copy-start.3
  385.1 3.3 copy-start.4
  386.4 2.9 copy-start

commit v6 on v5

--- a/solution.py
+++ b/solution.py
@@ -32,7 +32,7 @@
 def swap(a):
     return jnp.concatenate([a[:,HALF:],a[:,:HALF]],axis=1)
 
-def attention_rows(heads, order, after, slope_ref, mixed_ref, out_ref, lse_ref, qs, ks, vs, bias, sc, mx, ls, acc):
+def attention_rows(heads, order, after, slopes, mixed_ref, out_ref, lse_ref, qs, ks, vs, bias, sc, mx, ls, acc):
     pairs=heads//2
     blocks=mixed_ref.shape[0]//BLOCK
     lo=low_lanes(BLOCK)
@@ -51,7 +51,7 @@
     jl=lax.broadcasted_iota(jnp.int32,(BLOCK,BLOCK),1)
     tent=jnp.minimum(jl,2*il-jl).astype(jnp.float32)
     for h in range(heads):
-        bias[h]=tent*slope_ref[h]
+        bias[h]=tent*slopes[h]
     jrow=lax.broadcasted_iota(jnp.int32,(1,BLOCK),1)
     @pl.loop(0,blocks)
     def _(it):
@@ -64,7 +64,7 @@
         def _(j):
             place=(jrow+(j-i)*BLOCK).astype(jnp.float32)
             for h in range(heads):
-                t=nt(qs[h,i],ks[h//2,j])*SCALE2+place*slope_ref[h]
+                t=nt(qs[h,i],ks[h//2,j])*SCALE2+place*slopes[h]
                 sc[h,j]=t
                 mx[h]=jnp.maximum(mx[h],jnp.maximum(t[:,:PAIR],t[:,PAIR:]))
         for h in range(heads):
@@ -92,7 +92,7 @@
                 lse_ref[h,pl.ds(i,1),:]=lse.T[:1]
         after(it,i)
 
-def attention_rows_backward(heads, after, slope_ref, mixed_ref, dout_ref, out_ref, lse_ref, grad_ref, qs, ks, km, vp, ds_, delta, bias, steep, dq, dk, dv):
+def attention_rows_backward(heads, after, slopes, mixed_ref, dout_ref, out_ref, lse_ref, grad_ref, qs, ks, km, vp, ds_, delta, bias, steep, dq, dk, dv):
     pairs=heads//2
     blocks=mixed_ref.shape[0]//BLOCK
     lo=low_lanes(BLOCK)
@@ -120,15 +120,15 @@
     tent=jnp.minimum(kl,2*ql-kl).astype(jnp.float32)
     ramp=kl.astype(jnp.float32)
     for h in range(heads):
-        bias[h]=tent*slope_ref[h]
-        steep[h]=ramp[:,:PAIR]*slope_ref[h]
+        bias[h]=tent*slopes[h]
+        steep[h]=ramp[:,:PAIR]*slopes[h]
     def block(i,j,first):
         for p in range(pairs):
             ps=[];gs=[]
             for n,h in enumerate((2*p,2*p+1)):
                 q=qs[p,i,n*BLOCK:(n+1)*BLOCK]
                 d=ds_[p,i,n*BLOCK:(n+1)*BLOCK]
-                row=slope_ref[h]*((j-i)*BLOCK).astype(jnp.float32)-lse_ref[h,pl.ds(i,1),:]
+                row=slopes[h]*((j-i)*BLOCK).astype(jnp.float32)-lse_ref[h,pl.ds(i,1),:]
                 t=nt(ks[p,j],q)*SCALE2+row+(bias[h] if first else jnp.concatenate([steep[h],steep[h]],1))
                 e=jnp.exp2(t)
                 g=e*(nt(vp[p,j],d)-delta[h,pl.ds(i,1),:])
@@ -234,21 +234,26 @@
 
 
 class Transpose:
-    def __init__(self, place, src, dst, relay, sems, first):
+    def __init__(self, place, src, dst, relay, sems, first, part=0, parts=1):
         self.p, self.src, self.dst, self.relay, self.sems, self.first = place, src, dst, relay, sems, first
-        self.rows, self.width = src.shape[0] // 4, src.shape[1]
+        self.quarter, self.width = src.shape[0] // 4, src.shape[1]
+        self.rows = self.quarter // parts
+        self.offset = part * self.rows
+
+    def tokens(self, quarter):
+        return self.src.at[pl.ds(pl.multiple_of(quarter * self.quarter + self.offset, self.rows), self.rows)]
 
     def part(self):
-        return self.dst.at[:, hint(self.p.row, self.width)]
+        return self.dst.at[pl.ds(self.offset, self.rows), hint(self.p.row, self.width)]
 
     def cross(self, n):
-        src = self.src.at[hint(2 * (1 - self.p.chip) + n, self.rows)]
+        src = self.tokens(2 * (1 - self.p.chip) + n)
         return remote(src, self.relay.at[n], self.sems, self.first + 4 + n, {"col": self.p.far})
 
     def out(self, relayed, n):
         p = self.p
         col = p.col if n == 0 else p.near
-        src = self.relay.at[col % 2] if relayed else self.src.at[hint(col, self.rows)]
+        src = self.relay.at[col % 2] if relayed else self.tokens(col)
         return pltpu.make_async_remote_copy(
             src_ref=src, dst_ref=self.part(),
             send_sem=self.sems[0].at[self.first + 2 * relayed + n], recv_sem=self.sems[1].at[self.first + p.row],
@@ -257,7 +262,7 @@
 
     def kept(self, relayed):
         p = self.p
-        src = self.relay.at[p.core] if relayed else self.src.at[hint(p.col, self.rows)]
+        src = self.relay.at[p.core] if relayed else self.tokens(p.col)
         return pltpu.make_async_copy(src, self.part(), self.sems[1].at[self.first + p.row])
 
     def leaves(self, relayed):
@@ -287,7 +292,7 @@
         p = self.p
         for other in range(4):
             mine = jnp.logical_and(p.home, p.row == other)
-            part = self.dst.at[:, pl.ds(other * self.width, self.width)]
+            part = self.dst.at[pl.ds(self.offset, self.rows), pl.ds(other * self.width, self.width)]
 
             @pl.when(jnp.logical_not(mine))
             def _():
@@ -313,6 +318,18 @@
 
 
 TRANSPOSE_SEMS = 6
+
+
+class Slopes:
+    def __init__(self, heads):
+        self.heads = heads
+        col = lax.axis_index("col")
+        self.column = jnp.float32(1.0)
+        for c in range(1, lax.axis_size("col")):
+            self.column = jnp.where(col == c, jnp.float32(2.0 ** (-8.0 * heads * c / HEADS)), self.column)
+
+    def __getitem__(self, head):
+        return self.column * (2.0 ** (-8.0 * (head + 1) / HEADS) * LOG2E)
 
 
 class Weight:
@@ -574,7 +591,7 @@
         p = self.p
         if self.kind == "xy":
             return [
-                remote(src.at[:, self.theirs], self.came.at[n], self.sems, self.first + n, {"dp": p.twin})
+                remote(src.at[:, self.theirs], self.came[n], self.sems, self.first + n, {"dp": p.twin})
                 for n, src in enumerate((self.own, self.far))
             ]
         if self.kind == "yx":
@@ -621,8 +638,8 @@
             copy.wait()
         if self.kind == "xy":
             self.gather_sum([
-                (self.totals[1], [self.came.at[1], self.far.at[:, self.mine]]),
-                (self.totals[0], [self.came.at[0], self.own.at[:, self.mine]]),
+                (self.totals[1], [self.came[1], self.far.at[:, self.mine]]),
+                (self.totals[0], [self.came[0], self.own.at[:, self.mine]]),
             ])
         elif self.kind == "yx":
             self.gather_sum([(self.totals[0], [self.came, self.own])])
@@ -733,30 +750,31 @@
 
 def layer_kernel(
     heads, token_total,
-    slope_ref, bias_ref, vector_ref, joined_ref, layer_ref, up_ref, down_ref, out_ref, up_bias_ref,
-    teacher_ref, cot_ref, valid_ref,
-    layer_out_ref, input_grad_ref, upg_ref, dng_ref, outg_ref, joinedg_ref, vector_sum_ref, scale_ref,
+    small_ref, joined_ref, layer_ref, up_ref, down_ref, out_ref, teacher_ref, cot_ref,
+    layer_out_ref, input_grad_ref, upg_ref, dng_ref, outg_ref, joinedg_ref, vector_sum_ref,
     upg_own, upg_far, dng_own, dng_far, came_up, came_down, came_out, came_joined, other_up, other_down, other_out,
     rows_up, rows_down, rows_out, rows_joined,
     xt_ref, nall_ref, mixed_ref, att_ref, lse_ref, jall_ref, vall_ref, early_ref, up_sums_ref,
     chip_ref, gt_ref, vt_ref, up2_ref, dn2_ref, ub2_ref, normed, gchip, bchip, give, take, middle, gres, low_ref, stage,
-    grad, gfar, dout, relay, vectors, late, count, sends, recvs,
+    grad, gfar, dout, relay, vectors, late, count, valid_ref, bias_ref, sync, sends, recvs,
 ):
     sems = (sends, recvs)
     f32, bf = jnp.float32, jnp.bfloat16
     p = Place()
     quarter, features = xt_ref.shape
     hidden = down_ref.shape[0]
-    moved = Transpose(p, layer_ref, xt_ref, relay.at[0], sems, 0)
-    target = Transpose(p, grad, gt_ref, relay.at[1], sems, TRANSPOSE_SEMS)
-    base = 2 * TRANSPOSE_SEMS
+    moved = [
+        Transpose(p, layer_ref, xt_ref, relay.at[0, :, pl.ds(256 * n, 256)], sems, n * TRANSPOSE_SEMS, n, 2) for n in (0, 1)
+    ]
+    target = Transpose(p, grad, gt_ref, relay.at[1], sems, 2 * TRANSPOSE_SEMS)
+    base = 3 * TRANSPOSE_SEMS
     back = Untranspose(p, low_ref, layer_out_ref, sems, base)
     base += 4
     w_out = Weight(p, out_ref, dn2_ref, hidden, False, "y", sems, base)
-    w_up = Weight(p, up_ref, up2_ref, 0, True, "y", sems, base + WEIGHT_SEMS)
+    w_up = Weight(p, up_ref, up2_ref, 0, True, "x", sems, base + WEIGHT_SEMS)
     w_downs = [
         Weight(
-            p, down_ref.at[pl.ds(n * (hidden // 2), hidden // 2)], dn2_ref, n * (hidden // 2), False, "x", sems,
+            p, down_ref.at[pl.ds(n * (hidden // 2), hidden // 2)], dn2_ref, n * (hidden // 2), False, "xy"[n], sems,
             base + (2 + n) * WEIGHT_SEMS,
         )
         for n in (0, 1)
@@ -769,45 +787,63 @@
     base += 6
 
     def small(step):
-        return remote(
-            vector_ref, vall_ref.at[:, hint(p.row, 256)], sems, small_base + step, {"row": (p.row + step) % 4}
-        )
+        part = vall_ref.at[:, hint(p.row, 256)]
+        return remote(part, part, sems, small_base + step, {"row": (p.row + step) % 4})
 
     def small_came(step):
         part = vall_ref.at[:, hint((p.row + 4 - step) % 4, 256)]
         return remote(part, part, sems, small_base + step, {"row": (p.row + step) % 4})
 
-    small_own = pltpu.make_async_copy(vector_ref, vall_ref.at[:, hint(p.row, 256)], recvs.at[small_base])
-    bias_own = pltpu.make_async_copy(up_bias_ref, ub2_ref.at[0], recvs.at[bias_base])
-    bias_far = remote(up_bias_ref, ub2_ref.at[1], sems, bias_base + 1, {"col": p.far})
+    bias_far = remote(ub2_ref.at[0], ub2_ref.at[1], sems, bias_base + 1, {"col": p.far})
     counted = Tally(p, count, ("col", "dp"), sems, base)
     base = counted.next_sem
-    tokens = valid_ref.shape[0]
-    number = jnp.zeros((8, 128), f32)
-    for n in range(tokens // 256):
-        number = number + jnp.sum(valid_ref[n * 256 : (n + 1) * 256, :].astype(f32), axis=0, keepdims=True)
-    count[0] = number
+    tokens = nall_ref.shape[0]
     greet(p)
+    for half in moved:
+        half.start_cross()
+    moved[0].send(0)
+    width = layer_ref.shape[1]
+    lanes = width // 128
+    for n in range(6):
+        for m in range(lanes):
+            place = pl.ds(pl.multiple_of(p.row * width + m * 128, 128), 128)
+            vall_ref[n : n + 1, place] = small_ref[lanes * n + m : lanes * n + m + 1, :]
+    vall_ref[6:8, hint(p.row, width)] = jnp.zeros((2, width), f32)
+    at = 6 * lanes
+    for n in range(hidden // 128):
+        ub2_ref[0, :, n * 128 : (n + 1) * 128] = jnp.broadcast_to(small_ref[at + n : at + n + 1, :], (8, 128))
+    at += hidden // 128
+    lo = low_lanes(1)
+    for n in range(heads // 2):
+        even, odd = (small_ref[at + 2 * n + m : at + 2 * n + m + 1, :] for m in (0, 1))
+        for m, part in enumerate(
+            (jnp.where(lo, even, 0.0), jnp.where(lo, swap(even), swap(odd)), jnp.where(lo, 0.0, odd))
+        ):
+            bias_ref[0:1, (3 * n + m) * 128 : (3 * n + m + 1) * 128] = part
+    at += heads
+    number = jnp.zeros((1, 128), f32)
+    for n in range(tokens // 128):
+        row = small_ref[at + n : at + n + 1, :]
+        number = number + row
+        valid_ref[n * 128 : (n + 1) * 128, :] = jnp.broadcast_to(row, (128, 128)).T.astype(bf)
+    count[0] = jnp.broadcast_to(jnp.sum(number, axis=1, keepdims=True), (8, 128))
     counted.send(0)
     for step in (1, 2, 3):
         small(step).start()
-    moved.start_cross()
-    moved.send(0)
     bias_far.start()
     w_out.across().start()
     w_up.across().start()
-    small_own.start()
-    bias_own.start()
     for w in weights:
         w.own().start()
+    moved[0].forward()
+    moved[1].send(0)
+    moved[1].forward()
     for n in range(len(counted.stages)):
         counted.add(n)
         if n + 1 < len(counted.stages):
             counted.send(n + 1)
-    moved.forward()
-
-    scale_ref[...] = token_total / count[counted.last]
-    scale = scale_ref[:1, :1]
+
+    scale = token_total / count[counted.last, :1, :1]
 
     @pl.loop(0, 32)
     def _(n):
@@ -835,10 +871,6 @@
     for step in (1, 2, 3):
         small_came(step).wait_recv()
         small(step).wait_send()
-    small_own.wait()
-    moved.wait_recv()
-    w_joined.start()
-
     first = p.col * quarter
 
     def norm_one(n):
@@ -847,20 +879,30 @@
         place = pl.ds(pl.multiple_of(first + n * 128, 128), 128)
         nall_ref[place, :] = (standard * vall_ref[0:1, :] + vall_ref[1:2, :]).astype(bf)
 
-    pl.loop(0, quarter // 128)(norm_one)
-    mine = nall_ref.at[hint(p.col, quarter)]
-    to_far = remote(mine, mine, sems, base, {"col": p.far})
-    to_near = remote(mine, mine, sems, base + 1, {"col": p.near})
-    theirs = nall_ref.at[hint(p.far, quarter)]
-    far_came = remote(theirs, theirs, sems, base, {"col": p.far})
-    pass_on = remote(theirs, theirs, sems, base + 2, {"col": p.near})
-    beside = nall_ref.at[hint(p.near, quarter)]
-    near_came = remote(beside, beside, sems, base + 1, {"col": p.near})
-    across = nall_ref.at[hint(p.corner, quarter)]
-    corner_came = remote(across, across, sems, base + 2, {"col": p.near})
-    base += 3
-    to_far.start()
-    to_near.start()
+    def half_of(col, n):
+        return nall_ref.at[pl.ds(pl.multiple_of(col * quarter + n * 256, 256), 256)]
+
+    def spread_copy(col, n, number, to):
+        return remote(half_of(col, n), half_of(col, n), sems, gather_base + 2 * number + n, {"col": to})
+
+    gather_base = base
+    base += 6
+    to_far = [spread_copy(p.col, n, 0, p.far) for n in (0, 1)]
+    to_near = [spread_copy(p.col, n, 1, p.near) for n in (0, 1)]
+    far_came = [spread_copy(p.far, n, 0, p.far) for n in (0, 1)]
+    near_came = [spread_copy(p.near, n, 1, p.near) for n in (0, 1)]
+    pass_on = [spread_copy(p.far, n, 2, p.near) for n in (0, 1)]
+    corner_came = [spread_copy(p.corner, n, 2, p.near) for n in (0, 1)]
+    for n in (0, 1):
+        moved[n].wait_recv()
+        pl.loop(2 * n, 2 * n + 2)(norm_one)
+        to_far[n].start()
+        to_near[n].start()
+    for step in (1, 2, 3):
+        pl.semaphore_signal(sync, inc=1, device_id={"row": (p.row + step) % 4}, device_id_type=MESH)
+    pl.semaphore_wait(sync, 3)
+    w_joined.start()
+    target.start_cross()
     for w in w_downs:
         w.across().start()
 
@@ -872,24 +914,25 @@
     def _():
         valid_kept.start()
 
-    def project(index):
-        @pl.loop(0, quarter // 256)
-        def _(n):
-            rows = pl.ds(pl.multiple_of(index * quarter + n * 256, 256), 256)
-            mixed_ref[rows, :] = (nn(nall_ref[rows, :], jall_ref[...]) + bias_ref[...]).astype(bf)
-
+    def project(index, n):
+        rows = pl.ds(pl.multiple_of(index * quarter + n * 256, 256), 256)
+        mixed_ref[rows, :] = (nn(nall_ref[rows, :], jall_ref[...]) + bias_ref[0:1, :]).astype(bf)
+
+    far_came[0].wait_recv()
+    pass_on[0].start()
     w_joined.spread()
     for w in weights:
         w.start_along()
+    far_came[1].wait_recv()
+    pass_on[1].start()
     w_joined.ready()
-    project(p.col)
-    near_came.wait_recv()
-    project(p.near)
-    far_came.wait_recv()
-    pass_on.start()
-    project(p.far)
-    corner_came.wait_recv()
-    project(p.corner)
+    for came in near_came + corner_came:
+        came.wait_recv()
+
+    @pl.loop(0, tokens // 256)
+    def _(n):
+        project(n // 2, n % 2)
+
     w_out.spread()
 
     own_heads = att_ref.shape[1]
@@ -945,13 +988,14 @@
         (11, lambda: w_up.spread((2,))),
         (18, lambda: w_up.spread((3,))),
         (27, lambda: w_up.spread_last((1, 2))),
+        (29, lambda: (target.send(0), target.forward())),
         (32, lambda: w_downs[0].spread((1, 2))),
     ]
 
     def attend(*scratch):
         attention_rows(
             heads, lambda it: (it + per_chip * (1 - p.chip)) % blocks, after,
-            slope_ref, mixed_ref, att_ref, lse_ref, *scratch,
+            Slopes(heads), mixed_ref, att_ref, lse_ref, *scratch,
         )
 
     pairs = heads // 2
@@ -965,11 +1009,10 @@
 
     @pl.loop(0, per_chip)
     def _(n):
-        share(n, n + per_chip * (1 - p.chip)).wait()
+        share(n, n + per_chip * (1 - p.chip)).wait_recv()
 
     w_up.spread_last((3,))
     w_downs[0].spread((3,))
-    target.start_cross()
     w_out.ready(0)
     w_out.ready(1)
     core = Chip(p, sems, base)
@@ -1010,7 +1053,6 @@
         False,
     )
     w_downs[1].spread()
-    target.send(0)
     for n in range(halves):
         take_rows(0, n).wait_recv()
 
@@ -1026,19 +1068,25 @@
 
         swap_rows(2, normed, n).start()
     w_up.ready(0)
-    bias_own.wait()
     bias_far.wait()
 
     slots = [give.at[pl.ds(256 * (n // 2), 256), pl.ds(hidden // 2 * (n % 2), hidden // 2)] for n in range(4)]
     outg_own, outg_far = (dn2_ref.at[0, :features, pl.ds(own_heads * n, own_heads)] for n in (0, 1))
     jgrad = dn2_ref.at[1, :features, : mixed_ref.shape[1]]
     s_down = Share(
-        p, "xy", dng_own, dng_far, dng_ref, came_down, other_down, rows_down,
+        p, "xy", dng_own, dng_far, dng_ref, [came_down.at[n] for n in (0, 1)], other_down, rows_down,
         [up2_ref.at[1, :, pl.ds(hidden // 2 * n, hidden // 2)] for n in (0, 1)], slots, sems, base,
     )
+    low_part, high_part = pl.ds(0, hidden // 2), pl.ds(hidden // 2, hidden // 2)
+    quarters = [up2_ref.at[0, :, pl.ds(hidden // 4 * n, hidden // 4)] for n in range(3)]
     s_up = Share(
-        p, "xy", upg_own, upg_far, upg_ref, came_up, other_up, rows_up,
-        [up2_ref.at[0, :, pl.ds(hidden // 2 * n, hidden // 2)] for n in (0, 1)], slots, sems, base + SHARE_SEMS,
+        p, "yx", upg_own.at[:, low_part], upg_far.at[:, low_part], upg_ref.at[:, low_part], came_up.at[0], other_up.at[0],
+        rows_up.at[0], [chip_ref, quarters[0]], slots, sems, base + SHARE_SEMS,
+    )
+    s_up_high = Share(
+        p, "xy", upg_own.at[:, high_part], upg_far.at[:, high_part], upg_ref.at[:, high_part],
+        [came_up.at[1, :, pl.ds(hidden // 4 * n, hidden // 4)] for n in (0, 1)], other_up.at[1], rows_up.at[1],
+        [quarters[1], quarters[2]], slots, sems, base + 4 * SHARE_SEMS,
     )
     s_out = Share(
         p, "yx", outg_own, outg_far, outg_ref, came_out, other_out, rows_out,
@@ -1049,7 +1097,7 @@
         p, "x", jgrad, None, joinedg_ref, came_joined, None, rows_joined,
         [dn2_ref.at[0, :features, pl.ds(512, 384)]], slots, sems, base + 3 * SHARE_SEMS,
     )
-    base += 4 * SHARE_SEMS
+    base += 5 * SHARE_SEMS
 
     def natural(chip, n):
         return hint(2 * chip + (p.core + n) % 2, quarter)
@@ -1089,11 +1137,11 @@
         pl.loop(0, halves)(up_rows(0))
         for n in range(halves):
             swap_came(2, normed, n).wait_recv()
-        w_downs[0].spread_last()
-        target.forward()
         pl.loop(halves, 2 * halves)(up_rows(0))
         w_up.ready(1)
-        pl.loop(0, 2 * halves)(up_rows(1))
+        pl.loop(0, halves)(up_rows(1))
+        w_downs[0].spread_last()
+        pl.loop(halves, 2 * halves)(up_rows(1))
         w_downs[1].spread_last()
         for w in w_downs:
             w.ready(0)
@@ -1209,6 +1257,7 @@
                 share_grad(n // halves).start()
         weight_grad(stage_base, normed, der, (upg_own, upg_far))
         s_up.start()
+        s_up_high.start()
 
     pl.run_scoped(
         middle_part,
@@ -1249,6 +1298,7 @@
     base = summed.next_sem
     lately = Tally(p, late, ("row", "dp", "col"), sems, base)
     base = lately.next_sem
+    summed.send(0)
     for n in (0, 1):
         share_grad_came(n).wait_recv()
         share_grad(n).wait_send()
@@ -1256,20 +1306,23 @@
 
 
     def turn(i):
-        for at, stage_number in ((0, 0), (2, 1), (3, 2)):
-            @pl.when(i == at)
-            def _():
-                if stage_number > 0:
-                    summed.add(stage_number - 1)
-                summed.send(stage_number)
+        @pl.when(i == 1)
+        def _():
+            summed.add(0)
+            summed.send(1)
 
         @pl.when(i == 4)
         def _():
             s_down.first_sum()
             s_down.second_copy().start()
 
+        @pl.when(i == 6)
+        def _():
+            s_up.first_sum()
+            s_up.second_copy().start()
+
     def attend_back(*scratch):
-        attention_rows_backward(heads, turn, slope_ref, mixed_ref, dout, att_ref, lse_ref, mixed_ref, *scratch)
+        attention_rows_backward(heads, turn, Slopes(heads), mixed_ref, dout, att_ref, lse_ref, mixed_ref, *scratch)
 
     pl.run_scoped(
         attend_back,
@@ -1280,6 +1333,13 @@
         pltpu.VMEM((pairs, blocks, BLOCK, PAIR), f32), pltpu.VMEM((pairs, blocks, BLOCK, PAIR), f32),
         pltpu.VMEM((pairs, blocks, BLOCK, PAIR), f32),
     )
+
+    @pl.loop(0, features // 128)
+    def _(f):
+        cols = hint(f, 128)
+        jgrad[cols, :] = tn(nall_ref[:, cols], mixed_ref[...]).astype(bf)
+
+    s_joined.start()
 
     sums_at = [bchip.at[pl.ds(0, quarter)], bchip.at[pl.ds(quarter, quarter)],
                normed.at[pl.ds(0, quarter)], normed.at[pl.ds(quarter, quarter)]]
@@ -1306,12 +1366,8 @@
     s_down.second_sum()
     s_down.start_rows()
 
-    @pl.loop(0, features // 128)
-    def _(f):
-        cols = hint(f, 128)
-        jgrad[cols, :] = tn(nall_ref[:, cols], mixed_ref[...]).astype(bf)
-
-    s_joined.start()
+    s_up.second_sum()
+    s_up.start_rows()
     s_out.first_sum()
     s_out.second_copy().start()
     sums = jnp.zeros((1, mixed_ref.shape[1]), f32)
@@ -1319,9 +1375,12 @@
         sums = sums + jnp.sum(mixed_ref[n * 256 : (n + 1) * 256, :].astype(f32), axis=0, keepdims=True)
     late[0] = jnp.zeros((8, features), f32)
     late[0, 2:3, 0 : sums.shape[1]] = sums
+    s_up_high.first_sum()
+    s_up_high.second_copy().start()
     s_down.row_half()
-    s_up.first_sum()
-    s_up.second_copy().start()
+    s_up.row_half()
+    s_joined.first_sum()
+    s_joined.start_rows()
     grad_near[1].wait()
     grad_far.wait()
     gin = bchip.at[pl.ds(0, quarter)]
@@ -1342,45 +1401,66 @@
 
     lately.send(0)
     grad_back.start()
-    s_joined.first_sum()
-    s_joined.start_rows()
     s_out.second_sum()
     s_out.start_rows()
     s_down.row_sum()
-    for n in range(2, len(summed.stages)):
+    s_up.row_sum()
+    s_joined.row_half()
+    s_up_high.second_sum()
+    s_up_high.start_rows()
+    for n in range(1, len(summed.stages)):
         summed.add(n)
         if n + 1 < len(summed.stages):
             summed.send(n + 1)
     lately.add(0)
     lately.send(1)
-    s_up.second_sum()
-    s_up.start_rows()
-    s_joined.row_half()
-    s_out.row_half()
+    s_joined.row_sum()
     for n in range(1, len(lately.stages)):
         lately.add(n)
         if n + 1 < len(lately.stages):
             lately.send(n + 1)
-    s_up.row_half()
-    vector_sum_ref[...] = vectors[summed.last]
-    vector_sum_ref[0:2, :] = late[lately.last, 0:2, :]
+    s_out.row_half()
+    s_up_high.row_half()
     joined_at = lately.after(len(lately.stages) - 2)
-    vector_sum_ref[7:8, :] = late[joined_at, 2:3, :]
-    for share in (s_joined, s_out, s_up):
-        share.row_sum()
-    for share in (s_down, s_joined, s_out, s_up):
-        share.finish()
+    at = 0
+    for n in range(6):
+        place = hint(p.row, width)
+        value = late[lately.last, n : n + 1, place] if n < 2 else vectors[summed.last, n : n + 1, place]
+        for m in range(lanes):
+            vector_sum_ref[at : at + 1, :] = value[:, m * 128 : (m + 1) * 128]
+            at += 1
+    value = vectors[summed.last, pl.ds(8 + p.col, 1), :]
+    for m in range(hidden // 128):
+        vector_sum_ref[at : at + 1, :] = value[:, m * 128 : (m + 1) * 128]
+        at += 1
+    for n in range(heads // 2):
+        first, second, third = (
+            late[joined_at, 2:3, (3 * n + m) * 128 : (3 * n + m + 1) * 128] for m in range(3)
+        )
+        vector_sum_ref[at : at + 1, :] = jnp.where(lo, first, swap(second))
+        vector_sum_ref[at + 1 : at + 2, :] = jnp.where(lo, swap(second), third)
+        at += 2
+    value = jnp.sum(vectors[summed.last, 6:7, 0:128], axis=1, keepdims=True) * (scale * (1.0 / (features * token_total)))
+    vector_sum_ref[at:, :] = jnp.broadcast_to(value, (vector_sum_ref.shape[0] - at, 128))
+    s_out.row_sum()
+    s_up_high.row_sum()
+    for part in (s_down, s_up, s_joined, s_out, s_up_high):
+        part.finish()
     grad_back.wait_recv()
     grad_back.wait_send()
-    moved.wait_send()
-    to_far.wait_send()
-    to_near.wait_send()
-    pass_on.wait_send()
+    for n in (0, 1):
+        moved[n].wait_send()
+        for copies in (to_far, to_near, pass_on):
+            copies[n].wait_send()
     w_joined.sent()
     back.wait_send()
 
-
-def layer_stage(slopes, bias_rows, vectors, joined, layer_in, up, down, out, up_bias, teacher, cot, valid, token_total):
+    @pl.loop(0, per_chip)
+    def _(n):
+        share(n, n + per_chip * (1 - p.chip)).wait_send()
+
+
+def layer_stage(small, joined, layer_in, up, down, out, teacher, cot, token_total):
     tokens, width = layer_in.shape
     quarter = tokens // 4
     features = width * lax.axis_size("row")
@@ -1395,22 +1475,23 @@
     while (1 << bits) < lax.axis_size("dp"):
         bits += 1
     count = (
-        2 * TRANSPOSE_SEMS + 4 + 4 * WEIGHT_SEMS + HALVES_SEMS + 6 + (3 + bits) + 1 + 3 + blocks // 2 + 12
-        + 4 * SHARE_SEMS + 2 + 2 + 2 * (6 + bits) + 3 + 4
+        3 * TRANSPOSE_SEMS + 4 + 4 * WEIGHT_SEMS + HALVES_SEMS + 6 + (3 + bits) + 1 + 6 + blocks // 2 + 12
+        + 5 * SHARE_SEMS + 2 + 2 + 2 * (6 + bits) + 3 + 4
     )
+    small_rows = 8 * ((6 * width // 128 + hidden // 128 + heads) // 8 + 1)
     outs = pl.pallas_call(
         functools.partial(layer_kernel, heads, token_total),
         out_shape=(
             shape((tokens, width), bf), shape((tokens, width), bf), shape((width, hidden), bf), shape((width, hidden), bf),
-            shape((width, head_rows), bf), shape((width, joined_width), bf), shape((16, features), f32), shape((8, 128), f32),
+            shape((width, head_rows), bf), shape((width, joined_width), bf), shape((small_rows, 128), f32),
         ) + (shape((features, hidden), bf),) * 4 + (
             shape((2, features, hidden // 2), bf), shape((2, features, hidden // 2), bf), shape((features, head_rows), bf),
-            shape((features, joined_width // 2), bf), shape((features, hidden // 2), bf), shape((features, hidden // 2), bf),
-            shape((features, head_rows // 2), bf), shape((3, width, hidden // 2), bf), shape((3, width, hidden // 2), bf),
+            shape((features, joined_width // 2), bf), shape((2, features, hidden // 4), bf), shape((features, hidden // 2), bf),
+            shape((features, head_rows // 2), bf), shape((2, 3, width, hidden // 4), bf), shape((3, width, hidden // 2), bf),
             shape((3, width, head_rows // 2), bf), shape((3, width, joined_width // 2), bf),
         ),
-        in_specs=[pl.BlockSpec(memory_space=pltpu.SMEM), vmem, vmem] + [anyspace] * 6 + [vmem] * 3,
-        out_specs=(anyspace,) * 2 + (vmem,) * 6 + (anyspace,) * 15,
+        in_specs=[vmem] + [anyspace] * 5 + [vmem] * 2,
+        out_specs=(anyspace,) * 2 + (vmem,) * 5 + (anyspace,) * 15,
         scratch_shapes=[
             pltpu.VMEM((quarter, features), bf), pltpu.VMEM((tokens, features), bf), pltpu.VMEM((tokens, joined_width), bf),
             pltpu.VMEM((tokens, heads * HEAD_DIM), bf), pltpu.VMEM((heads, blocks, BLOCK), f32),
@@ -1426,12 +1507,13 @@
             pltpu.VMEM((tally_slots(bits, ("row", "col", "dp")), 16, features), f32),
             pltpu.VMEM((tally_slots(bits, ("row", "col", "dp")), 8, features), f32),
             pltpu.VMEM((tally_slots(bits, ("col", "dp")), 8, 128), f32),
-            pltpu.SemaphoreType.DMA((count,)), pltpu.SemaphoreType.DMA((count,)),
+            pltpu.VMEM((tokens, 128), bf), pltpu.VMEM((8, joined_width), f32),
+            pltpu.SemaphoreType.REGULAR, pltpu.SemaphoreType.DMA((count,)), pltpu.SemaphoreType.DMA((count,)),
         ],
         compiler_params=pltpu.CompilerParams(vmem_limit_bytes=63 << 20, collective_id=1, has_side_effects=True),
         name="layer_stage",
-    )(slopes, bias_rows, vectors, joined, layer_in, up, down, out, up_bias, teacher, cot, valid)
-    return outs[:8]
+    )(small, joined, layer_in, up, down, out, teacher, cot)
+    return outs[:7]
 
 
 def swap_with(value, axis, bit):
@@ -1441,10 +1523,6 @@
 
 def low(value):
     return value.astype(jnp.bfloat16)
-
-
-def pick(stacked, index):
-    return lax.dynamic_index_in_dim(stacked, index, 0, keepdims=False)
 
 
 def sum_other_pairs(value):
@@ -1473,52 +1551,39 @@
     valid,
     cotangent,
 ):
-    row_size, col_size = lax.axis_size("row"), lax.axis_size("col")
-    row, col = lax.axis_index("row"), lax.axis_index("col")
     f32 = jnp.float32
-    head_count = joined_bias.shape[0]
-    quarter = layer_in.shape[0] // col_size
-    head_index = col * head_count + jnp.arange(head_count, dtype=jnp.int32)
-    slopes = jnp.exp2(-8.0 * (head_index.astype(f32) + 1.0) / HEADS) * LOG2E
-
-    zero_rows = jnp.zeros_like(joined_bias[:, :HEAD_DIM])
-    bias_rows = jnp.stack(
-        [joined_bias[:, :HEAD_DIM], zero_rows, joined_bias[:, HEAD_DIM:]], axis=1
-    ).reshape(1, -1).astype(f32)
-    nothing = jnp.zeros_like(first_gain)
-    vectors = jnp.stack(
-        [first_gain, first_shift, out_bias, second_gain, second_shift, down_bias, nothing, nothing]
-    ).astype(f32)
-    token_total = layer_in.shape[0] * lax.axis_size("dp") * col_size
-    layer_out, input_grad, up_grad, down_grad, out_grad, joined_grad, sums, scale = layer_stage(
-        slopes, bias_rows, vectors, joined_weight, layer_in, up_weight, down_weight, out_weight,
-        jnp.broadcast_to(up_bias.astype(f32), (8, up_bias.shape[0])), teacher, cotangent,
-        jnp.broadcast_to(low(valid)[:, None], (valid.shape[0], 128)), token_total,
+    token_total = layer_in.shape[0] * lax.axis_size("dp") * lax.axis_size("col")
+    arrays = (
+        first_gain, first_shift, out_bias, second_gain, second_shift, down_bias, up_bias, joined_bias.reshape(-1), valid,
+    )
+    small = jnp.concatenate([a.astype(f32) for a in arrays]).reshape(-1, 128)
+    layer_out, input_grad, up_grad, down_grad, out_grad, joined_grad, sums = layer_stage(
+        small, joined_weight, layer_in, up_weight, down_weight, out_weight, teacher, cotangent, token_total
     )
     up_grad, down_grad, out_grad, joined_grad = (
         sum_other_pairs(g.astype(f32)) for g in (up_grad, down_grad, out_grad, joined_grad)
     )
-    mine = lax.dynamic_slice_in_dim(sums, row * (D // row_size), D // row_size, 1)
-    loss = jnp.sum(sums[6, :128]) * scale[0, 0] / (D * token_total)
-    up_bias_grad = pick(sums[8:12], col)
-    column_sums = sums[7, : joined_weight.shape[1]].reshape(head_count, 3, HEAD_DIM)
-    joined_bias_grad = jnp.concatenate([column_sums[:, 0], column_sums[:, 2]], axis=1)
+    sums = sums.reshape(-1)
+    pieces, at = [], 0
+    for size in [layer_in.shape[1]] * 6 + [up_bias.shape[0], joined_bias.size, 1]:
+        pieces.append(sums[at : at + size])
+        at += size
     return (
         layer_out,
-        loss,
+        pieces[8][0],
         input_grad.astype(f32),
-        mine[0],
-        mine[1],
+        pieces[0],
+        pieces[1],
         joined_grad,
-        joined_bias_grad,
+        pieces[7].reshape(joined_bias.shape),
         out_grad.T,
-        mine[2],
-        mine[3],
-        mine[4],
+        pieces[2],
+        pieces[3],
+        pieces[4],
         up_grad,
-        up_bias_grad,
+        pieces[6],
         down_grad.T,
-        mine[5],
+        pieces[5],
     )
 
 

time: 398 us -> 371 us (0.932)
  Pallas kernels: 363 us -> 345 us
  local copies, waits for them, and re-layouts: 16.1 us -> 8.97 us
    pallas_call x1, Pallas kernels: 363 us -> 345 us  [layer_stage(): pl.pallas_call(functools.partial(layer_kernel, heads, token_total), out_s...]
    unnamed x0 -> x9, other arithmetic: none -> 5.35 us
    another operation x11 -> x0, local copies, waits for them, and re-layouts: 4.96 us -> none  [the longest x8 3.98 us: on_device(): jnp.stack([first_gain, first_shift, out_bias, second_gain, second_shift,...]
where the time goes in v6:
time: 371 us; the launch traced here: 366 us
  Pallas kernels  345 us (93%)
  other arithmetic  11.6 us (3%)
  local copies, waits for them, and re-layouts  8.97 us (2%)
    pallas_call x1, Pallas kernels, layer_stage(): pl.pallas_call(functools.partial(layer_kernel, heads, token_total), out_s...  345 us

profile of v6, /device:TPU:13, one launch (start us, length us, event | category | flops | bytes accessed | tf_op | source)
XLA Modules:
  0.0 366.2 jit_solution(8397824535261034715)
XLA Ops:
  0.7 0.7 constant_dynamic-update-slice_fusion.7
  1.3 0.7 constant_dynamic-update-slice_fusion.6
  2.0 0.7 constant_dynamic-update-slice_fusion.5
  2.6 0.7 constant_dynamic-update-slice_fusion.4
  3.3 0.7 constant_dynamic-update-slice_fusion.3
  4.0 0.7 constant_dynamic-update-slice_fusion.2
  4.6 0.7 constant_dynamic-update-slice_fusion.1
  5.3 0.7 constant_dynamic-update-slice_fusion
  6.0 0.7 convert_dynamic-update-slice_fusion
  6.7 0.0 copy-start.4
  6.7 0.6 copy-done.4
  7.3 345.0 %layer_stage.1 = (bf16[2048,256]{1,0:T(8,128)(2,1)}, bf16[2048,256]{1,0:T(8,128)(2,1)}, bf16[256,1024]{1,0:T(8,128)(2,1)}, bf16[256,1024]{1,0:T(8,128)(2,1)}, bf...) custom-call(f32[40,128]{1,0:T(8,128)} %bitcast.24, ...), custom_call_target="tpu_custom_call" | custom-call | tf_op jit(solution)/shard_map/layer_stage/pallas_call | solution.py:1482
  352.3 0.0 copy-start.3
  352.3 0.0 copy-start.2
  352.3 1.3 slice.65
  353.6 1.3 slice.54
  354.8 1.3 slice_bitcast_fusion
  356.1 1.4 slice_bitcast_fusion.1
  357.5 0.9 convert_bitcast_fusion.1
  358.5 0.8 copy.31
  359.3 1.9 convert_element_type.52
  361.2 0.0 copy-done.3
  361.2 1.1 convert_element_type.53
  362.3 0.0 copy-done.2
  362.3 0.0 copy-start
  362.3 0.1 convert_bitcast_fusion
  362.4 0.0 copy-start.1
  362.4 1.3 copy.32
  363.7 0.0 copy-done
  363.7 1.5 convert_element_type.51
  365.2 0.0 copy-done.1
  365.2 1.0 copy.43
  (1 shorter events, 0.0 us)
Async XLA Ops:
  6.7 0.6 copy-start.4
  352.3 8.9 %copy-start.3 = (bf16[256,1024]{1,0:T(8,128)(2,1)S(1)}, bf16[256,1024]{1,0:T(8,128)(2,1)}, u32[]{:S(2)}) copy-start(bf16[256,1024]{1,0:T(8,128)(2,1)} %get-tuple-element.27) | copy-start | bytes 1572868
  352.3 10.0 %copy-start.2 = (bf16[256,1024]{1,0:T(8,128)(2,1)S(1)}, bf16[256,1024]{1,0:T(8,128)(2,1)}, u32[]{:S(2)}) copy-start(bf16[256,1024]{1,0:T(8,128)(2,1)} %get-tuple-element.28) | copy-start | bytes 1572868
  362.3 1.4 copy-start
  362.4 2.8 copy-start.1

commit v7 on v6

--- a/solution.py
+++ b/solution.py
@@ -608,6 +608,9 @@
             for n in range(4):
                 part = pl.ds(n * self.block, self.block)
                 blocks.append((total.at[part], [src.at[part] for src in sources]))
+        self.block_sums(blocks)
+
+    def block_sums(self, blocks):
         copies = []
         for n, (_, sources) in enumerate(blocks):
             copies.append([
@@ -699,6 +702,80 @@
 
 
 SHARE_SEMS = 12
+
+
+class RowsFirst(Share):
+    def __init__(self, place, own, far, result, from_next, from_other, from_far, from_twin, total, slots, sems, first):
+        super().__init__(place, "zyx", own, far, result, None, None, None, None, slots, sems, first)
+        self.from_next, self.from_other, self.from_far, self.from_twin = from_next, from_other, from_far, from_twin
+        self.parts = [[total.at[pl.ds((2 * side + n) * self.block, self.block)] for n in (0, 1)] for side in (0, 1)]
+
+    def next_copies(self):
+        target = partner(self.p.row, 1)
+        rows = (target, partner(target, 2))
+        return [
+            remote(
+                source.at[hint(rows[n], self.block)], self.from_next.at[2 * side + n], self.sems,
+                self.first + 2 * side + n, {"row": target},
+            )
+            for side, source in enumerate((self.own, self.far))
+            for n in (0, 1)
+        ]
+
+    def start(self):
+        for copy in self.next_copies():
+            copy.start()
+
+    def other_copies(self):
+        return [
+            remote(
+                self.parts[side][1], self.from_other.at[side], self.sems, self.first + 4 + side,
+                {"row": partner(self.p.row, 2)},
+            )
+            for side in (0, 1)
+        ]
+
+    def row_half(self):
+        for copy in self.next_copies():
+            copy.wait()
+        rows = (self.p.row, partner(self.p.row, 2))
+        for n in (1, 0):
+            self.block_sums([
+                (self.parts[side][n], [source.at[hint(rows[n], self.block)], self.from_next.at[2 * side + n]])
+                for side, source in enumerate((self.own, self.far))
+            ])
+            if n == 1:
+                for copy in self.other_copies():
+                    copy.start()
+
+    def far_copy(self):
+        return remote(self.parts[1][0], self.from_far, self.sems, self.first + 6, {"col": self.p.far})
+
+    def row_sum(self):
+        for copy in self.other_copies():
+            copy.wait()
+        self.block_sums([(self.parts[side][0], [self.parts[side][0], self.from_other.at[side]]) for side in (1, 0)])
+        self.far_copy().start()
+
+    def twin_copy(self):
+        return remote(self.parts[0][0].at[:, self.theirs], self.from_twin, self.sems, self.first + 7, {"dp": self.p.twin})
+
+    def far_sum(self):
+        self.far_copy().wait()
+        self.block_sums([(self.parts[0][0], [self.parts[0][0], self.from_far])])
+        self.twin_copy().start()
+
+    def last_copy(self, half):
+        part = self.result.at[:, hint(half, self.part)]
+        return remote(part, part, self.sems, self.first + 12, {"dp": self.p.twin})
+
+    def twin_sum(self):
+        self.twin_copy().wait()
+        self.block_sums([(self.result.at[:, self.mine], [self.parts[0][0].at[:, self.mine], self.from_twin])])
+        self.last_copy(self.p.half).start()
+
+
+ROWS_FIRST_SEMS = 13
 
 
 class Tally:
@@ -753,7 +830,7 @@
     small_ref, joined_ref, layer_ref, up_ref, down_ref, out_ref, teacher_ref, cot_ref,
     layer_out_ref, input_grad_ref, upg_ref, dng_ref, outg_ref, joinedg_ref, vector_sum_ref,
     upg_own, upg_far, dng_own, dng_far, came_up, came_down, came_out, came_joined, other_up, other_down, other_out,
-    rows_up, rows_down, rows_out, rows_joined,
+    rows_up, rows_down, rows_out, rows_joined, from_next, from_other, from_far, from_twin,
     xt_ref, nall_ref, mixed_ref, att_ref, lse_ref, jall_ref, vall_ref, early_ref, up_sums_ref,
     chip_ref, gt_ref, vt_ref, up2_ref, dn2_ref, ub2_ref, normed, gchip, bchip, give, take, middle, gres, low_ref, stage,
     grad, gfar, dout, relay, vectors, late, count, valid_ref, bias_ref, sync, sends, recvs,
@@ -1073,20 +1150,26 @@
     slots = [give.at[pl.ds(256 * (n // 2), 256), pl.ds(hidden // 2 * (n % 2), hidden // 2)] for n in range(4)]
     outg_own, outg_far = (dn2_ref.at[0, :features, pl.ds(own_heads * n, own_heads)] for n in (0, 1))
     jgrad = dn2_ref.at[1, :features, : mixed_ref.shape[1]]
+    low_part, high_part = pl.ds(0, hidden // 2), pl.ds(hidden // 2, hidden // 2)
+
+    def both(ref, n):
+        return [ref.at[n, :, pl.ds(hidden // 4 * m, hidden // 4)] for m in (0, 1)]
+
     s_down = Share(
-        p, "xy", dng_own, dng_far, dng_ref, [came_down.at[n] for n in (0, 1)], other_down, rows_down,
-        [up2_ref.at[1, :, pl.ds(hidden // 2 * n, hidden // 2)] for n in (0, 1)], slots, sems, base,
+        p, "xy", dng_own.at[:, low_part], dng_far.at[:, low_part], dng_ref.at[:, low_part], both(came_down, 0), other_down,
+        rows_down, both(up2_ref, 1), slots, sems, base,
     )
-    low_part, high_part = pl.ds(0, hidden // 2), pl.ds(hidden // 2, hidden // 2)
-    quarters = [up2_ref.at[0, :, pl.ds(hidden // 4 * n, hidden // 4)] for n in range(3)]
     s_up = Share(
-        p, "yx", upg_own.at[:, low_part], upg_far.at[:, low_part], upg_ref.at[:, low_part], came_up.at[0], other_up.at[0],
-        rows_up.at[0], [chip_ref, quarters[0]], slots, sems, base + SHARE_SEMS,
+        p, "xy", upg_own.at[:, low_part], upg_far.at[:, low_part], upg_ref.at[:, low_part], both(came_up, 0), other_up,
+        rows_up, both(up2_ref, 0), slots, sems, base + SHARE_SEMS,
     )
-    s_up_high = Share(
-        p, "xy", upg_own.at[:, high_part], upg_far.at[:, high_part], upg_ref.at[:, high_part],
-        [came_up.at[1, :, pl.ds(hidden // 4 * n, hidden // 4)] for n in (0, 1)], other_up.at[1], rows_up.at[1],
-        [quarters[1], quarters[2]], slots, sems, base + 4 * SHARE_SEMS,
+    z_down = RowsFirst(
+        p, dng_own.at[:, high_part], dng_far.at[:, high_part], dng_ref.at[:, high_part], from_next.at[0], from_other.at[0],
+        from_far.at[0], from_twin.at[0], up2_ref.at[1, :, high_part], slots, sems, base + 4 * SHARE_SEMS,
+    )
+    z_up = RowsFirst(
+        p, upg_own.at[:, high_part], upg_far.at[:, high_part], upg_ref.at[:, high_part], from_next.at[1], from_other.at[1],
+        from_far.at[1], from_twin.at[1], chip_ref, slots, sems, base + 4 * SHARE_SEMS + ROWS_FIRST_SEMS,
     )
     s_out = Share(
         p, "yx", outg_own, outg_far, outg_ref, came_out, other_out, rows_out,
@@ -1097,7 +1180,7 @@
         p, "x", jgrad, None, joinedg_ref, came_joined, None, rows_joined,
         [dn2_ref.at[0, :features, pl.ds(512, 384)]], slots, sems, base + 3 * SHARE_SEMS,
     )
-    base += 5 * SHARE_SEMS
+    base += 4 * SHARE_SEMS + 2 * ROWS_FIRST_SEMS
 
     def natural(chip, n):
         return hint(2 * chip + (p.core + n) % 2, quarter)
@@ -1216,6 +1299,7 @@
             swap_came(6, gchip, n).wait_recv()
         weight_grad(stage_base, gchip, act, (dng_own, dng_far))
         s_down.start()
+        z_down.start()
         pl.loop(halves, 2 * halves)(before_rows)
         partial(
             8, keep, lambda rows: nt(der[0, rows, :], up2_ref[0]) + nt(der[1, rows, :], up2_ref[1]), True
@@ -1257,7 +1341,7 @@
                 share_grad(n // halves).start()
         weight_grad(stage_base, normed, der, (upg_own, upg_far))
         s_up.start()
-        s_up_high.start()
+        z_up.start()
 
     pl.run_scoped(
         middle_part,
@@ -1306,20 +1390,19 @@
 
 
     def turn(i):
-        @pl.when(i == 1)
-        def _():
-            summed.add(0)
-            summed.send(1)
-
-        @pl.when(i == 4)
-        def _():
-            s_down.first_sum()
-            s_down.second_copy().start()
-
-        @pl.when(i == 6)
-        def _():
-            s_up.first_sum()
-            s_up.second_copy().start()
+        for at, action in back_plan:
+            @pl.when(i == at)
+            def _():
+                action()
+
+    back_plan = [
+        (2, lambda: (s_down.first_sum(), s_down.second_copy().start())),
+        (3, lambda: (s_out.first_sum(), s_out.second_copy().start())),
+        (4, lambda: z_down.row_half()),
+        (5, lambda: (s_down.second_sum(), s_down.start_rows(), s_out.second_sum(), s_out.start_rows())),
+        (6, lambda: (s_up.first_sum(), s_up.second_copy().start())),
+        (7, lambda: (z_up.row_half(), z_down.row_sum(), summed.add(0), summed.send(1))),
+    ]
 
     def attend_back(*scratch):
         attention_rows_backward(heads, turn, Slopes(heads), mixed_ref, dout, att_ref, lse_ref, mixed_ref, *scratch)
@@ -1363,24 +1446,21 @@
     add_rows(sums_at[2], [sums_at[2], near_in[0]])
     grad_far.start()
     product(p.col, 3)
-    s_down.second_sum()
-    s_down.start_rows()
-
     s_up.second_sum()
     s_up.start_rows()
-    s_out.first_sum()
-    s_out.second_copy().start()
+    z_down.far_sum()
+    s_down.row_half()
+    s_out.row_half()
+    z_up.row_sum()
     sums = jnp.zeros((1, mixed_ref.shape[1]), f32)
     for n in range(tokens // 256):
         sums = sums + jnp.sum(mixed_ref[n * 256 : (n + 1) * 256, :].astype(f32), axis=0, keepdims=True)
     late[0] = jnp.zeros((8, features), f32)
     late[0, 2:3, 0 : sums.shape[1]] = sums
-    s_up_high.first_sum()
-    s_up_high.second_copy().start()
-    s_down.row_half()
-    s_up.row_half()
     s_joined.first_sum()
     s_joined.start_rows()
+    s_up.row_half()
+    z_down.twin_sum()
     grad_near[1].wait()
     grad_far.wait()
     gin = bchip.at[pl.ds(0, quarter)]
@@ -1400,14 +1480,13 @@
         gin[rows, :] = (gres[rows, :] + inverse * (scaled - one - standard * two)).astype(bf)
 
     lately.send(0)
+    s_joined.row_half()
     grad_back.start()
-    s_out.second_sum()
-    s_out.start_rows()
+    z_up.far_sum()
     s_down.row_sum()
+    z_up.twin_sum()
     s_up.row_sum()
-    s_joined.row_half()
-    s_up_high.second_sum()
-    s_up_high.start_rows()
+    s_out.row_sum()
     for n in range(1, len(summed.stages)):
         summed.add(n)
         if n + 1 < len(summed.stages):
@@ -1419,8 +1498,6 @@
         lately.add(n)
         if n + 1 < len(lately.stages):
             lately.send(n + 1)
-    s_out.row_half()
-    s_up_high.row_half()
     joined_at = lately.after(len(lately.stages) - 2)
     at = 0
     for n in range(6):
@@ -1442,9 +1519,7 @@
         at += 2
     value = jnp.sum(vectors[summed.last, 6:7, 0:128], axis=1, keepdims=True) * (scale * (1.0 / (features * token_total)))
     vector_sum_ref[at:, :] = jnp.broadcast_to(value, (vector_sum_ref.shape[0] - at, 128))
-    s_out.row_sum()
-    s_up_high.row_sum()
-    for part in (s_down, s_up, s_joined, s_out, s_up_high):
+    for part in (s_down, s_up, z_down, z_up, s_joined, s_out):
         part.finish()
     grad_back.wait_recv()
     grad_back.wait_send()
@@ -1476,7 +1551,7 @@
         bits += 1
     count = (
         3 * TRANSPOSE_SEMS + 4 + 4 * WEIGHT_SEMS + HALVES_SEMS + 6 + (3 + bits) + 1 + 6 + blocks // 2 + 12
-        + 5 * SHARE_SEMS + 2 + 2 + 2 * (6 + bits) + 3 + 4
+        + 4 * SHARE_SEMS + 2 * ROWS_FIRST_SEMS + 2 + 2 + 2 * (6 + bits) + 3 + 4
     )
     small_rows = 8 * ((6 * width // 128 + hidden // 128 + heads) // 8 + 1)
     outs = pl.pallas_call(
@@ -1485,13 +1560,15 @@
             shape((tokens, width), bf), shape((tokens, width), bf), shape((width, hidden), bf), shape((width, hidden), bf),
             shape((width, head_rows), bf), shape((width, joined_width), bf), shape((small_rows, 128), f32),
         ) + (shape((features, hidden), bf),) * 4 + (
-            shape((2, features, hidden // 2), bf), shape((2, features, hidden // 2), bf), shape((features, head_rows), bf),
-            shape((features, joined_width // 2), bf), shape((2, features, hidden // 4), bf), shape((features, hidden // 2), bf),
-            shape((features, head_rows // 2), bf), shape((2, 3, width, hidden // 4), bf), shape((3, width, hidden // 2), bf),
+            shape((1, features, hidden // 2), bf), shape((1, features, hidden // 2), bf), shape((features, head_rows), bf),
+            shape((features, joined_width // 2), bf), shape((features, hidden // 4), bf), shape((features, hidden // 4), bf),
+            shape((features, head_rows // 2), bf), shape((3, width, hidden // 4), bf), shape((3, width, hidden // 4), bf),
             shape((3, width, head_rows // 2), bf), shape((3, width, joined_width // 2), bf),
+            shape((2, 4, width, hidden // 2), bf), shape((2, 2, width, hidden // 2), bf), shape((2, width, hidden // 2), bf),
+            shape((2, width, hidden // 4), bf),
         ),
         in_specs=[vmem] + [anyspace] * 5 + [vmem] * 2,
-        out_specs=(anyspace,) * 2 + (vmem,) * 5 + (anyspace,) * 15,
+        out_specs=(anyspace,) * 2 + (vmem,) * 5 + (anyspace,) * 19,
         scratch_shapes=[
             pltpu.VMEM((quarter, features), bf), pltpu.VMEM((tokens, features), bf), pltpu.VMEM((tokens, joined_width), bf),
             pltpu.VMEM((tokens, heads * HEAD_DIM), bf), pltpu.VMEM((heads, blocks, BLOCK), f32),

time: 371 us -> 352 us (0.949)
  Pallas kernels: 345 us -> 330 us
    pallas_call x1, Pallas kernels: 345 us -> 330 us  [layer_stage(): pl.pallas_call(functools.partial(layer_kernel, heads, token_total), out_s...]
where the time goes in v7:
time: 352 us; the launch traced here: 351 us
  Pallas kernels  330 us (94%)
  other arithmetic  11.6 us (3%)
  local copies, waits for them, and re-layouts  8.97 us (3%)
    pallas_call x1, Pallas kernels, layer_stage(): pl.pallas_call(functools.partial(layer_kernel, heads, token_total), out_s...  330 us

profile of v7, /device:TPU:13, one launch (start us, length us, event | category | flops | bytes accessed | tf_op | source)
XLA Modules:
  0.0 350.9 jit_solution(11567900768151884389)
XLA Ops:
  0.7 0.7 constant_dynamic-update-slice_fusion.7
  1.3 0.7 constant_dynamic-update-slice_fusion.6
  2.0 0.7 constant_dynamic-update-slice_fusion.5
  2.6 0.7 constant_dynamic-update-slice_fusion.4
  3.3 0.7 constant_dynamic-update-slice_fusion.3
  4.0 0.7 constant_dynamic-update-slice_fusion.2
  4.6 0.7 constant_dynamic-update-slice_fusion.1
  5.3 0.7 constant_dynamic-update-slice_fusion
  6.0 0.7 convert_dynamic-update-slice_fusion
  6.7 0.0 copy-start.4
  6.7 0.6 copy-done.4
  7.3 329.7 %layer_stage.1 = (bf16[2048,256]{1,0:T(8,128)(2,1)}, bf16[2048,256]{1,0:T(8,128)(2,1)}, bf16[256,1024]{1,0:T(8,128)(2,1)}, bf16[256,1024]{1,0:T(8,128)(2,1)}, bf...) custom-call(f32[40,128]{1,0:T(8,128)} %bitcast.24, ...), custom_call_target="tpu_custom_call" | custom-call | tf_op jit(solution)/shard_map/layer_stage/pallas_call | solution.py:1557
  337.0 0.0 copy-start.3
  337.0 0.0 copy-start.2
  337.0 1.3 slice.65
  338.3 1.3 slice.54
  339.5 1.3 slice_bitcast_fusion
  340.8 1.4 slice_bitcast_fusion.1
  342.2 0.9 convert_bitcast_fusion.1
  343.2 0.8 copy.31
  344.0 1.9 convert_element_type.52
  345.9 0.0 copy-done.3
  345.9 1.1 convert_element_type.53
  347.0 0.0 copy-done.2
  347.0 0.0 copy-start
  347.0 0.1 convert_bitcast_fusion
  347.1 0.0 copy-start.1
  347.1 1.3 copy.32
  348.4 0.0 copy-done
  348.4 1.5 convert_element_type.51
  349.9 0.0 copy-done.1
  349.9 1.0 copy.43
  (1 shorter events, 0.0 us)
Async XLA Ops:
  6.7 0.6 copy-start.4
  337.0 8.9 %copy-start.3 = (bf16[256,1024]{1,0:T(8,128)(2,1)S(1)}, bf16[256,1024]{1,0:T(8,128)(2,1)}, u32[]{:S(2)}) copy-start(bf16[256,1024]{1,0:T(8,128)(2,1)} %get-tuple-element.27) | copy-start | bytes 1572868
  337.0 10.0 %copy-start.2 = (bf16[256,1024]{1,0:T(8,128)(2,1)S(1)}, bf16[256,1024]{1,0:T(8,128)(2,1)}, u32[]{:S(2)}) copy-start(bf16[256,1024]{1,0:T(8,128)(2,1)} %get-tuple-element.28) | copy-start | bytes 1572868
  347.0 1.4 copy-start
  347.1 2.8 copy-start.1

commit v8 on v7

--- a/solution.py
+++ b/solution.py
@@ -1205,7 +1205,7 @@
 
         def up_rows(side):
             def body(n):
-                rows = pl.ds(pl.multiple_of(n * ROWS, ROWS), ROWS)
+                rows = hint(n, quarter)
 
                 @pl.loop(0, hidden // wide, unroll=2)
                 def _(m):
@@ -1217,14 +1217,14 @@
 
             return body
 
-        pl.loop(0, halves)(up_rows(0))
+        up_rows(0)(0)
         for n in range(halves):
             swap_came(2, normed, n).wait_recv()
-        pl.loop(halves, 2 * halves)(up_rows(0))
+        up_rows(0)(1)
         w_up.ready(1)
-        pl.loop(0, halves)(up_rows(1))
+        up_rows(1)(0)
         w_downs[0].spread_last()
-        pl.loop(halves, 2 * halves)(up_rows(1))
+        up_rows(1)(1)
         w_downs[1].spread_last()
         for w in w_downs:
             w.ready(0)
@@ -1266,7 +1266,7 @@
         up_sums_ref[...] = jnp.zeros_like(up_sums_ref)
 
         def before_rows(n):
-            rows = pl.ds(pl.multiple_of(n * ROWS, ROWS), ROWS)
+            rows = hint(n, quarter)
 
             @pl.loop(0, 2 * hidden // wide, unroll=2)
             def _(m):
@@ -1277,9 +1277,9 @@
                 up_sums_ref[side, 0:1, cols] += jnp.sum(rounded.astype(f32), axis=0, keepdims=True)
 
         def weight_grad(slot, source, values, sinks):
-            @pl.loop(0, features // 256)
+            @pl.loop(0, features // 512)
             def _(f):
-                cols = hint(f, 256)
+                cols = hint(f, 512)
                 turned = source[:, cols].T
                 for side, sink in enumerate(sinks):
                     copy = pltpu.make_async_copy(stage.at[side], sink.at[cols], recvs.at[slot + side])
@@ -1292,15 +1292,15 @@
                     copy.start()
 
             for side, sink in enumerate(sinks):
-                pltpu.make_async_copy(stage.at[side], sink.at[pl.ds(0, 256)], recvs.at[slot + side]).wait()
-
-        pl.loop(0, halves)(before_rows)
+                pltpu.make_async_copy(stage.at[side], sink.at[pl.ds(0, 512)], recvs.at[slot + side]).wait()
+
+        before_rows(0)
         for n in range(halves):
             swap_came(6, gchip, n).wait_recv()
         weight_grad(stage_base, gchip, act, (dng_own, dng_far))
         s_down.start()
         z_down.start()
-        pl.loop(halves, 2 * halves)(before_rows)
+        before_rows(1)
         partial(
             8, keep, lambda rows: nt(der[0, rows, :], up2_ref[0]) + nt(der[1, rows, :], up2_ref[1]), True
         )
@@ -1579,7 +1579,7 @@
             pltpu.VMEM((2, 8, hidden), f32), pltpu.VMEM((2 * quarter, features), bf), pltpu.VMEM((2 * quarter, features), bf),
             pltpu.VMEM((2 * quarter, features), bf), pltpu.VMEM((quarter, features), bf), pltpu.VMEM((quarter, features), bf),
             pltpu.VMEM((quarter, features), f32), pltpu.VMEM((quarter, features), f32), pltpu.VMEM((quarter, features), bf),
-            pltpu.VMEM((2, 256, hidden), bf), pltpu.VMEM((tokens, width), bf), pltpu.VMEM((2 * quarter, head_rows), bf),
+            pltpu.VMEM((2, 512, hidden), bf), pltpu.VMEM((tokens, width), bf), pltpu.VMEM((2 * quarter, head_rows), bf),
             pltpu.VMEM((tokens, head_rows), bf), pltpu.VMEM((2, 2, quarter, width), bf),
             pltpu.VMEM((tally_slots(bits, ("row", "col", "dp")), 16, features), f32),
             pltpu.VMEM((tally_slots(bits, ("row", "col", "dp")), 8, features), f32),
@@ -1633,7 +1633,12 @@
     arrays = (
         first_gain, first_shift, out_bias, second_gain, second_shift, down_bias, up_bias, joined_bias.reshape(-1), valid,
     )
-    small = jnp.concatenate([a.astype(f32) for a in arrays]).reshape(-1, 128)
+    rows, at = sum(a.size for a in arrays), 0
+    small = jnp.zeros((rows,), f32)
+    for a in arrays:
+        small = small + jnp.pad(a.astype(f32), (at, rows - at - a.size))
+        at += a.size
+    small = small.reshape(-1, 128)
     layer_out, input_grad, up_grad, down_grad, out_grad, joined_grad, sums = layer_stage(
         small, joined_weight, layer_in, up_weight, down_weight, out_weight, teacher, cotangent, token_total
     )

time: 352 us -> 346 us (0.983)
  other arithmetic: 11.6 us -> 7.6 us
    unnamed x9 -> x0, other arithmetic: 5.35 us -> none
where the time goes in v8:
time: 346 us; the launch traced here: 344 us
  Pallas kernels  327 us (95%)
  local copies, waits for them, and re-layouts  8.37 us (2%)
  other arithmetic  7.6 us (2%)
    pallas_call x1, Pallas kernels, layer_stage(): pl.pallas_call(functools.partial(layer_kernel, heads, token_total), out_s...  327 us

profile of v8, /device:TPU:13, one launch (start us, length us, event | category | flops | bytes accessed | tf_op | source)
XLA Modules:
  0.0 344.1 jit_solution(17248250741199222749)
XLA Ops:
  0.6 0.7 convert_element_type.30
  1.3 1.4 add_bitcast_fusion.small_ref
  2.7 327.4 %layer_stage.1 = (bf16[2048,256]{1,0:T(8,128)(2,1)}, bf16[2048,256]{1,0:T(8,128)(2,1)}, bf16[256,1024]{1,0:T(8,128)(2,1)}, bf16[256,1024]{1,0:T(8,128)(2,1)}, bf...) custom-call(f32[40,128]{1,0:T(8,128)} %add_bitcast_fusion.small_ref,, ...), custom_call_target="tpu_custom_call" | custom-call | tf_op jit(solution)/shard_map/layer_stage/pallas_call | solution.py:1557
  330.2 0.0 copy-start.3
  330.2 0.0 copy-start.2
  330.2 1.3 slice.65
  331.5 1.3 slice.54
  332.7 1.3 slice_bitcast_fusion
  334.0 1.4 slice_bitcast_fusion.1
  335.4 0.9 convert_bitcast_fusion.1
  336.3 0.8 copy.31
  337.2 1.9 convert_element_type.46
  339.1 0.0 copy-done.3
  339.1 1.1 convert_element_type.47
  340.2 0.0 copy-done.2
  340.2 0.0 copy-start
  340.2 0.1 convert_bitcast_fusion
  340.3 0.0 copy-start.1
  340.3 1.3 copy.32
  341.6 0.0 copy-done
  341.6 1.5 convert_element_type.31
  343.1 0.0 copy-done.1
  343.1 1.0 copy.34
Async XLA Ops:
  330.2 9.0 %copy-start.3 = (bf16[256,1024]{1,0:T(8,128)(2,1)S(1)}, bf16[256,1024]{1,0:T(8,128)(2,1)}, u32[]{:S(2)}) copy-start(bf16[256,1024]{1,0:T(8,128)(2,1)} %get-tuple-element.27) | copy-start | bytes 1572868
  330.2 10.0 %copy-start.2 = (bf16[256,1024]{1,0:T(8,128)(2,1)S(1)}, bf16[256,1024]{1,0:T(8,128)(2,1)}, u32[]{:S(2)}) copy-start(bf16[256,1024]{1,0:T(8,128)(2,1)} %get-tuple-element.28) | copy-start | bytes 1572868
  340.2 1.4 copy-start
  340.3 2.8 copy-start.1

commit v9 on v8

--- a/solution.py
+++ b/solution.py
@@ -1065,7 +1065,6 @@
         (11, lambda: w_up.spread((2,))),
         (18, lambda: w_up.spread((3,))),
         (27, lambda: w_up.spread_last((1, 2))),
-        (29, lambda: (target.send(0), target.forward())),
         (32, lambda: w_downs[0].spread((1, 2))),
     ]
 
@@ -1130,6 +1129,8 @@
         False,
     )
     w_downs[1].spread()
+    target.send(0)
+    target.forward()
     for n in range(halves):
         take_rows(0, n).wait_recv()
 

time: 346 us -> 345 us (level)
  no operation moved by 1% of the time
where the time goes in v9:
time: 345 us; the launch traced here: 344 us
  Pallas kernels  327 us (95%)
  local copies, waits for them, and re-layouts  8.37 us (2%)
  other arithmetic  7.6 us (2%)
    pallas_call x1, Pallas kernels, layer_stage(): pl.pallas_call(functools.partial(layer_kernel, heads, token_total), out_s...  327 us

profile of v9, /device:TPU:13, one launch (start us, length us, event | category | flops | bytes accessed | tf_op | source)
XLA Modules:
  0.0 344.0 jit_solution(10107572334112237077)
XLA Ops:
  0.6 0.7 convert_element_type.30
  1.3 1.4 add_bitcast_fusion.small_ref
  2.7 327.3 %layer_stage.1 = (bf16[2048,256]{1,0:T(8,128)(2,1)}, bf16[2048,256]{1,0:T(8,128)(2,1)}, bf16[256,1024]{1,0:T(8,128)(2,1)}, bf16[256,1024]{1,0:T(8,128)(2,1)}, bf...) custom-call(f32[40,128]{1,0:T(8,128)} %add_bitcast_fusion.small_ref,, ...), custom_call_target="tpu_custom_call" | custom-call | tf_op jit(solution)/shard_map/layer_stage/pallas_call | solution.py:1558
  330.1 0.0 copy-start.3
  330.1 0.0 copy-start.2
  330.1 1.3 slice.65
  331.4 1.3 slice.54
  332.6 1.3 slice_bitcast_fusion
  333.9 1.4 slice_bitcast_fusion.1
  335.3 0.9 convert_bitcast_fusion.1
  336.3 0.8 copy.31
  337.1 1.9 convert_element_type.46
  339.0 0.0 copy-done.3
  339.0 1.1 convert_element_type.47
  340.1 0.0 copy-done.2
  340.1 0.0 copy-start
  340.1 0.1 convert_bitcast_fusion
  340.2 0.0 copy-start.1
  340.2 1.3 copy.32
  341.5 0.0 copy-done
  341.5 1.5 convert_element_type.31
  343.0 0.0 copy-done.1
  343.0 1.0 copy.34
Async XLA Ops:
  330.1 9.0 %copy-start.3 = (bf16[256,1024]{1,0:T(8,128)(2,1)S(1)}, bf16[256,1024]{1,0:T(8,128)(2,1)}, u32[]{:S(2)}) copy-start(bf16[256,1024]{1,0:T(8,128)(2,1)} %get-tuple-element.27) | copy-start | bytes 1572868
  330.1 10.0 %copy-start.2 = (bf16[256,1024]{1,0:T(8,128)(2,1)S(1)}, bf16[256,1024]{1,0:T(8,128)(2,1)}, u32[]{:S(2)}) copy-start(bf16[256,1024]{1,0:T(8,128)(2,1)} %get-tuple-element.28) | copy-start | bytes 1572868
  340.1 1.4 copy-start
  340.2 2.8 copy-start.1
